TPU v7x, 32 devices: a whole 2x2x4 slice. The times are simulated.
32 devices in a mesh: level: 4 (over x, core), dom: 8 (over z, y).
Axes of the slice: x: 2, y: 2, z: 4, core: 2. Of those that a mesh axis runs over, the one named last changes fastest.
Arguments:
- loads: float32 [4, 64, 16384], P('level', None, 'dom'), may hold values from -6 to 6
- level_blocks: bfloat16 [4, 128, 12, 128, 128], P('level', 'dom'), may hold values from -0.15625 to 0.15625
- level_cols: int32 [4, 128, 12], P('level', 'dom'), may hold values from 0 to 27, as said below
- smoother: bfloat16 [4, 128, 128, 128], P('level', 'dom'), may hold values from -0.375 to 0.375
- transfer_blocks: bfloat16 [4, 128, 8, 128, 128], P('level', 'dom'), may hold values from -0.1875 to 0.1875
- transfer_cols: int32 [4, 128, 8], P('level', 'dom'), may hold values from 0 to 15
- bound_rows: int32 [4, 8, 3, 4], P('level', 'dom'), may hold values from 0 to 15, as said below
Outputs:
- final_state: float32 [4, 64, 16384], P('level', None, 'dom')
Inputs may be any that keep to these rules, and one draw needn't show every extreme that they name: `level_cols`: values below 16 name a device's own block rows; 16 + side * 4 + j names entry j of bound_rows[g, d, side]. On sections 2 and 3 a block row below 8 names only own block rows below 8 and entries j < 2; any other block row there names only own block rows from 8 on and entries j >= 2. Each list bound_rows[g, d, side] holds 4 distinct block rows of the device on that side; its first 2 entries lie below 8, the others at or above 8.
All inputs are finite; a program needn't handle non-finite values.
Results may differ from a plain program's by a relative error of at most 0.007.
Values may be sent and summed in bfloat16 or wider, within the bound.
No kernel may reach another device: no remote copies, remote signals or barrier semaphores. Data moves between devices by JAX's collectives and lax.ppermute only.
A program may use at most 64 MiB of HBM per device.

v0:
```python
import jax
import jax.numpy as jnp
from jax import lax
from jax.sharding import PartitionSpec as P

ITERS = 2


def partner(x, axis, apart):
    return lax.ppermute(x, axis, [(i, i ^ 1 << apart) for i in range(lax.axis_size(axis))])


def passed_along(value, axis, steps):
    count = lax.axis_size(axis)
    pairs = [(source, (source + steps) % count) for source in range(count)]
    return lax.ppermute(value, axis, pairs)


def from_behind(x, axis, by):
    size = lax.axis_size(axis)
    pairs = [(i, i + by) for i in range(size) if 0 <= i + by < size]
    return lax.ppermute(x, axis, pairs)


def apply_blocks(panels, columns, blocks):
    rows_here = columns.shape[0]
    per_row = columns.shape[1]
    picked = jnp.take(panels, columns.reshape(-1), axis=1)
    picked = picked.reshape(panels.shape[0], rows_here, per_row, panels.shape[2])
    return jnp.einsum("cskb,skab->csa", picked, blocks, preferred_element_type=jnp.float32)


def smooth(panels, smoother_here):
    return jnp.einsum("csb,sab->csa", panels, smoother_here, preferred_element_type=jnp.float32)


def local(loads, level_blocks, level_cols, smoother, transfer_blocks, transfer_cols, bound_rows):
    block_rows = level_cols.shape[1]
    width_block = level_blocks.shape[-1]
    load_cols = loads.shape[1]
    list_width = bound_rows.shape[-1]
    section_fine = lax.axis_index("level") < 2
    bound_lists = bound_rows[0, 0]
    blocks_here = level_blocks[0]
    smoother_here = smoother[0]
    transfer_here = transfer_blocks[0]
    transfer_pattern = transfer_cols[0]
    load_panels = loads[0].reshape(load_cols, block_rows, width_block)
    sibling_wants = partner(bound_lists[2], "level", 0)
    slot_map = jnp.arange(block_rows + 3 * list_width, dtype=jnp.int32)
    right_wants = passed_along(bound_lists[0], "dom", -1)
    left_wants = passed_along(bound_lists[1], "dom", 1)
    pattern_ext = jnp.take(slot_map, level_cols[0])

    def extend(rounded):
        flat_panels = rounded.reshape(load_cols, block_rows * width_block)
        sibling_pack = jnp.take(rounded, sibling_wants, axis=1).reshape(
            load_cols, list_width * width_block
        )
        from_sibling = partner(sibling_pack, "level", 0)
        to_right = jnp.take(rounded, right_wants, axis=1).reshape(
            load_cols, list_width * width_block
        )
        to_left = jnp.take(rounded, left_wants, axis=1).reshape(load_cols, list_width * width_block)
        from_left = passed_along(to_right, "dom", 1)
        from_right = passed_along(to_left, "dom", -1)
        joined = jnp.concatenate([flat_panels, from_left, from_right, from_sibling], axis=1)
        return joined.reshape(load_cols, -1, width_block)

    iterate = jnp.zeros((load_cols, block_rows, width_block), jnp.float32)
    residual = load_panels
    correction = iterate
    for cycle_index in range(ITERS):
        if cycle_index > 0:
            extended = extend(iterate.astype(jnp.bfloat16))
            residual = lax.cond(
                section_fine,
                lambda: load_panels - apply_blocks(extended, pattern_ext, blocks_here),
                lambda: load_panels,
            )
        residual_b = residual.astype(jnp.bfloat16)
        arrived = from_behind(residual_b.reshape(load_cols, -1), "level", 2)
        arrived = arrived.reshape(load_cols, block_rows, width_block)
        current = lax.cond(
            section_fine,
            lambda: residual,
            lambda: load_panels + apply_blocks(arrived, transfer_pattern, transfer_here),
        )
        first_step = smooth(current.astype(jnp.bfloat16), smoother_here).astype(jnp.bfloat16)
        applied = apply_blocks(extend(first_step), pattern_ext, blocks_here)
        second_in = (current - applied).astype(jnp.bfloat16)
        correction = first_step.astype(jnp.float32) + smooth(second_in, smoother_here)
        returned = from_behind(correction.astype(jnp.bfloat16).reshape(load_cols, -1), "level", -2)
        returned = returned.reshape(load_cols, block_rows, width_block)
        iterate = lax.cond(
            section_fine,
            lambda: iterate + correction + apply_blocks(returned, transfer_pattern, transfer_here),
            lambda: iterate,
        )
    final_state = jnp.where(section_fine, iterate, correction)
    return final_state.reshape(1, load_cols, block_rows * width_block)


def solution(mesh):
    in_specs = (
        P("level", None, "dom"),
        P("level", "dom", None, None, None),
        P("level", "dom", None),
        P("level", "dom", None, None),
        P("level", "dom", None, None, None),
        P("level", "dom", None),
        P("level", "dom", None, None),
    )
    out_specs = P("level", None, "dom")
    return jax.shard_map(local, mesh=mesh, in_specs=in_specs, out_specs=out_specs, check_vma=False)
```

profile of v0, /device:TPU:0, one launch (start us, length us, event | category | flops | bytes accessed | tf_op | source)
XLA Modules:
  0.0 144.9 jit_solution(14302002168449742327)
XLA Ops:
  0.0 0.7 slice_bitcast_fusion.2
  0.8 6.0 %collective-permute-start.1 = (s32[4]{0:T(128)S(1)}, s32[4]{0:T(128)S(1)}, u32[]{:S(2)}, u32[]{:S(2)}) collective-permute-start(s32[4]{0:T(128)S(1)} %get-tuple-element.257), channel_id=1, source_target_pairs={{0,7},{1,0},{2,1},{3,2},{4,3},{5,4},{6,5},{7,6},{8,15},{9,8},{10,9... | collective-permute-start | bytes 56 | tf_op jit(solution)/shard_map/ppermute | solution.py:16
  6.8 1.1 convert_bitcast_fusion.3
  7.9 3.4 %collective-permute-start = (bf16[64,2048]{1,0:T(8,128)(2,1)S(1)}, bf16[64,2048]{1,0:T(8,128)(2,1)S(1)}, u32[]{:S(2)}, u32[]{:S(2)}) collective-permute-start(bf16[64,2048]{1,0:T(8,128)(2,1)S(1)} %convert_bitcast_fusion.3), channel_id=1, source_target_pairs={{0,16},{8,24},{1,17},{9,25},{2,18},{10,26},{3,19},{11,27},{4,20},{... | collective-permute-start | bytes 786440 | tf_op jit(solution)/shard_map/ppermute | solution.py:22
  11.3 0.7 compare_select_fusion.5
  12.0 0.8 copy.62
  13.1 1.6 %gather_fusion.5 = s32[192]{0:T(256)S(1)} fusion(s32[28]{0:T(128)S(1)} %iota.3, s32[1024]{0:T(1024)S(1)} %pad_clamp_fusion.9), kind=kCustom, calls=%fused_computation.16 | custom fusion | bytes 2304 | tf_op jit(solution)/shard_map/jit(_take)/gather | solution.py:53
  14.7 0.1 copy.120
  14.8 0.2 copy.61
  15.1 2.4 %collective-permute-done = bf16[64,2048]{1,0:T(8,128)(2,1)S(1)} collective-permute-done((bf16[64,2048]{1,0:T(8,128)(2,1)S(1)}, bf16[64,2048]{1,0:T(8,128)(2,1)S(1)}, u32[]{:S(2)}, u32[]{:S(2)}) %collective-permute-start) | collective-permute-done | bytes 262176 | tf_op jit(solution)/shard_map/ppermute | solution.py:22
  17.5 0.5 convolution_convert_fusion.1
  18.0 0.6 gather_fusion.6
  18.6 0.6 gather_fusion.8
  19.1 0.6 gather_fusion.7
  19.8 4.5 %collective-permute-start.4 = (bf16[64,512]{1,0:T(8,128)(2,1)S(1)}, bf16[64,512]{1,0:T(8,128)(2,1)S(1)}, u32[]{:S(2)}, u32[]{:S(2)}) collective-permute-start(bf16[64,512]{1,0:T(8,128)(2,1)S(1)} %copy_bitcast_fusion.20), channel_id=1, source_target_pairs={{0,7},{1,0},{2,1},{3,2},{4,3},{5,4},{6,5},{7,6},{8,15},{9,8},{10,9... | collective-permute-start | bytes 196616 | tf_op jit(solution)/shard_map/ppermute | solution.py:16
  24.6 1.6 %collective-permute-done.4 = bf16[64,512]{1,0:T(8,128)(2,1)S(1)} collective-permute-done((bf16[64,512]{1,0:T(8,128)(2,1)S(1)}, bf16[64,512]{1,0:T(8,128)(2,1)S(1)}, u32[]{:S(2)}, u32[]{:S(2)}) %collective-permute-start.4) | collective-permute-done | bytes 65568 | tf_op jit(solution)/shard_map/ppermute | solution.py:16
  26.2 5.6 %collective-permute-done.2 = bf16[64,512]{1,0:T(8,128)(2,1)S(1)} collective-permute-done((bf16[64,512]{1,0:T(8,128)(2,1)S(1)}, bf16[64,512]{1,0:T(8,128)(2,1)S(1)}, u32[]{:S(2)}, u32[]{:S(2)}) %collective-permute-start.2) | collective-permute-done | bytes 65568 | tf_op jit(solution)/shard_map/ppermute | solution.py:16
  31.7 0.1 copy_bitcast_fusion.6
  31.9 2.7 %gather_fusion.9 = bf16[192,64,128]{2,1,0:T(8,128)(2,1)} fusion(bf16[64,28,128]{2,0,1:T(8,128)(2,1)S(1)} %copy_bitcast_fusion.6, s32[1024]{0:T(1024)S(1)} %pad_clamp_fusion.5), kind=kCustom, calls=%fused_computation.14.clone | custom fusion | bytes 6292224 | tf_op jit(solution)/shard_map/jit(_take)/gather | solution.py:28
  34.6 3.4 %broadcast_select_fusion.6 = bf16[192,64,128]{2,1,0:T(8,128)(2,1)} fusion(bf16[192,64,128]{2,1,0:T(8,128)(2,1)} %gather_fusion.9, pred[192]{0:T(512)(128)(4,1)S(1)} %get-tuple-element.255), kind=kLoop, calls=%fused_computation.56 | loop fusion | flops 1572864 | bytes 6291648 | tf_op jit(solution)/shard_map/jit(_take)/select_n | solution.py:28
  38.0 6.3 %fusion.8 = f32[64,16,128]{2,0,1:T(8,128)S(1)} fusion(f32[64,16,128]{2,0,1:T(8,128)S(1)} %get-tuple-element.260, bf16[64,16,12,128]{3,0,2,1:T(8,128)(2,1)} %bitcast.266, bf16[1,16,128,128]{3,2,1,0:T(8,128)(2,1)S(1)} %copy-done, bf16[1,16,12,128,128]{4,3,2,1,0:T(8,128)(2,1)} %param.24, bf16[16,64,128]{2,1,0:T(8,128)(2,1)S(1)} %convolution_convert_fusion.1), kind=kOutput, calls=%fused_computation.63 | convolution fusion | flops 436731904 | bytes 11272192 | tf_op jit(solution)/shard_map/csb,sab->csa/dot_general | solution.py:34
  44.3 1.3 collective-permute-start.7
  45.6 15.3 %collective-permute-done.7 = bf16[64,2048]{1,0:T(8,128)(2,1)S(1)} collective-permute-done((bf16[64,2048]{1,0:T(8,128)(2,1)S(1)}, bf16[64,2048]{1,0:T(8,128)(2,1)S(1)}, u32[]{:S(2)}, u32[]{:S(2)}) %collective-permute-start.7) | collective-permute-done | bytes 262176 | tf_op jit(solution)/shard_map/ppermute | solution.py:22
  61.0 6.8 %conditional.14 = (f32[64,16,128]{2,0,1:T(8,128)S(1)}) conditional(s32[]{:T(128)} %convert_element_type.68, () %tuple.74, (s32[1,16,8]{1,2,0:T(8,128)S(1)}, bf16[64,2048]{1,0:T(8,128)(2,1)S(1)}, bf16[16,8,128,128]{3,2,1,0:T(8,128)(2,1)}, f32[64,16,128]{2,0,1:T(8,128)S(1)}) %tuple.120), branch_computations={%region_2.6_spmd, %region_3.7_spmd} | conditional | flops 269617280 | bytes 33039140 | solution.py:95
  61.1 0.1 reshape_squeeze.23
  61.3 2.2 %gather_fusion.1 = bf16[128,64,128]{2,1,0:T(8,128)(2,1)} fusion(bf16[64,16,128]{2,0,1:T(8,128)(2,1)S(1)} %copy_bitcast_fusion.1, s32[1024]{0:T(1024)S(1)} %pad_clamp_fusion.1), kind=kCustom, calls=%fused_computation.3.clone | custom fusion | bytes 4194816 | tf_op jit(solution)/shard_map/cond/branch_1_fun/jit(_take)/gather | solution.py:28
  63.4 2.0 %broadcast_select_fusion.1 = bf16[128,64,128]{2,1,0:T(8,128)(2,1)S(1)} fusion(bf16[128,64,128]{2,1,0:T(8,128)(2,1)} %gather_fusion.1, pred[128]{0:T(512)(128)(4,1)S(1)} %compare_and_fusion.1), kind=kLoop, calls=%fused_computation.24 | loop fusion | flops 1048576 | bytes 4194432 | tf_op jit(solution)/shard_map/cond/branch_1_fun/jit(_take)/select_n | solution.py:28
  65.4 0.8 copy-done.2
  66.2 1.6 %fusion.1 = f32[64,16,128]{2,0,1:T(8,128)S(1)} fusion(f32[64,16,128]{2,0,1:T(8,128)S(1)} %get-tuple-element.122, bf16[64,16,8,128]{3,0,2,1:T(8,128)(2,1)S(1)} %bitcast.270, bf16[16,8,128,128]{3,2,1,0:T(8,128)(2,1)S(1)} %copy-done.2), kind=kOutput, calls=%fused_computation.26 | convolution fusion | flops 268566528 | bytes 7340032 | tf_op jit(solution)/shard_map/cond/branch_1_fun/cskb,skab->csa/dot_general | solution.py:30
  67.9 0.6 gather_fusion.11
  68.4 0.6 gather_fusion.10
  69.0 0.6 gather_fusion.12
  69.9 4.6 %collective-permute-start.9 = (bf16[64,512]{1,0:T(8,128)(2,1)S(1)}, bf16[64,512]{1,0:T(8,128)(2,1)S(1)}, u32[]{:S(2)}, u32[]{:S(2)}) collective-permute-start(bf16[64,512]{1,0:T(8,128)(2,1)S(1)} %copy_bitcast_fusion.17), channel_id=1, source_target_pairs={{0,7},{1,0},{2,1},{3,2},{4,3},{5,4},{6,5},{7,6},{8,15},{9,8},{10,9... | collective-permute-start | bytes 196616 | tf_op jit(solution)/shard_map/ppermute | solution.py:16
  74.6 2.2 %collective-permute-done.8 = bf16[64,512]{1,0:T(8,128)(2,1)S(1)} collective-permute-done((bf16[64,512]{1,0:T(8,128)(2,1)S(1)}, bf16[64,512]{1,0:T(8,128)(2,1)S(1)}, u32[]{:S(2)}, u32[]{:S(2)}) %collective-permute-start.8) | collective-permute-done | bytes 65568 | tf_op jit(solution)/shard_map/ppermute | solution.py:16
  76.9 9.1 %conditional.15 = (f32[64,16,128]{2,0,1:T(8,128)S(1)}) conditional(s32[]{:T(128)} %convert_element_type.68, f32[64,16,128]{2,0,1:T(8,128)S(1)} %copy.61, (s32[16,12]{1,0:T(8,128)S(1)}, bf16[64,3584]{1,0:T(8,128)(2,1)S(1)}, bf16[16,12,128,128]{3,2,1,0:T(8,128)(2,1)}, f32[64,16,128]{2,1,0:T(8,128)S(1)}, s32[192]{0:T(256)S(1)}, ...), branch_computations={%region_4.8_spmd, %region_5.9_spmd.clone} | conditional | flops 404361216 | bytes 49168048 | solution.py:76
  77.0 0.1 reshape.384
  77.1 0.1 copy_bitcast_fusion.4
  77.2 2.7 %gather_fusion.4 = bf16[192,64,128]{2,1,0:T(8,128)(2,1)} fusion(bf16[64,28,128]{2,0,1:T(8,128)(2,1)S(1)} %copy_bitcast_fusion.4, s32[1024]{0:T(1024)S(1)} %pad_clamp_fusion.4), kind=kCustom, calls=%fused_computation.2.clone.clone | custom fusion | bytes 6292224 | tf_op jit(solution)/shard_map/cond/branch_1_fun/jit(_take)/gather | solution.py:28
  79.9 2.4 %broadcast_select_fusion.4 = bf16[192,64,128]{2,1,0:T(8,128)(2,1)S(1)} fusion(bf16[192,64,128]{2,1,0:T(8,128)(2,1)} %gather_fusion.4, pred[192]{0:T(512)(128)(4,1)S(1)} %compare_and_fusion.5), kind=kLoop, calls=%fused_computation.45 | loop fusion | flops 1572864 | bytes 6291648 | tf_op jit(solution)/shard_map/cond/branch_1_fun/jit(_take)/select_n | solution.py:28
  82.4 1.3 copy-done.5
  83.7 2.3 %fusion.4 = f32[64,16,128]{2,0,1:T(8,128)S(1)} fusion(bf16[64,16,12,128]{3,0,2,1:T(8,128)(2,1)S(1)} %bitcast.267, bf16[16,12,128,128]{3,2,1,0:T(8,128)(2,1)S(1)} %copy-done.5, f32[64,16,128]{2,1,0:T(8,128)S(1)} %get-tuple-element.234), kind=kOutput, calls=%fused_computation.47 | convolution fusion | flops 402784256 | bytes 10485760 | tf_op jit(solution)/shard_map/cond/branch_1_fun/cskb,skab->csa/dot_general | solution.py:30
  86.0 1.3 collective-permute-start.11
  87.3 5.4 %collective-permute-done.11 = bf16[64,2048]{1,0:T(8,128)(2,1)S(1)} collective-permute-done((bf16[64,2048]{1,0:T(8,128)(2,1)S(1)}, bf16[64,2048]{1,0:T(8,128)(2,1)S(1)}, u32[]{:S(2)}, u32[]{:S(2)}) %collective-permute-start.11) | collective-permute-done | bytes 262176 | tf_op jit(solution)/shard_map/ppermute | solution.py:22
  92.7 0.5 convolution_convert_fusion
  93.1 0.6 gather_fusion.13
  93.7 0.6 gather_fusion.15
  94.3 0.6 gather_fusion.14
  95.1 5.2 %collective-permute-start.13 = (bf16[64,512]{1,0:T(8,128)(2,1)S(1)}, bf16[64,512]{1,0:T(8,128)(2,1)S(1)}, u32[]{:S(2)}, u32[]{:S(2)}) collective-permute-start(bf16[64,512]{1,0:T(8,128)(2,1)S(1)} %copy_bitcast_fusion.14), channel_id=1, source_target_pairs={{0,7},{1,0},{2,1},{3,2},{4,3},{5,4},{6,5},{7,6},{8,15},{9,8},{10,9... | collective-permute-start | bytes 196616 | tf_op jit(solution)/shard_map/ppermute | solution.py:16
  100.4 1.9 %collective-permute-done.13 = bf16[64,512]{1,0:T(8,128)(2,1)S(1)} collective-permute-done((bf16[64,512]{1,0:T(8,128)(2,1)S(1)}, bf16[64,512]{1,0:T(8,128)(2,1)S(1)}, u32[]{:S(2)}, u32[]{:S(2)}) %collective-permute-start.13) | collective-permute-done | bytes 65568 | tf_op jit(solution)/shard_map/ppermute | solution.py:16
  102.2 5.3 %collective-permute-done.12 = bf16[64,512]{1,0:T(8,128)(2,1)S(1)} collective-permute-done((bf16[64,512]{1,0:T(8,128)(2,1)S(1)}, bf16[64,512]{1,0:T(8,128)(2,1)S(1)}, u32[]{:S(2)}, u32[]{:S(2)}) %collective-permute-start.12) | collective-permute-done | bytes 65568 | tf_op jit(solution)/shard_map/ppermute | solution.py:16
  107.5 0.1 copy_bitcast_fusion.5
  107.6 2.7 %gather_fusion.16 = bf16[192,64,128]{2,1,0:T(8,128)(2,1)} fusion(bf16[64,28,128]{2,0,1:T(8,128)(2,1)S(1)} %copy_bitcast_fusion.5, s32[1024]{0:T(1024)S(1)} %pad_clamp_fusion.5), kind=kCustom, calls=%fused_computation.15.clone | custom fusion | bytes 6292224 | tf_op jit(solution)/shard_map/jit(_take)/gather | solution.py:28
  110.3 3.4 %broadcast_select_fusion.5 = bf16[192,64,128]{2,1,0:T(8,128)(2,1)} fusion(bf16[192,64,128]{2,1,0:T(8,128)(2,1)} %gather_fusion.16, pred[192]{0:T(512)(128)(4,1)S(1)} %get-tuple-element.255), kind=kLoop, calls=%fused_computation.55 | loop fusion | flops 1572864 | bytes 6291648 | tf_op jit(solution)/shard_map/jit(_take)/select_n | solution.py:28
  113.8 6.3 %fusion.9 = f32[64,16,128]{2,0,1:T(8,128)S(1)} fusion(f32[64,16,128]{2,0,1:T(8,128)S(1)} %get-tuple-element.263, bf16[64,16,12,128]{3,0,2,1:T(8,128)(2,1)} %bitcast.265, bf16[1,16,128,128]{3,2,1,0:T(8,128)(2,1)S(1)} %copy-done, bf16[16,64,128]{2,1,0:T(8,128)(2,1)S(1)} %convolution_convert_fusion, bf16[1,16,12,128,128]{4,3,2,1,0:T(8,128)(2,1)} %param.24), kind=kOutput, calls=%fused_computation.64 | convolution fusion | flops 436731904 | bytes 11272192 | tf_op jit(solution)/shard_map/csb,sab->csa/dot_general | solution.py:34
  120.1 1.3 collective-permute-start.15
  121.4 15.4 %collective-permute-done.15 = bf16[64,2048]{1,0:T(8,128)(2,1)S(1)} collective-permute-done((bf16[64,2048]{1,0:T(8,128)(2,1)S(1)}, bf16[64,2048]{1,0:T(8,128)(2,1)S(1)}, u32[]{:S(2)}, u32[]{:S(2)}) %collective-permute-start.15) | collective-permute-done | bytes 262176 | tf_op jit(solution)/shard_map/ppermute | solution.py:22
  136.8 6.8 %conditional.17 = (f32[64,16,128]{2,0,1:T(8,128)S(1)}) conditional(s32[]{:T(128)} %convert_element_type.68, f32[64,16,128]{2,0,1:T(8,128)S(1)} %get-tuple-element.261, (f32[64,16,128]{2,0,1:T(8,128)S(1)}, f32[64,16,128]{2,0,1:T(8,128)S(1)}, bf16[64,2048]{1,0:T(8,128)(2,1)S(1)}, s32[1,16,8]{1,2,0:T(8,128)S(1)}, ...), branch_computations={%region_8.12_spmd, %region_9.13_spmd} | conditional | flops 269748352 | bytes 33563428 | solution.py:95
  136.9 0.1 reshape_squeeze.25
  137.1 2.2 %gather_fusion.3 = bf16[128,64,128]{2,1,0:T(8,128)(2,1)} fusion(bf16[64,16,128]{2,0,1:T(8,128)(2,1)S(1)} %copy_bitcast_fusion.3, s32[1024]{0:T(1024)S(1)} %pad_clamp_fusion.3), kind=kCustom, calls=%fused_computation.5.clone | custom fusion | bytes 4194816 | tf_op jit(solution)/shard_map/cond/branch_1_fun/jit(_take)/gather | solution.py:28
  139.3 2.0 %broadcast_select_fusion.3 = bf16[128,64,128]{2,1,0:T(8,128)(2,1)S(1)} fusion(bf16[128,64,128]{2,1,0:T(8,128)(2,1)} %gather_fusion.3, pred[128]{0:T(512)(128)(4,1)S(1)} %compare_and_fusion.3), kind=kLoop, calls=%fused_computation.38 | loop fusion | flops 1048576 | bytes 4194432 | tf_op jit(solution)/shard_map/cond/branch_1_fun/jit(_take)/select_n | solution.py:28
  141.3 0.8 copy-done.4
  142.1 1.6 %fusion.3 = f32[64,16,128]{2,0,1:T(8,128)S(1)} fusion(bf16[64,16,8,128]{3,0,2,1:T(8,128)(2,1)S(1)} %bitcast.271, bf16[16,8,128,128]{3,2,1,0:T(8,128)(2,1)S(1)} %copy-done.4, f32[64,16,128]{2,0,1:T(8,128)S(1)} %get-tuple-element.134, f32[64,16,128]{2,0,1:T(8,128)S(1)} %get-tuple-element.135), kind=kOutput, calls=%fused_computation.40 | convolution fusion | flops 268697600 | bytes 7864320 | tf_op jit(solution)/shard_map/cond/branch_1_fun/cskb,skab->csa/dot_general | solution.py:30
  143.7 0.3 copy.88
  144.0 0.9 reshape.183
  (77 shorter events, 2.1 us)
Async XLA Ops:
  0.0 17.5 %copy-start = (bf16[1,16,128,128]{3,2,1,0:T(8,128)(2,1)S(1)}, bf16[1,16,128,128]{3,2,1,0:T(8,128)(2,1)}, u32[]{:S(2)}) copy-start(bf16[1,16,128,128]{3,2,1,0:T(8,128)(2,1)} %param.26) | copy-start | bytes 1572868
  0.8 14.2 %collective-permute-start.1 = (s32[4]{0:T(128)S(1)}, s32[4]{0:T(128)S(1)}, u32[]{:S(2)}, u32[]{:S(2)}) collective-permute-start(s32[4]{0:T(128)S(1)} %get-tuple-element.257), channel_id=1, source_target_pairs={{0,7},{1,0},{2,1},{3,2},{4,3},{5,4},{6,5},{7,6},{8,15},{9,8},{10,9... | collective-permute-start | bytes 56 | tf_op jit(solution)/shard_map/ppermute | solution.py:16
  6.8 8.2 %collective-permute-start.5 = (s32[4]{0:T(128)S(1)}, s32[4]{0:T(128)S(1)}, u32[]{:S(2)}, u32[]{:S(2)}) collective-permute-start(s32[4]{0:T(128)S(1)} %get-tuple-element.258), channel_id=1, source_target_pairs={{0,8},{8,0},{16,24},{24,16},{1,9},{9,1},{17,25},{25,17},{2,10},{10... | collective-permute-start | bytes 56 | tf_op jit(solution)/shard_map/ppermute | solution.py:10
  6.8 8.3 %collective-permute-start.3 = (s32[4]{0:T(128)S(1)}, s32[4]{0:T(128)S(1)}, u32[]{:S(2)}, u32[]{:S(2)}) collective-permute-start(s32[4]{0:T(128)S(1)} %get-tuple-element.259), channel_id=1, source_target_pairs={{0,1},{1,2},{2,3},{3,4},{4,5},{5,6},{6,7},{7,0},{8,9},{9,10},{10,1... | collective-permute-start | bytes 56 | tf_op jit(solution)/shard_map/ppermute | solution.py:16
  7.9 9.6 %collective-permute-start = (bf16[64,2048]{1,0:T(8,128)(2,1)S(1)}, bf16[64,2048]{1,0:T(8,128)(2,1)S(1)}, u32[]{:S(2)}, u32[]{:S(2)}) collective-permute-start(bf16[64,2048]{1,0:T(8,128)(2,1)S(1)} %convert_bitcast_fusion.3), channel_id=1, source_target_pairs={{0,16},{8,24},{1,17},{9,25},{2,18},{10,26},{3,19},{11,27},{4,20},{... | collective-permute-start | bytes 786440 | tf_op jit(solution)/shard_map/ppermute | solution.py:22
  13.0 1.6 %copy-start.6 = (f32[1,64,2048]{2,1,0:T(8,128)S(1)}, f32[1,64,2048]{2,1,0:T(8,128)}, u32[]{:S(2)}) copy-start(f32[1,64,2048]{2,1,0:T(8,128)} %param.23) | copy-start | bytes 1572868
  13.0 4.4 %copy-start.7 = (s32[1,16,8]{1,2,0:T(8,128)S(1)}, s32[1,16,8]{1,2,0:T(8,128)}, u32[]{:S(2)}) copy-start(s32[1,16,8]{1,2,0:T(8,128)} %param.28) | copy-start | bytes 1540
  19.8 6.4 %collective-permute-start.4 = (bf16[64,512]{1,0:T(8,128)(2,1)S(1)}, bf16[64,512]{1,0:T(8,128)(2,1)S(1)}, u32[]{:S(2)}, u32[]{:S(2)}) collective-permute-start(bf16[64,512]{1,0:T(8,128)(2,1)S(1)} %copy_bitcast_fusion.20), channel_id=1, source_target_pairs={{0,7},{1,0},{2,1},{3,2},{4,3},{5,4},{6,5},{7,6},{8,15},{9,8},{10,9... | collective-permute-start | bytes 196616 | tf_op jit(solution)/shard_map/ppermute | solution.py:16
  24.3 1.8 %collective-permute-start.6 = (bf16[64,512]{1,0:T(8,128)(2,1)S(1)}, bf16[64,512]{1,0:T(8,128)(2,1)S(1)}, u32[]{:S(2)}, u32[]{:S(2)}) collective-permute-start(bf16[64,512]{1,0:T(8,128)(2,1)S(1)} %copy_bitcast_fusion.19), channel_id=1, source_target_pairs={{0,8},{8,0},{16,24},{24,16},{1,9},{9,1},{17,25},{25,17},{2,10},{10... | collective-permute-start | bytes 196616 | tf_op jit(solution)/shard_map/ppermute | solution.py:10
  24.5 7.2 %collective-permute-start.2 = (bf16[64,512]{1,0:T(8,128)(2,1)S(1)}, bf16[64,512]{1,0:T(8,128)(2,1)S(1)}, u32[]{:S(2)}, u32[]{:S(2)}) collective-permute-start(bf16[64,512]{1,0:T(8,128)(2,1)S(1)} %copy_bitcast_fusion.21), channel_id=1, source_target_pairs={{0,1},{1,2},{2,3},{3,4},{4,5},{5,6},{6,7},{7,0},{8,9},{9,10},{10,1... | collective-permute-start | bytes 196616 | tf_op jit(solution)/shard_map/ppermute | solution.py:16
  44.3 16.6 %collective-permute-start.7 = (bf16[64,2048]{1,0:T(8,128)(2,1)S(1)}, bf16[64,2048]{1,0:T(8,128)(2,1)S(1)}, u32[]{:S(2)}, u32[]{:S(2)}) collective-permute-start(bf16[64,2048]{1,0:T(8,128)(2,1)S(1)} %copy_bitcast_fusion.11), channel_id=1, source_target_pairs={{16,0},{24,8},{17,1},{25,9},{18,2},{26,10},{19,3},{27,11},{20,4},{... | collective-permute-start | bytes 786440 | tf_op jit(solution)/shard_map/ppermute | solution.py:22
  63.4 2.8 %copy-start.2 = (bf16[16,8,128,128]{3,2,1,0:T(8,128)(2,1)S(1)}, bf16[16,8,128,128]{3,2,1,0:T(8,128)(2,1)}, u32[]{:S(2)}) copy-start(bf16[16,8,128,128]{3,2,1,0:T(8,128)(2,1)} %get-tuple-element.125) | copy-start | bytes 12582916 | tf_op jit(solution)/shard_map/cond
  69.8 7.0 %collective-permute-start.8 = (bf16[64,512]{1,0:T(8,128)(2,1)S(1)}, bf16[64,512]{1,0:T(8,128)(2,1)S(1)}, u32[]{:S(2)}, u32[]{:S(2)}) collective-permute-start(bf16[64,512]{1,0:T(8,128)(2,1)S(1)} %copy_bitcast_fusion.18), channel_id=1, source_target_pairs={{0,1},{1,2},{2,3},{3,4},{4,5},{5,6},{6,7},{7,0},{8,9},{9,10},{10,1... | collective-permute-start | bytes 196616 | tf_op jit(solution)/shard_map/ppermute | solution.py:16
  69.9 7.0 %collective-permute-start.10 = (bf16[64,512]{1,0:T(8,128)(2,1)S(1)}, bf16[64,512]{1,0:T(8,128)(2,1)S(1)}, u32[]{:S(2)}, u32[]{:S(2)}) collective-permute-start(bf16[64,512]{1,0:T(8,128)(2,1)S(1)} %copy_bitcast_fusion.16), channel_id=1, source_target_pairs={{0,8},{8,0},{16,24},{24,16},{1,9},{9,1},{17,25},{25,17},{2,10},{10... | collective-permute-start | bytes 196616 | tf_op jit(solution)/shard_map/ppermute | solution.py:10
  69.9 6.9 %collective-permute-start.9 = (bf16[64,512]{1,0:T(8,128)(2,1)S(1)}, bf16[64,512]{1,0:T(8,128)(2,1)S(1)}, u32[]{:S(2)}, u32[]{:S(2)}) collective-permute-start(bf16[64,512]{1,0:T(8,128)(2,1)S(1)} %copy_bitcast_fusion.17), channel_id=1, source_target_pairs={{0,7},{1,0},{2,1},{3,2},{4,3},{5,4},{6,5},{7,6},{8,15},{9,8},{10,9... | collective-permute-start | bytes 196616 | tf_op jit(solution)/shard_map/ppermute | solution.py:16
  79.9 3.7 %copy-start.5 = (bf16[16,12,128,128]{3,2,1,0:T(8,128)(2,1)S(1)}, bf16[16,12,128,128]{3,2,1,0:T(8,128)(2,1)}, u32[]{:S(2)}) copy-start(bf16[16,12,128,128]{3,2,1,0:T(8,128)(2,1)} %get-tuple-element.233) | copy-start | bytes 18874372 | tf_op jit(solution)/shard_map/cond
  86.0 6.7 %collective-permute-start.11 = (bf16[64,2048]{1,0:T(8,128)(2,1)S(1)}, bf16[64,2048]{1,0:T(8,128)(2,1)S(1)}, u32[]{:S(2)}, u32[]{:S(2)}) collective-permute-start(bf16[64,2048]{1,0:T(8,128)(2,1)S(1)} %copy_bitcast_fusion.9), channel_id=1, source_target_pairs={{0,16},{8,24},{1,17},{9,25},{2,18},{10,26},{3,19},{11,27},{4,20},{... | collective-permute-start | bytes 786440 | tf_op jit(solution)/shard_map/ppermute | solution.py:22
  95.1 7.1 %collective-permute-start.13 = (bf16[64,512]{1,0:T(8,128)(2,1)S(1)}, bf16[64,512]{1,0:T(8,128)(2,1)S(1)}, u32[]{:S(2)}, u32[]{:S(2)}) collective-permute-start(bf16[64,512]{1,0:T(8,128)(2,1)S(1)} %copy_bitcast_fusion.14), channel_id=1, source_target_pairs={{0,7},{1,0},{2,1},{3,2},{4,3},{5,4},{6,5},{7,6},{8,15},{9,8},{10,9... | collective-permute-start | bytes 196616 | tf_op jit(solution)/shard_map/ppermute | solution.py:16
  100.3 1.9 %collective-permute-start.14 = (bf16[64,512]{1,0:T(8,128)(2,1)S(1)}, bf16[64,512]{1,0:T(8,128)(2,1)S(1)}, u32[]{:S(2)}, u32[]{:S(2)}) collective-permute-start(bf16[64,512]{1,0:T(8,128)(2,1)S(1)} %copy_bitcast_fusion.13), channel_id=1, source_target_pairs={{0,8},{8,0},{16,24},{24,16},{1,9},{9,1},{17,25},{25,17},{2,10},{10... | collective-permute-start | bytes 196616 | tf_op jit(solution)/shard_map/ppermute | solution.py:10
  100.3 7.2 %collective-permute-start.12 = (bf16[64,512]{1,0:T(8,128)(2,1)S(1)}, bf16[64,512]{1,0:T(8,128)(2,1)S(1)}, u32[]{:S(2)}, u32[]{:S(2)}) collective-permute-start(bf16[64,512]{1,0:T(8,128)(2,1)S(1)} %copy_bitcast_fusion.15), channel_id=1, source_target_pairs={{0,1},{1,2},{2,3},{3,4},{4,5},{5,6},{6,7},{7,0},{8,9},{9,10},{10,1... | collective-permute-start | bytes 196616 | tf_op jit(solution)/shard_map/ppermute | solution.py:16
  120.1 16.7 %collective-permute-start.15 = (bf16[64,2048]{1,0:T(8,128)(2,1)S(1)}, bf16[64,2048]{1,0:T(8,128)(2,1)S(1)}, u32[]{:S(2)}, u32[]{:S(2)}) collective-permute-start(bf16[64,2048]{1,0:T(8,128)(2,1)S(1)} %copy_bitcast_fusion.7), channel_id=1, source_target_pairs={{16,0},{24,8},{17,1},{25,9},{18,2},{26,10},{19,3},{27,11},{20,4},{... | collective-permute-start | bytes 786440 | tf_op jit(solution)/shard_map/ppermute | solution.py:22
  139.2 2.8 %copy-start.4 = (bf16[16,8,128,128]{3,2,1,0:T(8,128)(2,1)S(1)}, bf16[16,8,128,128]{3,2,1,0:T(8,128)(2,1)}, u32[]{:S(2)}) copy-start(bf16[16,8,128,128]{3,2,1,0:T(8,128)(2,1)} %get-tuple-element.138) | copy-start | bytes 12582916 | tf_op jit(solution)/shard_map/cond
where the time goes:
time: 145 us
  waiting for transfers between devices  55 us (38%)
  starting transfers between devices  27.9 us (19%)
  local copies, waits for them, and re-layouts  26 us (18%)
  matrix products  19 us (13%)
  other arithmetic  16.4 us (11%)
    ppermute x4, waiting for transfers between devices, from_behind(): return lax.ppermute(x, axis, pairs)  38.5 us
    ppermute x8, starting transfers between devices, passed_along(): return lax.ppermute(value, axis, pairs)  20.5 us
    ppermute x8, waiting for transfers between devices, passed_along(): return lax.ppermute(value, axis, pairs)  16.5 us
    dot_general x4, matrix products, smooth(): jnp.einsum('csb,sab->csa', panels, smoother_here, preferred_element_type=...  13.6 us
    select_n x8, other arithmetic, apply_blocks(): picked = jnp.take(panels, columns.reshape(-1), axis=1)  13.3 us
    gather x5, local copies, waits for them, and re-layouts, apply_blocks(): picked = jnp.take(panels, columns.reshape(-1), axis=1)  12.4 us
    ppermute x4, starting transfers between devices, from_behind(): return lax.ppermute(x, axis, pairs)  7.3 us
    dot_general x3, matrix products, apply_blocks(): jnp.einsum('cskb,skab->csa', picked, blocks, preferred_element_type=jnp.f...  5.41 us
  transfers between devices with their start and end apart: 16, of which 9 were waited for; matrix products, arithmetic and copies ran while one was open for 3% of the time, Pallas kernels for 0%

commit v1 on v0

v1 whole, which is shorter than its diff:
```python
import jax
import jax.numpy as jnp
from jax import lax
from jax.experimental import pallas as pl
from jax.experimental.pallas import tpu as pltpu
from jax.sharding import PartitionSpec as P

ITERS = 2
VMEM = pl.BlockSpec(memory_space=pltpu.VMEM)
SMEM = pl.BlockSpec(memory_space=pltpu.SMEM)
NT = (((1,), (1,)), ((), ()))


def partner(x, axis, apart):
    return lax.ppermute(x, axis, [(i, i ^ 1 << apart) for i in range(lax.axis_size(axis))])


def passed_along(value, axis, steps):
    count = lax.axis_size(axis)
    pairs = [(source, (source + steps) % count) for source in range(count)]
    return lax.ppermute(value, axis, pairs)


def from_behind(x, axis, by):
    size = lax.axis_size(axis)
    pairs = [(i, i + by) for i in range(size) if 0 <= i + by < size]
    return lax.ppermute(x, axis, pairs)


def times(panel, block):
    return lax.dot_general(panel, block, NT, preferred_element_type=jnp.float32)


def gathered(source, table, row, base, blocks):
    count = blocks.shape[1]
    left = jnp.concatenate([source[table[base + row * count + k]] for k in range(count)], axis=1)
    right = jnp.concatenate([blocks[row, k] for k in range(count)], axis=1)
    return times(left, right)


def packed(source, table, base, outs):
    for side, out in enumerate(outs):
        for j in range(out.shape[0]):
            out[j] = source[table[base + side * out.shape[0] + j]]


def first_body(where, table, loads, residual, arrived, transfer, smoother, current, first, *outs):
    rows, _, width = first.shape

    def step(i, value):
        current[i] = value
        first[i] = times(value.astype(jnp.bfloat16), smoother[i]).astype(jnp.bfloat16)

    @pl.when(table[where["fine"]] == 1)
    def _():
        for i in range(rows):
            step(i, residual[i])

    @pl.when(table[where["fine"]] == 0)
    def _():
        for i in range(rows):
            load = loads[:, i * width : (i + 1) * width]
            step(i, load + gathered(arrived, table, i, where["transfer"], transfer))

    packed(first, table, where["wanted"], outs)


def extended(own, sides, scratch):
    rows = own.shape[0]
    for i in range(rows):
        scratch[i] = own[i]
    for side, ref in enumerate(sides):
        for j in range(ref.shape[0]):
            scratch[rows + side * ref.shape[0] + j] = ref[j]


def second_body(where, table, current, first, left, right, sibling, blocks, smoother, full, rounded, scratch):
    extended(first, (left, right, sibling), scratch)
    for i in range(first.shape[0]):
        applied = gathered(scratch, table, i, where["level"], blocks)
        second = (current[i] - applied).astype(jnp.bfloat16)
        value = first[i].astype(jnp.float32) + times(second, smoother[i])
        full[i] = value
        rounded[i] = value.astype(jnp.bfloat16)


def update_body(where, table, correction, arrived, transfer, iterate, rounded, *outs):
    @pl.when(table[where["fine"]] == 1)
    def _():
        for i in range(iterate.shape[0]):
            value = correction[i] + gathered(arrived, table, i, where["transfer"], transfer)
            iterate[i] = value
            rounded[i] = value.astype(jnp.bfloat16)
        packed(rounded, table, where["wanted"], outs)


def residual_body(where, table, loads, rounded, left, right, sibling, blocks, residual, sent, scratch):
    @pl.when(table[where["fine"]] == 1)
    def _():
        width = residual.shape[2]
        extended(rounded, (left, right, sibling), scratch)
        for i in range(residual.shape[0]):
            load = loads[:, i * width : (i + 1) * width]
            value = load - gathered(scratch, table, i, where["level"], blocks)
            residual[i] = value
            sent[i] = value.astype(jnp.bfloat16)


def last_body(where, table, iterate, correction, arrived, transfer, out):
    width = correction.shape[2]

    @pl.when(table[where["fine"]] == 1)
    def _():
        for i in range(correction.shape[0]):
            value = iterate[i] + correction[i]
            value = value + gathered(arrived, table, i, where["transfer"], transfer)
            out[:, i * width : (i + 1) * width] = value

    @pl.when(table[where["fine"]] == 0)
    def _():
        for i in range(correction.shape[0]):
            out[:, i * width : (i + 1) * width] = correction[i]


def local(loads, level_blocks, level_cols, smoother, transfer_blocks, transfer_cols, bound_rows):
    block_rows, level_count = level_cols.shape[1:]
    width = level_blocks.shape[-1]
    load_cols = loads.shape[1]
    list_width = bound_rows.shape[-1]
    transfer_count = transfer_cols.shape[-1]
    section_fine = lax.axis_index("level") < 2
    bound_lists = bound_rows[0, 0]
    blocks, smooth, transfer, loads = level_blocks[0], smoother[0], transfer_blocks[0], loads[0]

    load_panels = loads.reshape(load_cols, block_rows, width).transpose(1, 0, 2)
    sent = load_panels.astype(jnp.bfloat16)
    arrived = from_behind(sent, "level", 2)

    wanted = (
        passed_along(bound_lists[0], "dom", -1),
        passed_along(bound_lists[1], "dom", 1),
        partner(bound_lists[2], "level", 0),
    )
    fine = section_fine.astype(jnp.int32).reshape(1)
    parts = {
        "fine": fine,
        "level": level_cols.reshape(-1),
        "transfer": transfer_cols.reshape(-1),
        "wanted": jnp.concatenate(wanted),
    }
    where, at = {}, 0
    for name, part in parts.items():
        where[name] = at
        at += part.shape[0]
    table = jnp.concatenate(list(parts.values()))

    panels = (block_rows, load_cols, width)
    wide = jax.ShapeDtypeStruct(panels, jnp.float32)
    narrow = jax.ShapeDtypeStruct(panels, jnp.bfloat16)
    listed = jax.ShapeDtypeStruct((list_width, load_cols, width), jnp.bfloat16)
    extension = pltpu.VMEM((block_rows + 3 * list_width, load_cols, width), jnp.bfloat16)

    def run(body, outs, *args, scratch=(), name=None):
        def kernel(*refs):
            body(where, *refs)

        return pl.pallas_call(
            kernel,
            out_shape=outs,
            in_specs=[SMEM] + [VMEM] * len(args),
            out_specs=jax.tree.map(lambda _: VMEM, outs),
            scratch_shapes=list(scratch),
            name=name,
            compiler_params=pltpu.CompilerParams(vmem_limit_bytes=24 << 20),
        )(table, *args)

    def exchanged(packs):
        to_right, to_left, to_sibling = packs
        return (
            passed_along(to_right, "dom", 1),
            passed_along(to_left, "dom", -1),
            partner(to_sibling, "level", 0),
        )

    residual = load_panels
    iterate = None
    for cycle_index in range(ITERS):
        if cycle_index > 0:
            residual, sent = run(
                residual_body, (wide, narrow), loads, rounded, *sides, blocks,
                scratch=[extension], name="residual",
            )
            arrived = from_behind(sent, "level", 2)
        current, first, *packs = run(
            first_body, (wide, narrow, listed, listed, listed),
            loads, residual, arrived, transfer, smooth, name="first",
        )
        correction, rounded = run(
            second_body, (wide, narrow), current, first, *exchanged(packs), blocks, smooth,
            scratch=[extension], name="second",
        )
        returned = from_behind(rounded, "level", -2)
        if cycle_index + 1 < ITERS:
            if iterate is not None:
                correction = iterate + correction
            iterate, rounded, *packs = run(
                update_body, (wide, narrow, listed, listed, listed),
                correction, returned, transfer, name="update",
            )
            sides = exchanged(packs)
    out = jax.ShapeDtypeStruct((load_cols, block_rows * width), jnp.float32)
    final = run(last_body, out, iterate, correction, returned, transfer, name="last")
    return final[None]


def solution(mesh):
    in_specs = (
        P("level", None, "dom"),
        P("level", "dom", None, None, None),
        P("level", "dom", None),
        P("level", "dom", None, None),
        P("level", "dom", None, None, None),
        P("level", "dom", None),
        P("level", "dom", None, None),
    )
    out_specs = P("level", None, "dom")
    return jax.shard_map(local, mesh=mesh, in_specs=in_specs, out_specs=out_specs, check_vma=False)
```

time: 145 us -> 96.5 us (0.67)
  Pallas kernels: 0 us -> 22.1 us
  waiting for transfers between devices: 55 us -> 35.1 us
  matrix products: 19 us -> 0 us
  other arithmetic: 16.4 us -> 0 us
  local copies, waits for them, and re-layouts: 26 us -> 11.1 us
    pallas_call x0 -> x7, Pallas kernels: none -> 22.1 us  [run(): pl.pallas_call(kernel, out_shape=outs, in_specs=[SMEM] + [VMEM] * len(arg...]
    gather x16 -> x0, local copies, waits for them, and re-layouts: 19.1 us -> none  [the longest x5 12.4 us: apply_blocks(): picked = jnp.take(panels, columns.reshape(-1), axis=1)]
    dot_general x7 -> x0, matrix products: 19 us -> none  [the longest x4 13.6 us: smooth(): jnp.einsum('csb,sab->csa', panels, smoother_here, preferred_element_type=...]
    ppermute x4, waiting for transfers between devices: 38.5 us -> 24 us  [from_behind(): return lax.ppermute(x, axis, pairs)]
    select_n x14 -> x0, other arithmetic: 14.1 us -> none  [the longest x8 13.3 us: apply_blocks(): picked = jnp.take(panels, columns.reshape(-1), axis=1)]
    unnamed x8 -> x17, local copies, waits for them, and re-layouts: 0.88 us -> 9.78 us
    ppermute x8, waiting for transfers between devices: 16.5 us -> 11.1 us  [passed_along(): return lax.ppermute(value, axis, pairs)]
    cond x6 -> x0, local copies, waits for them, and re-layouts: 2.91 us -> none
  transfers between devices with their start and end apart: 16 -> 16, of which waited for: 9 -> 7; matrix products, arithmetic and copies ran while one was open for 3% -> 3% of each run, Pallas kernels for 0% -> 0%
where the time goes in v1:
time: 96.5 us; the launch traced here: 96.1 us
  waiting for transfers between devices  35.1 us (36%)
  starting transfers between devices  27.7 us (29%)
  Pallas kernels  22.1 us (23%)
  local copies, waits for them, and re-layouts  11.1 us (12%)
    ppermute x4, waiting for transfers between devices, from_behind(): return lax.ppermute(x, axis, pairs)  24 us
    pallas_call x7, Pallas kernels, run(): pl.pallas_call(kernel, out_shape=outs, in_specs=[SMEM] + [VMEM] * len(arg...  22.1 us
    ppermute x8, starting transfers between devices, passed_along(): return lax.ppermute(value, axis, pairs)  18.9 us
    ppermute x8, waiting for transfers between devices, passed_along(): return lax.ppermute(value, axis, pairs)  11.1 us
    unnamed x17, local copies, waits for them, and re-layouts  9.78 us
    ppermute x4, starting transfers between devices, from_behind(): return lax.ppermute(x, axis, pairs)  8.78 us
  transfers between devices with their start and end apart: 16, of which 7 were waited for; matrix products, arithmetic and copies ran while one was open for 3% of the time, Pallas kernels for 0%

profile of v1, /device:TPU:0, one launch (start us, length us, event | category | flops | bytes accessed | tf_op | source)
XLA Modules:
  0.0 96.1 jit_solution(15224133819066487794)
XLA Ops:
  0.0 0.0 copy-start.5
  0.0 1.2 %copy.12 = f32[8,8,16,128]{3,2,1,0:T(8,128)S(1)} copy(f32[8,8,16,128]{3,1,2,0:T(8,128)} %bitcast.32) | data formatting | bytes 1048576
  1.2 0.2 copy.17
  1.4 4.9 %collective-permute-start.3 = (bf16[16,64,128]{2,1,0:T(8,128)(2,1)S(1)}, bf16[16,64,128]{2,1,0:T(8,128)(2,1)S(1)}, u32[]{:S(2)}, u32[]{:S(2)}) collective-permute-start(bf16[16,64,128]{2,1,0:T(8,128)(2,1)S(1)} %bitcast.39), channel_id=1, source_target_pairs={{0,16},{8,24},{1,17},{9,25},{2,18},{10,26},{3,19},{11,27},{4,20},{... | collective-permute-start | bytes 786440 | tf_op jit(solution)/shard_map/ppermute | solution.py:27
  6.3 0.7 slice_bitcast_fusion
  7.0 0.0 collective-permute-start.2
  7.0 4.6 %collective-permute-start = (s32[4]{0:T(128)S(1)}, s32[4]{0:T(128)S(1)}, u32[]{:S(2)}, u32[]{:S(2)}) collective-permute-start(s32[4]{0:T(128)S(1)} %get-tuple-element.48), channel_id=1, source_target_pairs={{0,7},{1,0},{2,1},{3,2},{4,3},{5,4},{6,5},{7,6},{8,15},{9,8},{10,9... | collective-permute-start | bytes 56 | tf_op jit(solution)/shard_map/ppermute | solution.py:21
  11.5 0.0 collective-permute-start.1
  11.5 0.2 copy.16
  11.7 0.8 copy.9
  12.5 0.1 reshape.20
  12.6 0.8 copy.10
  13.3 0.1 reshape.21
  13.4 0.0 collective-permute-done.2
  13.4 0.0 collective-permute-done
  13.4 4.4 %collective-permute-done.1 = s32[4]{0:T(128)S(1)} collective-permute-done((s32[4]{0:T(128)S(1)}, s32[4]{0:T(128)S(1)}, u32[]{:S(2)}, u32[]{:S(2)}) %collective-permute-start.1) | collective-permute-done | bytes 48 | tf_op jit(solution)/shard_map/ppermute | solution.py:21
  17.8 0.1 concatenate.3.refs_0_
  17.9 0.0 collective-permute-done.3.refs_3_
  17.9 0.0 copy-start
  17.9 2.2 %copy-done = bf16[1,16,8,128,128]{4,3,2,1,0:T(8,128)(2,1)S(1)} copy-done((bf16[1,16,8,128,128]{4,3,2,1,0:T(8,128)(2,1)S(1)}, bf16[1,16,8,128,128]{4,3,2,1,0:T(8,128)(2,1)}, u32[]{:S(2)}) %copy-start) | copy-done | bytes 4194328
  20.1 0.0 copy-start.4
  20.1 1.0 %copy-done.4 = bf16[1,16,128,128]{3,2,1,0:T(8,128)(2,1)S(1)} copy-done((bf16[1,16,128,128]{3,2,1,0:T(8,128)(2,1)S(1)}, bf16[1,16,128,128]{3,2,1,0:T(8,128)(2,1)}, u32[]{:S(2)}) %copy-start.4) | copy-done | bytes 524312
  21.1 0.0 copy-start.6
  21.1 1.0 %copy-done.6 = f32[1,64,2048]{2,1,0:T(8,128)S(1)} copy-done((f32[1,64,2048]{2,1,0:T(8,128)S(1)}, f32[1,64,2048]{2,1,0:T(8,128)}, u32[]{:S(2)}) %copy-start.6) | copy-done | bytes 524312
  22.2 0.0 copy-start.1
  22.2 1.0 %first.2 = (f32[16,64,128]{2,1,0:T(8,128)S(1)}, bf16[16,64,128]{2,1,0:T(8,128)(2,1)S(1)}, bf16[4,64,128]{2,1,0:T(8,128)(2,1)S(1)}, bf16[4,64,128]{2,1,0:T(8,128)(2,1)S(1)}, bf16[4,64,128]{2,1,0:T(8,128)(2,1)S(1)}) custom-call(s32[333]{0:T(512)S(1)} %concatenate.3.refs_0_, f32[64,2048]{1,0:T(8,128)S(1)} %bitcast.33, f32[16,64,128]{2,1,0:T(8,128)S(1)} %bitcast.36, ...), custom_call_target="tpu_custom_call" | custom-call | tf_op jit(solution)/shard_map/first/pallas_call | solution.py:167
  23.2 0.1 collective-permute-start.4
  23.3 4.7 %collective-permute-start.5 = (bf16[4,64,128]{2,1,0:T(8,128)(2,1)S(1)}, bf16[4,64,128]{2,1,0:T(8,128)(2,1)S(1)}, u32[]{:S(2)}, u32[]{:S(2)}) collective-permute-start(bf16[4,64,128]{2,1,0:T(8,128)(2,1)S(1)} %get-tuple-element.29), channel_id=1, source_target_pairs={{0,7},{1,0},{2,1},{3,2},{4,3},{5,4},{6,5},{7,6},{8,15},{9,8},{10,9... | collective-permute-start | bytes 196616 | tf_op jit(solution)/shard_map/ppermute | solution.py:21
  28.0 0.0 collective-permute-start.6
  28.0 2.2 %collective-permute-done.4.refs_3_ = bf16[4,64,128]{2,1,0:T(8,128)(2,1)S(1)} collective-permute-done((bf16[4,64,128]{2,1,0:T(8,128)(2,1)S(1)}, bf16[4,64,128]{2,1,0:T(8,128)(2,1)S(1)}, u32[]{:S(2)}, u32[]{:S(2)}) %collective-permute-start.4) | collective-permute-done | bytes 65568 | tf_op jit(solution)/shard_map/ppermute | solution.py:21
  30.2 0.0 collective-permute-done.5.refs_4_
  30.2 0.0 collective-permute-done.6.refs_5_
  30.2 0.0 copy-done.5
  30.2 0.0 copy-start.2
  30.2 2.8 %copy-done.2 = bf16[1,16,12,128,128]{4,3,2,1,0:T(8,128)(2,1)S(1)} copy-done((bf16[1,16,12,128,128]{4,3,2,1,0:T(8,128)(2,1)S(1)}, bf16[1,16,12,128,128]{4,3,2,1,0:T(8,128)(2,1)}, u32[]{:S(2)}) %copy-start.2) | copy-done | bytes 6291480
  33.0 0.0 copy-start.3
  33.0 6.1 %second.2 = (f32[16,64,128]{2,1,0:T(8,128)S(1)}, bf16[16,64,128]{2,1,0:T(8,128)(2,1)S(1)}) custom-call(s32[333]{0:T(512)S(1)} %concatenate.3.refs_0_, f32[16,64,128]{2,1,0:T(8,128)S(1)} %get-tuple-element.26.refs_1_, bf16[16,64,128]{2,1,0:T(8,128)(2,1)S(1)} %get-tuple-element.27.refs_2_, bf16[4,64,128]{2,1,0:T(8,128)(2,1)S(1)} %collective-permute-done.4.refs_3_, ...), custom_call_target="tpu_custom_call" | custom-call | tf_op jit(solution)/shard_map/second/pallas_call | solution.py:167
  39.1 1.3 %collective-permute-start.7 = (bf16[16,64,128]{2,1,0:T(8,128)(2,1)S(1)}, bf16[16,64,128]{2,1,0:T(8,128)(2,1)S(1)}, u32[]{:S(2)}, u32[]{:S(2)}) collective-permute-start(bf16[16,64,128]{2,1,0:T(8,128)(2,1)S(1)} %get-tuple-element.32), channel_id=1, source_target_pairs={{16,0},{24,8},{17,1},{25,9},{18,2},{26,10},{19,3},{27,11},{20,4},{... | collective-permute-start | bytes 786440 | tf_op jit(solution)/shard_map/ppermute | solution.py:27
  40.4 8.0 %collective-permute-done.7.refs_2_ = bf16[16,64,128]{2,1,0:T(8,128)(2,1)S(1)} collective-permute-done((bf16[16,64,128]{2,1,0:T(8,128)(2,1)S(1)}, bf16[16,64,128]{2,1,0:T(8,128)(2,1)S(1)}, u32[]{:S(2)}, u32[]{:S(2)}) %collective-permute-start.7) | collective-permute-done | bytes 262176 | tf_op jit(solution)/shard_map/ppermute | solution.py:27
  48.4 0.0 copy-done.1
  48.4 2.1 %update.1 = (f32[16,64,128]{2,1,0:T(8,128)S(1)}, bf16[16,64,128]{2,1,0:T(8,128)(2,1)S(1)}, bf16[4,64,128]{2,1,0:T(8,128)(2,1)S(1)}, bf16[4,64,128]{2,1,0:T(8,128)(2,1)S(1)}, bf16[4,64,128]{2,1,0:T(8,128)(2,1)S(1)}) custom-call(s32[333]{0:T(512)S(1)} %concatenate.3.refs_0_, f32[16,64,128]{2,1,0:T(8,128)S(1)} %get-tuple-element.31.refs_1_, ...), custom_call_target="tpu_custom_call" | custom-call | tf_op jit(solution)/shard_map/update/pallas_call | solution.py:167
  50.5 0.1 collective-permute-start.8
  50.6 4.7 %collective-permute-start.9 = (bf16[4,64,128]{2,1,0:T(8,128)(2,1)S(1)}, bf16[4,64,128]{2,1,0:T(8,128)(2,1)S(1)}, u32[]{:S(2)}, u32[]{:S(2)}) collective-permute-start(bf16[4,64,128]{2,1,0:T(8,128)(2,1)S(1)} %get-tuple-element.36), channel_id=1, source_target_pairs={{0,7},{1,0},{2,1},{3,2},{4,3},{5,4},{6,5},{7,6},{8,15},{9,8},{10,9... | collective-permute-start | bytes 196616 | tf_op jit(solution)/shard_map/ppermute | solution.py:21
  55.3 0.0 collective-permute-start.10
  55.3 2.2 %collective-permute-done.8.refs_3_ = bf16[4,64,128]{2,1,0:T(8,128)(2,1)S(1)} collective-permute-done((bf16[4,64,128]{2,1,0:T(8,128)(2,1)S(1)}, bf16[4,64,128]{2,1,0:T(8,128)(2,1)S(1)}, u32[]{:S(2)}, u32[]{:S(2)}) %collective-permute-start.8) | collective-permute-done | bytes 65568 | tf_op jit(solution)/shard_map/ppermute | solution.py:21
  57.5 0.0 collective-permute-done.9.refs_4_
  57.5 0.0 collective-permute-done.10.refs_5_
  57.5 0.0 copy-done.3
  57.5 2.8 %residual.1 = (f32[16,64,128]{2,1,0:T(8,128)S(1)}, bf16[16,64,128]{2,1,0:T(8,128)(2,1)S(1)}) custom-call(s32[333]{0:T(512)S(1)} %concatenate.3.refs_0_, f32[64,2048]{1,0:T(8,128)S(1)} %bitcast.34, bf16[16,64,128]{2,1,0:T(8,128)(2,1)S(1)} %get-tuple-element.34.refs_2_, bf16[4,64,128]{2,1,0:T(8,128)(2,1)S(1)} %collective-permute-done.8.refs_3_, ...), custom_call_target="tpu_custom_call" | custom-call | tf_op jit(solution)/shard_map/residual/pallas_call | solution.py:167
  60.4 1.3 %collective-permute-start.11 = (bf16[16,64,128]{2,1,0:T(8,128)(2,1)S(1)}, bf16[16,64,128]{2,1,0:T(8,128)(2,1)S(1)}, u32[]{:S(2)}, u32[]{:S(2)}) collective-permute-start(bf16[16,64,128]{2,1,0:T(8,128)(2,1)S(1)} %get-tuple-element.39), channel_id=1, source_target_pairs={{0,16},{8,24},{1,17},{9,25},{2,18},{10,26},{3,19},{11,27},{4,20},{... | collective-permute-start | bytes 786440 | tf_op jit(solution)/shard_map/ppermute | solution.py:27
  61.7 5.1 %collective-permute-done.11.refs_3_ = bf16[16,64,128]{2,1,0:T(8,128)(2,1)S(1)} collective-permute-done((bf16[16,64,128]{2,1,0:T(8,128)(2,1)S(1)}, bf16[16,64,128]{2,1,0:T(8,128)(2,1)S(1)}, u32[]{:S(2)}, u32[]{:S(2)}) %collective-permute-start.11) | collective-permute-done | bytes 262176 | tf_op jit(solution)/shard_map/ppermute | solution.py:27
  66.8 1.0 %first.3 = (f32[16,64,128]{2,1,0:T(8,128)S(1)}, bf16[16,64,128]{2,1,0:T(8,128)(2,1)S(1)}, bf16[4,64,128]{2,1,0:T(8,128)(2,1)S(1)}, bf16[4,64,128]{2,1,0:T(8,128)(2,1)S(1)}, bf16[4,64,128]{2,1,0:T(8,128)(2,1)S(1)}) custom-call(s32[333]{0:T(512)S(1)} %concatenate.3.refs_0_, f32[64,2048]{1,0:T(8,128)S(1)} %bitcast.35, ...), custom_call_target="tpu_custom_call" | custom-call | tf_op jit(solution)/shard_map/first/pallas_call | solution.py:167
  67.9 0.1 collective-permute-start.12
  67.9 4.7 %collective-permute-start.13 = (bf16[4,64,128]{2,1,0:T(8,128)(2,1)S(1)}, bf16[4,64,128]{2,1,0:T(8,128)(2,1)S(1)}, u32[]{:S(2)}, u32[]{:S(2)}) collective-permute-start(bf16[4,64,128]{2,1,0:T(8,128)(2,1)S(1)} %get-tuple-element.43), channel_id=1, source_target_pairs={{0,7},{1,0},{2,1},{3,2},{4,3},{5,4},{6,5},{7,6},{8,15},{9,8},{10,9... | collective-permute-start | bytes 196616 | tf_op jit(solution)/shard_map/ppermute | solution.py:21
  72.6 0.0 collective-permute-start.14
  72.6 2.2 %collective-permute-done.12.refs_3_ = bf16[4,64,128]{2,1,0:T(8,128)(2,1)S(1)} collective-permute-done((bf16[4,64,128]{2,1,0:T(8,128)(2,1)S(1)}, bf16[4,64,128]{2,1,0:T(8,128)(2,1)S(1)}, u32[]{:S(2)}, u32[]{:S(2)}) %collective-permute-start.12) | collective-permute-done | bytes 65568 | tf_op jit(solution)/shard_map/ppermute | solution.py:21
  74.9 0.0 collective-permute-done.13.refs_4_
  74.9 0.0 collective-permute-done.14.refs_5_
  74.9 6.1 %second.3 = (f32[16,64,128]{2,1,0:T(8,128)S(1)}, bf16[16,64,128]{2,1,0:T(8,128)(2,1)S(1)}) custom-call(s32[333]{0:T(512)S(1)} %concatenate.3.refs_0_, f32[16,64,128]{2,1,0:T(8,128)S(1)} %get-tuple-element.40.refs_1_, bf16[16,64,128]{2,1,0:T(8,128)(2,1)S(1)} %get-tuple-element.41.refs_2_, bf16[4,64,128]{2,1,0:T(8,128)(2,1)S(1)} %collective-permute-done.12.refs_3_, ...), custom_call_target="tpu_custom_call" | custom-call | tf_op jit(solution)/shard_map/second/pallas_call | solution.py:167
  81.0 1.3 %collective-permute-start.15 = (bf16[16,64,128]{2,1,0:T(8,128)(2,1)S(1)}, bf16[16,64,128]{2,1,0:T(8,128)(2,1)S(1)}, u32[]{:S(2)}, u32[]{:S(2)}) collective-permute-start(bf16[16,64,128]{2,1,0:T(8,128)(2,1)S(1)} %get-tuple-element.46), channel_id=1, source_target_pairs={{16,0},{24,8},{17,1},{25,9},{18,2},{26,10},{19,3},{27,11},{20,4},{... | collective-permute-start | bytes 786440 | tf_op jit(solution)/shard_map/ppermute | solution.py:27
  82.3 10.9 %collective-permute-done.15.refs_3_ = bf16[16,64,128]{2,1,0:T(8,128)(2,1)S(1)} collective-permute-done((bf16[16,64,128]{2,1,0:T(8,128)(2,1)S(1)}, bf16[16,64,128]{2,1,0:T(8,128)(2,1)S(1)}, u32[]{:S(2)}, u32[]{:S(2)}) %collective-permute-start.15) | collective-permute-done | bytes 262176 | tf_op jit(solution)/shard_map/ppermute | solution.py:27
  93.1 2.9 %last.1 = f32[64,2048]{1,0:T(8,128)} custom-call(s32[333]{0:T(512)S(1)} %concatenate.3.refs_0_, f32[16,64,128]{2,1,0:T(8,128)S(1)} %get-tuple-element.33.refs_1_, f32[16,64,128]{2,1,0:T(8,128)S(1)} %get-tuple-element.45.refs_2_, bf16[16,64,128]{2,1,0:T(8,128)(2,1)S(1)} %collective-permute-done.15.refs_3_, bf16[16,8,128,128]{3,2,1,0:T(8,128)(2,1)S(1)} %bitcast.24), custom_call_target="tpu_custom_call" | custom-call | tf_op jit(solution)/shard_map/last/pallas_call | solution.py:167
Async XLA Ops:
  0.0 30.2 %copy-start.5 = (bf16[1,16,128,128]{3,2,1,0:T(8,128)(2,1)S(1)}, bf16[1,16,128,128]{3,2,1,0:T(8,128)(2,1)}, u32[]{:S(2)}) copy-start(bf16[1,16,128,128]{3,2,1,0:T(8,128)(2,1)} %param.10) | copy-start | bytes 1572868
  1.4 16.5 %collective-permute-start.3 = (bf16[16,64,128]{2,1,0:T(8,128)(2,1)S(1)}, bf16[16,64,128]{2,1,0:T(8,128)(2,1)S(1)}, u32[]{:S(2)}, u32[]{:S(2)}) collective-permute-start(bf16[16,64,128]{2,1,0:T(8,128)(2,1)S(1)} %bitcast.39), channel_id=1, source_target_pairs={{0,16},{8,24},{1,17},{9,25},{2,18},{10,26},{3,19},{11,27},{4,20},{... | collective-permute-start | bytes 786440 | tf_op jit(solution)/shard_map/ppermute | solution.py:27
  7.0 6.5 %collective-permute-start.2 = (s32[4]{0:T(128)S(1)}, s32[4]{0:T(128)S(1)}, u32[]{:S(2)}, u32[]{:S(2)}) collective-permute-start(s32[4]{0:T(128)S(1)} %get-tuple-element.47), channel_id=1, source_target_pairs={{0,8},{8,0},{16,24},{24,16},{1,9},{9,1},{17,25},{25,17},{2,10},{10... | collective-permute-start | bytes 56 | tf_op jit(solution)/shard_map/ppermute | solution.py:15
  7.0 6.5 %collective-permute-start = (s32[4]{0:T(128)S(1)}, s32[4]{0:T(128)S(1)}, u32[]{:S(2)}, u32[]{:S(2)}) collective-permute-start(s32[4]{0:T(128)S(1)} %get-tuple-element.48), channel_id=1, source_target_pairs={{0,7},{1,0},{2,1},{3,2},{4,3},{5,4},{6,5},{7,6},{8,15},{9,8},{10,9... | collective-permute-start | bytes 56 | tf_op jit(solution)/shard_map/ppermute | solution.py:21
  11.5 6.3 %collective-permute-start.1 = (s32[4]{0:T(128)S(1)}, s32[4]{0:T(128)S(1)}, u32[]{:S(2)}, u32[]{:S(2)}) collective-permute-start(s32[4]{0:T(128)S(1)} %get-tuple-element.49), channel_id=1, source_target_pairs={{0,1},{1,2},{2,3},{3,4},{4,5},{5,6},{6,7},{7,0},{8,9},{9,10},{10,1... | collective-permute-start | bytes 56 | tf_op jit(solution)/shard_map/ppermute | solution.py:21
  17.9 2.2 %copy-start = (bf16[1,16,8,128,128]{4,3,2,1,0:T(8,128)(2,1)S(1)}, bf16[1,16,8,128,128]{4,3,2,1,0:T(8,128)(2,1)}, u32[]{:S(2)}) copy-start(bf16[1,16,8,128,128]{4,3,2,1,0:T(8,128)(2,1)} %param.11) | copy-start | bytes 12582916
  20.1 1.0 %copy-start.4 = (bf16[1,16,128,128]{3,2,1,0:T(8,128)(2,1)S(1)}, bf16[1,16,128,128]{3,2,1,0:T(8,128)(2,1)}, u32[]{:S(2)}) copy-start(bf16[1,16,128,128]{3,2,1,0:T(8,128)(2,1)} %param.10) | copy-start | bytes 1572868
  21.1 1.0 %copy-start.6 = (f32[1,64,2048]{2,1,0:T(8,128)S(1)}, f32[1,64,2048]{2,1,0:T(8,128)}, u32[]{:S(2)}) copy-start(f32[1,64,2048]{2,1,0:T(8,128)} %param.7) | copy-start | bytes 1572868
  22.2 26.2 %copy-start.1 = (bf16[1,16,8,128,128]{4,3,2,1,0:T(8,128)(2,1)S(1)}, bf16[1,16,8,128,128]{4,3,2,1,0:T(8,128)(2,1)}, u32[]{:S(2)}) copy-start(bf16[1,16,8,128,128]{4,3,2,1,0:T(8,128)(2,1)} %param.11) | copy-start | bytes 12582916
  23.2 7.0 %collective-permute-start.4 = (bf16[4,64,128]{2,1,0:T(8,128)(2,1)S(1)}, bf16[4,64,128]{2,1,0:T(8,128)(2,1)S(1)}, u32[]{:S(2)}, u32[]{:S(2)}) collective-permute-start(bf16[4,64,128]{2,1,0:T(8,128)(2,1)S(1)} %get-tuple-element.28), channel_id=1, source_target_pairs={{0,1},{1,2},{2,3},{3,4},{4,5},{5,6},{6,7},{7,0},{8,9},{9,10},{10,1... | collective-permute-start | bytes 196616 | tf_op jit(solution)/shard_map/ppermute | solution.py:21
  23.3 7.0 %collective-permute-start.5 = (bf16[4,64,128]{2,1,0:T(8,128)(2,1)S(1)}, bf16[4,64,128]{2,1,0:T(8,128)(2,1)S(1)}, u32[]{:S(2)}, u32[]{:S(2)}) collective-permute-start(bf16[4,64,128]{2,1,0:T(8,128)(2,1)S(1)} %get-tuple-element.29), channel_id=1, source_target_pairs={{0,7},{1,0},{2,1},{3,2},{4,3},{5,4},{6,5},{7,6},{8,15},{9,8},{10,9... | collective-permute-start | bytes 196616 | tf_op jit(solution)/shard_map/ppermute | solution.py:21
  28.0 2.2 %collective-permute-start.6 = (bf16[4,64,128]{2,1,0:T(8,128)(2,1)S(1)}, bf16[4,64,128]{2,1,0:T(8,128)(2,1)S(1)}, u32[]{:S(2)}, u32[]{:S(2)}) collective-permute-start(bf16[4,64,128]{2,1,0:T(8,128)(2,1)S(1)} %get-tuple-element.30), channel_id=1, source_target_pairs={{0,8},{8,0},{16,24},{24,16},{1,9},{9,1},{17,25},{25,17},{2,10},{10... | collective-permute-start | bytes 196616 | tf_op jit(solution)/shard_map/ppermute | solution.py:15
  30.2 2.8 %copy-start.2 = (bf16[1,16,12,128,128]{4,3,2,1,0:T(8,128)(2,1)S(1)}, bf16[1,16,12,128,128]{4,3,2,1,0:T(8,128)(2,1)}, u32[]{:S(2)}) copy-start(bf16[1,16,12,128,128]{4,3,2,1,0:T(8,128)(2,1)} %param.8) | copy-start | bytes 18874372
  33.0 24.5 %copy-start.3 = (bf16[1,16,12,128,128]{4,3,2,1,0:T(8,128)(2,1)S(1)}, bf16[1,16,12,128,128]{4,3,2,1,0:T(8,128)(2,1)}, u32[]{:S(2)}) copy-start(bf16[1,16,12,128,128]{4,3,2,1,0:T(8,128)(2,1)} %param.8) | copy-start | bytes 18874372
  39.1 9.3 %collective-permute-start.7 = (bf16[16,64,128]{2,1,0:T(8,128)(2,1)S(1)}, bf16[16,64,128]{2,1,0:T(8,128)(2,1)S(1)}, u32[]{:S(2)}, u32[]{:S(2)}) collective-permute-start(bf16[16,64,128]{2,1,0:T(8,128)(2,1)S(1)} %get-tuple-element.32), channel_id=1, source_target_pairs={{16,0},{24,8},{17,1},{25,9},{18,2},{26,10},{19,3},{27,11},{20,4},{... | collective-permute-start | bytes 786440 | tf_op jit(solution)/shard_map/ppermute | solution.py:27
  50.5 7.0 %collective-permute-start.8 = (bf16[4,64,128]{2,1,0:T(8,128)(2,1)S(1)}, bf16[4,64,128]{2,1,0:T(8,128)(2,1)S(1)}, u32[]{:S(2)}, u32[]{:S(2)}) collective-permute-start(bf16[4,64,128]{2,1,0:T(8,128)(2,1)S(1)} %get-tuple-element.35), channel_id=1, source_target_pairs={{0,1},{1,2},{2,3},{3,4},{4,5},{5,6},{6,7},{7,0},{8,9},{9,10},{10,1... | collective-permute-start | bytes 196616 | tf_op jit(solution)/shard_map/ppermute | solution.py:21
  50.6 7.0 %collective-permute-start.9 = (bf16[4,64,128]{2,1,0:T(8,128)(2,1)S(1)}, bf16[4,64,128]{2,1,0:T(8,128)(2,1)S(1)}, u32[]{:S(2)}, u32[]{:S(2)}) collective-permute-start(bf16[4,64,128]{2,1,0:T(8,128)(2,1)S(1)} %get-tuple-element.36), channel_id=1, source_target_pairs={{0,7},{1,0},{2,1},{3,2},{4,3},{5,4},{6,5},{7,6},{8,15},{9,8},{10,9... | collective-permute-start | bytes 196616 | tf_op jit(solution)/shard_map/ppermute | solution.py:21
  55.3 2.2 %collective-permute-start.10 = (bf16[4,64,128]{2,1,0:T(8,128)(2,1)S(1)}, bf16[4,64,128]{2,1,0:T(8,128)(2,1)S(1)}, u32[]{:S(2)}, u32[]{:S(2)}) collective-permute-start(bf16[4,64,128]{2,1,0:T(8,128)(2,1)S(1)} %get-tuple-element.37), channel_id=1, source_target_pairs={{0,8},{8,0},{16,24},{24,16},{1,9},{9,1},{17,25},{25,17},{2,10},{10... | collective-permute-start | bytes 196616 | tf_op jit(solution)/shard_map/ppermute | solution.py:15
  60.4 6.5 %collective-permute-start.11 = (bf16[16,64,128]{2,1,0:T(8,128)(2,1)S(1)}, bf16[16,64,128]{2,1,0:T(8,128)(2,1)S(1)}, u32[]{:S(2)}, u32[]{:S(2)}) collective-permute-start(bf16[16,64,128]{2,1,0:T(8,128)(2,1)S(1)} %get-tuple-element.39), channel_id=1, source_target_pairs={{0,16},{8,24},{1,17},{9,25},{2,18},{10,26},{3,19},{11,27},{4,20},{... | collective-permute-start | bytes 786440 | tf_op jit(solution)/shard_map/ppermute | solution.py:27
  67.9 7.0 %collective-permute-start.12 = (bf16[4,64,128]{2,1,0:T(8,128)(2,1)S(1)}, bf16[4,64,128]{2,1,0:T(8,128)(2,1)S(1)}, u32[]{:S(2)}, u32[]{:S(2)}) collective-permute-start(bf16[4,64,128]{2,1,0:T(8,128)(2,1)S(1)} %get-tuple-element.42), channel_id=1, source_target_pairs={{0,1},{1,2},{2,3},{3,4},{4,5},{5,6},{6,7},{7,0},{8,9},{9,10},{10,1... | collective-permute-start | bytes 196616 | tf_op jit(solution)/shard_map/ppermute | solution.py:21
  67.9 7.0 %collective-permute-start.13 = (bf16[4,64,128]{2,1,0:T(8,128)(2,1)S(1)}, bf16[4,64,128]{2,1,0:T(8,128)(2,1)S(1)}, u32[]{:S(2)}, u32[]{:S(2)}) collective-permute-start(bf16[4,64,128]{2,1,0:T(8,128)(2,1)S(1)} %get-tuple-element.43), channel_id=1, source_target_pairs={{0,7},{1,0},{2,1},{3,2},{4,3},{5,4},{6,5},{7,6},{8,15},{9,8},{10,9... | collective-permute-start | bytes 196616 | tf_op jit(solution)/shard_map/ppermute | solution.py:21
  72.6 2.2 %collective-permute-start.14 = (bf16[4,64,128]{2,1,0:T(8,128)(2,1)S(1)}, bf16[4,64,128]{2,1,0:T(8,128)(2,1)S(1)}, u32[]{:S(2)}, u32[]{:S(2)}) collective-permute-start(bf16[4,64,128]{2,1,0:T(8,128)(2,1)S(1)} %get-tuple-element.44), channel_id=1, source_target_pairs={{0,8},{8,0},{16,24},{24,16},{1,9},{9,1},{17,25},{25,17},{2,10},{10... | collective-permute-start | bytes 196616 | tf_op jit(solution)/shard_map/ppermute | solution.py:15
  81.0 12.2 %collective-permute-start.15 = (bf16[16,64,128]{2,1,0:T(8,128)(2,1)S(1)}, bf16[16,64,128]{2,1,0:T(8,128)(2,1)S(1)}, u32[]{:S(2)}, u32[]{:S(2)}) collective-permute-start(bf16[16,64,128]{2,1,0:T(8,128)(2,1)S(1)} %get-tuple-element.46), channel_id=1, source_target_pairs={{16,0},{24,8},{17,1},{25,9},{18,2},{26,10},{19,3},{27,11},{20,4},{... | collective-permute-start | bytes 786440 | tf_op jit(solution)/shard_map/ppermute | solution.py:27

commit v2 on v1

v2 whole, which is shorter than its diff:
```python
import functools

import jax
import jax.numpy as jnp
from jax import lax
from jax.experimental import pallas as pl
from jax.experimental.pallas import tpu as pltpu
from jax.sharding import PartitionSpec as P

ITERS = 2
CHUNK = 4
LIMIT = 16 << 20
VMEM = pl.BlockSpec(memory_space=pltpu.VMEM)
SMEM = pl.BlockSpec(memory_space=pltpu.SMEM)
HBM = pl.BlockSpec(memory_space=pltpu.HBM)
NT = (((1,), (1,)), ((), ()))


def partner(x, axis, apart):
    return lax.ppermute(x, axis, [(i, i ^ 1 << apart) for i in range(lax.axis_size(axis))])


def passed_along(value, axis, steps):
    count = lax.axis_size(axis)
    pairs = [(source, (source + steps) % count) for source in range(count)]
    return lax.ppermute(value, axis, pairs)


def like(x):
    return jax.ShapeDtypeStruct(x.shape, x.dtype)


def times(panel, block):
    return lax.dot_general(panel, block, NT, preferred_element_type=jnp.float32)


def gathered(source, table, row, base, blocks):
    count = blocks.shape[1]
    left = jnp.concatenate([source[table[base + row * count + k]] for k in range(count)], axis=1)
    right = jnp.concatenate([blocks[row, k] for k in range(count)], axis=1)
    return times(left, right)


def packed(source, table, base, outs):
    for side, out in enumerate(outs):
        for j in range(out.shape[0]):
            out[j] = source[table[base + side * out.shape[0] + j]]


def open_body(loads, panels, sent, arrivals):
    rows, _, width = panels.shape

    def copy(i):
        return pltpu.make_async_copy(
            loads.at[:, pl.ds(i * width, width)], panels.at[i], arrivals.at[i]
        )

    for i in range(rows):
        copy(i).start()
    for i in range(rows):
        copy(i).wait()
        sent[i] = panels[i].astype(jnp.bfloat16)


def fetched(source, target, arrivals):
    return [
        pltpu.make_async_copy(source.at[i], target.at[i], arrivals.at[i])
        for i in range(source.shape[0])
    ]


def first_body(fetch, where, table, loads, residual, arrived, transfer, smoother, current, first, *rest):
    rows = first.shape[0]
    if fetch:
        outs, (kept, kept_smoother, arrivals, smoother_arrivals) = rest[:-4], rest[-4:]
        copies = fetched(transfer, kept, arrivals)
        smoother_copies = fetched(smoother, kept_smoother, smoother_arrivals)
        for copy in copies + smoother_copies:
            copy.start()
        transfer, smoother = kept, kept_smoother
    else:
        outs = rest

    @pl.when(table[where["fine"]] == 1)
    def _():
        for i in range(rows):
            current[i] = residual[i]
            if fetch:
                copies[i].wait()

    @pl.when(table[where["fine"]] == 0)
    def _():
        for i in range(rows):
            if fetch and i % CHUNK == 0:
                for copy in copies[i : i + CHUNK]:
                    copy.wait()
            added = gathered(arrived, table, i, where["transfer"], transfer)
            current[i] = loads[i] + added

    if fetch:
        for copy in smoother_copies:
            copy.wait()
    for i in range(rows):
        value = times(current[i].astype(jnp.bfloat16), smoother[i])
        first[i] = value.astype(jnp.bfloat16)
    packed(first, table, where["wanted"], outs)


def extended(own, sides, scratch):
    rows = own.shape[0]
    for i in range(rows):
        scratch[i] = own[i]
    for side, ref in enumerate(sides):
        for j in range(ref.shape[0]):
            scratch[rows + side * ref.shape[0] + j] = ref[j]


def second_body(fetch, where, table, current, first, left, right, sibling, blocks, smoother, full, rounded, *rest):
    if fetch:
        kept, scratch, arrivals = rest
        copies = fetched(blocks, kept, arrivals)
        for copy in copies:
            copy.start()
        blocks = kept
    else:
        scratch = rest[0]
    extended(first, (left, right, sibling), scratch)
    for i in range(first.shape[0]):
        if fetch and i % CHUNK == 0:
            for copy in copies[i : i + CHUNK]:
                copy.wait()
        applied = gathered(scratch, table, i, where["level"], blocks)
        rounded[i] = (current[i] - applied).astype(jnp.bfloat16)
    for i in range(first.shape[0]):
        value = first[i].astype(jnp.float32) + times(rounded[i], smoother[i])
        full[i] = value
        rounded[i] = value.astype(jnp.bfloat16)


def update_body(where, table, correction, arrived, transfer, iterate, rounded, *outs):
    @pl.when(table[where["fine"]] == 1)
    def _():
        for i in range(iterate.shape[0]):
            added = gathered(arrived, table, i, where["transfer"], transfer)
            value = correction[i] + added
            iterate[i] = value
            rounded[i] = value.astype(jnp.bfloat16)
        packed(rounded, table, where["wanted"], outs)


def residual_body(where, table, loads, rounded, left, right, sibling, blocks, residual, sent, scratch):
    @pl.when(table[where["fine"]] == 1)
    def _():
        extended(rounded, (left, right, sibling), scratch)
        for i in range(residual.shape[0]):
            value = loads[i] - gathered(scratch, table, i, where["level"], blocks)
            residual[i] = value
            sent[i] = value.astype(jnp.bfloat16)


def last_body(where, table, iterate, correction, arrived, transfer, out, total, leaves):
    rows, _, width = correction.shape

    def copy(i):
        return pltpu.make_async_copy(total.at[i], out.at[:, pl.ds(i * width, width)], leaves.at[i])

    @pl.when(table[where["fine"]] == 1)
    def _():
        for i in range(rows):
            added = gathered(arrived, table, i, where["transfer"], transfer)
            total[i] = (iterate[i] + correction[i]) + added
            copy(i).start()

    @pl.when(table[where["fine"]] == 0)
    def _():
        for i in range(rows):
            total[i] = correction[i]
            copy(i).start()

    for i in range(rows):
        copy(i).wait()


def local(loads, level_blocks, level_cols, smoother, transfer_blocks, transfer_cols, bound_rows):
    block_rows, level_count = level_cols.shape[1:]
    width = level_blocks.shape[-1]
    load_cols = loads.shape[1]
    list_width = bound_rows.shape[-1]
    transfer_count = transfer_cols.shape[-1]
    section_fine = lax.axis_index("level") < 2
    bound_lists = bound_rows[0, 0]
    blocks, smooth, transfer, loads = level_blocks[0], smoother[0], transfer_blocks[0], loads[0]

    panels = (block_rows, load_cols, width)
    wide = jax.ShapeDtypeStruct(panels, jnp.float32)
    narrow = jax.ShapeDtypeStruct(panels, jnp.bfloat16)
    load_panels, sent = pl.pallas_call(
        open_body,
        out_shape=(wide, narrow),
        in_specs=[HBM],
        out_specs=(VMEM, VMEM),
        scratch_shapes=[pltpu.SemaphoreType.DMA((block_rows,))],
        name="open",
        cost_estimate=pl.CostEstimate(flops=0, bytes_accessed=30 << 20, transcendentals=0),
        compiler_params=pltpu.CompilerParams(vmem_limit_bytes=LIMIT),
    )(pltpu.with_memory_space_constraint(loads, pltpu.HBM))
    arrived = partner(sent, "level", 1)

    wanted = (
        passed_along(bound_lists[0], "dom", -1),
        passed_along(bound_lists[1], "dom", 1),
        partner(bound_lists[2], "level", 0),
    )
    fine = section_fine.astype(jnp.int32).reshape(1)
    parts = {
        "fine": fine,
        "level": level_cols.reshape(-1),
        "transfer": transfer_cols.reshape(-1),
        "wanted": jnp.concatenate(wanted),
    }
    where, at = {}, 0
    for name, part in parts.items():
        where[name] = at
        at += part.shape[0]
    table = jnp.concatenate(list(parts.values()))

    listed = jax.ShapeDtypeStruct((list_width, load_cols, width), jnp.bfloat16)
    rowwise = pltpu.SemaphoreType.DMA((block_rows,))
    extension = pltpu.VMEM((block_rows + 3 * list_width, load_cols, width), jnp.bfloat16)

    def run(body, outs, *args, here=(), out_specs=None, scratch=(), name=None):
        def kernel(*refs):
            body(where, *refs)

        args = [
            pltpu.with_memory_space_constraint(x, pltpu.HBM) if i in here else x
            for i, x in enumerate(args)
        ]

        return pl.pallas_call(
            kernel,
            out_shape=outs,
            in_specs=[SMEM] + [HBM if i in here else VMEM for i in range(len(args))],
            out_specs=out_specs or jax.tree.map(lambda _: VMEM, outs),
            scratch_shapes=list(scratch),
            name=name,
            compiler_params=pltpu.CompilerParams(vmem_limit_bytes=LIMIT),
        )(table, *args)

    def exchanged(packs):
        to_right, to_left, to_sibling = packs
        return (
            passed_along(to_right, "dom", 1),
            passed_along(to_left, "dom", -1),
            partner(to_sibling, "level", 0),
        )

    residual = load_panels
    iterate = None
    for cycle_index in range(ITERS):
        if cycle_index > 0:
            residual, sent = run(
                residual_body, (wide, narrow), load_panels, rounded, *sides, blocks,
                scratch=[extension], name="residual",
            )
            arrived = partner(sent, "level", 1)
        fetch = cycle_index == 0
        outs = (wide, narrow, listed, listed, listed)
        args = (load_panels, residual, arrived, transfer, smooth)
        body = functools.partial(first_body, fetch)
        if fetch:
            current, first, *packs, transfer, smooth = run(
                body, outs + (like(transfer), like(smooth)),
                *args, here=(3, 4), scratch=[rowwise, rowwise], name="first",
            )
        else:
            current, first, *packs = run(body, outs, *args, name="first")
        args = (current, first, *exchanged(packs), blocks, smooth)
        body = functools.partial(second_body, fetch)
        if fetch:
            correction, rounded, blocks = run(
                body, (wide, narrow, like(blocks)), *args, here=(5,),
                scratch=[extension, rowwise], name="second",
            )
        else:
            correction, rounded = run(body, (wide, narrow), *args, scratch=[extension], name="second")
        returned = partner(rounded, "level", 1)
        if cycle_index + 1 < ITERS:
            if iterate is not None:
                correction = iterate + correction
            iterate, rounded, *packs = run(
                update_body, (wide, narrow, listed, listed, listed),
                correction, returned, transfer, name="update",
            )
            sides = exchanged(packs)
    final = run(
        last_body, jax.ShapeDtypeStruct((load_cols, block_rows * width), jnp.float32),
        iterate, correction, returned, transfer, out_specs=HBM,
        scratch=[pltpu.VMEM(panels, jnp.float32), pltpu.SemaphoreType.DMA((block_rows,))], name="last",
    )
    return final[None]


def solution(mesh):
    in_specs = (
        P("level", None, "dom"),
        P("level", "dom", None, None, None),
        P("level", "dom", None),
        P("level", "dom", None, None),
        P("level", "dom", None, None, None),
        P("level", "dom", None),
        P("level", "dom", None, None),
    )
    out_specs = P("level", None, "dom")
    return jax.shard_map(local, mesh=mesh, in_specs=in_specs, out_specs=out_specs, check_vma=False)
```

time: 96.5 us -> 80.4 us (0.83)
  local copies, waits for them, and re-layouts: 11.1 us -> 2.47 us
  waiting for transfers between devices: 35.1 us -> 30.2 us
  starting transfers between devices: 27.7 us -> 25.4 us
    ppermute x4 -> x0, waiting for transfers between devices: 24 us -> none  [from_behind(): return lax.ppermute(x, axis, pairs)]
    ppermute x4 -> x8, waiting for transfers between devices: 0.01 us -> 18.9 us  [partner(): lax.ppermute(x, axis, [(i, i ^ 1 << apart) for i in range(lax.axis_size(a...]
    ppermute x4 -> x0, starting transfers between devices: 8.78 us -> none  [from_behind(): return lax.ppermute(x, axis, pairs)]
    unnamed x17 -> x2, local copies, waits for them, and re-layouts: 9.78 us -> 1.53 us
    ppermute x4 -> x8, starting transfers between devices: 0.01 us -> 6.52 us  [partner(): lax.ppermute(x, axis, [(i, i ^ 1 << apart) for i in range(lax.axis_size(a...]
    pallas_call x7 -> x8, Pallas kernels: 22.1 us -> 22 us  [the longest x7 20.8 us: run(): pl.pallas_call(kernel, out_shape=outs, in_specs=[SMEM] + [HBM if i in her...]
where the time goes in v2:
time: 80.4 us; the launch traced here: 80.1 us
  waiting for transfers between devices  30.2 us (38%)
  starting transfers between devices  25.4 us (32%)
  Pallas kernels  22 us (27%)
  local copies, waits for them, and re-layouts  2.47 us (3%)
    pallas_call x7, Pallas kernels, run(): pl.pallas_call(kernel, out_shape=outs, in_specs=[SMEM] + [HBM if i in her...  20.8 us
    ppermute x8, waiting for transfers between devices, partner(): lax.ppermute(x, axis, [(i, i ^ 1 << apart) for i in range(lax.axis_size(a...  18.9 us
    ppermute x8, starting transfers between devices, passed_along(): return lax.ppermute(value, axis, pairs)  18.9 us
    ppermute x8, waiting for transfers between devices, passed_along(): return lax.ppermute(value, axis, pairs)  11.3 us
    ppermute x8, starting transfers between devices, partner(): lax.ppermute(x, axis, [(i, i ^ 1 << apart) for i in range(lax.axis_size(a...  6.52 us
  transfers between devices with their start and end apart: 16, of which 7 were waited for; matrix products, arithmetic and copies ran while one was open for 3% of the time, Pallas kernels for 0%

profile of v2, /device:TPU:0, one launch (start us, length us, event | category | flops | bytes accessed | tf_op | source)
XLA Modules:
  0.0 80.1 jit_solution(13993860045579539759)
XLA Ops:
  0.0 1.1 %open.1 = (f32[16,64,128]{2,1,0:T(8,128)S(1)}, bf16[16,64,128]{2,1,0:T(8,128)(2,1)S(1)}) custom-call(f32[64,2048]{1,0:T(8,128)} %bitcast.14), custom_call_target="tpu_custom_call" | custom-call | bytes 31457280 | tf_op jit(solution)/shard_map/open/pallas_call | solution.py:197
  1.1 3.0 %collective-permute-start.3 = (bf16[16,64,128]{2,1,0:T(8,128)(2,1)S(1)}, bf16[16,64,128]{2,1,0:T(8,128)(2,1)S(1)}, u32[]{:S(2)}, u32[]{:S(2)}) collective-permute-start(bf16[16,64,128]{2,1,0:T(8,128)(2,1)S(1)} %get-tuple-element.32), channel_id=1, source_target_pairs={{0,16},{8,24},{16,0},{24,8},{1,17},{9,25},{17,1},{25,9},{2,18},{10... | collective-permute-start | bytes 786440 | tf_op jit(solution)/shard_map/ppermute | solution.py:20
  4.2 0.7 slice_bitcast_fusion
  4.9 0.0 collective-permute-start.2
  4.9 4.6 %collective-permute-start = (s32[4]{0:T(128)S(1)}, s32[4]{0:T(128)S(1)}, u32[]{:S(2)}, u32[]{:S(2)}) collective-permute-start(s32[4]{0:T(128)S(1)} %get-tuple-element.58), channel_id=1, source_target_pairs={{0,7},{1,0},{2,1},{3,2},{4,3},{5,4},{6,5},{7,6},{8,15},{9,8},{10,9... | collective-permute-start | bytes 56 | tf_op jit(solution)/shard_map/ppermute | solution.py:26
  9.4 0.0 collective-permute-start.1
  9.4 0.8 copy.9
  10.2 0.1 reshape.20
  10.3 0.8 copy.10
  11.1 0.1 reshape.21
  11.1 0.0 collective-permute-done.2
  11.2 0.0 collective-permute-done
  11.2 4.5 %collective-permute-done.1 = s32[4]{0:T(128)S(1)} collective-permute-done((s32[4]{0:T(128)S(1)}, s32[4]{0:T(128)S(1)}, u32[]{:S(2)}, u32[]{:S(2)}) %collective-permute-start.1) | collective-permute-done | bytes 48 | tf_op jit(solution)/shard_map/ppermute | solution.py:26
  15.7 0.1 concatenate.3.refs_0_
  15.8 0.0 collective-permute-done.3.refs_3_
  15.8 3.7 %first.2 = (f32[16,64,128]{2,1,0:T(8,128)S(1)}, bf16[16,64,128]{2,1,0:T(8,128)(2,1)S(1)}, bf16[4,64,128]{2,1,0:T(8,128)(2,1)S(1)}, bf16[4,64,128]{2,1,0:T(8,128)...) custom-call(s32[333]{0:T(512)S(1)} %concatenate.3.refs_0_, ...), custom_call_target="tpu_custom_call" | custom-call | tf_op jit(solution)/shard_map/first/pallas_call | solution.py:240
  19.4 0.1 collective-permute-start.4
  19.5 4.7 %collective-permute-start.5 = (bf16[4,64,128]{2,1,0:T(8,128)(2,1)S(1)}, bf16[4,64,128]{2,1,0:T(8,128)(2,1)S(1)}, u32[]{:S(2)}, u32[]{:S(2)}) collective-permute-start(bf16[4,64,128]{2,1,0:T(8,128)(2,1)S(1)} %get-tuple-element.36), channel_id=1, source_target_pairs={{0,7},{1,0},{2,1},{3,2},{4,3},{5,4},{6,5},{7,6},{8,15},{9,8},{10,9... | collective-permute-start | bytes 196616 | tf_op jit(solution)/shard_map/ppermute | solution.py:26
  24.2 0.0 collective-permute-start.6
  24.2 2.2 %collective-permute-done.4.refs_3_ = bf16[4,64,128]{2,1,0:T(8,128)(2,1)S(1)} collective-permute-done((bf16[4,64,128]{2,1,0:T(8,128)(2,1)S(1)}, bf16[4,64,128]{2,1,0:T(8,128)(2,1)S(1)}, u32[]{:S(2)}, u32[]{:S(2)}) %collective-permute-start.4) | collective-permute-done | bytes 65568 | tf_op jit(solution)/shard_map/ppermute | solution.py:26
  26.5 0.0 collective-permute-done.5.refs_4_
  26.5 0.0 collective-permute-done.6.refs_5_
  26.5 5.0 %second.2 = (f32[16,64,128]{2,1,0:T(8,128)S(1)}, bf16[16,64,128]{2,1,0:T(8,128)(2,1)S(1)}, bf16[16,12,128,128]{3,2,1,0:T(8,128)(2,1)S(1)}) custom-call(s32[333]{0:T(512)S(1)} %concatenate.3.refs_0_, f32[16,64,128]{2,1,0:T(8,128)S(1)} %get-tuple-element.33.refs_1_, bf16[16,64,128]{2,1,0:T(8,128)(2,1)S(1)} %get-tuple-element.34.refs_2_, ...), custom_call_target="tpu_custom_call" | custom-call | tf_op jit(solution)/shard_map/second/pallas_call | solution.py:240
  31.5 1.5 %collective-permute-start.7 = (bf16[16,64,128]{2,1,0:T(8,128)(2,1)S(1)}, bf16[16,64,128]{2,1,0:T(8,128)(2,1)S(1)}, u32[]{:S(2)}, u32[]{:S(2)}) collective-permute-start(bf16[16,64,128]{2,1,0:T(8,128)(2,1)S(1)} %get-tuple-element.40), channel_id=1, source_target_pairs={{0,16},{8,24},{16,0},{24,8},{1,17},{9,25},{17,1},{25,9},{2,18},{10... | collective-permute-start | bytes 786440 | tf_op jit(solution)/shard_map/ppermute | solution.py:20
  33.0 5.9 %collective-permute-done.7.refs_2_ = bf16[16,64,128]{2,1,0:T(8,128)(2,1)S(1)} collective-permute-done((bf16[16,64,128]{2,1,0:T(8,128)(2,1)S(1)}, bf16[16,64,128]{2,1,0:T(8,128)(2,1)S(1)}, u32[]{:S(2)}, u32[]{:S(2)}) %collective-permute-start.7) | collective-permute-done | bytes 262176 | tf_op jit(solution)/shard_map/ppermute | solution.py:20
  39.0 2.1 %update.1 = (f32[16,64,128]{2,1,0:T(8,128)S(1)}, bf16[16,64,128]{2,1,0:T(8,128)(2,1)S(1)}, bf16[4,64,128]{2,1,0:T(8,128)(2,1)S(1)}, bf16[4,64,128]{2,1,0:T(8,128)(2,1)S(1)}, bf16[4,64,128]{2,1,0:T(8,128)(2,1)S(1)}) custom-call(s32[333]{0:T(512)S(1)} %concatenate.3.refs_0_, f32[16,64,128]{2,1,0:T(8,128)S(1)} %get-tuple-element.39.refs_1_, ...), custom_call_target="tpu_custom_call" | custom-call | tf_op jit(solution)/shard_map/update/pallas_call | solution.py:240
  41.1 0.1 collective-permute-start.8
  41.2 4.7 %collective-permute-start.9 = (bf16[4,64,128]{2,1,0:T(8,128)(2,1)S(1)}, bf16[4,64,128]{2,1,0:T(8,128)(2,1)S(1)}, u32[]{:S(2)}, u32[]{:S(2)}) collective-permute-start(bf16[4,64,128]{2,1,0:T(8,128)(2,1)S(1)} %get-tuple-element.45), channel_id=1, source_target_pairs={{0,7},{1,0},{2,1},{3,2},{4,3},{5,4},{6,5},{7,6},{8,15},{9,8},{10,9... | collective-permute-start | bytes 196616 | tf_op jit(solution)/shard_map/ppermute | solution.py:26
  45.9 0.0 collective-permute-start.10
  45.9 2.2 %collective-permute-done.8.refs_3_ = bf16[4,64,128]{2,1,0:T(8,128)(2,1)S(1)} collective-permute-done((bf16[4,64,128]{2,1,0:T(8,128)(2,1)S(1)}, bf16[4,64,128]{2,1,0:T(8,128)(2,1)S(1)}, u32[]{:S(2)}, u32[]{:S(2)}) %collective-permute-start.8) | collective-permute-done | bytes 65568 | tf_op jit(solution)/shard_map/ppermute | solution.py:26
  48.1 0.0 collective-permute-done.9.refs_4_
  48.1 0.0 collective-permute-done.10.refs_5_
  48.1 2.8 %residual.1 = (f32[16,64,128]{2,1,0:T(8,128)S(1)}, bf16[16,64,128]{2,1,0:T(8,128)(2,1)S(1)}) custom-call(s32[333]{0:T(512)S(1)} %concatenate.3.refs_0_, f32[16,64,128]{2,1,0:T(8,128)S(1)} %get-tuple-element.31.refs_1_.refs_2_, bf16[16,64,128]{2,1,0:T(8,128)(2,1)S(1)} %get-tuple-element.43.refs_2_, bf16[4,64,128]{2,1,0:T(8,128)(2,1)S(1)} %collective-permute-done.8.refs_3_, ...), custom_call_target="tpu_custom_call" | custom-call | tf_op jit(solution)/shard_map/residual/pallas_call | solution.py:240
  51.0 0.1 collective-permute-start.11
  51.1 7.4 %collective-permute-done.11.refs_3_ = bf16[16,64,128]{2,1,0:T(8,128)(2,1)S(1)} collective-permute-done((bf16[16,64,128]{2,1,0:T(8,128)(2,1)S(1)}, bf16[16,64,128]{2,1,0:T(8,128)(2,1)S(1)}, u32[]{:S(2)}, u32[]{:S(2)}) %collective-permute-start.11) | collective-permute-done | bytes 262176 | tf_op jit(solution)/shard_map/ppermute | solution.py:20
  58.4 1.1 %first.3 = (f32[16,64,128]{2,1,0:T(8,128)S(1)}, bf16[16,64,128]{2,1,0:T(8,128)(2,1)S(1)}, bf16[4,64,128]{2,1,0:T(8,128)(2,1)S(1)}, bf16[4,64,128]{2,1,0:T(8,128)(2,1)S(1)}, bf16[4,64,128]{2,1,0:T(8,128)(2,1)S(1)}) custom-call(s32[333]{0:T(512)S(1)} %concatenate.3.refs_0_, f32[16,64,128]{2,1,0:T(8,128)S(1)} %get-tuple-element.31.refs_1_.refs_2_, ...), custom_call_target="tpu_custom_call" | custom-call | tf_op jit(solution)/shard_map/first/pallas_call | solution.py:240
  59.5 0.1 collective-permute-start.12
  59.6 4.7 %collective-permute-start.13 = (bf16[4,64,128]{2,1,0:T(8,128)(2,1)S(1)}, bf16[4,64,128]{2,1,0:T(8,128)(2,1)S(1)}, u32[]{:S(2)}, u32[]{:S(2)}) collective-permute-start(bf16[4,64,128]{2,1,0:T(8,128)(2,1)S(1)} %get-tuple-element.53), channel_id=1, source_target_pairs={{0,7},{1,0},{2,1},{3,2},{4,3},{5,4},{6,5},{7,6},{8,15},{9,8},{10,9... | collective-permute-start | bytes 196616 | tf_op jit(solution)/shard_map/ppermute | solution.py:26
  64.3 0.0 collective-permute-start.14
  64.3 2.2 %collective-permute-done.12.refs_3_ = bf16[4,64,128]{2,1,0:T(8,128)(2,1)S(1)} collective-permute-done((bf16[4,64,128]{2,1,0:T(8,128)(2,1)S(1)}, bf16[4,64,128]{2,1,0:T(8,128)(2,1)S(1)}, u32[]{:S(2)}, u32[]{:S(2)}) %collective-permute-start.12) | collective-permute-done | bytes 65568 | tf_op jit(solution)/shard_map/ppermute | solution.py:26
  66.5 0.0 collective-permute-done.13.refs_4_
  66.5 0.0 collective-permute-done.14.refs_5_
  66.5 3.2 %second.3 = (f32[16,64,128]{2,1,0:T(8,128)S(1)}, bf16[16,64,128]{2,1,0:T(8,128)(2,1)S(1)}) custom-call(s32[333]{0:T(512)S(1)} %concatenate.3.refs_0_, f32[16,64,128]{2,1,0:T(8,128)S(1)} %get-tuple-element.50.refs_1_, bf16[16,64,128]{2,1,0:T(8,128)(2,1)S(1)} %get-tuple-element.51.refs_2_, bf16[4,64,128]{2,1,0:T(8,128)(2,1)S(1)} %collective-permute-done.12.refs_3_, ...), custom_call_target="tpu_custom_call" | custom-call | tf_op jit(solution)/shard_map/second/pallas_call | solution.py:240
  69.7 1.9 %collective-permute-start.15 = (bf16[16,64,128]{2,1,0:T(8,128)(2,1)S(1)}, bf16[16,64,128]{2,1,0:T(8,128)(2,1)S(1)}, u32[]{:S(2)}, u32[]{:S(2)}) collective-permute-start(bf16[16,64,128]{2,1,0:T(8,128)(2,1)S(1)} %get-tuple-element.56), channel_id=1, source_target_pairs={{0,16},{8,24},{16,0},{24,8},{1,17},{9,25},{17,1},{25,9},{2,18},{10... | collective-permute-start | bytes 786440 | tf_op jit(solution)/shard_map/ppermute | solution.py:20
  71.6 5.6 %collective-permute-done.15.refs_3_ = bf16[16,64,128]{2,1,0:T(8,128)(2,1)S(1)} collective-permute-done((bf16[16,64,128]{2,1,0:T(8,128)(2,1)S(1)}, bf16[16,64,128]{2,1,0:T(8,128)(2,1)S(1)}, u32[]{:S(2)}, u32[]{:S(2)}) %collective-permute-start.15) | collective-permute-done | bytes 262176 | tf_op jit(solution)/shard_map/ppermute | solution.py:20
  77.2 2.9 %last.1 = f32[64,2048]{1,0:T(8,128)} custom-call(s32[333]{0:T(512)S(1)} %concatenate.3.refs_0_, f32[16,64,128]{2,1,0:T(8,128)S(1)} %get-tuple-element.42.refs_1_, f32[16,64,128]{2,1,0:T(8,128)S(1)} %get-tuple-element.55.refs_2_, bf16[16,64,128]{2,1,0:T(8,128)(2,1)S(1)} %collective-permute-done.15.refs_3_, ...), custom_call_target="tpu_custom_call" | custom-call | tf_op jit(solution)/shard_map/last/pallas_call | solution.py:240
Async XLA Ops:
  1.1 14.6 %collective-permute-start.3 = (bf16[16,64,128]{2,1,0:T(8,128)(2,1)S(1)}, bf16[16,64,128]{2,1,0:T(8,128)(2,1)S(1)}, u32[]{:S(2)}, u32[]{:S(2)}) collective-permute-start(bf16[16,64,128]{2,1,0:T(8,128)(2,1)S(1)} %get-tuple-element.32), channel_id=1, source_target_pairs={{0,16},{8,24},{16,0},{24,8},{1,17},{9,25},{17,1},{25,9},{2,18},{10... | collective-permute-start | bytes 786440 | tf_op jit(solution)/shard_map/ppermute | solution.py:20
  4.9 6.3 %collective-permute-start.2 = (s32[4]{0:T(128)S(1)}, s32[4]{0:T(128)S(1)}, u32[]{:S(2)}, u32[]{:S(2)}) collective-permute-start(s32[4]{0:T(128)S(1)} %get-tuple-element.57), channel_id=1, source_target_pairs={{0,8},{8,0},{16,24},{24,16},{1,9},{9,1},{17,25},{25,17},{2,10},{10... | collective-permute-start | bytes 56 | tf_op jit(solution)/shard_map/ppermute | solution.py:20
  4.9 6.3 %collective-permute-start = (s32[4]{0:T(128)S(1)}, s32[4]{0:T(128)S(1)}, u32[]{:S(2)}, u32[]{:S(2)}) collective-permute-start(s32[4]{0:T(128)S(1)} %get-tuple-element.58), channel_id=1, source_target_pairs={{0,7},{1,0},{2,1},{3,2},{4,3},{5,4},{6,5},{7,6},{8,15},{9,8},{10,9... | collective-permute-start | bytes 56 | tf_op jit(solution)/shard_map/ppermute | solution.py:26
  9.4 6.3 %collective-permute-start.1 = (s32[4]{0:T(128)S(1)}, s32[4]{0:T(128)S(1)}, u32[]{:S(2)}, u32[]{:S(2)}) collective-permute-start(s32[4]{0:T(128)S(1)} %get-tuple-element.59), channel_id=1, source_target_pairs={{0,1},{1,2},{2,3},{3,4},{4,5},{5,6},{6,7},{7,0},{8,9},{9,10},{10,1... | collective-permute-start | bytes 56 | tf_op jit(solution)/shard_map/ppermute | solution.py:26
  19.4 7.0 %collective-permute-start.4 = (bf16[4,64,128]{2,1,0:T(8,128)(2,1)S(1)}, bf16[4,64,128]{2,1,0:T(8,128)(2,1)S(1)}, u32[]{:S(2)}, u32[]{:S(2)}) collective-permute-start(bf16[4,64,128]{2,1,0:T(8,128)(2,1)S(1)} %get-tuple-element.35), channel_id=1, source_target_pairs={{0,1},{1,2},{2,3},{3,4},{4,5},{5,6},{6,7},{7,0},{8,9},{9,10},{10,1... | collective-permute-start | bytes 196616 | tf_op jit(solution)/shard_map/ppermute | solution.py:26
  19.5 7.0 %collective-permute-start.5 = (bf16[4,64,128]{2,1,0:T(8,128)(2,1)S(1)}, bf16[4,64,128]{2,1,0:T(8,128)(2,1)S(1)}, u32[]{:S(2)}, u32[]{:S(2)}) collective-permute-start(bf16[4,64,128]{2,1,0:T(8,128)(2,1)S(1)} %get-tuple-element.36), channel_id=1, source_target_pairs={{0,7},{1,0},{2,1},{3,2},{4,3},{5,4},{6,5},{7,6},{8,15},{9,8},{10,9... | collective-permute-start | bytes 196616 | tf_op jit(solution)/shard_map/ppermute | solution.py:26
  24.2 2.2 %collective-permute-start.6 = (bf16[4,64,128]{2,1,0:T(8,128)(2,1)S(1)}, bf16[4,64,128]{2,1,0:T(8,128)(2,1)S(1)}, u32[]{:S(2)}, u32[]{:S(2)}) collective-permute-start(bf16[4,64,128]{2,1,0:T(8,128)(2,1)S(1)} %get-tuple-element.37), channel_id=1, source_target_pairs={{0,8},{8,0},{16,24},{24,16},{1,9},{9,1},{17,25},{25,17},{2,10},{10... | collective-permute-start | bytes 196616 | tf_op jit(solution)/shard_map/ppermute | solution.py:20
  31.5 7.4 %collective-permute-start.7 = (bf16[16,64,128]{2,1,0:T(8,128)(2,1)S(1)}, bf16[16,64,128]{2,1,0:T(8,128)(2,1)S(1)}, u32[]{:S(2)}, u32[]{:S(2)}) collective-permute-start(bf16[16,64,128]{2,1,0:T(8,128)(2,1)S(1)} %get-tuple-element.40), channel_id=1, source_target_pairs={{0,16},{8,24},{16,0},{24,8},{1,17},{9,25},{17,1},{25,9},{2,18},{10... | collective-permute-start | bytes 786440 | tf_op jit(solution)/shard_map/ppermute | solution.py:20
  41.1 7.0 %collective-permute-start.8 = (bf16[4,64,128]{2,1,0:T(8,128)(2,1)S(1)}, bf16[4,64,128]{2,1,0:T(8,128)(2,1)S(1)}, u32[]{:S(2)}, u32[]{:S(2)}) collective-permute-start(bf16[4,64,128]{2,1,0:T(8,128)(2,1)S(1)} %get-tuple-element.44), channel_id=1, source_target_pairs={{0,1},{1,2},{2,3},{3,4},{4,5},{5,6},{6,7},{7,0},{8,9},{9,10},{10,1... | collective-permute-start | bytes 196616 | tf_op jit(solution)/shard_map/ppermute | solution.py:26
  41.2 7.0 %collective-permute-start.9 = (bf16[4,64,128]{2,1,0:T(8,128)(2,1)S(1)}, bf16[4,64,128]{2,1,0:T(8,128)(2,1)S(1)}, u32[]{:S(2)}, u32[]{:S(2)}) collective-permute-start(bf16[4,64,128]{2,1,0:T(8,128)(2,1)S(1)} %get-tuple-element.45), channel_id=1, source_target_pairs={{0,7},{1,0},{2,1},{3,2},{4,3},{5,4},{6,5},{7,6},{8,15},{9,8},{10,9... | collective-permute-start | bytes 196616 | tf_op jit(solution)/shard_map/ppermute | solution.py:26
  45.9 2.2 %collective-permute-start.10 = (bf16[4,64,128]{2,1,0:T(8,128)(2,1)S(1)}, bf16[4,64,128]{2,1,0:T(8,128)(2,1)S(1)}, u32[]{:S(2)}, u32[]{:S(2)}) collective-permute-start(bf16[4,64,128]{2,1,0:T(8,128)(2,1)S(1)} %get-tuple-element.46), channel_id=1, source_target_pairs={{0,8},{8,0},{16,24},{24,16},{1,9},{9,1},{17,25},{25,17},{2,10},{10... | collective-permute-start | bytes 196616 | tf_op jit(solution)/shard_map/ppermute | solution.py:20
  51.0 7.4 %collective-permute-start.11 = (bf16[16,64,128]{2,1,0:T(8,128)(2,1)S(1)}, bf16[16,64,128]{2,1,0:T(8,128)(2,1)S(1)}, u32[]{:S(2)}, u32[]{:S(2)}) collective-permute-start(bf16[16,64,128]{2,1,0:T(8,128)(2,1)S(1)} %get-tuple-element.49), channel_id=1, source_target_pairs={{0,16},{8,24},{16,0},{24,8},{1,17},{9,25},{17,1},{25,9},{2,18},{10... | collective-permute-start | bytes 786440 | tf_op jit(solution)/shard_map/ppermute | solution.py:20
  59.5 7.0 %collective-permute-start.12 = (bf16[4,64,128]{2,1,0:T(8,128)(2,1)S(1)}, bf16[4,64,128]{2,1,0:T(8,128)(2,1)S(1)}, u32[]{:S(2)}, u32[]{:S(2)}) collective-permute-start(bf16[4,64,128]{2,1,0:T(8,128)(2,1)S(1)} %get-tuple-element.52), channel_id=1, source_target_pairs={{0,1},{1,2},{2,3},{3,4},{4,5},{5,6},{6,7},{7,0},{8,9},{9,10},{10,1... | collective-permute-start | bytes 196616 | tf_op jit(solution)/shard_map/ppermute | solution.py:26
  59.6 7.0 %collective-permute-start.13 = (bf16[4,64,128]{2,1,0:T(8,128)(2,1)S(1)}, bf16[4,64,128]{2,1,0:T(8,128)(2,1)S(1)}, u32[]{:S(2)}, u32[]{:S(2)}) collective-permute-start(bf16[4,64,128]{2,1,0:T(8,128)(2,1)S(1)} %get-tuple-element.53), channel_id=1, source_target_pairs={{0,7},{1,0},{2,1},{3,2},{4,3},{5,4},{6,5},{7,6},{8,15},{9,8},{10,9... | collective-permute-start | bytes 196616 | tf_op jit(solution)/shard_map/ppermute | solution.py:26
  64.3 2.2 %collective-permute-start.14 = (bf16[4,64,128]{2,1,0:T(8,128)(2,1)S(1)}, bf16[4,64,128]{2,1,0:T(8,128)(2,1)S(1)}, u32[]{:S(2)}, u32[]{:S(2)}) collective-permute-start(bf16[4,64,128]{2,1,0:T(8,128)(2,1)S(1)} %get-tuple-element.54), channel_id=1, source_target_pairs={{0,8},{8,0},{16,24},{24,16},{1,9},{9,1},{17,25},{25,17},{2,10},{10... | collective-permute-start | bytes 196616 | tf_op jit(solution)/shard_map/ppermute | solution.py:20
  69.7 7.5 %collective-permute-start.15 = (bf16[16,64,128]{2,1,0:T(8,128)(2,1)S(1)}, bf16[16,64,128]{2,1,0:T(8,128)(2,1)S(1)}, u32[]{:S(2)}, u32[]{:S(2)}) collective-permute-start(bf16[16,64,128]{2,1,0:T(8,128)(2,1)S(1)} %get-tuple-element.56), channel_id=1, source_target_pairs={{0,16},{8,24},{16,0},{24,8},{1,17},{9,25},{17,1},{25,9},{2,18},{10... | collective-permute-start | bytes 786440 | tf_op jit(solution)/shard_map/ppermute | solution.py:20

commit v3 on v0

v3 whole, which is shorter than its diff:
```python
import jax
import jax.numpy as jnp
from jax import lax
from jax.experimental import pallas as pl
from jax.experimental.pallas import tpu as pltpu
from jax.sharding import PartitionSpec as P

ITERS = 2
PARTS = 2
LIMIT = 16 << 20
LANES = 128
VMEM = pl.BlockSpec(memory_space=pltpu.VMEM)
HBM = pl.BlockSpec(memory_space=pltpu.HBM)
NT = (((1,), (1,)), ((), ()))


def partner(x, axis, apart):
    return lax.ppermute(x, axis, [(i, i ^ 1 << apart) for i in range(lax.axis_size(axis))])


def swapped(x, axis, first):
    size = lax.axis_size(axis)
    pairs = [(i % size, (i + 1) % size) for i in range(first, first + size, 2)]
    return lax.ppermute(x, axis, pairs + [(b, a) for a, b in pairs])


def like(x):
    return jax.ShapeDtypeStruct(x.shape, x.dtype)


def inside(x):
    return pltpu.with_memory_space_constraint(x, pltpu.HBM)


def call(body, outs, *args, in_specs=None, out_specs=None, scratch=(), cost=None):
    if cost is None:
        size = sum(x.size * x.dtype.itemsize for x in (*args, *jax.tree.leaves(outs)))
        cost = pl.CostEstimate(flops=64 * size, bytes_accessed=size, transcendentals=0)
    return pl.pallas_call(
        body,
        out_shape=outs,
        in_specs=in_specs or [VMEM] * len(args),
        out_specs=out_specs or jax.tree.map(lambda _: VMEM, outs),
        scratch_shapes=list(scratch),
        cost_estimate=cost,
        compiler_params=pltpu.CompilerParams(vmem_limit_bytes=LIMIT),
    )(*args)


def entry(table, at):
    return table[at : at + 1, 0:1][0, 0]


def is_fine(table):
    return entry(table, table.shape[0] - 1) == 1


def times(panel, block):
    return lax.dot_general(panel, block, NT, preferred_element_type=jnp.float32)


def gathered(source, table, row, blocks):
    count = blocks.shape[1]
    left = jnp.concatenate([source[entry(table, row * count + k)] for k in range(count)], axis=1)
    right = jnp.concatenate([blocks[row, k] for k in range(count)], axis=1)
    return times(left, right)


def joined(parts, scratch):
    at = 0
    for part in parts:
        for i in range(part.shape[0]):
            scratch[at + i] = part[i]
        at += part.shape[0]


def open_body(loads, panels, sent, arrivals):
    rows, _, width = panels.shape
    copies = [
        pltpu.make_async_copy(
            loads.at[:, pl.ds(i * width, width)], panels.at[i], arrivals.at[i]
        )
        for i in range(rows)
    ]
    for copy in copies:
        copy.start()
    for i, copy in enumerate(copies):
        copy.wait()
        sent[i] = panels[i].astype(jnp.bfloat16)


def fetch_body(*refs):
    count = (len(refs) - 1) // 3
    sources, targets, arrivals = refs[1 : 1 + count], refs[1 + count : 1 + 2 * count], refs[1 + 2 * count :]
    copies = [
        pltpu.make_async_copy(source.at[i], target.at[i], arrival.at[i])
        for source, target, arrival in zip(sources, targets, arrivals)
        for i in range(source.shape[0])
    ]
    for copy in copies:
        copy.start()
    for copy in copies:
        copy.wait()


def pack_body(table, source, *outs):
    for side, out in enumerate(outs):
        for j in range(out.shape[0]):
            out[j] = source[entry(table, side * out.shape[0] + j)]


def first_body(table, loads, *refs):
    *pieces, transfer, smoother, current, first, scratch = refs
    residual, arrived = pieces[: len(pieces) // 2], pieces[len(pieces) // 2 :]
    rows = first.shape[0]

    @pl.when(is_fine(table))
    def _():
        joined(residual, current)

    @pl.when(jnp.logical_not(is_fine(table)))
    def _():
        joined(arrived, scratch)
        for i in range(rows):
            current[i] = loads[i] + gathered(scratch, table, i, transfer)

    for i in range(rows):
        value = times(current[i].astype(jnp.bfloat16), smoother[i])
        first[i] = value.astype(jnp.bfloat16)


def second_body(part, table, current, first, *refs):
    *sources, blocks, smoother, full, rounded = refs[: len(refs) - (part == 0)]
    if part == 0:
        extension = refs[-1]
        joined([first, *sources], extension)
    else:
        (extension,) = sources
    rows = full.shape[0]
    low = part * rows
    for i in range(rows):
        applied = gathered(extension, table, low + i, blocks)
        rounded[i] = (current[low + i] - applied).astype(jnp.bfloat16)
    for i in range(rows):
        value = first[low + i].astype(jnp.float32) + times(rounded[i], smoother[low + i])
        full[i] = value
        rounded[i] = value.astype(jnp.bfloat16)


def update_body(table, *refs):
    *pieces, transfer, iterate, rounded, scratch = refs
    arrived, terms = pieces[:PARTS], pieces[PARTS:]

    @pl.when(is_fine(table))
    def _():
        joined(arrived, scratch)
        rows = terms[0].shape[0]
        for i in range(iterate.shape[0]):
            value = gathered(scratch, table, i, transfer)
            for at in range(0, len(terms), PARTS):
                value = terms[at + i // rows][i % rows] + value
            iterate[i] = value
            rounded[i] = value.astype(jnp.bfloat16)


def residual_body(part, table, loads, *refs):
    *sources, blocks, residual, sent = refs[: len(refs) - (part == 0)]

    @pl.when(is_fine(table))
    def _():
        if part == 0:
            extension = refs[-1]
            joined(sources, extension)
        else:
            (extension,) = sources
        rows = residual.shape[0]
        low = part * rows
        for i in range(rows):
            value = loads[low + i] - gathered(extension, table, low + i, blocks)
            residual[i] = value
            sent[i] = value.astype(jnp.bfloat16)


def last_body(table, *refs):
    *pieces, iterate, transfer, out, total, scratch, leaves = refs
    arrived, correction = pieces[:PARTS], pieces[PARTS:]
    rows, _, width = total.shape
    piece = correction[0].shape[0]
    copies = [
        pltpu.make_async_copy(total.at[i], out.at[:, pl.ds(i * width, width)], leaves.at[i])
        for i in range(rows)
    ]

    @pl.when(is_fine(table))
    def _():
        joined(arrived, scratch)
        for i in range(rows):
            value = iterate[i] + correction[i // piece][i % piece]
            total[i] = value + gathered(scratch, table, i, transfer)
            copies[i].start()

    @pl.when(jnp.logical_not(is_fine(table)))
    def _():
        for i in range(rows):
            total[i] = correction[i // piece][i % piece]
            copies[i].start()

    for copy in copies:
        copy.wait()


def local(loads, level_blocks, level_cols, smoother, transfer_blocks, transfer_cols, bound_rows):
    block_rows = level_cols.shape[1]
    width = level_blocks.shape[-1]
    load_cols = loads.shape[1]
    list_width = bound_rows.shape[-1]
    left_list, right_list, sibling_list = bound_rows[0, 0]
    blocks, smooth, transfer, loads = level_blocks[0], smoother[0], transfer_blocks[0], loads[0]

    def panels(count, kind):
        return jax.ShapeDtypeStruct((count, load_cols, width), kind)

    def held(count):
        return pltpu.VMEM((count, load_cols, width), jnp.bfloat16)

    wide, narrow = panels(block_rows, jnp.float32), panels(block_rows, jnp.bfloat16)
    wide_part = panels(block_rows // PARTS, jnp.float32)
    narrow_part = panels(block_rows // PARTS, jnp.bfloat16)
    listed = panels(list_width, jnp.bfloat16)
    extended = panels(block_rows + 3 * list_width, jnp.bfloat16)
    rowwise = pltpu.SemaphoreType.DMA((block_rows,))

    load_panels, sent = call(
        open_body, (wide, narrow), inside(loads), in_specs=[HBM], scratch=[rowwise]
    )
    arrived = [partner(sent, "level", 1)]

    even = lax.axis_index("dom") % 2 == 0
    ahead = swapped(jnp.where(even, right_list, left_list), "dom", 0)
    behind = swapped(jnp.where(even, left_list, right_list), "dom", 1)
    wanted = jnp.concatenate([ahead, behind, partner(sibling_list, "level", 0)])
    columns = level_cols.reshape(-1)
    from_left = (columns >= block_rows) & (columns < block_rows + list_width)
    from_right = (columns >= block_rows + list_width) & (columns < block_rows + 2 * list_width)
    moved = jnp.where(from_left, list_width, 0) - jnp.where(from_right, list_width, 0)
    columns = columns + jnp.where(even, moved, 0)
    fine = (lax.axis_index("level") < 2).astype(jnp.int32).reshape(1)

    def spread(values):
        return jnp.broadcast_to(values[:, None], (values.shape[0], LANES))

    level_table = spread(jnp.concatenate([columns, fine]))
    transfer_table = spread(jnp.concatenate([transfer_cols.reshape(-1), fine]))
    wanted_table = spread(wanted)

    def fetched(after, *sources):
        size = sum(x.size * x.dtype.itemsize for x in sources)
        return call(
            fetch_body, tuple(like(x) for x in sources), inside(after), *[inside(x) for x in sources],
            in_specs=[HBM] * (1 + len(sources)), scratch=[rowwise] * len(sources),
            cost=pl.CostEstimate(flops=0, bytes_accessed=2 * size, transcendentals=0),
        )

    def exchanged(source):
        ahead, behind, beside = call(pack_body, (listed,) * 3, wanted_table, source)
        ahead = swapped(ahead, "dom", 0)
        behind = swapped(behind, "dom", 1)
        return ahead, behind, partner(beside, "level", 0)

    def in_parts(body, args, sources, rest):
        fulls, passed = [], []
        for part in range(PARTS):
            outs = (wide_part, narrow_part) + ((extended,) if part == 0 else ())
            full, rounded, *more = call(
                lambda *refs, part=part: body(part, *refs), outs, *args, *sources, *rest
            )
            sources = more or sources
            fulls.append(full)
            passed.append(partner(rounded, "level", 1))
        return fulls, passed

    transfer, smooth = fetched(loads, transfer, smooth)
    residual, iterate = [load_panels], None
    for cycle_index in range(ITERS):
        if cycle_index > 0:
            residual, arrived = in_parts(
                residual_body, (level_table, load_panels), (rounded, *sides), (blocks,)
            )
        current, first = call(
            first_body, (wide, narrow), transfer_table, load_panels, *residual, *arrived,
            transfer, smooth, scratch=[held(block_rows)],
        )
        sides = exchanged(first)
        if cycle_index == 0:
            (blocks,) = fetched(loads, blocks)
        correction, returned = in_parts(
            second_body, (level_table, current, first), (*sides,), (blocks, smooth)
        )
        if cycle_index + 1 < ITERS:
            terms = [] if iterate is None else [iterate]
            iterate, rounded = call(
                update_body, (wide, narrow), transfer_table, *returned, *correction,
                *terms, transfer, scratch=[held(block_rows)],
            )
            sides = exchanged(rounded)
    final = call(
        last_body, jax.ShapeDtypeStruct((load_cols, block_rows * width), jnp.float32),
        transfer_table, *returned, *correction, iterate, transfer, out_specs=HBM,
        scratch=[pltpu.VMEM(wide.shape, jnp.float32), held(block_rows), rowwise],
    )
    return final[None]


def solution(mesh):
    in_specs = (
        P("level", None, "dom"),
        P("level", "dom", None, None, None),
        P("level", "dom", None),
        P("level", "dom", None, None),
        P("level", "dom", None, None, None),
        P("level", "dom", None),
        P("level", "dom", None, None),
    )
    out_specs = P("level", None, "dom")

    return jax.shard_map(local, mesh=mesh, in_specs=in_specs, out_specs=out_specs, check_vma=False)
```

time: 145 us -> 73.1 us (0.50)
  waiting for transfers between devices: 55 us -> 29.4 us
  local copies, waits for them, and re-layouts: 26 us -> 1.92 us
  Pallas kernels: 0 us -> 20.1 us
  matrix products: 19 us -> 0 us
  other arithmetic: 16.4 us -> 0.86 us
  starting transfers between devices: 27.9 us -> 20.4 us
    ppermute x12 -> x8, waiting for transfers between devices: 55 us -> 15.4 us  [swapped(): return lax.ppermute(x, axis, pairs + [(b, a) for a, b in pairs])]
    pallas_call x0 -> x16, Pallas kernels: none -> 20.1 us  [call(): pl.pallas_call(body, out_shape=outs, in_specs=in_specs or [VMEM] * len(ar...]
    gather x16 -> x0, local copies, waits for them, and re-layouts: 19.1 us -> none  [the longest x5 12.4 us: apply_blocks(): picked = jnp.take(panels, columns.reshape(-1), axis=1)]
    dot_general x7 -> x0, matrix products: 19 us -> none  [the longest x4 13.6 us: smooth(): jnp.einsum('csb,sab->csa', panels, smoother_here, preferred_element_type=...]
    ppermute x12 -> x8, starting transfers between devices: 27.8 us -> 12.5 us  [swapped(): return lax.ppermute(x, axis, pairs + [(b, a) for a, b in pairs])]
    ppermute x4 -> x11, waiting for transfers between devices: 0.01 us -> 14 us  [partner(): lax.ppermute(x, axis, [(i, i ^ 1 << apart) for i in range(lax.axis_size(a...]
    select_n x14 -> x1, other arithmetic: 14.1 us -> 0.69 us  [local(): ahead = swapped(jnp.where(even, right_list, left_list), 'dom', 0)]
    ppermute x4 -> x11, starting transfers between devices: 0.14 us -> 7.9 us  [partner(): lax.ppermute(x, axis, [(i, i ^ 1 << apart) for i in range(lax.axis_size(a...]
  transfers between devices with their start and end apart: 16 -> 19, of which waited for: 9 -> 12; matrix products, arithmetic and copies ran while one was open for 3% -> 3% of each run, Pallas kernels for 0% -> 11%
where the time goes in v3:
time: 73.1 us; the launch traced here: 72.8 us
  waiting for transfers between devices  29.4 us (40%)
  starting transfers between devices  20.4 us (28%)
  Pallas kernels  20.1 us (27%)
  local copies, waits for them, and re-layouts  1.92 us (3%)
  other arithmetic  0.86 us (1%)
    pallas_call x16, Pallas kernels, call(): pl.pallas_call(body, out_shape=outs, in_specs=in_specs or [VMEM] * len(ar...  20.1 us
    ppermute x8, waiting for transfers between devices, swapped(): return lax.ppermute(x, axis, pairs + [(b, a) for a, b in pairs])  15.4 us
    ppermute x11, waiting for transfers between devices, partner(): lax.ppermute(x, axis, [(i, i ^ 1 << apart) for i in range(lax.axis_size(a...  14 us
    ppermute x8, starting transfers between devices, swapped(): return lax.ppermute(x, axis, pairs + [(b, a) for a, b in pairs])  12.5 us
    ppermute x11, starting transfers between devices, partner(): lax.ppermute(x, axis, [(i, i ^ 1 << apart) for i in range(lax.axis_size(a...  7.9 us
    unnamed x2, local copies, waits for them, and re-layouts  1.53 us
  transfers between devices with their start and end apart: 19, of which 12 were waited for; matrix products, arithmetic and copies ran while one was open for 3% of the time, Pallas kernels for 11%

profile of v3, /device:TPU:0, one launch (start us, length us, event | category | flops | bytes accessed | tf_op | source)
XLA Modules:
  0.0 72.8 jit_solution(12677233087013973998)
XLA Ops:
  0.0 0.7 fusion.3
  0.7 3.0 %collective-permute-start.1 = (s32[4]{0:T(128)S(1)}, s32[4]{0:T(128)S(1)}, u32[]{:S(2)}, u32[]{:S(2)}) collective-permute-start(s32[4]{0:T(128)S(1)} %get-tuple-element.73), channel_id=1, source_target_pairs={{0,1},{2,3},{4,5},{6,7},{1,0},{3,2},{5,4},{7,6},{8,9},{10,11},{12,... | collective-permute-start | bytes 56 | tf_op jit(solution)/shard_map/ppermute | solution.py:24
  3.7 0.0 collective-permute-start.3
  3.7 3.5 %collective-permute-start.2 = (s32[4]{0:T(128)S(1)}, s32[4]{0:T(128)S(1)}, u32[]{:S(2)}, u32[]{:S(2)}) collective-permute-start(s32[4]{0:T(128)S(1)} %get-tuple-element.75), channel_id=1, source_target_pairs={{1,2},{3,4},{5,6},{7,0},{2,1},{4,3},{6,5},{0,7},{9,10},{11,12},{13... | collective-permute-start | bytes 56 | tf_op jit(solution)/shard_map/ppermute | solution.py:24
  7.2 1.1 %shard_map.73 = (f32[16,64,128]{2,1,0:T(8,128)S(1)}, bf16[16,64,128]{2,1,0:T(8,128)(2,1)S(1)}) custom-call(f32[64,2048]{1,0:T(8,128)} %bitcast.13), custom_call_target="tpu_custom_call" | custom-call | flops 83886080 | bytes 1310720 | tf_op jit(solution)/shard_map/pallas_call | solution.py:39
  8.4 1.6 %collective-permute-start = (bf16[16,64,128]{2,1,0:T(8,128)(2,1)S(1)}, bf16[16,64,128]{2,1,0:T(8,128)(2,1)S(1)}, u32[]{:S(2)}, u32[]{:S(2)}) collective-permute-start(bf16[16,64,128]{2,1,0:T(8,128)(2,1)S(1)} %get-tuple-element.40), channel_id=1, source_target_pairs={{0,16},{8,24},{16,0},{24,8},{1,17},{9,25},{17,1},{25,9},{2,18},{10... | collective-permute-start | bytes 786440 | tf_op jit(solution)/shard_map/ppermute | solution.py:18
  9.9 0.8 %copy.10 = s32[1,16,12]{2,1,0:T(8,128)S(1)} copy(s32[1,16,12]{1,0,2:T(1,128)} %param.9) | data formatting | bytes 1536 | tf_op args[2]
  10.7 0.1 reshape.28
  10.8 0.8 %copy.9 = s32[1,16,8]{2,1,0:T(8,128)S(1)} copy(s32[1,16,8]{1,2,0:T(8,128)} %param.12) | data formatting | bytes 1024 | tf_op args[5]
  11.6 0.1 reshape.25
  11.7 2.9 %shard_map.77.refs_6_.refs_4_.refs_3_ = bf16[16,12,128,128]{3,2,1,0:T(8,128)(2,1)S(1)} custom-call(f32[64,2048]{1,0:T(8,128)} %bitcast.14, bf16[16,12,128,128]{3,2,1,0:T(8,128)(2,1)} %bitcast.12), custom_call_target="tpu_custom_call" | custom-call | bytes 12582912 | tf_op jit(solution)/shard_map/pallas_call | solution.py:39
  14.6 2.6 %shard_map.74 = (bf16[16,8,128,128]{3,2,1,0:T(8,128)(2,1)S(1)}, bf16[16,128,128]{2,1,0:T(8,128)(2,1)S(1)}) custom-call(f32[64,2048]{1,0:T(8,128)} %bitcast.15, bf16[16,8,128,128]{3,2,1,0:T(8,128)(2,1)} %bitcast.16, bf16[16,128,128]{2,1,0:T(8,128)(2,1)} %bitcast.17), custom_call_target="tpu_custom_call" | custom-call | bytes 9437184 | tf_op jit(solution)/shard_map/pallas_call | solution.py:39
  17.2 0.0 collective-permute-done.1
  17.2 0.0 collective-permute-done.3
  17.3 0.0 collective-permute-done.2
  17.3 0.1 pad_add_fusion.2
  17.3 0.0 collective-permute-done.refs_1_
  17.3 0.1 broadcast_in_dim.33.table
  17.4 0.6 shard_map.75
  18.0 0.1 broadcast_in_dim.37.table
  18.1 0.1 shard_map.76
  18.1 0.1 collective-permute-start.4
  18.2 1.9 %collective-permute-start.5 = (bf16[4,64,128]{2,1,0:T(8,128)(2,1)S(1)}, bf16[4,64,128]{2,1,0:T(8,128)(2,1)S(1)}, u32[]{:S(2)}, u32[]{:S(2)}) collective-permute-start(bf16[4,64,128]{2,1,0:T(8,128)(2,1)S(1)} %get-tuple-element.46), channel_id=1, source_target_pairs={{1,2},{3,4},{5,6},{7,0},{2,1},{4,3},{6,5},{0,7},{9,10},{11,12},{13... | collective-permute-start | bytes 196616 | tf_op jit(solution)/shard_map/ppermute | solution.py:24
  20.1 0.0 collective-permute-start.6
  20.1 0.1 pad_add_fusion.1
  20.2 2.3 %collective-permute-done.4.refs_3_ = bf16[4,64,128]{2,1,0:T(8,128)(2,1)S(1)} collective-permute-done((bf16[4,64,128]{2,1,0:T(8,128)(2,1)S(1)}, bf16[4,64,128]{2,1,0:T(8,128)(2,1)S(1)}, u32[]{:S(2)}, u32[]{:S(2)}) %collective-permute-start.4) | collective-permute-done | bytes 65568 | tf_op jit(solution)/shard_map/ppermute | solution.py:24
  22.5 2.8 %collective-permute-done.5.refs_4_ = bf16[4,64,128]{2,1,0:T(8,128)(2,1)S(1)} collective-permute-done((bf16[4,64,128]{2,1,0:T(8,128)(2,1)S(1)}, bf16[4,64,128]{2,1,0:T(8,128)(2,1)S(1)}, u32[]{:S(2)}, u32[]{:S(2)}) %collective-permute-start.5) | collective-permute-done | bytes 65568 | tf_op jit(solution)/shard_map/ppermute | solution.py:24
  25.2 0.0 collective-permute-done.6.refs_5_
  25.2 0.1 broadcast_in_dim.36.refs_0_
  25.3 1.4 %shard_map.78 = (f32[8,64,128]{2,1,0:T(8,128)S(1)}, bf16[8,64,128]{2,1,0:T(8,128)(2,1)S(1)}, bf16[28,64,128]{2,1,0:T(8,128)(2,1)S(1)}) custom-call(s32[193,128]{1,0:T(8,128)S(1)} %broadcast_in_dim.36.refs_0_, f32[16,64,128]{2,1,0:T(8,128)S(1)} %get-tuple-element.43.refs_1_, bf16[16,64,128]{2,1,0:T(8,128)(2,1)S(1)} %get-tuple-element.44.source.refs_2_, ...), custom_call_target="tpu_custom_call" | custom-call | flops 559972352 | bytes 8749568 | tf_op jit(solution)/shard_map/pallas_call | solution.py:39
  26.7 1.3 %shard_map.79 = (f32[8,64,128]{2,1,0:T(8,128)S(1)}, bf16[8,64,128]{2,1,0:T(8,128)(2,1)S(1)}) custom-call(s32[193,128]{1,0:T(8,128)S(1)} %broadcast_in_dim.36.refs_0_, f32[16,64,128]{2,1,0:T(8,128)S(1)} %get-tuple-element.43.refs_1_, bf16[16,64,128]{2,1,0:T(8,128)(2,1)S(1)} %get-tuple-element.44.source.refs_2_, ...), custom_call_target="tpu_custom_call" | custom-call | flops 547389440 | bytes 8552960 | tf_op jit(solution)/shard_map/pallas_call | solution.py:39
  28.1 2.7 %collective-permute-start.8 = (bf16[8,64,128]{2,1,0:T(8,128)(2,1)S(1)}, bf16[8,64,128]{2,1,0:T(8,128)(2,1)S(1)}, u32[]{:S(2)}, u32[]{:S(2)}) collective-permute-start(bf16[8,64,128]{2,1,0:T(8,128)(2,1)S(1)} %get-tuple-element.50), channel_id=1, source_target_pairs={{0,16},{8,24},{16,0},{24,8},{1,17},{9,25},{17,1},{25,9},{2,18},{10... | collective-permute-start | bytes 393224 | tf_op jit(solution)/shard_map/ppermute | solution.py:18
  30.8 0.1 collective-permute-start.7
  30.9 3.3 %collective-permute-done.8.refs_1_ = bf16[8,64,128]{2,1,0:T(8,128)(2,1)S(1)} collective-permute-done((bf16[8,64,128]{2,1,0:T(8,128)(2,1)S(1)}, bf16[8,64,128]{2,1,0:T(8,128)(2,1)S(1)}, u32[]{:S(2)}, u32[]{:S(2)}) %collective-permute-start.8) | collective-permute-done | bytes 131104 | tf_op jit(solution)/shard_map/ppermute | solution.py:18
  34.2 1.5 %collective-permute-done.7.refs_0_ = bf16[8,64,128]{2,1,0:T(8,128)(2,1)S(1)} collective-permute-done((bf16[8,64,128]{2,1,0:T(8,128)(2,1)S(1)}, bf16[8,64,128]{2,1,0:T(8,128)(2,1)S(1)}, u32[]{:S(2)}, u32[]{:S(2)}) %collective-permute-start.7) | collective-permute-done | bytes 131104 | tf_op jit(solution)/shard_map/ppermute | solution.py:18
  35.8 1.7 %shard_map.80 = (f32[16,64,128]{2,1,0:T(8,128)S(1)}, bf16[16,64,128]{2,1,0:T(8,128)(2,1)S(1)}) custom-call(s32[129,128]{1,0:T(8,128)S(1)} %broadcast_in_dim.33.table, bf16[8,64,128]{2,1,0:T(8,128)(2,1)S(1)} %collective-permute-done.7.refs_0_, bf16[8,64,128]{2,1,0:T(8,128)(2,1)S(1)} %collective-permute-done.8.refs_1_, ...), custom_call_target="tpu_custom_call" | custom-call | flops 373325824 | bytes 5833216 | tf_op jit(solution)/shard_map/pallas_call | solution.py:39
  37.5 0.1 shard_map.81
  37.6 0.2 collective-permute-start.9
  37.8 1.8 %collective-permute-start.10 = (bf16[4,64,128]{2,1,0:T(8,128)(2,1)S(1)}, bf16[4,64,128]{2,1,0:T(8,128)(2,1)S(1)}, u32[]{:S(2)}, u32[]{:S(2)}) collective-permute-start(bf16[4,64,128]{2,1,0:T(8,128)(2,1)S(1)} %get-tuple-element.55), channel_id=1, source_target_pairs={{1,2},{3,4},{5,6},{7,0},{2,1},{4,3},{6,5},{0,7},{9,10},{11,12},{13... | collective-permute-start | bytes 196616 | tf_op jit(solution)/shard_map/ppermute | solution.py:24
  39.5 0.0 collective-permute-start.11
  39.5 2.5 %collective-permute-done.9.refs_3_ = bf16[4,64,128]{2,1,0:T(8,128)(2,1)S(1)} collective-permute-done((bf16[4,64,128]{2,1,0:T(8,128)(2,1)S(1)}, bf16[4,64,128]{2,1,0:T(8,128)(2,1)S(1)}, u32[]{:S(2)}, u32[]{:S(2)}) %collective-permute-start.9) | collective-permute-done | bytes 65568 | tf_op jit(solution)/shard_map/ppermute | solution.py:24
  42.0 2.7 %collective-permute-done.10.refs_4_ = bf16[4,64,128]{2,1,0:T(8,128)(2,1)S(1)} collective-permute-done((bf16[4,64,128]{2,1,0:T(8,128)(2,1)S(1)}, bf16[4,64,128]{2,1,0:T(8,128)(2,1)S(1)}, u32[]{:S(2)}, u32[]{:S(2)}) %collective-permute-start.10) | collective-permute-done | bytes 65568 | tf_op jit(solution)/shard_map/ppermute | solution.py:24
  44.7 0.0 collective-permute-done.11.refs_5_
  44.7 1.3 %shard_map.82 = (f32[8,64,128]{2,1,0:T(8,128)S(1)}, bf16[8,64,128]{2,1,0:T(8,128)(2,1)S(1)}, bf16[28,64,128]{2,1,0:T(8,128)(2,1)S(1)}) custom-call(s32[193,128]{1,0:T(8,128)S(1)} %broadcast_in_dim.36.refs_0_, f32[16,64,128]{2,1,0:T(8,128)S(1)} %get-tuple-element.39.loads.refs_0_.refs_1_, bf16[16,64,128]{2,1,0:T(8,128)(2,1)S(1)} %get-tuple-element.53.source.refs_2_, ...), custom_call_target="tpu_custom_call" | custom-call | flops 526417920 | bytes 8225280 | tf_op jit(solution)/shard_map/pallas_call | solution.py:39
  46.0 0.1 collective-permute-start.12
  46.1 1.2 %shard_map.83 = (f32[8,64,128]{2,1,0:T(8,128)S(1)}, bf16[8,64,128]{2,1,0:T(8,128)(2,1)S(1)}) custom-call(s32[193,128]{1,0:T(8,128)S(1)} %broadcast_in_dim.36.refs_0_, f32[16,64,128]{2,1,0:T(8,128)S(1)} %get-tuple-element.39.loads.refs_0_.refs_1_, bf16[28,64,128]{2,1,0:T(8,128)(2,1)S(1)} %get-tuple-element.58.refs_2_, ...), custom_call_target="tpu_custom_call" | custom-call | flops 497057792 | bytes 7766528 | tf_op jit(solution)/shard_map/pallas_call | solution.py:39
  47.3 0.9 %collective-permute-start.13 = (bf16[8,64,128]{2,1,0:T(8,128)(2,1)S(1)}, bf16[8,64,128]{2,1,0:T(8,128)(2,1)S(1)}, u32[]{:S(2)}, u32[]{:S(2)}) collective-permute-start(bf16[8,64,128]{2,1,0:T(8,128)(2,1)S(1)} %get-tuple-element.61), channel_id=1, source_target_pairs={{0,16},{8,24},{16,0},{24,8},{1,17},{9,25},{17,1},{25,9},{2,18},{10... | collective-permute-start | bytes 393224 | tf_op jit(solution)/shard_map/ppermute | solution.py:18
  48.2 2.8 %collective-permute-done.12.refs_2_ = bf16[8,64,128]{2,1,0:T(8,128)(2,1)S(1)} collective-permute-done((bf16[8,64,128]{2,1,0:T(8,128)(2,1)S(1)}, bf16[8,64,128]{2,1,0:T(8,128)(2,1)S(1)}, u32[]{:S(2)}, u32[]{:S(2)}) %collective-permute-start.12) | collective-permute-done | bytes 131104 | tf_op jit(solution)/shard_map/ppermute | solution.py:18
  51.0 1.4 %collective-permute-done.13.refs_3_ = bf16[8,64,128]{2,1,0:T(8,128)(2,1)S(1)} collective-permute-done((bf16[8,64,128]{2,1,0:T(8,128)(2,1)S(1)}, bf16[8,64,128]{2,1,0:T(8,128)(2,1)S(1)}, u32[]{:S(2)}, u32[]{:S(2)}) %collective-permute-start.13) | collective-permute-done | bytes 131104 | tf_op jit(solution)/shard_map/ppermute | solution.py:18
  52.4 0.6 shard_map.84
  53.0 0.1 shard_map.85
  53.1 0.1 collective-permute-start.14
  53.2 1.8 %collective-permute-start.15 = (bf16[4,64,128]{2,1,0:T(8,128)(2,1)S(1)}, bf16[4,64,128]{2,1,0:T(8,128)(2,1)S(1)}, u32[]{:S(2)}, u32[]{:S(2)}) collective-permute-start(bf16[4,64,128]{2,1,0:T(8,128)(2,1)S(1)} %get-tuple-element.65), channel_id=1, source_target_pairs={{1,2},{3,4},{5,6},{7,0},{2,1},{4,3},{6,5},{0,7},{9,10},{11,12},{13... | collective-permute-start | bytes 196616 | tf_op jit(solution)/shard_map/ppermute | solution.py:24
  55.1 0.0 collective-permute-start.16
  55.1 2.3 %collective-permute-done.14.refs_3_ = bf16[4,64,128]{2,1,0:T(8,128)(2,1)S(1)} collective-permute-done((bf16[4,64,128]{2,1,0:T(8,128)(2,1)S(1)}, bf16[4,64,128]{2,1,0:T(8,128)(2,1)S(1)}, u32[]{:S(2)}, u32[]{:S(2)}) %collective-permute-start.14) | collective-permute-done | bytes 65568 | tf_op jit(solution)/shard_map/ppermute | solution.py:24
  57.4 2.8 %collective-permute-done.15.refs_4_ = bf16[4,64,128]{2,1,0:T(8,128)(2,1)S(1)} collective-permute-done((bf16[4,64,128]{2,1,0:T(8,128)(2,1)S(1)}, bf16[4,64,128]{2,1,0:T(8,128)(2,1)S(1)}, u32[]{:S(2)}, u32[]{:S(2)}) %collective-permute-start.15) | collective-permute-done | bytes 65568 | tf_op jit(solution)/shard_map/ppermute | solution.py:24
  60.2 0.0 collective-permute-done.16.refs_5_
  60.2 1.4 %shard_map.86 = (f32[8,64,128]{2,1,0:T(8,128)S(1)}, bf16[8,64,128]{2,1,0:T(8,128)(2,1)S(1)}, bf16[28,64,128]{2,1,0:T(8,128)(2,1)S(1)}) custom-call(s32[193,128]{1,0:T(8,128)S(1)} %broadcast_in_dim.36.refs_0_, f32[16,64,128]{2,1,0:T(8,128)S(1)} %get-tuple-element.62.refs_1_, bf16[16,64,128]{2,1,0:T(8,128)(2,1)S(1)} %get-tuple-element.63.source.refs_2_, ...), custom_call_target="tpu_custom_call" | custom-call | flops 559972352 | bytes 8749568 | tf_op jit(solution)/shard_map/pallas_call | solution.py:39
  61.6 1.3 %shard_map.87 = (f32[8,64,128]{2,1,0:T(8,128)S(1)}, bf16[8,64,128]{2,1,0:T(8,128)(2,1)S(1)}) custom-call(s32[193,128]{1,0:T(8,128)S(1)} %broadcast_in_dim.36.refs_0_, f32[16,64,128]{2,1,0:T(8,128)S(1)} %get-tuple-element.62.refs_1_, bf16[16,64,128]{2,1,0:T(8,128)(2,1)S(1)} %get-tuple-element.63.source.refs_2_, ...), custom_call_target="tpu_custom_call" | custom-call | flops 547389440 | bytes 8552960 | tf_op jit(solution)/shard_map/pallas_call | solution.py:39
  62.9 2.5 %collective-permute-start.18 = (bf16[8,64,128]{2,1,0:T(8,128)(2,1)S(1)}, bf16[8,64,128]{2,1,0:T(8,128)(2,1)S(1)}, u32[]{:S(2)}, u32[]{:S(2)}) collective-permute-start(bf16[8,64,128]{2,1,0:T(8,128)(2,1)S(1)} %get-tuple-element.69), channel_id=1, source_target_pairs={{0,16},{8,24},{16,0},{24,8},{1,17},{9,25},{17,1},{25,9},{2,18},{10... | collective-permute-start | bytes 393224 | tf_op jit(solution)/shard_map/ppermute | solution.py:18
  65.4 0.1 collective-permute-start.17
  65.5 2.9 %collective-permute-done.18.refs_1_ = bf16[8,64,128]{2,1,0:T(8,128)(2,1)S(1)} collective-permute-done((bf16[8,64,128]{2,1,0:T(8,128)(2,1)S(1)}, bf16[8,64,128]{2,1,0:T(8,128)(2,1)S(1)}, u32[]{:S(2)}, u32[]{:S(2)}) %collective-permute-start.18) | collective-permute-done | bytes 131104 | tf_op jit(solution)/shard_map/ppermute | solution.py:18
  68.3 2.0 %collective-permute-done.17.refs_0_ = bf16[8,64,128]{2,1,0:T(8,128)(2,1)S(1)} collective-permute-done((bf16[8,64,128]{2,1,0:T(8,128)(2,1)S(1)}, bf16[8,64,128]{2,1,0:T(8,128)(2,1)S(1)}, u32[]{:S(2)}, u32[]{:S(2)}) %collective-permute-start.17) | collective-permute-done | bytes 131104 | tf_op jit(solution)/shard_map/ppermute | solution.py:18
  70.4 2.5 %shard_map.88 = f32[64,2048]{1,0:T(8,128)} custom-call(s32[129,128]{1,0:T(8,128)S(1)} %broadcast_in_dim.33.table, bf16[8,64,128]{2,1,0:T(8,128)(2,1)S(1)} %collective-permute-done.17.refs_0_, bf16[8,64,128]{2,1,0:T(8,128)(2,1)S(1)} %collective-permute-done.18.refs_1_, f32[8,64,128]{2,1,0:T(8,128)S(1)} %get-tuple-element.70.refs_2_, ...), custom_call_target="tpu_custom_call" | custom-call | flops 390103040 | bytes 6095360 | tf_op jit(solution)/shard_map/pallas_call | solution.py:39
  (2 shorter events, 0.0 us)
Async XLA Ops:
  0.7 16.5 %collective-permute-start.1 = (s32[4]{0:T(128)S(1)}, s32[4]{0:T(128)S(1)}, u32[]{:S(2)}, u32[]{:S(2)}) collective-permute-start(s32[4]{0:T(128)S(1)} %get-tuple-element.73), channel_id=1, source_target_pairs={{0,1},{2,3},{4,5},{6,7},{1,0},{3,2},{5,4},{7,6},{8,9},{10,11},{12,... | collective-permute-start | bytes 56 | tf_op jit(solution)/shard_map/ppermute | solution.py:24
  3.7 13.6 %collective-permute-start.3 = (s32[4]{0:T(128)S(1)}, s32[4]{0:T(128)S(1)}, u32[]{:S(2)}, u32[]{:S(2)}) collective-permute-start(s32[4]{0:T(128)S(1)} %get-tuple-element.74), channel_id=1, source_target_pairs={{0,8},{8,0},{16,24},{24,16},{1,9},{9,1},{17,25},{25,17},{2,10},{10... | collective-permute-start | bytes 56 | tf_op jit(solution)/shard_map/ppermute | solution.py:18
  3.7 13.6 %collective-permute-start.2 = (s32[4]{0:T(128)S(1)}, s32[4]{0:T(128)S(1)}, u32[]{:S(2)}, u32[]{:S(2)}) collective-permute-start(s32[4]{0:T(128)S(1)} %get-tuple-element.75), channel_id=1, source_target_pairs={{1,2},{3,4},{5,6},{7,0},{2,1},{4,3},{6,5},{0,7},{9,10},{11,12},{13... | collective-permute-start | bytes 56 | tf_op jit(solution)/shard_map/ppermute | solution.py:24
  8.4 9.0 %collective-permute-start = (bf16[16,64,128]{2,1,0:T(8,128)(2,1)S(1)}, bf16[16,64,128]{2,1,0:T(8,128)(2,1)S(1)}, u32[]{:S(2)}, u32[]{:S(2)}) collective-permute-start(bf16[16,64,128]{2,1,0:T(8,128)(2,1)S(1)} %get-tuple-element.40), channel_id=1, source_target_pairs={{0,16},{8,24},{16,0},{24,8},{1,17},{9,25},{17,1},{25,9},{2,18},{10... | collective-permute-start | bytes 786440 | tf_op jit(solution)/shard_map/ppermute | solution.py:18
  18.1 4.3 %collective-permute-start.4 = (bf16[4,64,128]{2,1,0:T(8,128)(2,1)S(1)}, bf16[4,64,128]{2,1,0:T(8,128)(2,1)S(1)}, u32[]{:S(2)}, u32[]{:S(2)}) collective-permute-start(bf16[4,64,128]{2,1,0:T(8,128)(2,1)S(1)} %get-tuple-element.45), channel_id=1, source_target_pairs={{0,1},{2,3},{4,5},{6,7},{1,0},{3,2},{5,4},{7,6},{8,9},{10,11},{12,... | collective-permute-start | bytes 196616 | tf_op jit(solution)/shard_map/ppermute | solution.py:24
  18.2 7.0 %collective-permute-start.5 = (bf16[4,64,128]{2,1,0:T(8,128)(2,1)S(1)}, bf16[4,64,128]{2,1,0:T(8,128)(2,1)S(1)}, u32[]{:S(2)}, u32[]{:S(2)}) collective-permute-start(bf16[4,64,128]{2,1,0:T(8,128)(2,1)S(1)} %get-tuple-element.46), channel_id=1, source_target_pairs={{1,2},{3,4},{5,6},{7,0},{2,1},{4,3},{6,5},{0,7},{9,10},{11,12},{13... | collective-permute-start | bytes 196616 | tf_op jit(solution)/shard_map/ppermute | solution.py:24
  20.1 5.1 %collective-permute-start.6 = (bf16[4,64,128]{2,1,0:T(8,128)(2,1)S(1)}, bf16[4,64,128]{2,1,0:T(8,128)(2,1)S(1)}, u32[]{:S(2)}, u32[]{:S(2)}) collective-permute-start(bf16[4,64,128]{2,1,0:T(8,128)(2,1)S(1)} %get-tuple-element.47), channel_id=1, source_target_pairs={{0,8},{8,0},{16,24},{24,16},{1,9},{9,1},{17,25},{25,17},{2,10},{10... | collective-permute-start | bytes 196616 | tf_op jit(solution)/shard_map/ppermute | solution.py:18
  28.1 6.2 %collective-permute-start.8 = (bf16[8,64,128]{2,1,0:T(8,128)(2,1)S(1)}, bf16[8,64,128]{2,1,0:T(8,128)(2,1)S(1)}, u32[]{:S(2)}, u32[]{:S(2)}) collective-permute-start(bf16[8,64,128]{2,1,0:T(8,128)(2,1)S(1)} %get-tuple-element.50), channel_id=1, source_target_pairs={{0,16},{8,24},{16,0},{24,8},{1,17},{9,25},{17,1},{25,9},{2,18},{10... | collective-permute-start | bytes 393224 | tf_op jit(solution)/shard_map/ppermute | solution.py:18
  30.8 5.0 %collective-permute-start.7 = (bf16[8,64,128]{2,1,0:T(8,128)(2,1)S(1)}, bf16[8,64,128]{2,1,0:T(8,128)(2,1)S(1)}, u32[]{:S(2)}, u32[]{:S(2)}) collective-permute-start(bf16[8,64,128]{2,1,0:T(8,128)(2,1)S(1)} %get-tuple-element.48), channel_id=1, source_target_pairs={{0,16},{8,24},{16,0},{24,8},{1,17},{9,25},{17,1},{25,9},{2,18},{10... | collective-permute-start | bytes 393224 | tf_op jit(solution)/shard_map/ppermute | solution.py:18
  37.6 4.5 %collective-permute-start.9 = (bf16[4,64,128]{2,1,0:T(8,128)(2,1)S(1)}, bf16[4,64,128]{2,1,0:T(8,128)(2,1)S(1)}, u32[]{:S(2)}, u32[]{:S(2)}) collective-permute-start(bf16[4,64,128]{2,1,0:T(8,128)(2,1)S(1)} %get-tuple-element.54), channel_id=1, source_target_pairs={{0,1},{2,3},{4,5},{6,7},{1,0},{3,2},{5,4},{7,6},{8,9},{10,11},{12,... | collective-permute-start | bytes 196616 | tf_op jit(solution)/shard_map/ppermute | solution.py:24
  37.8 7.0 %collective-permute-start.10 = (bf16[4,64,128]{2,1,0:T(8,128)(2,1)S(1)}, bf16[4,64,128]{2,1,0:T(8,128)(2,1)S(1)}, u32[]{:S(2)}, u32[]{:S(2)}) collective-permute-start(bf16[4,64,128]{2,1,0:T(8,128)(2,1)S(1)} %get-tuple-element.55), channel_id=1, source_target_pairs={{1,2},{3,4},{5,6},{7,0},{2,1},{4,3},{6,5},{0,7},{9,10},{11,12},{13... | collective-permute-start | bytes 196616 | tf_op jit(solution)/shard_map/ppermute | solution.py:24
  39.5 5.2 %collective-permute-start.11 = (bf16[4,64,128]{2,1,0:T(8,128)(2,1)S(1)}, bf16[4,64,128]{2,1,0:T(8,128)(2,1)S(1)}, u32[]{:S(2)}, u32[]{:S(2)}) collective-permute-start(bf16[4,64,128]{2,1,0:T(8,128)(2,1)S(1)} %get-tuple-element.56), channel_id=1, source_target_pairs={{0,8},{8,0},{16,24},{24,16},{1,9},{9,1},{17,25},{25,17},{2,10},{10... | collective-permute-start | bytes 196616 | tf_op jit(solution)/shard_map/ppermute | solution.py:18
  46.0 5.0 %collective-permute-start.12 = (bf16[8,64,128]{2,1,0:T(8,128)(2,1)S(1)}, bf16[8,64,128]{2,1,0:T(8,128)(2,1)S(1)}, u32[]{:S(2)}, u32[]{:S(2)}) collective-permute-start(bf16[8,64,128]{2,1,0:T(8,128)(2,1)S(1)} %get-tuple-element.60), channel_id=1, source_target_pairs={{0,16},{8,24},{16,0},{24,8},{1,17},{9,25},{17,1},{25,9},{2,18},{10... | collective-permute-start | bytes 393224 | tf_op jit(solution)/shard_map/ppermute | solution.py:18
  47.3 5.1 %collective-permute-start.13 = (bf16[8,64,128]{2,1,0:T(8,128)(2,1)S(1)}, bf16[8,64,128]{2,1,0:T(8,128)(2,1)S(1)}, u32[]{:S(2)}, u32[]{:S(2)}) collective-permute-start(bf16[8,64,128]{2,1,0:T(8,128)(2,1)S(1)} %get-tuple-element.61), channel_id=1, source_target_pairs={{0,16},{8,24},{16,0},{24,8},{1,17},{9,25},{17,1},{25,9},{2,18},{10... | collective-permute-start | bytes 393224 | tf_op jit(solution)/shard_map/ppermute | solution.py:18
  53.1 4.3 %collective-permute-start.14 = (bf16[4,64,128]{2,1,0:T(8,128)(2,1)S(1)}, bf16[4,64,128]{2,1,0:T(8,128)(2,1)S(1)}, u32[]{:S(2)}, u32[]{:S(2)}) collective-permute-start(bf16[4,64,128]{2,1,0:T(8,128)(2,1)S(1)} %get-tuple-element.64), channel_id=1, source_target_pairs={{0,1},{2,3},{4,5},{6,7},{1,0},{3,2},{5,4},{7,6},{8,9},{10,11},{12,... | collective-permute-start | bytes 196616 | tf_op jit(solution)/shard_map/ppermute | solution.py:24
  53.2 7.0 %collective-permute-start.15 = (bf16[4,64,128]{2,1,0:T(8,128)(2,1)S(1)}, bf16[4,64,128]{2,1,0:T(8,128)(2,1)S(1)}, u32[]{:S(2)}, u32[]{:S(2)}) collective-permute-start(bf16[4,64,128]{2,1,0:T(8,128)(2,1)S(1)} %get-tuple-element.65), channel_id=1, source_target_pairs={{1,2},{3,4},{5,6},{7,0},{2,1},{4,3},{6,5},{0,7},{9,10},{11,12},{13... | collective-permute-start | bytes 196616 | tf_op jit(solution)/shard_map/ppermute | solution.py:24
  55.1 5.1 %collective-permute-start.16 = (bf16[4,64,128]{2,1,0:T(8,128)(2,1)S(1)}, bf16[4,64,128]{2,1,0:T(8,128)(2,1)S(1)}, u32[]{:S(2)}, u32[]{:S(2)}) collective-permute-start(bf16[4,64,128]{2,1,0:T(8,128)(2,1)S(1)} %get-tuple-element.66), channel_id=1, source_target_pairs={{0,8},{8,0},{16,24},{24,16},{1,9},{9,1},{17,25},{25,17},{2,10},{10... | collective-permute-start | bytes 196616 | tf_op jit(solution)/shard_map/ppermute | solution.py:18
  62.9 5.4 %collective-permute-start.18 = (bf16[8,64,128]{2,1,0:T(8,128)(2,1)S(1)}, bf16[8,64,128]{2,1,0:T(8,128)(2,1)S(1)}, u32[]{:S(2)}, u32[]{:S(2)}) collective-permute-start(bf16[8,64,128]{2,1,0:T(8,128)(2,1)S(1)} %get-tuple-element.69), channel_id=1, source_target_pairs={{0,16},{8,24},{16,0},{24,8},{1,17},{9,25},{17,1},{25,9},{2,18},{10... | collective-permute-start | bytes 393224 | tf_op jit(solution)/shard_map/ppermute | solution.py:18
  65.4 5.0 %collective-permute-start.17 = (bf16[8,64,128]{2,1,0:T(8,128)(2,1)S(1)}, bf16[8,64,128]{2,1,0:T(8,128)(2,1)S(1)}, u32[]{:S(2)}, u32[]{:S(2)}) collective-permute-start(bf16[8,64,128]{2,1,0:T(8,128)(2,1)S(1)} %get-tuple-element.67), channel_id=1, source_target_pairs={{0,16},{8,24},{16,0},{24,8},{1,17},{9,25},{17,1},{25,9},{2,18},{10... | collective-permute-start | bytes 393224 | tf_op jit(solution)/shard_map/ppermute | solution.py:18

commit v4 on v3

v4 whole, which is shorter than its diff:
```python
import jax
import jax.numpy as jnp
from jax import lax
from jax.experimental import pallas as pl
from jax.experimental.pallas import tpu as pltpu
from jax.sharding import PartitionSpec as P

ITERS = 2
CHUNK = 4
LIMIT = 16 << 20
LANES = 128
VMEM = pl.BlockSpec(memory_space=pltpu.VMEM)
HBM = pl.BlockSpec(memory_space=pltpu.HBM)
NT = (((1,), (1,)), ((), ()))


def partner(x, axis, apart):
    return lax.ppermute(x, axis, [(i, i ^ 1 << apart) for i in range(lax.axis_size(axis))])


def swapped(x, axis, first):
    size = lax.axis_size(axis)
    pairs = [(i % size, (i + 1) % size) for i in range(first, first + size, 2)]
    return lax.ppermute(x, axis, pairs + [(b, a) for a, b in pairs])


def like(x):
    return jax.ShapeDtypeStruct(x.shape, x.dtype)


def inside(x):
    return pltpu.with_memory_space_constraint(x, pltpu.HBM)


def call(body, outs, *args, in_specs=None, out_specs=None, scratch=(), cost=None):
    if cost is None:
        size = sum(x.size * x.dtype.itemsize for x in (*args, *jax.tree.leaves(outs)))
        cost = pl.CostEstimate(flops=64 * size, bytes_accessed=size, transcendentals=0)
    return pl.pallas_call(
        body,
        out_shape=outs,
        in_specs=in_specs or [VMEM] * len(args),
        out_specs=out_specs or jax.tree.map(lambda _: VMEM, outs),
        scratch_shapes=list(scratch),
        cost_estimate=cost,
        compiler_params=pltpu.CompilerParams(vmem_limit_bytes=LIMIT),
    )(*args)


def entry(table, at):
    return table[at : at + 1, 0:1][0, 0]


def is_fine(table):
    return entry(table, table.shape[0] - 1) == 1


def times(panel, block):
    return lax.dot_general(panel, block, NT, preferred_element_type=jnp.float32)


def gathered(source, table, row, blocks):
    count = blocks.shape[1]
    left = jnp.concatenate([source[entry(table, row * count + k)] for k in range(count)], axis=1)
    right = jnp.concatenate([blocks[row, k] for k in range(count)], axis=1)
    return times(left, right)


def joined(parts, scratch):
    at = 0
    for part in parts:
        for i in range(part.shape[0]):
            scratch[at + i] = part[i]
        at += part.shape[0]


def open_body(loads, panels, sent, arrivals):
    rows, _, width = panels.shape
    copies = [
        pltpu.make_async_copy(
            loads.at[:, pl.ds(i * width, width)], panels.at[i], arrivals.at[i]
        )
        for i in range(rows)
    ]
    for copy in copies:
        copy.start()
    for i, copy in enumerate(copies):
        copy.wait()
        sent[i] = panels[i].astype(jnp.bfloat16)


def pack_body(table, source, *outs):
    for side, out in enumerate(outs):
        for j in range(out.shape[0]):
            out[j] = source[entry(table, side * out.shape[0] + j)]


def first_body(fetch, table, loads, *refs):
    if fetch:
        *refs, arrivals = refs
        *pieces, source, smoother, current, first, transfer, scratch = refs
        copies = [
            pltpu.make_async_copy(source.at[i], transfer.at[i], arrivals.at[i])
            for i in range(source.shape[0])
        ]
    else:
        *pieces, transfer, smoother, current, first, scratch = refs
        copies = []
    for copy in copies:
        copy.start()
    residual, arrived = pieces[: len(pieces) // 2], pieces[len(pieces) // 2 :]
    rows = first.shape[0]

    @pl.when(is_fine(table))
    def _():
        joined(residual, current)
        for copy in copies:
            copy.wait()

    @pl.when(jnp.logical_not(is_fine(table)))
    def _():
        joined(arrived, scratch)
        for i in range(rows):
            if i % CHUNK == 0:
                for copy in copies[i : i + CHUNK]:
                    copy.wait()
            current[i] = loads[i] + gathered(scratch, table, i, transfer)

    for i in range(rows):
        value = times(current[i].astype(jnp.bfloat16), smoother[i])
        first[i] = value.astype(jnp.bfloat16)


def second_rows(low, targets, table, current, first, extension, blocks, smoother, rounded):
    places = [(full, i) for full in targets for i in range(full.shape[0])]
    for at in range(len(places)):
        applied = gathered(extension, table, low + at, blocks)
        rounded[at] = (current[low + at] - applied).astype(jnp.bfloat16)
    for at, (full, i) in enumerate(places):
        value = first[low + at].astype(jnp.float32) + times(rounded[at], smoother[low + at])
        full[i] = value
        if full is targets[0]:
            rounded[at] = value.astype(jnp.bfloat16)


def second_start_body(table, current, first, left, right, sibling, blocks, smoother, full, rounded, extension, rest, scratch):
    joined([first, left, right, sibling], extension)

    @pl.when(is_fine(table))
    def _():
        second_rows(0, (full, rest), table, current, first, extension, blocks, smoother, scratch)

    @pl.when(jnp.logical_not(is_fine(table)))
    def _():
        second_rows(0, (full,), table, current, first, extension, blocks, smoother, rounded)


def second_end_body(table, current, first, extension, blocks, smoother, full, rounded):
    @pl.when(jnp.logical_not(is_fine(table)))
    def _():
        low = first.shape[0] - full.shape[0]
        second_rows(low, (full,), table, current, first, extension, blocks, smoother, rounded)


def row_of(parts, at):
    for part in parts:
        if at < part.shape[0]:
            return part[at]
        at -= part.shape[0]


def update_body(table, early, late, correction, rest, *refs):
    *terms, transfer, iterate, rounded, scratch = refs

    @pl.when(is_fine(table))
    def _():
        joined((early, late), scratch)
        for i in range(iterate.shape[0]):
            value = row_of((correction, rest), i)
            for term in terms:
                value = term[i] + value
            value = value + gathered(scratch, table, i, transfer)
            iterate[i] = value
            rounded[i] = value.astype(jnp.bfloat16)


def residual_body(low, table, loads, *refs):
    *sources, blocks, residual, sent = refs[: len(refs) - (low == 0)]

    @pl.when(is_fine(table))
    def _():
        if low == 0:
            extension = refs[-1]
            joined(sources, extension)
        else:
            (extension,) = sources
        for i in range(residual.shape[0]):
            value = loads[low + i] - gathered(extension, table, low + i, blocks)
            residual[i] = value
            sent[i] = value.astype(jnp.bfloat16)


def last_body(table, early, late, correction, rest, end, iterate, transfer, out, total, scratch, leaves):
    rows, _, width = total.shape
    copies = [
        pltpu.make_async_copy(total.at[i], out.at[:, pl.ds(i * width, width)], leaves.at[i])
        for i in range(rows)
    ]

    @pl.when(is_fine(table))
    def _():
        joined((early, late), scratch)
        for i in range(rows):
            value = iterate[i] + row_of((correction, rest), i)
            total[i] = value + gathered(scratch, table, i, transfer)
            copies[i].start()

    @pl.when(jnp.logical_not(is_fine(table)))
    def _():
        for i in range(rows):
            total[i] = row_of((correction, end), i)
            copies[i].start()

    for copy in copies:
        copy.wait()


def local(loads, level_blocks, level_cols, smoother, transfer_blocks, transfer_cols, bound_rows):
    block_rows = level_cols.shape[1]
    width = level_blocks.shape[-1]
    load_cols = loads.shape[1]
    list_width = bound_rows.shape[-1]
    left_list, right_list, sibling_list = bound_rows[0, 0]
    blocks, smooth, transfer, loads = level_blocks[0], smoother[0], transfer_blocks[0], loads[0]

    def panels(count, kind):
        return jax.ShapeDtypeStruct((count, load_cols, width), kind)

    def held(count):
        return pltpu.VMEM((count, load_cols, width), jnp.bfloat16)

    wide, narrow = panels(block_rows, jnp.float32), panels(block_rows, jnp.bfloat16)
    early_rows = block_rows // 4
    late_rows = block_rows - early_rows
    listed = panels(list_width, jnp.bfloat16)
    extended = panels(block_rows + 3 * list_width, jnp.bfloat16)
    rowwise = pltpu.SemaphoreType.DMA((block_rows,))

    load_panels, sent = call(
        open_body, (wide, narrow), inside(loads), in_specs=[HBM], scratch=[rowwise],
        cost=pl.CostEstimate(flops=5_000_000_000, bytes_accessed=2 * loads.size * 4, transcendentals=0),
    )
    arrived = [partner(sent, "level", 1)]

    even = lax.axis_index("dom") % 2 == 0
    ahead = swapped(jnp.where(even, right_list, left_list), "dom", 0)
    behind = swapped(jnp.where(even, left_list, right_list), "dom", 1)
    wanted = jnp.concatenate([ahead, behind, partner(sibling_list, "level", 0)])
    columns = level_cols.reshape(-1)
    from_left = (columns >= block_rows) & (columns < block_rows + list_width)
    from_right = (columns >= block_rows + list_width) & (columns < block_rows + 2 * list_width)
    moved = jnp.where(from_left, list_width, 0) - jnp.where(from_right, list_width, 0)
    columns = columns + jnp.where(even, moved, 0)
    fine = (lax.axis_index("level") < 2).astype(jnp.int32).reshape(1)

    def spread(values):
        return jnp.broadcast_to(values[:, None], (values.shape[0], LANES))

    level_table = spread(jnp.concatenate([columns, fine]))
    transfer_table = spread(jnp.concatenate([transfer_cols.reshape(-1), fine]))
    wanted_table = spread(wanted)

    def exchanged(source):
        ahead, behind, beside = call(pack_body, (listed,) * 3, wanted_table, source)
        ahead = swapped(ahead, "dom", 0)
        behind = swapped(behind, "dom", 1)
        return ahead, behind, partner(beside, "level", 0)

    def part(rows):
        return panels(rows, jnp.float32), panels(rows, jnp.bfloat16)

    def sent_on(x):
        return partner(x, "level", 1)

    residual, iterate = [load_panels], None
    for cycle_index in range(ITERS):
        if cycle_index > 0:
            args = (level_table, load_panels)
            early, sent, extension = call(
                lambda *refs: residual_body(0, *refs), part(early_rows) + (extended,),
                *args, rounded, *sides, blocks,
            )
            arrived = [sent_on(sent)]
            late, sent = call(
                lambda *refs: residual_body(early_rows, *refs), part(late_rows),
                *args, extension, blocks,
            )
            arrived.append(partner(sent, "level", 1))
            residual = [early, late]
        fetch = cycle_index == 0
        current, first, *kept = call(
            lambda *refs: first_body(fetch, *refs), (wide, narrow) + (like(transfer),) * fetch,
            transfer_table, load_panels, *residual, *arrived,
            inside(transfer) if fetch else transfer, smooth,
            in_specs=[VMEM] * (2 + len(residual) + len(arrived)) + [HBM if fetch else VMEM, VMEM],
            scratch=[held(block_rows)] + [rowwise] * fetch,
        )
        (transfer,) = kept or (transfer,)
        sides = exchanged(first)
        args = (level_table, current, first)
        correction, rounded, extension, rest = call(
            second_start_body,
            part(early_rows) + (extended, panels(late_rows, jnp.float32)),
            *args, *sides, blocks, smooth, scratch=[held(block_rows)],
        )
        returned = [sent_on(rounded)]
        end, rounded = call(second_end_body, part(late_rows), *args, extension, blocks, smooth)
        returned.append(partner(rounded, "level", 1))
        if cycle_index + 1 < ITERS:
            terms = [] if iterate is None else [iterate]
            iterate, rounded = call(
                update_body, (wide, narrow), transfer_table, *returned, correction, rest,
                *terms, transfer, scratch=[held(block_rows)],
            )
            sides = exchanged(rounded)
    final = call(
        last_body, jax.ShapeDtypeStruct((load_cols, block_rows * width), jnp.float32),
        transfer_table, *returned, correction, rest, end, iterate, transfer, out_specs=HBM,
        scratch=[pltpu.VMEM(wide.shape, jnp.float32), held(block_rows), rowwise],
    )
    return final[None]


def solution(mesh):
    in_specs = (
        P("level", None, "dom"),
        P("level", "dom", None, None, None),
        P("level", "dom", None),
        P("level", "dom", None, None),
        P("level", "dom", None, None, None),
        P("level", "dom", None),
        P("level", "dom", None, None),
    )
    out_specs = P("level", None, "dom")

    return jax.shard_map(local, mesh=mesh, in_specs=in_specs, out_specs=out_specs, check_vma=False)
```

time: 73.1 us -> 80.6 us (1.10)
  waiting for transfers between devices: 29.4 us -> 35.9 us
  Pallas kernels: 20.1 us -> 18.3 us
  local copies, waits for them, and re-layouts: 1.92 us -> 3.35 us
  starting transfers between devices: 20.4 us -> 21.8 us
    ppermute x11, waiting for transfers between devices: 14 us -> 20 us  [partner(): lax.ppermute(x, axis, [(i, i ^ 1 << apart) for i in range(lax.axis_size(a...]
    ppermute x11, starting transfers between devices: 7.9 us -> 9.81 us  [partner(): lax.ppermute(x, axis, [(i, i ^ 1 << apart) for i in range(lax.axis_size(a...]
    pallas_call x16 -> x14, Pallas kernels: 20.1 us -> 18.3 us  [call(): pl.pallas_call(body, out_shape=outs, in_specs=in_specs or [VMEM] * len(ar...]
    unnamed x2 -> x14, local copies, waits for them, and re-layouts: 1.53 us -> 2.96 us
  transfers between devices with their start and end apart: 19 -> 19, of which waited for: 12 -> 10; matrix products, arithmetic and copies ran while one was open for 3% -> 1% of each run, Pallas kernels for 11% -> 2%
where the time goes in v4:
time: 80.6 us; the launch traced here: 80.4 us
  waiting for transfers between devices  35.9 us (45%)
  starting transfers between devices  21.8 us (27%)
  Pallas kernels  18.3 us (23%)
  local copies, waits for them, and re-layouts  3.35 us (4%)
  other arithmetic  0.86 us (1%)
    ppermute x11, waiting for transfers between devices, partner(): lax.ppermute(x, axis, [(i, i ^ 1 << apart) for i in range(lax.axis_size(a...  20 us
    pallas_call x14, Pallas kernels, call(): pl.pallas_call(body, out_shape=outs, in_specs=in_specs or [VMEM] * len(ar...  18.3 us
    ppermute x8, waiting for transfers between devices, swapped(): return lax.ppermute(x, axis, pairs + [(b, a) for a, b in pairs])  15.8 us
    ppermute x8, starting transfers between devices, swapped(): return lax.ppermute(x, axis, pairs + [(b, a) for a, b in pairs])  12 us
    ppermute x11, starting transfers between devices, partner(): lax.ppermute(x, axis, [(i, i ^ 1 << apart) for i in range(lax.axis_size(a...  9.81 us
    unnamed x14, local copies, waits for them, and re-layouts  2.96 us
  transfers between devices with their start and end apart: 19, of which 10 were waited for; matrix products, arithmetic and copies ran while one was open for 1% of the time, Pallas kernels for 2%

profile of v4, /device:TPU:0, one launch (start us, length us, event | category | flops | bytes accessed | tf_op | source)
XLA Modules:
  0.0 80.4 jit_solution(12122542136241698136)
XLA Ops:
  0.0 0.7 fusion.3
  0.7 3.0 %collective-permute-start.1 = (s32[4]{0:T(128)S(1)}, s32[4]{0:T(128)S(1)}, u32[]{:S(2)}, u32[]{:S(2)}) collective-permute-start(s32[4]{0:T(128)S(1)} %get-tuple-element.73), channel_id=1, source_target_pairs={{0,1},{2,3},{4,5},{6,7},{1,0},{3,2},{5,4},{7,6},{8,9},{10,11},{12,... | collective-permute-start | bytes 56 | tf_op jit(solution)/shard_map/ppermute | solution.py:24
  3.7 0.0 collective-permute-start.3
  3.7 3.5 %collective-permute-start.2 = (s32[4]{0:T(128)S(1)}, s32[4]{0:T(128)S(1)}, u32[]{:S(2)}, u32[]{:S(2)}) collective-permute-start(s32[4]{0:T(128)S(1)} %get-tuple-element.75), channel_id=1, source_target_pairs={{1,2},{3,4},{5,6},{7,0},{2,1},{4,3},{6,5},{0,7},{9,10},{11,12},{13... | collective-permute-start | bytes 56 | tf_op jit(solution)/shard_map/ppermute | solution.py:24
  7.2 1.9 %shard_map.73 = (f32[16,64,128]{2,1,0:T(8,128)S(1)}, bf16[16,64,128]{2,1,0:T(8,128)(2,1)}) custom-call(f32[64,2048]{1,0:T(8,128)} %bitcast.27), custom_call_target="tpu_custom_call" | custom-call | flops 5000000000 | bytes 1048576 | tf_op jit(solution)/shard_map/pallas_call | solution.py:39
  9.1 1.6 %collective-permute-start = (bf16[16,64,128]{2,1,0:T(8,128)(2,1)}, bf16[16,64,128]{2,1,0:T(8,128)(2,1)S(1)}, u32[]{:S(2)}, u32[]{:S(2)}) collective-permute-start(bf16[16,64,128]{2,1,0:T(8,128)(2,1)} %get-tuple-element.40), channel_id=1, source_target_pairs={{0,16},{8,24},{16,0},{24,8},{1,17},{9,25},{17,1},{25,9},{2,18},{10... | collective-permute-start | bytes 786440 | tf_op jit(solution)/shard_map/ppermute | solution.py:18
  10.7 0.1 copy.10
  10.8 0.1 reshape.28
  10.9 0.1 copy.9
  11.0 0.1 reshape.25
  11.1 0.0 collective-permute-done.1
  11.1 0.0 collective-permute-done.3
  11.1 0.0 collective-permute-done.2
  11.1 0.1 pad_add_fusion.2
  11.2 6.7 %collective-permute-done.refs_3_ = bf16[16,64,128]{2,1,0:T(8,128)(2,1)S(1)} collective-permute-done((bf16[16,64,128]{2,1,0:T(8,128)(2,1)}, bf16[16,64,128]{2,1,0:T(8,128)(2,1)S(1)}, u32[]{:S(2)}, u32[]{:S(2)}) %collective-permute-start) | collective-permute-done | bytes 262176 | tf_op jit(solution)/shard_map/ppermute | solution.py:18
  17.9 0.1 broadcast_in_dim.33.refs_0_.table
  17.9 0.0 copy-done.1
  17.9 2.8 %shard_map.74 = (f32[16,64,128]{2,1,0:T(8,128)S(1)}, bf16[16,64,128]{2,1,0:T(8,128)(2,1)S(1)}, bf16[16,8,128,128]{3,2,1,0:T(8,128)(2,1)S(1)}) custom-call(s32[129,128]{1,0:T(8,128)S(1)} %broadcast_in_dim.33.refs_0_.table, f32[16,64,128]{2,1,0:T(8,128)S(1)} %get-tuple-element.39.refs_1_.refs_2_, f32[16,64,128]{2,1,0:T(8,128)S(1)} %get-tuple-element.39.refs_1_.refs_2_, ...), custom_call_target="tpu_custom_call" | custom-call | flops 708870144 | bytes 11076096 | tf_op jit(solution)/shard_map/pallas_call | solution.py:39
  20.7 0.1 broadcast_in_dim.37.table
  20.8 0.1 shard_map.75
  20.9 0.1 collective-permute-start.4
  21.0 1.9 %collective-permute-start.5 = (bf16[4,64,128]{2,1,0:T(8,128)(2,1)S(1)}, bf16[4,64,128]{2,1,0:T(8,128)(2,1)S(1)}, u32[]{:S(2)}, u32[]{:S(2)}) collective-permute-start(bf16[4,64,128]{2,1,0:T(8,128)(2,1)S(1)} %get-tuple-element.44), channel_id=1, source_target_pairs={{1,2},{3,4},{5,6},{7,0},{2,1},{4,3},{6,5},{0,7},{9,10},{11,12},{13... | collective-permute-start | bytes 196616 | tf_op jit(solution)/shard_map/ppermute | solution.py:24
  22.9 0.0 collective-permute-start.6
  22.9 0.1 pad_add_fusion.1
  22.9 2.3 %collective-permute-done.4.left = bf16[4,64,128]{2,1,0:T(8,128)(2,1)S(1)} collective-permute-done((bf16[4,64,128]{2,1,0:T(8,128)(2,1)S(1)}, bf16[4,64,128]{2,1,0:T(8,128)(2,1)S(1)}, u32[]{:S(2)}, u32[]{:S(2)}) %collective-permute-start.4) | collective-permute-done | bytes 65568 | tf_op jit(solution)/shard_map/ppermute | solution.py:24
  25.2 2.8 %collective-permute-done.5.right = bf16[4,64,128]{2,1,0:T(8,128)(2,1)S(1)} collective-permute-done((bf16[4,64,128]{2,1,0:T(8,128)(2,1)S(1)}, bf16[4,64,128]{2,1,0:T(8,128)(2,1)S(1)}, u32[]{:S(2)}, u32[]{:S(2)}) %collective-permute-start.5) | collective-permute-done | bytes 65568 | tf_op jit(solution)/shard_map/ppermute | solution.py:24
  28.0 0.0 collective-permute-done.6.sibling
  28.0 0.1 broadcast_in_dim.36.table.refs_0_
  28.1 0.0 copy-start
  28.1 2.8 %copy-done = bf16[1,16,12,128,128]{4,3,2,1,0:T(8,128)(2,1)S(1)} copy-done((bf16[1,16,12,128,128]{4,3,2,1,0:T(8,128)(2,1)S(1)}, bf16[1,16,12,128,128]{4,3,2,1,0:T(8,128)(2,1)}, u32[]{:S(2)}) %copy-start) | copy-done | bytes 6291480
  30.9 2.6 %shard_map.76 = (f32[4,64,128]{2,1,0:T(8,128)S(1)}, bf16[4,64,128]{2,1,0:T(8,128)(2,1)S(1)}, bf16[28,64,128]{2,1,0:T(8,128)(2,1)S(1)}, f32[12,64,128]{2,1,0:T(8,128)S(1)}) custom-call(s32[193,128]{1,0:T(8,128)S(1)} %broadcast_in_dim.36.table.refs_0_, f32[16,64,128]{2,1,0:T(8,128)S(1)} %get-tuple-element.41.current, ...), custom_call_target="tpu_custom_call" | custom-call | flops 572555264 | bytes 8946176 | tf_op jit(solution)/shard_map/pallas_call | solution.py:39
  33.5 0.8 shard_map.77
  34.3 4.0 %collective-permute-start.8 = (bf16[12,64,128]{2,1,0:T(8,128)(2,1)S(1)}, bf16[12,64,128]{2,1,0:T(8,128)(2,1)S(1)}, u32[]{:S(2)}, u32[]{:S(2)}) collective-permute-start(bf16[12,64,128]{2,1,0:T(8,128)(2,1)S(1)} %get-tuple-element.48), channel_id=1, source_target_pairs={{0,16},{8,24},{16,0},{24,8},{1,17},{9,25},{17,1},{25,9},{2,18},{10... | collective-permute-start | bytes 589832 | tf_op jit(solution)/shard_map/ppermute | solution.py:18
  38.4 0.0 collective-permute-start.7
  38.4 4.7 %collective-permute-done.7.early = bf16[4,64,128]{2,1,0:T(8,128)(2,1)S(1)} collective-permute-done((bf16[4,64,128]{2,1,0:T(8,128)(2,1)S(1)}, bf16[4,64,128]{2,1,0:T(8,128)(2,1)S(1)}, u32[]{:S(2)}, u32[]{:S(2)}) %collective-permute-start.7) | collective-permute-done | bytes 65568 | tf_op jit(solution)/shard_map/ppermute | solution.py:18
  43.1 0.0 collective-permute-done.8.late
  43.1 1.7 %shard_map.78 = (f32[16,64,128]{2,1,0:T(8,128)S(1)}, bf16[16,64,128]{2,1,0:T(8,128)(2,1)S(1)}) custom-call(s32[129,128]{1,0:T(8,128)S(1)} %broadcast_in_dim.33.refs_0_.table, bf16[4,64,128]{2,1,0:T(8,128)(2,1)S(1)} %collective-permute-done.7.early, bf16[12,64,128]{2,1,0:T(8,128)(2,1)S(1)} %collective-permute-done.8.late, ...), custom_call_target="tpu_custom_call" | custom-call | flops 373325824 | bytes 5833216 | tf_op jit(solution)/shard_map/pallas_call | solution.py:39
  44.8 0.1 shard_map.79
  44.9 0.1 collective-permute-start.9
  44.9 1.6 %collective-permute-start.10 = (bf16[4,64,128]{2,1,0:T(8,128)(2,1)S(1)}, bf16[4,64,128]{2,1,0:T(8,128)(2,1)S(1)}, u32[]{:S(2)}, u32[]{:S(2)}) collective-permute-start(bf16[4,64,128]{2,1,0:T(8,128)(2,1)S(1)} %get-tuple-element.54), channel_id=1, source_target_pairs={{1,2},{3,4},{5,6},{7,0},{2,1},{4,3},{6,5},{0,7},{9,10},{11,12},{13... | collective-permute-start | bytes 196616 | tf_op jit(solution)/shard_map/ppermute | solution.py:24
  46.6 0.0 collective-permute-start.11
  46.6 2.8 %collective-permute-done.9.refs_3_ = bf16[4,64,128]{2,1,0:T(8,128)(2,1)S(1)} collective-permute-done((bf16[4,64,128]{2,1,0:T(8,128)(2,1)S(1)}, bf16[4,64,128]{2,1,0:T(8,128)(2,1)S(1)}, u32[]{:S(2)}, u32[]{:S(2)}) %collective-permute-start.9) | collective-permute-done | bytes 65568 | tf_op jit(solution)/shard_map/ppermute | solution.py:24
  49.3 2.6 %collective-permute-done.10.refs_4_ = bf16[4,64,128]{2,1,0:T(8,128)(2,1)S(1)} collective-permute-done((bf16[4,64,128]{2,1,0:T(8,128)(2,1)S(1)}, bf16[4,64,128]{2,1,0:T(8,128)(2,1)S(1)}, u32[]{:S(2)}, u32[]{:S(2)}) %collective-permute-start.10) | collective-permute-done | bytes 65568 | tf_op jit(solution)/shard_map/ppermute | solution.py:24
  52.0 0.0 collective-permute-done.11.refs_5_
  52.0 0.7 shard_map.80
  52.7 1.8 %shard_map.81 = (f32[12,64,128]{2,1,0:T(8,128)S(1)}, bf16[12,64,128]{2,1,0:T(8,128)(2,1)S(1)}) custom-call(s32[193,128]{1,0:T(8,128)S(1)} %broadcast_in_dim.36.table.refs_0_, f32[16,64,128]{2,1,0:T(8,128)S(1)} %get-tuple-element.39.refs_1_.refs_2_, bf16[28,64,128]{2,1,0:T(8,128)(2,1)S(1)} %get-tuple-element.57.refs_2_, bf16[16,12,128,128]{3,2,1,0:T(8,128)(2,1)S(1)} %bitcast.17), custom_call_target="tpu_custom_call" | custom-call | flops 509640704 | bytes 7963136 | tf_op jit(solution)/shard_map/pallas_call | solution.py:39
  54.5 0.1 collective-permute-start.13
  54.6 2.0 %collective-permute-start.12 = (bf16[4,64,128]{2,1,0:T(8,128)(2,1)S(1)}, bf16[4,64,128]{2,1,0:T(8,128)(2,1)S(1)}, u32[]{:S(2)}, u32[]{:S(2)}) collective-permute-start(bf16[4,64,128]{2,1,0:T(8,128)(2,1)S(1)} %get-tuple-element.59), channel_id=1, source_target_pairs={{0,16},{8,24},{16,0},{24,8},{1,17},{9,25},{17,1},{25,9},{2,18},{10... | collective-permute-start | bytes 196616 | tf_op jit(solution)/shard_map/ppermute | solution.py:18
  56.6 4.3 %collective-permute-done.12.refs_4_ = bf16[4,64,128]{2,1,0:T(8,128)(2,1)S(1)} collective-permute-done((bf16[4,64,128]{2,1,0:T(8,128)(2,1)S(1)}, bf16[4,64,128]{2,1,0:T(8,128)(2,1)S(1)}, u32[]{:S(2)}, u32[]{:S(2)}) %collective-permute-start.12) | collective-permute-done | bytes 65568 | tf_op jit(solution)/shard_map/ppermute | solution.py:18
  61.0 0.0 collective-permute-done.13.refs_5_
  61.0 0.6 shard_map.82
  61.5 0.1 shard_map.83
  61.6 0.2 collective-permute-start.14
  61.8 1.6 %collective-permute-start.15 = (bf16[4,64,128]{2,1,0:T(8,128)(2,1)S(1)}, bf16[4,64,128]{2,1,0:T(8,128)(2,1)S(1)}, u32[]{:S(2)}, u32[]{:S(2)}) collective-permute-start(bf16[4,64,128]{2,1,0:T(8,128)(2,1)S(1)} %get-tuple-element.64), channel_id=1, source_target_pairs={{1,2},{3,4},{5,6},{7,0},{2,1},{4,3},{6,5},{0,7},{9,10},{11,12},{13... | collective-permute-start | bytes 196616 | tf_op jit(solution)/shard_map/ppermute | solution.py:24
  63.4 0.0 collective-permute-start.16
  63.4 2.6 %collective-permute-done.14.left = bf16[4,64,128]{2,1,0:T(8,128)(2,1)S(1)} collective-permute-done((bf16[4,64,128]{2,1,0:T(8,128)(2,1)S(1)}, bf16[4,64,128]{2,1,0:T(8,128)(2,1)S(1)}, u32[]{:S(2)}, u32[]{:S(2)}) %collective-permute-start.14) | collective-permute-done | bytes 65568 | tf_op jit(solution)/shard_map/ppermute | solution.py:24
  65.9 2.8 %collective-permute-done.15.right = bf16[4,64,128]{2,1,0:T(8,128)(2,1)S(1)} collective-permute-done((bf16[4,64,128]{2,1,0:T(8,128)(2,1)S(1)}, bf16[4,64,128]{2,1,0:T(8,128)(2,1)S(1)}, u32[]{:S(2)}, u32[]{:S(2)}) %collective-permute-start.15) | collective-permute-done | bytes 65568 | tf_op jit(solution)/shard_map/ppermute | solution.py:24
  68.8 0.0 collective-permute-done.16.sibling
  68.8 2.6 %shard_map.84 = (f32[4,64,128]{2,1,0:T(8,128)S(1)}, bf16[4,64,128]{2,1,0:T(8,128)(2,1)S(1)}, bf16[28,64,128]{2,1,0:T(8,128)(2,1)S(1)}, f32[12,64,128]{2,1,0:T(8,128)S(1)}) custom-call(s32[193,128]{1,0:T(8,128)S(1)} %broadcast_in_dim.36.table.refs_0_, f32[16,64,128]{2,1,0:T(8,128)S(1)} %get-tuple-element.61.current, ...), custom_call_target="tpu_custom_call" | custom-call | flops 572555264 | bytes 8946176 | tf_op jit(solution)/shard_map/pallas_call | solution.py:39
  71.5 2.0 %collective-permute-start.18 = (bf16[12,64,128]{2,1,0:T(8,128)(2,1)S(1)}, bf16[12,64,128]{2,1,0:T(8,128)(2,1)S(1)}, u32[]{:S(2)}, u32[]{:S(2)}) collective-permute-start(bf16[12,64,128]{2,1,0:T(8,128)(2,1)S(1)} %get-tuple-element.68), channel_id=1, source_target_pairs={{0,16},{8,24},{16,0},{24,8},{1,17},{9,25},{17,1},{25,9},{2,18},{10... | collective-permute-start | bytes 589832 | tf_op jit(solution)/shard_map/ppermute | solution.py:18
  73.4 0.1 collective-permute-start.17
  73.6 4.3 %collective-permute-done.17.early = bf16[4,64,128]{2,1,0:T(8,128)(2,1)S(1)} collective-permute-done((bf16[4,64,128]{2,1,0:T(8,128)(2,1)S(1)}, bf16[4,64,128]{2,1,0:T(8,128)(2,1)S(1)}, u32[]{:S(2)}, u32[]{:S(2)}) %collective-permute-start.17) | collective-permute-done | bytes 65568 | tf_op jit(solution)/shard_map/ppermute | solution.py:18
  77.9 0.0 collective-permute-done.18.late
  77.9 2.5 %shard_map.86 = f32[64,2048]{1,0:T(8,128)} custom-call(s32[129,128]{1,0:T(8,128)S(1)} %broadcast_in_dim.33.refs_0_.table, bf16[4,64,128]{2,1,0:T(8,128)(2,1)S(1)} %collective-permute-done.17.early, bf16[12,64,128]{2,1,0:T(8,128)(2,1)S(1)} %collective-permute-done.18.late, f32[4,64,128]{2,1,0:T(8,128)S(1)} %get-tuple-element.69.correction, ...), custom_call_target="tpu_custom_call" | custom-call | flops 415268864 | bytes 6488576 | tf_op jit(solution)/shard_map/pallas_call | solution.py:39
  (13 shorter events, 0.1 us)
Async XLA Ops:
  0.7 10.4 %collective-permute-start.1 = (s32[4]{0:T(128)S(1)}, s32[4]{0:T(128)S(1)}, u32[]{:S(2)}, u32[]{:S(2)}) collective-permute-start(s32[4]{0:T(128)S(1)} %get-tuple-element.73), channel_id=1, source_target_pairs={{0,1},{2,3},{4,5},{6,7},{1,0},{3,2},{5,4},{7,6},{8,9},{10,11},{12,... | collective-permute-start | bytes 56 | tf_op jit(solution)/shard_map/ppermute | solution.py:24
  3.7 7.4 %collective-permute-start.3 = (s32[4]{0:T(128)S(1)}, s32[4]{0:T(128)S(1)}, u32[]{:S(2)}, u32[]{:S(2)}) collective-permute-start(s32[4]{0:T(128)S(1)} %get-tuple-element.74), channel_id=1, source_target_pairs={{0,8},{8,0},{16,24},{24,16},{1,9},{9,1},{17,25},{25,17},{2,10},{10... | collective-permute-start | bytes 56 | tf_op jit(solution)/shard_map/ppermute | solution.py:18
  3.7 7.4 %collective-permute-start.2 = (s32[4]{0:T(128)S(1)}, s32[4]{0:T(128)S(1)}, u32[]{:S(2)}, u32[]{:S(2)}) collective-permute-start(s32[4]{0:T(128)S(1)} %get-tuple-element.75), channel_id=1, source_target_pairs={{1,2},{3,4},{5,6},{7,0},{2,1},{4,3},{6,5},{0,7},{9,10},{11,12},{13... | collective-permute-start | bytes 56 | tf_op jit(solution)/shard_map/ppermute | solution.py:24
  7.2 3.5 %copy-start.2 = (s32[1,16,12]{1,0,2:T(1,128)S(1)}, s32[1,16,12]{1,0,2:T(1,128)}, u32[]{:S(2)}) copy-start(s32[1,16,12]{1,0,2:T(1,128)} %param.9) | copy-start | bytes 2308
  7.2 3.7 %copy-start.3 = (s32[1,16,8]{1,2,0:T(8,128)S(1)}, s32[1,16,8]{1,2,0:T(8,128)}, u32[]{:S(2)}) copy-start(s32[1,16,8]{1,2,0:T(8,128)} %param.12) | copy-start | bytes 1540
  7.2 10.7 %copy-start.1 = (bf16[1,16,128,128]{3,2,1,0:T(8,128)(2,1)S(1)}, bf16[1,16,128,128]{3,2,1,0:T(8,128)(2,1)}, u32[]{:S(2)}) copy-start(bf16[1,16,128,128]{3,2,1,0:T(8,128)(2,1)} %param.10) | copy-start | bytes 1572868
  9.1 8.7 %collective-permute-start = (bf16[16,64,128]{2,1,0:T(8,128)(2,1)}, bf16[16,64,128]{2,1,0:T(8,128)(2,1)S(1)}, u32[]{:S(2)}, u32[]{:S(2)}) collective-permute-start(bf16[16,64,128]{2,1,0:T(8,128)(2,1)} %get-tuple-element.40), channel_id=1, source_target_pairs={{0,16},{8,24},{16,0},{24,8},{1,17},{9,25},{17,1},{25,9},{2,18},{10... | collective-permute-start | bytes 786440 | tf_op jit(solution)/shard_map/ppermute | solution.py:18
  11.0 22.5 %slice-start = ((s8[6291456]{0:T(1024)(128)(4,1)}), s8[2097152]{0:T(1024)(128)(4,1)S(1)}, s32[]{:S(2)}) async-start(s8[6291456]{0:T(1024)(128)(4,1)} %bitcast.13), calls=%async_computation | async-start | bytes 4194304
  20.9 4.3 %collective-permute-start.4 = (bf16[4,64,128]{2,1,0:T(8,128)(2,1)S(1)}, bf16[4,64,128]{2,1,0:T(8,128)(2,1)S(1)}, u32[]{:S(2)}, u32[]{:S(2)}) collective-permute-start(bf16[4,64,128]{2,1,0:T(8,128)(2,1)S(1)} %get-tuple-element.43), channel_id=1, source_target_pairs={{0,1},{2,3},{4,5},{6,7},{1,0},{3,2},{5,4},{7,6},{8,9},{10,11},{12,... | collective-permute-start | bytes 196616 | tf_op jit(solution)/shard_map/ppermute | solution.py:24
  21.0 7.0 %collective-permute-start.5 = (bf16[4,64,128]{2,1,0:T(8,128)(2,1)S(1)}, bf16[4,64,128]{2,1,0:T(8,128)(2,1)S(1)}, u32[]{:S(2)}, u32[]{:S(2)}) collective-permute-start(bf16[4,64,128]{2,1,0:T(8,128)(2,1)S(1)} %get-tuple-element.44), channel_id=1, source_target_pairs={{1,2},{3,4},{5,6},{7,0},{2,1},{4,3},{6,5},{0,7},{9,10},{11,12},{13... | collective-permute-start | bytes 196616 | tf_op jit(solution)/shard_map/ppermute | solution.py:24
  22.9 5.1 %collective-permute-start.6 = (bf16[4,64,128]{2,1,0:T(8,128)(2,1)S(1)}, bf16[4,64,128]{2,1,0:T(8,128)(2,1)S(1)}, u32[]{:S(2)}, u32[]{:S(2)}) collective-permute-start(bf16[4,64,128]{2,1,0:T(8,128)(2,1)S(1)} %get-tuple-element.45), channel_id=1, source_target_pairs={{0,8},{8,0},{16,24},{24,16},{1,9},{9,1},{17,25},{25,17},{2,10},{10... | collective-permute-start | bytes 196616 | tf_op jit(solution)/shard_map/ppermute | solution.py:18
  28.1 2.8 %copy-start = (bf16[1,16,12,128,128]{4,3,2,1,0:T(8,128)(2,1)S(1)}, bf16[1,16,12,128,128]{4,3,2,1,0:T(8,128)(2,1)}, u32[]{:S(2)}) copy-start(bf16[1,16,12,128,128]{4,3,2,1,0:T(8,128)(2,1)} %param.8) | copy-start | bytes 18874372
  30.9 2.7 %slice-start.1 = ((s8[6291456]{0:T(1024)(128)(4,1)}), s8[4194304]{0:T(1024)(128)(4,1)S(1)}, s32[]{:S(2)}) async-start(s8[6291456]{0:T(1024)(128)(4,1)} %bitcast.13), calls=%async_computation.1 | async-start | bytes 8388608
  34.3 8.7 %collective-permute-start.8 = (bf16[12,64,128]{2,1,0:T(8,128)(2,1)S(1)}, bf16[12,64,128]{2,1,0:T(8,128)(2,1)S(1)}, u32[]{:S(2)}, u32[]{:S(2)}) collective-permute-start(bf16[12,64,128]{2,1,0:T(8,128)(2,1)S(1)} %get-tuple-element.48), channel_id=1, source_target_pairs={{0,16},{8,24},{16,0},{24,8},{1,17},{9,25},{17,1},{25,9},{2,18},{10... | collective-permute-start | bytes 589832 | tf_op jit(solution)/shard_map/ppermute | solution.py:18
  38.4 4.7 %collective-permute-start.7 = (bf16[4,64,128]{2,1,0:T(8,128)(2,1)S(1)}, bf16[4,64,128]{2,1,0:T(8,128)(2,1)S(1)}, u32[]{:S(2)}, u32[]{:S(2)}) collective-permute-start(bf16[4,64,128]{2,1,0:T(8,128)(2,1)S(1)} %get-tuple-element.46), channel_id=1, source_target_pairs={{0,16},{8,24},{16,0},{24,8},{1,17},{9,25},{17,1},{25,9},{2,18},{10... | collective-permute-start | bytes 196616 | tf_op jit(solution)/shard_map/ppermute | solution.py:18
  44.9 4.5 %collective-permute-start.9 = (bf16[4,64,128]{2,1,0:T(8,128)(2,1)S(1)}, bf16[4,64,128]{2,1,0:T(8,128)(2,1)S(1)}, u32[]{:S(2)}, u32[]{:S(2)}) collective-permute-start(bf16[4,64,128]{2,1,0:T(8,128)(2,1)S(1)} %get-tuple-element.53), channel_id=1, source_target_pairs={{0,1},{2,3},{4,5},{6,7},{1,0},{3,2},{5,4},{7,6},{8,9},{10,11},{12,... | collective-permute-start | bytes 196616 | tf_op jit(solution)/shard_map/ppermute | solution.py:24
  44.9 7.0 %collective-permute-start.10 = (bf16[4,64,128]{2,1,0:T(8,128)(2,1)S(1)}, bf16[4,64,128]{2,1,0:T(8,128)(2,1)S(1)}, u32[]{:S(2)}, u32[]{:S(2)}) collective-permute-start(bf16[4,64,128]{2,1,0:T(8,128)(2,1)S(1)} %get-tuple-element.54), channel_id=1, source_target_pairs={{1,2},{3,4},{5,6},{7,0},{2,1},{4,3},{6,5},{0,7},{9,10},{11,12},{13... | collective-permute-start | bytes 196616 | tf_op jit(solution)/shard_map/ppermute | solution.py:24
  46.6 5.4 %collective-permute-start.11 = (bf16[4,64,128]{2,1,0:T(8,128)(2,1)S(1)}, bf16[4,64,128]{2,1,0:T(8,128)(2,1)S(1)}, u32[]{:S(2)}, u32[]{:S(2)}) collective-permute-start(bf16[4,64,128]{2,1,0:T(8,128)(2,1)S(1)} %get-tuple-element.55), channel_id=1, source_target_pairs={{0,8},{8,0},{16,24},{24,16},{1,9},{9,1},{17,25},{25,17},{2,10},{10... | collective-permute-start | bytes 196616 | tf_op jit(solution)/shard_map/ppermute | solution.py:18
  54.5 6.4 %collective-permute-start.13 = (bf16[12,64,128]{2,1,0:T(8,128)(2,1)S(1)}, bf16[12,64,128]{2,1,0:T(8,128)(2,1)S(1)}, u32[]{:S(2)}, u32[]{:S(2)}) collective-permute-start(bf16[12,64,128]{2,1,0:T(8,128)(2,1)S(1)} %get-tuple-element.60), channel_id=1, source_target_pairs={{0,16},{8,24},{16,0},{24,8},{1,17},{9,25},{17,1},{25,9},{2,18},{10... | collective-permute-start | bytes 589832 | tf_op jit(solution)/shard_map/ppermute | solution.py:18
  54.6 6.4 %collective-permute-start.12 = (bf16[4,64,128]{2,1,0:T(8,128)(2,1)S(1)}, bf16[4,64,128]{2,1,0:T(8,128)(2,1)S(1)}, u32[]{:S(2)}, u32[]{:S(2)}) collective-permute-start(bf16[4,64,128]{2,1,0:T(8,128)(2,1)S(1)} %get-tuple-element.59), channel_id=1, source_target_pairs={{0,16},{8,24},{16,0},{24,8},{1,17},{9,25},{17,1},{25,9},{2,18},{10... | collective-permute-start | bytes 196616 | tf_op jit(solution)/shard_map/ppermute | solution.py:18
  61.6 4.3 %collective-permute-start.14 = (bf16[4,64,128]{2,1,0:T(8,128)(2,1)S(1)}, bf16[4,64,128]{2,1,0:T(8,128)(2,1)S(1)}, u32[]{:S(2)}, u32[]{:S(2)}) collective-permute-start(bf16[4,64,128]{2,1,0:T(8,128)(2,1)S(1)} %get-tuple-element.63), channel_id=1, source_target_pairs={{0,1},{2,3},{4,5},{6,7},{1,0},{3,2},{5,4},{7,6},{8,9},{10,11},{12,... | collective-permute-start | bytes 196616 | tf_op jit(solution)/shard_map/ppermute | solution.py:24
  61.8 7.0 %collective-permute-start.15 = (bf16[4,64,128]{2,1,0:T(8,128)(2,1)S(1)}, bf16[4,64,128]{2,1,0:T(8,128)(2,1)S(1)}, u32[]{:S(2)}, u32[]{:S(2)}) collective-permute-start(bf16[4,64,128]{2,1,0:T(8,128)(2,1)S(1)} %get-tuple-element.64), channel_id=1, source_target_pairs={{1,2},{3,4},{5,6},{7,0},{2,1},{4,3},{6,5},{0,7},{9,10},{11,12},{13... | collective-permute-start | bytes 196616 | tf_op jit(solution)/shard_map/ppermute | solution.py:24
  63.4 5.4 %collective-permute-start.16 = (bf16[4,64,128]{2,1,0:T(8,128)(2,1)S(1)}, bf16[4,64,128]{2,1,0:T(8,128)(2,1)S(1)}, u32[]{:S(2)}, u32[]{:S(2)}) collective-permute-start(bf16[4,64,128]{2,1,0:T(8,128)(2,1)S(1)} %get-tuple-element.65), channel_id=1, source_target_pairs={{0,8},{8,0},{16,24},{24,16},{1,9},{9,1},{17,25},{25,17},{2,10},{10... | collective-permute-start | bytes 196616 | tf_op jit(solution)/shard_map/ppermute | solution.py:18
  71.5 6.4 %collective-permute-start.18 = (bf16[12,64,128]{2,1,0:T(8,128)(2,1)S(1)}, bf16[12,64,128]{2,1,0:T(8,128)(2,1)S(1)}, u32[]{:S(2)}, u32[]{:S(2)}) collective-permute-start(bf16[12,64,128]{2,1,0:T(8,128)(2,1)S(1)} %get-tuple-element.68), channel_id=1, source_target_pairs={{0,16},{8,24},{16,0},{24,8},{1,17},{9,25},{17,1},{25,9},{2,18},{10... | collective-permute-start | bytes 589832 | tf_op jit(solution)/shard_map/ppermute | solution.py:18
  73.4 4.5 %collective-permute-start.17 = (bf16[4,64,128]{2,1,0:T(8,128)(2,1)S(1)}, bf16[4,64,128]{2,1,0:T(8,128)(2,1)S(1)}, u32[]{:S(2)}, u32[]{:S(2)}) collective-permute-start(bf16[4,64,128]{2,1,0:T(8,128)(2,1)S(1)} %get-tuple-element.66), channel_id=1, source_target_pairs={{0,16},{8,24},{16,0},{24,8},{1,17},{9,25},{17,1},{25,9},{2,18},{10... | collective-permute-start | bytes 196616 | tf_op jit(solution)/shard_map/ppermute | solution.py:18

commit v5 on v4

--- a/solution.py
+++ b/solution.py
@@ -6,7 +6,6 @@
 from jax.sharding import PartitionSpec as P
 
 ITERS = 2
-CHUNK = 4
 LIMIT = 16 << 20
 LANES = 128
 VMEM = pl.BlockSpec(memory_space=pltpu.VMEM)
@@ -95,35 +94,30 @@
             out[j] = source[entry(table, side * out.shape[0] + j)]
 
 
-def first_body(fetch, table, loads, *refs):
-    if fetch:
-        *refs, arrivals = refs
-        *pieces, source, smoother, current, first, transfer, scratch = refs
-        copies = [
-            pltpu.make_async_copy(source.at[i], transfer.at[i], arrivals.at[i])
-            for i in range(source.shape[0])
-        ]
-    else:
-        *pieces, transfer, smoother, current, first, scratch = refs
-        copies = []
+def fetch_body(_, source, target, arrivals):
+    copies = [
+        pltpu.make_async_copy(source.at[i], target.at[i], arrivals.at[i])
+        for i in range(source.shape[0])
+    ]
     for copy in copies:
         copy.start()
+    for copy in copies:
+        copy.wait()
+
+
+def first_body(table, loads, *refs):
+    *pieces, transfer, smoother, current, first, scratch = refs
     residual, arrived = pieces[: len(pieces) // 2], pieces[len(pieces) // 2 :]
     rows = first.shape[0]
 
     @pl.when(is_fine(table))
     def _():
         joined(residual, current)
-        for copy in copies:
-            copy.wait()
 
     @pl.when(jnp.logical_not(is_fine(table)))
     def _():
         joined(arrived, scratch)
         for i in range(rows):
-            if i % CHUNK == 0:
-                for copy in copies[i : i + CHUNK]:
-                    copy.wait()
             current[i] = loads[i] + gathered(scratch, table, i, transfer)
 
     for i in range(rows):
@@ -131,35 +125,36 @@
         first[i] = value.astype(jnp.bfloat16)
 
 
-def second_rows(low, targets, table, current, first, extension, blocks, smoother, rounded):
-    places = [(full, i) for full in targets for i in range(full.shape[0])]
-    for at in range(len(places)):
-        applied = gathered(extension, table, low + at, blocks)
-        rounded[at] = (current[low + at] - applied).astype(jnp.bfloat16)
-    for at, (full, i) in enumerate(places):
-        value = first[low + at].astype(jnp.float32) + times(rounded[at], smoother[low + at])
+def second_rows(low, table, current, first, extension, blocks, smoother, full, rounded):
+    rows = full.shape[0]
+    for i in range(rows):
+        applied = gathered(extension, table, low + i, blocks)
+        rounded[i] = (current[low + i] - applied).astype(jnp.bfloat16)
+    for i in range(rows):
+        value = first[low + i].astype(jnp.float32) + times(rounded[i], smoother[low + i])
         full[i] = value
-        if full is targets[0]:
-            rounded[at] = value.astype(jnp.bfloat16)
-
-
-def second_start_body(table, current, first, left, right, sibling, blocks, smoother, full, rounded, extension, rest, scratch):
+        rounded[i] = value.astype(jnp.bfloat16)
+
+
+def second_start_body(table, current, first, left, right, sibling, blocks, smoother, full, rounded, extension):
     joined([first, left, right, sibling], extension)
 
-    @pl.when(is_fine(table))
-    def _():
-        second_rows(0, (full, rest), table, current, first, extension, blocks, smoother, scratch)
-
     @pl.when(jnp.logical_not(is_fine(table)))
     def _():
-        second_rows(0, (full,), table, current, first, extension, blocks, smoother, rounded)
+        second_rows(0, table, current, first, extension, blocks, smoother, full, rounded)
 
 
 def second_end_body(table, current, first, extension, blocks, smoother, full, rounded):
     @pl.when(jnp.logical_not(is_fine(table)))
     def _():
         low = first.shape[0] - full.shape[0]
-        second_rows(low, (full,), table, current, first, extension, blocks, smoother, rounded)
+        second_rows(low, table, current, first, extension, blocks, smoother, full, rounded)
+
+
+def second_fine_body(table, current, first, extension, blocks, smoother, full, scratch):
+    @pl.when(is_fine(table))
+    def _():
+        second_rows(0, table, current, first, extension, blocks, smoother, full, scratch)
 
 
 def row_of(parts, at):
@@ -169,14 +164,14 @@
         at -= part.shape[0]
 
 
-def update_body(table, early, late, correction, rest, *refs):
+def update_body(table, early, late, correction, *refs):
     *terms, transfer, iterate, rounded, scratch = refs
 
     @pl.when(is_fine(table))
     def _():
         joined((early, late), scratch)
         for i in range(iterate.shape[0]):
-            value = row_of((correction, rest), i)
+            value = correction[i]
             for term in terms:
                 value = term[i] + value
             value = value + gathered(scratch, table, i, transfer)
@@ -200,7 +195,7 @@
             sent[i] = value.astype(jnp.bfloat16)
 
 
-def last_body(table, early, late, correction, rest, end, iterate, transfer, out, total, scratch, leaves):
+def last_body(table, early, late, correction, start, end, iterate, transfer, out, total, scratch, leaves):
     rows, _, width = total.shape
     copies = [
         pltpu.make_async_copy(total.at[i], out.at[:, pl.ds(i * width, width)], leaves.at[i])
@@ -211,14 +206,14 @@
     def _():
         joined((early, late), scratch)
         for i in range(rows):
-            value = iterate[i] + row_of((correction, rest), i)
+            value = iterate[i] + correction[i]
             total[i] = value + gathered(scratch, table, i, transfer)
             copies[i].start()
 
     @pl.when(jnp.logical_not(is_fine(table)))
     def _():
         for i in range(rows):
-            total[i] = row_of((correction, end), i)
+            total[i] = row_of((start, end), i)
             copies[i].start()
 
     for copy in copies:
@@ -240,7 +235,7 @@
         return pltpu.VMEM((count, load_cols, width), jnp.bfloat16)
 
     wide, narrow = panels(block_rows, jnp.float32), panels(block_rows, jnp.bfloat16)
-    early_rows = block_rows // 4
+    early_rows = block_rows * 3 // 8
     late_rows = block_rows - early_rows
     listed = panels(list_width, jnp.bfloat16)
     extended = panels(block_rows + 3 * list_width, jnp.bfloat16)
@@ -270,11 +265,15 @@
     transfer_table = spread(jnp.concatenate([transfer_cols.reshape(-1), fine]))
     wanted_table = spread(wanted)
 
+    def fetched(source):
+        return call(fetch_body, like(source), inside(loads), inside(source), in_specs=[HBM, HBM], scratch=[rowwise])
+
     def exchanged(source):
         ahead, behind, beside = call(pack_body, (listed,) * 3, wanted_table, source)
         ahead = swapped(ahead, "dom", 0)
         behind = swapped(behind, "dom", 1)
-        return ahead, behind, partner(beside, "level", 0)
+        beside = partner(beside, "level", 0)
+        return ahead, behind, beside
 
     def part(rows):
         return panels(rows, jnp.float32), panels(rows, jnp.bfloat16)
@@ -282,6 +281,7 @@
     def sent_on(x):
         return partner(x, "level", 1)
 
+    transfer = fetched(transfer)
     residual, iterate = [load_panels], None
     for cycle_index in range(ITERS):
         if cycle_index > 0:
@@ -297,35 +297,31 @@
             )
             arrived.append(partner(sent, "level", 1))
             residual = [early, late]
-        fetch = cycle_index == 0
-        current, first, *kept = call(
-            lambda *refs: first_body(fetch, *refs), (wide, narrow) + (like(transfer),) * fetch,
-            transfer_table, load_panels, *residual, *arrived,
-            inside(transfer) if fetch else transfer, smooth,
-            in_specs=[VMEM] * (2 + len(residual) + len(arrived)) + [HBM if fetch else VMEM, VMEM],
-            scratch=[held(block_rows)] + [rowwise] * fetch,
+        current, first = call(
+            first_body, (wide, narrow), transfer_table, load_panels, *residual, *arrived,
+            transfer, smooth, scratch=[held(block_rows)],
         )
-        (transfer,) = kept or (transfer,)
         sides = exchanged(first)
+        if cycle_index == 0:
+            blocks = fetched(blocks)
         args = (level_table, current, first)
-        correction, rounded, extension, rest = call(
-            second_start_body,
-            part(early_rows) + (extended, panels(late_rows, jnp.float32)),
-            *args, *sides, blocks, smooth, scratch=[held(block_rows)],
+        start, rounded, extension = call(
+            second_start_body, part(early_rows) + (extended,), *args, *sides, blocks, smooth
         )
         returned = [sent_on(rounded)]
         end, rounded = call(second_end_body, part(late_rows), *args, extension, blocks, smooth)
-        returned.append(partner(rounded, "level", 1))
+        returned.append(sent_on(rounded))
+        correction = call(second_fine_body, wide, *args, extension, blocks, smooth, scratch=[held(block_rows)])
         if cycle_index + 1 < ITERS:
             terms = [] if iterate is None else [iterate]
             iterate, rounded = call(
-                update_body, (wide, narrow), transfer_table, *returned, correction, rest,
+                update_body, (wide, narrow), transfer_table, *returned, correction,
                 *terms, transfer, scratch=[held(block_rows)],
             )
             sides = exchanged(rounded)
     final = call(
         last_body, jax.ShapeDtypeStruct((load_cols, block_rows * width), jnp.float32),
-        transfer_table, *returned, correction, rest, end, iterate, transfer, out_specs=HBM,
+        transfer_table, *returned, correction, start, end, iterate, transfer, out_specs=HBM,
         scratch=[pltpu.VMEM(wide.shape, jnp.float32), held(block_rows), rowwise],
     )
     return final[None]

time: 80.6 us -> 75.7 us (0.939)
  waiting for transfers between devices: 35.9 us -> 23.8 us
  starting transfers between devices: 21.8 us -> 28.5 us
  Pallas kernels: 18.3 us -> 21.3 us
  local copies, waits for them, and re-layouts: 3.35 us -> 0.57 us
    ppermute x11, waiting for transfers between devices: 20 us -> 12.4 us  [partner(): lax.ppermute(x, axis, [(i, i ^ 1 << apart) for i in range(lax.axis_size(a...]
    ppermute x11, starting transfers between devices: 9.81 us -> 14.4 us  [partner(): lax.ppermute(x, axis, [(i, i ^ 1 << apart) for i in range(lax.axis_size(a...]
    ppermute x8, waiting for transfers between devices: 15.8 us -> 11.4 us  [swapped(): return lax.ppermute(x, axis, pairs + [(b, a) for a, b in pairs])]
    pallas_call x14 -> x18, Pallas kernels: 18.3 us -> 21.3 us  [call(): pl.pallas_call(body, out_shape=outs, in_specs=in_specs or [VMEM] * len(ar...]
    unnamed x14 -> x8, local copies, waits for them, and re-layouts: 2.96 us -> 0.17 us
    ppermute x8, starting transfers between devices: 12 us -> 14.1 us  [swapped(): return lax.ppermute(x, axis, pairs + [(b, a) for a, b in pairs])]
  transfers between devices with their start and end apart: 19 -> 19, of which waited for: 10 -> 9; matrix products, arithmetic and copies ran while one was open for 1% -> 1% of each run, Pallas kernels for 2% -> 15%
where the time goes in v5:
time: 75.7 us; the launch traced here: 75.4 us
  starting transfers between devices  28.5 us (38%)
  waiting for transfers between devices  23.8 us (31%)
  Pallas kernels  21.3 us (28%)
  other arithmetic  0.86 us (1%)
    pallas_call x18, Pallas kernels, call(): pl.pallas_call(body, out_shape=outs, in_specs=in_specs or [VMEM] * len(ar...  21.3 us
    ppermute x11, starting transfers between devices, partner(): lax.ppermute(x, axis, [(i, i ^ 1 << apart) for i in range(lax.axis_size(a...  14.4 us
    ppermute x8, starting transfers between devices, swapped(): return lax.ppermute(x, axis, pairs + [(b, a) for a, b in pairs])  14.1 us
    ppermute x11, waiting for transfers between devices, partner(): lax.ppermute(x, axis, [(i, i ^ 1 << apart) for i in range(lax.axis_size(a...  12.4 us
    ppermute x8, waiting for transfers between devices, swapped(): return lax.ppermute(x, axis, pairs + [(b, a) for a, b in pairs])  11.4 us
  transfers between devices with their start and end apart: 19, of which 9 were waited for; matrix products, arithmetic and copies ran while one was open for 1% of the time, Pallas kernels for 15%

profile of v5, /device:TPU:0, one launch (start us, length us, event | category | flops | bytes accessed | tf_op | source)
XLA Modules:
  0.0 75.4 jit_solution(4630241619121328987)
XLA Ops:
  0.0 0.7 fusion.3
  0.7 3.0 %collective-permute-start.1 = (s32[4]{0:T(128)S(1)}, s32[4]{0:T(128)S(1)}, u32[]{:S(2)}, u32[]{:S(2)}) collective-permute-start(s32[4]{0:T(128)S(1)} %get-tuple-element.65), channel_id=1, source_target_pairs={{0,1},{2,3},{4,5},{6,7},{1,0},{3,2},{5,4},{7,6},{8,9},{10,11},{12,... | collective-permute-start | bytes 56 | tf_op jit(solution)/shard_map/ppermute | solution.py:23
  3.7 0.0 collective-permute-start.3
  3.7 3.5 %collective-permute-start.2 = (s32[4]{0:T(128)S(1)}, s32[4]{0:T(128)S(1)}, u32[]{:S(2)}, u32[]{:S(2)}) collective-permute-start(s32[4]{0:T(128)S(1)} %get-tuple-element.67), channel_id=1, source_target_pairs={{1,2},{3,4},{5,6},{7,0},{2,1},{4,3},{6,5},{0,7},{9,10},{11,12},{13... | collective-permute-start | bytes 56 | tf_op jit(solution)/shard_map/ppermute | solution.py:23
  7.2 1.2 %shard_map.73 = (f32[16,64,128]{2,1,0:T(8,128)S(1)}, bf16[16,64,128]{2,1,0:T(8,128)(2,1)S(1)}) custom-call(f32[64,2048]{1,0:T(8,128)} %bitcast.22), custom_call_target="tpu_custom_call" | custom-call | flops 5000000000 | bytes 1048576 | tf_op jit(solution)/shard_map/pallas_call | solution.py:38
  8.4 0.0 copy-start
  8.4 1.6 %collective-permute-start = (bf16[16,64,128]{2,1,0:T(8,128)(2,1)S(1)}, bf16[16,64,128]{2,1,0:T(8,128)(2,1)S(1)}, u32[]{:S(2)}, u32[]{:S(2)}) collective-permute-start(bf16[16,64,128]{2,1,0:T(8,128)(2,1)S(1)} %get-tuple-element.36), channel_id=1, source_target_pairs={{0,16},{8,24},{16,0},{24,8},{1,17},{9,25},{17,1},{25,9},{2,18},{10... | collective-permute-start | bytes 786440 | tf_op jit(solution)/shard_map/ppermute | solution.py:17
  10.0 0.1 copy.10
  10.1 0.1 reshape.28
  10.2 0.1 copy.9
  10.3 0.1 reshape.25
  10.3 0.1 pad_add_fusion.1
  10.4 2.3 %shard_map.74.refs_2_.refs_0_.refs_4_.transfer = bf16[16,8,128,128]{3,2,1,0:T(8,128)(2,1)S(1)} custom-call(f32[64,2048]{1,0:T(8,128)} %bitcast.23, bf16[16,8,128,128]{3,2,1,0:T(8,128)(2,1)} %bitcast.21), custom_call_target="tpu_custom_call" | custom-call | flops 570425344 | bytes 8912896 | tf_op jit(solution)/shard_map/pallas_call | solution.py:38
  12.7 0.0 collective-permute-done.1
  12.7 0.0 collective-permute-done.3
  12.7 0.0 collective-permute-done.2
  12.8 0.1 pad_add_fusion.2
  12.8 4.1 %collective-permute-done.refs_1_ = bf16[16,64,128]{2,1,0:T(8,128)(2,1)S(1)} collective-permute-done((bf16[16,64,128]{2,1,0:T(8,128)(2,1)S(1)}, bf16[16,64,128]{2,1,0:T(8,128)(2,1)S(1)}, u32[]{:S(2)}, u32[]{:S(2)}) %collective-permute-start) | collective-permute-done | bytes 262176 | tf_op jit(solution)/shard_map/ppermute | solution.py:17
  16.9 0.1 broadcast_in_dim.33.table
  17.0 0.0 copy-done
  17.0 0.6 shard_map.75
  17.6 0.1 broadcast_in_dim.37.table
  17.7 0.1 shard_map.76
  17.7 0.1 collective-permute-start.4
  17.8 1.9 %collective-permute-start.5 = (bf16[4,64,128]{2,1,0:T(8,128)(2,1)S(1)}, bf16[4,64,128]{2,1,0:T(8,128)(2,1)S(1)}, u32[]{:S(2)}, u32[]{:S(2)}) collective-permute-start(bf16[4,64,128]{2,1,0:T(8,128)(2,1)S(1)} %get-tuple-element.40), channel_id=1, source_target_pairs={{1,2},{3,4},{5,6},{7,0},{2,1},{4,3},{6,5},{0,7},{9,10},{11,12},{13... | collective-permute-start | bytes 196616 | tf_op jit(solution)/shard_map/ppermute | solution.py:23
  19.7 0.0 collective-permute-start.6
  19.7 2.9 %shard_map.77.blocks.refs_6_.refs_3_ = bf16[16,12,128,128]{3,2,1,0:T(8,128)(2,1)S(1)} custom-call(f32[64,2048]{1,0:T(8,128)} %bitcast.24, bf16[16,12,128,128]{3,2,1,0:T(8,128)(2,1)} %bitcast.20), custom_call_target="tpu_custom_call" | custom-call | flops 838860800 | bytes 13107200 | tf_op jit(solution)/shard_map/pallas_call | solution.py:38
  22.6 0.0 collective-permute-done.4.left
  22.6 2.2 %collective-permute-done.5.right = bf16[4,64,128]{2,1,0:T(8,128)(2,1)S(1)} collective-permute-done((bf16[4,64,128]{2,1,0:T(8,128)(2,1)S(1)}, bf16[4,64,128]{2,1,0:T(8,128)(2,1)S(1)}, u32[]{:S(2)}, u32[]{:S(2)}) %collective-permute-start.5) | collective-permute-done | bytes 65568 | tf_op jit(solution)/shard_map/ppermute | solution.py:23
  24.8 0.0 collective-permute-done.6.sibling
  24.8 0.1 broadcast_in_dim.36.table.refs_0_
  24.9 0.8 %shard_map.78 = (f32[6,64,128]{2,1,0:T(8,128)}, bf16[6,64,128]{2,1,0:T(8,128)(2,1)S(1)}, bf16[28,64,128]{2,1,0:T(8,128)(2,1)S(1)}) custom-call(s32[193,128]{1,0:T(8,128)S(1)} %broadcast_in_dim.36.table.refs_0_, f32[16,64,128]{2,1,0:T(8,128)S(1)} %get-tuple-element.37.current, bf16[16,64,128]{2,1,0:T(8,128)(2,1)S(1)} %get-tuple-element.38.source.first, ...), custom_call_target="tpu_custom_call" | custom-call | flops 553680896 | bytes 8651264 | tf_op jit(solution)/shard_map/pallas_call | solution.py:38
  25.7 0.8 %shard_map.79 = (f32[10,64,128]{2,1,0:T(8,128)}, bf16[10,64,128]{2,1,0:T(8,128)(2,1)S(1)}) custom-call(s32[193,128]{1,0:T(8,128)S(1)} %broadcast_in_dim.36.table.refs_0_, f32[16,64,128]{2,1,0:T(8,128)S(1)} %get-tuple-element.37.current, bf16[16,64,128]{2,1,0:T(8,128)(2,1)S(1)} %get-tuple-element.38.source.first, ...), custom_call_target="tpu_custom_call" | custom-call | flops 553680896 | bytes 8651264 | tf_op jit(solution)/shard_map/pallas_call | solution.py:38
  26.4 5.9 %collective-permute-start.8 = (bf16[10,64,128]{2,1,0:T(8,128)(2,1)S(1)}, bf16[10,64,128]{2,1,0:T(8,128)(2,1)S(1)}, u32[]{:S(2)}, u32[]{:S(2)}) collective-permute-start(bf16[10,64,128]{2,1,0:T(8,128)(2,1)S(1)} %get-tuple-element.44), channel_id=1, source_target_pairs={{0,16},{8,24},{16,0},{24,8},{1,17},{9,25},{17,1},{25,9},{2,18},{10... | collective-permute-start | bytes 491528 | tf_op jit(solution)/shard_map/ppermute | solution.py:17
  32.4 0.0 collective-permute-start.7
  32.4 2.6 %shard_map.80.correction = f32[16,64,128]{2,1,0:T(8,128)S(1)} custom-call(s32[193,128]{1,0:T(8,128)S(1)} %broadcast_in_dim.36.table.refs_0_, f32[16,64,128]{2,1,0:T(8,128)S(1)} %get-tuple-element.37.current, bf16[16,64,128]{2,1,0:T(8,128)(2,1)S(1)} %get-tuple-element.38.source.first, bf16[28,64,128]{2,1,0:T(8,128)(2,1)S(1)} %get-tuple-element.43.extension, ...), custom_call_target="tpu_custom_call" | custom-call | flops 555778048 | bytes 8684032 | tf_op jit(solution)/shard_map/pallas_call | solution.py:38
  34.9 2.2 %collective-permute-done.7.early = bf16[6,64,128]{2,1,0:T(8,128)(2,1)S(1)} collective-permute-done((bf16[6,64,128]{2,1,0:T(8,128)(2,1)S(1)}, bf16[6,64,128]{2,1,0:T(8,128)(2,1)S(1)}, u32[]{:S(2)}, u32[]{:S(2)}) %collective-permute-start.7) | collective-permute-done | bytes 98336 | tf_op jit(solution)/shard_map/ppermute | solution.py:17
  37.1 0.0 collective-permute-done.8.late
  37.1 1.7 %shard_map.81 = (f32[16,64,128]{2,1,0:T(8,128)S(1)}, bf16[16,64,128]{2,1,0:T(8,128)(2,1)S(1)}) custom-call(s32[129,128]{1,0:T(8,128)S(1)} %broadcast_in_dim.33.table, bf16[6,64,128]{2,1,0:T(8,128)(2,1)S(1)} %collective-permute-done.7.early, bf16[10,64,128]{2,1,0:T(8,128)(2,1)S(1)} %collective-permute-done.8.late, f32[16,64,128]{2,1,0:T(8,128)S(1)} %shard_map.80.correction, ...), custom_call_target="tpu_custom_call" | custom-call | flops 373325824 | bytes 5833216 | tf_op jit(solution)/shard_map/pallas_call | solution.py:38
  38.9 0.1 shard_map.82
  38.9 0.7 collective-permute-start.9
  39.6 2.3 %collective-permute-start.10 = (bf16[4,64,128]{2,1,0:T(8,128)(2,1)S(1)}, bf16[4,64,128]{2,1,0:T(8,128)(2,1)S(1)}, u32[]{:S(2)}, u32[]{:S(2)}) collective-permute-start(bf16[4,64,128]{2,1,0:T(8,128)(2,1)S(1)} %get-tuple-element.47), channel_id=1, source_target_pairs={{1,2},{3,4},{5,6},{7,0},{2,1},{4,3},{6,5},{0,7},{9,10},{11,12},{13... | collective-permute-start | bytes 196616 | tf_op jit(solution)/shard_map/ppermute | solution.py:23
  42.0 0.0 collective-permute-start.11
  42.0 2.0 %collective-permute-done.9.refs_3_ = bf16[4,64,128]{2,1,0:T(8,128)(2,1)S(1)} collective-permute-done((bf16[4,64,128]{2,1,0:T(8,128)(2,1)S(1)}, bf16[4,64,128]{2,1,0:T(8,128)(2,1)S(1)}, u32[]{:S(2)}, u32[]{:S(2)}) %collective-permute-start.9) | collective-permute-done | bytes 65568 | tf_op jit(solution)/shard_map/ppermute | solution.py:23
  44.0 2.6 %collective-permute-done.10.refs_4_ = bf16[4,64,128]{2,1,0:T(8,128)(2,1)S(1)} collective-permute-done((bf16[4,64,128]{2,1,0:T(8,128)(2,1)S(1)}, bf16[4,64,128]{2,1,0:T(8,128)(2,1)S(1)}, u32[]{:S(2)}, u32[]{:S(2)}) %collective-permute-start.10) | collective-permute-done | bytes 65568 | tf_op jit(solution)/shard_map/ppermute | solution.py:23
  46.6 1.0 %shard_map.83 = (f32[6,64,128]{2,1,0:T(8,128)S(1)}, bf16[6,64,128]{2,1,0:T(8,128)(2,1)S(1)}, bf16[28,64,128]{2,1,0:T(8,128)(2,1)S(1)}) custom-call(s32[193,128]{1,0:T(8,128)S(1)} %broadcast_in_dim.36.table.refs_0_, f32[16,64,128]{2,1,0:T(8,128)S(1)} %get-tuple-element.35.loads.refs_0_.refs_1_, bf16[16,64,128]{2,1,0:T(8,128)(2,1)S(1)} %get-tuple-element.45.source.refs_2_, ...), custom_call_target="tpu_custom_call" | custom-call | flops 520126464 | bytes 8126976 | tf_op jit(solution)/shard_map/pallas_call | solution.py:38
  47.6 1.5 %shard_map.84 = (f32[10,64,128]{2,1,0:T(8,128)S(1)}, bf16[10,64,128]{2,1,0:T(8,128)(2,1)S(1)}) custom-call(s32[193,128]{1,0:T(8,128)S(1)} %broadcast_in_dim.36.table.refs_0_, f32[16,64,128]{2,1,0:T(8,128)S(1)} %get-tuple-element.35.loads.refs_0_.refs_1_, bf16[28,64,128]{2,1,0:T(8,128)(2,1)S(1)} %get-tuple-element.50.refs_2_, ...), custom_call_target="tpu_custom_call" | custom-call | flops 503349248 | bytes 7864832 | tf_op jit(solution)/shard_map/pallas_call | solution.py:38
  49.1 0.1 collective-permute-start.13
  49.2 2.0 %collective-permute-start.12 = (bf16[6,64,128]{2,1,0:T(8,128)(2,1)S(1)}, bf16[6,64,128]{2,1,0:T(8,128)(2,1)S(1)}, u32[]{:S(2)}, u32[]{:S(2)}) collective-permute-start(bf16[6,64,128]{2,1,0:T(8,128)(2,1)S(1)} %get-tuple-element.52), channel_id=1, source_target_pairs={{0,16},{8,24},{16,0},{24,8},{1,17},{9,25},{17,1},{25,9},{2,18},{10... | collective-permute-start | bytes 294920 | tf_op jit(solution)/shard_map/ppermute | solution.py:17
  51.2 4.3 %collective-permute-done.12.refs_2_ = bf16[6,64,128]{2,1,0:T(8,128)(2,1)S(1)} collective-permute-done((bf16[6,64,128]{2,1,0:T(8,128)(2,1)S(1)}, bf16[6,64,128]{2,1,0:T(8,128)(2,1)S(1)}, u32[]{:S(2)}, u32[]{:S(2)}) %collective-permute-start.12) | collective-permute-done | bytes 98336 | tf_op jit(solution)/shard_map/ppermute | solution.py:17
  55.6 0.0 collective-permute-done.13.refs_3_
  55.6 0.6 shard_map.85
  56.1 0.1 shard_map.86
  56.2 0.1 collective-permute-start.14
  56.3 2.5 %collective-permute-start.15 = (bf16[4,64,128]{2,1,0:T(8,128)(2,1)S(1)}, bf16[4,64,128]{2,1,0:T(8,128)(2,1)S(1)}, u32[]{:S(2)}, u32[]{:S(2)}) collective-permute-start(bf16[4,64,128]{2,1,0:T(8,128)(2,1)S(1)} %get-tuple-element.57), channel_id=1, source_target_pairs={{1,2},{3,4},{5,6},{7,0},{2,1},{4,3},{6,5},{0,7},{9,10},{11,12},{13... | collective-permute-start | bytes 196616 | tf_op jit(solution)/shard_map/ppermute | solution.py:23
  58.8 0.0 collective-permute-start.16
  58.8 1.8 %collective-permute-done.14.left = bf16[4,64,128]{2,1,0:T(8,128)(2,1)S(1)} collective-permute-done((bf16[4,64,128]{2,1,0:T(8,128)(2,1)S(1)}, bf16[4,64,128]{2,1,0:T(8,128)(2,1)S(1)}, u32[]{:S(2)}, u32[]{:S(2)}) %collective-permute-start.14) | collective-permute-done | bytes 65568 | tf_op jit(solution)/shard_map/ppermute | solution.py:23
  60.5 2.8 %collective-permute-done.15.right = bf16[4,64,128]{2,1,0:T(8,128)(2,1)S(1)} collective-permute-done((bf16[4,64,128]{2,1,0:T(8,128)(2,1)S(1)}, bf16[4,64,128]{2,1,0:T(8,128)(2,1)S(1)}, u32[]{:S(2)}, u32[]{:S(2)}) %collective-permute-start.15) | collective-permute-done | bytes 65568 | tf_op jit(solution)/shard_map/ppermute | solution.py:23
  63.3 0.1 shard_map.87
  63.4 4.8 %collective-permute-start.18 = (bf16[10,64,128]{2,1,0:T(8,128)(2,1)S(1)}, bf16[10,64,128]{2,1,0:T(8,128)(2,1)S(1)}, u32[]{:S(2)}, u32[]{:S(2)}) collective-permute-start(bf16[10,64,128]{2,1,0:T(8,128)(2,1)S(1)} %get-tuple-element.61), channel_id=1, source_target_pairs={{0,16},{8,24},{16,0},{24,8},{1,17},{9,25},{17,1},{25,9},{2,18},{10... | collective-permute-start | bytes 491528 | tf_op jit(solution)/shard_map/ppermute | solution.py:17
  68.2 0.1 collective-permute-start.17
  68.3 2.8 %shard_map.89.correction = f32[16,64,128]{2,1,0:T(8,128)S(1)} custom-call(s32[193,128]{1,0:T(8,128)S(1)} %broadcast_in_dim.36.table.refs_0_, f32[16,64,128]{2,1,0:T(8,128)S(1)} %get-tuple-element.54.current, bf16[16,64,128]{2,1,0:T(8,128)(2,1)S(1)} %get-tuple-element.55.source.first, bf16[28,64,128]{2,1,0:T(8,128)(2,1)S(1)} %get-tuple-element.60.extension, ...), custom_call_target="tpu_custom_call" | custom-call | flops 555778048 | bytes 8684032 | tf_op jit(solution)/shard_map/pallas_call | solution.py:38
  71.0 1.8 %collective-permute-done.17.early = bf16[6,64,128]{2,1,0:T(8,128)(2,1)S(1)} collective-permute-done((bf16[6,64,128]{2,1,0:T(8,128)(2,1)S(1)}, bf16[6,64,128]{2,1,0:T(8,128)(2,1)S(1)}, u32[]{:S(2)}, u32[]{:S(2)}) %collective-permute-start.17) | collective-permute-done | bytes 98336 | tf_op jit(solution)/shard_map/ppermute | solution.py:17
  72.8 2.5 %shard_map.90 = f32[64,2048]{1,0:T(8,128)} custom-call(s32[129,128]{1,0:T(8,128)S(1)} %broadcast_in_dim.33.table, bf16[6,64,128]{2,1,0:T(8,128)(2,1)S(1)} %collective-permute-done.17.early, bf16[10,64,128]{2,1,0:T(8,128)(2,1)S(1)} %collective-permute-done.18.late, f32[16,64,128]{2,1,0:T(8,128)S(1)} %shard_map.89.correction, ...), custom_call_target="tpu_custom_call" | custom-call | flops 423657472 | bytes 6619648 | tf_op jit(solution)/shard_map/pallas_call | solution.py:38
  (10 shorter events, 0.1 us)
Async XLA Ops:
  0.7 12.0 %collective-permute-start.1 = (s32[4]{0:T(128)S(1)}, s32[4]{0:T(128)S(1)}, u32[]{:S(2)}, u32[]{:S(2)}) collective-permute-start(s32[4]{0:T(128)S(1)} %get-tuple-element.65), channel_id=1, source_target_pairs={{0,1},{2,3},{4,5},{6,7},{1,0},{3,2},{5,4},{7,6},{8,9},{10,11},{12,... | collective-permute-start | bytes 56 | tf_op jit(solution)/shard_map/ppermute | solution.py:23
  3.7 9.0 %collective-permute-start.3 = (s32[4]{0:T(128)S(1)}, s32[4]{0:T(128)S(1)}, u32[]{:S(2)}, u32[]{:S(2)}) collective-permute-start(s32[4]{0:T(128)S(1)} %get-tuple-element.66), channel_id=1, source_target_pairs={{0,8},{8,0},{16,24},{24,16},{1,9},{9,1},{17,25},{25,17},{2,10},{10... | collective-permute-start | bytes 56 | tf_op jit(solution)/shard_map/ppermute | solution.py:17
  3.7 9.1 %collective-permute-start.2 = (s32[4]{0:T(128)S(1)}, s32[4]{0:T(128)S(1)}, u32[]{:S(2)}, u32[]{:S(2)}) collective-permute-start(s32[4]{0:T(128)S(1)} %get-tuple-element.67), channel_id=1, source_target_pairs={{1,2},{3,4},{5,6},{7,0},{2,1},{4,3},{6,5},{0,7},{9,10},{11,12},{13... | collective-permute-start | bytes 56 | tf_op jit(solution)/shard_map/ppermute | solution.py:23
  7.2 2.8 %copy-start.1 = (s32[1,16,12]{1,0,2:T(1,128)S(1)}, s32[1,16,12]{1,0,2:T(1,128)}, u32[]{:S(2)}) copy-start(s32[1,16,12]{1,0,2:T(1,128)} %param.9) | copy-start | bytes 2308
  7.2 2.9 %copy-start.2 = (s32[1,16,8]{1,2,0:T(8,128)S(1)}, s32[1,16,8]{1,2,0:T(8,128)}, u32[]{:S(2)}) copy-start(s32[1,16,8]{1,2,0:T(8,128)} %param.12) | copy-start | bytes 1540
  8.4 8.6 %copy-start = (bf16[1,16,128,128]{3,2,1,0:T(8,128)(2,1)S(1)}, bf16[1,16,128,128]{3,2,1,0:T(8,128)(2,1)}, u32[]{:S(2)}) copy-start(bf16[1,16,128,128]{3,2,1,0:T(8,128)(2,1)} %param.10) | copy-start | bytes 1572868
  8.4 8.5 %collective-permute-start = (bf16[16,64,128]{2,1,0:T(8,128)(2,1)S(1)}, bf16[16,64,128]{2,1,0:T(8,128)(2,1)S(1)}, u32[]{:S(2)}, u32[]{:S(2)}) collective-permute-start(bf16[16,64,128]{2,1,0:T(8,128)(2,1)S(1)} %get-tuple-element.36), channel_id=1, source_target_pairs={{0,16},{8,24},{16,0},{24,8},{1,17},{9,25},{17,1},{25,9},{2,18},{10... | collective-permute-start | bytes 786440 | tf_op jit(solution)/shard_map/ppermute | solution.py:17
  17.7 4.9 %collective-permute-start.4 = (bf16[4,64,128]{2,1,0:T(8,128)(2,1)S(1)}, bf16[4,64,128]{2,1,0:T(8,128)(2,1)S(1)}, u32[]{:S(2)}, u32[]{:S(2)}) collective-permute-start(bf16[4,64,128]{2,1,0:T(8,128)(2,1)S(1)} %get-tuple-element.39), channel_id=1, source_target_pairs={{0,1},{2,3},{4,5},{6,7},{1,0},{3,2},{5,4},{7,6},{8,9},{10,11},{12,... | collective-permute-start | bytes 196616 | tf_op jit(solution)/shard_map/ppermute | solution.py:23
  17.8 7.0 %collective-permute-start.5 = (bf16[4,64,128]{2,1,0:T(8,128)(2,1)S(1)}, bf16[4,64,128]{2,1,0:T(8,128)(2,1)S(1)}, u32[]{:S(2)}, u32[]{:S(2)}) collective-permute-start(bf16[4,64,128]{2,1,0:T(8,128)(2,1)S(1)} %get-tuple-element.40), channel_id=1, source_target_pairs={{1,2},{3,4},{5,6},{7,0},{2,1},{4,3},{6,5},{0,7},{9,10},{11,12},{13... | collective-permute-start | bytes 196616 | tf_op jit(solution)/shard_map/ppermute | solution.py:23
  19.7 5.1 %collective-permute-start.6 = (bf16[4,64,128]{2,1,0:T(8,128)(2,1)S(1)}, bf16[4,64,128]{2,1,0:T(8,128)(2,1)S(1)}, u32[]{:S(2)}, u32[]{:S(2)}) collective-permute-start(bf16[4,64,128]{2,1,0:T(8,128)(2,1)S(1)} %get-tuple-element.41), channel_id=1, source_target_pairs={{0,8},{8,0},{16,24},{24,16},{1,9},{9,1},{17,25},{25,17},{2,10},{10... | collective-permute-start | bytes 196616 | tf_op jit(solution)/shard_map/ppermute | solution.py:17
  26.4 10.7 %collective-permute-start.8 = (bf16[10,64,128]{2,1,0:T(8,128)(2,1)S(1)}, bf16[10,64,128]{2,1,0:T(8,128)(2,1)S(1)}, u32[]{:S(2)}, u32[]{:S(2)}) collective-permute-start(bf16[10,64,128]{2,1,0:T(8,128)(2,1)S(1)} %get-tuple-element.44), channel_id=1, source_target_pairs={{0,16},{8,24},{16,0},{24,8},{1,17},{9,25},{17,1},{25,9},{2,18},{10... | collective-permute-start | bytes 491528 | tf_op jit(solution)/shard_map/ppermute | solution.py:17
  32.4 4.8 %collective-permute-start.7 = (bf16[6,64,128]{2,1,0:T(8,128)(2,1)S(1)}, bf16[6,64,128]{2,1,0:T(8,128)(2,1)S(1)}, u32[]{:S(2)}, u32[]{:S(2)}) collective-permute-start(bf16[6,64,128]{2,1,0:T(8,128)(2,1)S(1)} %get-tuple-element.42), channel_id=1, source_target_pairs={{0,16},{8,24},{16,0},{24,8},{1,17},{9,25},{17,1},{25,9},{2,18},{10... | collective-permute-start | bytes 294920 | tf_op jit(solution)/shard_map/ppermute | solution.py:17
  38.9 5.0 %collective-permute-start.9 = (bf16[4,64,128]{2,1,0:T(8,128)(2,1)S(1)}, bf16[4,64,128]{2,1,0:T(8,128)(2,1)S(1)}, u32[]{:S(2)}, u32[]{:S(2)}) collective-permute-start(bf16[4,64,128]{2,1,0:T(8,128)(2,1)S(1)} %get-tuple-element.46), channel_id=1, source_target_pairs={{0,1},{2,3},{4,5},{6,7},{1,0},{3,2},{5,4},{7,6},{8,9},{10,11},{12,... | collective-permute-start | bytes 196616 | tf_op jit(solution)/shard_map/ppermute | solution.py:23
  39.6 7.0 %collective-permute-start.10 = (bf16[4,64,128]{2,1,0:T(8,128)(2,1)S(1)}, bf16[4,64,128]{2,1,0:T(8,128)(2,1)S(1)}, u32[]{:S(2)}, u32[]{:S(2)}) collective-permute-start(bf16[4,64,128]{2,1,0:T(8,128)(2,1)S(1)} %get-tuple-element.47), channel_id=1, source_target_pairs={{1,2},{3,4},{5,6},{7,0},{2,1},{4,3},{6,5},{0,7},{9,10},{11,12},{13... | collective-permute-start | bytes 196616 | tf_op jit(solution)/shard_map/ppermute | solution.py:23
  42.0 4.6 %collective-permute-start.11 = (bf16[4,64,128]{2,1,0:T(8,128)(2,1)S(1)}, bf16[4,64,128]{2,1,0:T(8,128)(2,1)S(1)}, u32[]{:S(2)}, u32[]{:S(2)}) collective-permute-start(bf16[4,64,128]{2,1,0:T(8,128)(2,1)S(1)} %get-tuple-element.48), channel_id=1, source_target_pairs={{0,8},{8,0},{16,24},{24,16},{1,9},{9,1},{17,25},{25,17},{2,10},{10... | collective-permute-start | bytes 196616 | tf_op jit(solution)/shard_map/ppermute | solution.py:17
  49.1 6.4 %collective-permute-start.13 = (bf16[10,64,128]{2,1,0:T(8,128)(2,1)S(1)}, bf16[10,64,128]{2,1,0:T(8,128)(2,1)S(1)}, u32[]{:S(2)}, u32[]{:S(2)}) collective-permute-start(bf16[10,64,128]{2,1,0:T(8,128)(2,1)S(1)} %get-tuple-element.53), channel_id=1, source_target_pairs={{0,16},{8,24},{16,0},{24,8},{1,17},{9,25},{17,1},{25,9},{2,18},{10... | collective-permute-start | bytes 491528 | tf_op jit(solution)/shard_map/ppermute | solution.py:17
  49.2 6.4 %collective-permute-start.12 = (bf16[6,64,128]{2,1,0:T(8,128)(2,1)S(1)}, bf16[6,64,128]{2,1,0:T(8,128)(2,1)S(1)}, u32[]{:S(2)}, u32[]{:S(2)}) collective-permute-start(bf16[6,64,128]{2,1,0:T(8,128)(2,1)S(1)} %get-tuple-element.52), channel_id=1, source_target_pairs={{0,16},{8,24},{16,0},{24,8},{1,17},{9,25},{17,1},{25,9},{2,18},{10... | collective-permute-start | bytes 294920 | tf_op jit(solution)/shard_map/ppermute | solution.py:17
  56.2 4.3 %collective-permute-start.14 = (bf16[4,64,128]{2,1,0:T(8,128)(2,1)S(1)}, bf16[4,64,128]{2,1,0:T(8,128)(2,1)S(1)}, u32[]{:S(2)}, u32[]{:S(2)}) collective-permute-start(bf16[4,64,128]{2,1,0:T(8,128)(2,1)S(1)} %get-tuple-element.56), channel_id=1, source_target_pairs={{0,1},{2,3},{4,5},{6,7},{1,0},{3,2},{5,4},{7,6},{8,9},{10,11},{12,... | collective-permute-start | bytes 196616 | tf_op jit(solution)/shard_map/ppermute | solution.py:23
  56.3 7.0 %collective-permute-start.15 = (bf16[4,64,128]{2,1,0:T(8,128)(2,1)S(1)}, bf16[4,64,128]{2,1,0:T(8,128)(2,1)S(1)}, u32[]{:S(2)}, u32[]{:S(2)}) collective-permute-start(bf16[4,64,128]{2,1,0:T(8,128)(2,1)S(1)} %get-tuple-element.57), channel_id=1, source_target_pairs={{1,2},{3,4},{5,6},{7,0},{2,1},{4,3},{6,5},{0,7},{9,10},{11,12},{13... | collective-permute-start | bytes 196616 | tf_op jit(solution)/shard_map/ppermute | solution.py:23
  58.8 4.6 %collective-permute-start.16 = (bf16[4,64,128]{2,1,0:T(8,128)(2,1)S(1)}, bf16[4,64,128]{2,1,0:T(8,128)(2,1)S(1)}, u32[]{:S(2)}, u32[]{:S(2)}) collective-permute-start(bf16[4,64,128]{2,1,0:T(8,128)(2,1)S(1)} %get-tuple-element.58), channel_id=1, source_target_pairs={{0,8},{8,0},{16,24},{24,16},{1,9},{9,1},{17,25},{25,17},{2,10},{10... | collective-permute-start | bytes 196616 | tf_op jit(solution)/shard_map/ppermute | solution.py:17
  63.4 9.4 %collective-permute-start.18 = (bf16[10,64,128]{2,1,0:T(8,128)(2,1)S(1)}, bf16[10,64,128]{2,1,0:T(8,128)(2,1)S(1)}, u32[]{:S(2)}, u32[]{:S(2)}) collective-permute-start(bf16[10,64,128]{2,1,0:T(8,128)(2,1)S(1)} %get-tuple-element.61), channel_id=1, source_target_pairs={{0,16},{8,24},{16,0},{24,8},{1,17},{9,25},{17,1},{25,9},{2,18},{10... | collective-permute-start | bytes 491528 | tf_op jit(solution)/shard_map/ppermute | solution.py:17
  68.2 4.6 %collective-permute-start.17 = (bf16[6,64,128]{2,1,0:T(8,128)(2,1)S(1)}, bf16[6,64,128]{2,1,0:T(8,128)(2,1)S(1)}, u32[]{:S(2)}, u32[]{:S(2)}) collective-permute-start(bf16[6,64,128]{2,1,0:T(8,128)(2,1)S(1)} %get-tuple-element.59), channel_id=1, source_target_pairs={{0,16},{8,24},{16,0},{24,8},{1,17},{9,25},{17,1},{25,9},{2,18},{10... | collective-permute-start | bytes 294920 | tf_op jit(solution)/shard_map/ppermute | solution.py:17

commit v6 on v5

--- a/solution.py
+++ b/solution.py
@@ -125,36 +125,37 @@
         first[i] = value.astype(jnp.bfloat16)
 
 
-def second_rows(low, table, current, first, extension, blocks, smoother, full, rounded):
-    rows = full.shape[0]
+def second_rows(low, table, current, first, extension, blocks, smoother, rounded, full=None):
+    rows = rounded.shape[0]
     for i in range(rows):
         applied = gathered(extension, table, low + i, blocks)
         rounded[i] = (current[low + i] - applied).astype(jnp.bfloat16)
     for i in range(rows):
         value = first[low + i].astype(jnp.float32) + times(rounded[i], smoother[low + i])
-        full[i] = value
         rounded[i] = value.astype(jnp.bfloat16)
-
-
-def second_start_body(table, current, first, left, right, sibling, blocks, smoother, full, rounded, extension):
+        if full is not None:
+            full[i] = value
+
+
+def second_start_body(table, current, first, left, right, sibling, blocks, smoother, rounded, extension, *full):
     joined([first, left, right, sibling], extension)
 
     @pl.when(jnp.logical_not(is_fine(table)))
     def _():
-        second_rows(0, table, current, first, extension, blocks, smoother, full, rounded)
-
-
-def second_end_body(table, current, first, extension, blocks, smoother, full, rounded):
+        second_rows(0, table, current, first, extension, blocks, smoother, rounded, *full)
+
+
+def second_end_body(table, current, first, extension, blocks, smoother, rounded, *full):
     @pl.when(jnp.logical_not(is_fine(table)))
     def _():
-        low = first.shape[0] - full.shape[0]
-        second_rows(low, table, current, first, extension, blocks, smoother, full, rounded)
+        low = first.shape[0] - rounded.shape[0]
+        second_rows(low, table, current, first, extension, blocks, smoother, rounded, *full)
 
 
 def second_fine_body(table, current, first, extension, blocks, smoother, full, scratch):
     @pl.when(is_fine(table))
     def _():
-        second_rows(0, table, current, first, extension, blocks, smoother, full, scratch)
+        second_rows(0, table, current, first, extension, blocks, smoother, scratch, full)
 
 
 def row_of(parts, at):
@@ -305,14 +306,21 @@
         if cycle_index == 0:
             blocks = fetched(blocks)
         args = (level_table, current, first)
-        start, rounded, extension = call(
-            second_start_body, part(early_rows) + (extended,), *args, *sides, blocks, smooth
+        ends = cycle_index + 1 == ITERS
+        rounded, extension, *start = call(
+            second_start_body,
+            (panels(early_rows, jnp.bfloat16), extended) + (panels(early_rows, jnp.float32),) * ends,
+            *args, *sides, blocks, smooth,
         )
         returned = [sent_on(rounded)]
-        end, rounded = call(second_end_body, part(late_rows), *args, extension, blocks, smooth)
+        rounded, *end = call(
+            second_end_body,
+            (panels(late_rows, jnp.bfloat16),) + (panels(late_rows, jnp.float32),) * ends,
+            *args, extension, blocks, smooth,
+        )
         returned.append(sent_on(rounded))
         correction = call(second_fine_body, wide, *args, extension, blocks, smooth, scratch=[held(block_rows)])
-        if cycle_index + 1 < ITERS:
+        if not ends:
             terms = [] if iterate is None else [iterate]
             iterate, rounded = call(
                 update_body, (wide, narrow), transfer_table, *returned, correction,
@@ -321,7 +329,7 @@
             sides = exchanged(rounded)
     final = call(
         last_body, jax.ShapeDtypeStruct((load_cols, block_rows * width), jnp.float32),
-        transfer_table, *returned, correction, start, end, iterate, transfer, out_specs=HBM,
+        transfer_table, *returned, correction, *start, *end, iterate, transfer, out_specs=HBM,
         scratch=[pltpu.VMEM(wide.shape, jnp.float32), held(block_rows), rowwise],
     )
     return final[None]

time: 75.7 us -> 74.3 us (0.982)
  Pallas kernels: 21.3 us -> 19.9 us
    pallas_call x18, Pallas kernels: 21.3 us -> 19.9 us  [call(): pl.pallas_call(body, out_shape=outs, in_specs=in_specs or [VMEM] * len(ar...]
  transfers between devices with their start and end apart: 19 -> 19, of which waited for: 9 -> 9; matrix products, arithmetic and copies ran while one was open for 1% -> 1% of each run, Pallas kernels for 15% -> 16%
where the time goes in v6:
time: 74.3 us; the launch traced here: 74.1 us
  starting transfers between devices  28.6 us (38%)
  waiting for transfers between devices  23.7 us (32%)
  Pallas kernels  19.9 us (27%)
  other arithmetic  0.86 us (1%)
    pallas_call x18, Pallas kernels, call(): pl.pallas_call(body, out_shape=outs, in_specs=in_specs or [VMEM] * len(ar...  19.9 us
    ppermute x11, starting transfers between devices, partner(): lax.ppermute(x, axis, [(i, i ^ 1 << apart) for i in range(lax.axis_size(a...  14.5 us
    ppermute x8, starting transfers between devices, swapped(): return lax.ppermute(x, axis, pairs + [(b, a) for a, b in pairs])  14.1 us
    ppermute x11, waiting for transfers between devices, partner(): lax.ppermute(x, axis, [(i, i ^ 1 << apart) for i in range(lax.axis_size(a...  12.4 us
    ppermute x8, waiting for transfers between devices, swapped(): return lax.ppermute(x, axis, pairs + [(b, a) for a, b in pairs])  11.4 us
  transfers between devices with their start and end apart: 19, of which 9 were waited for; matrix products, arithmetic and copies ran while one was open for 1% of the time, Pallas kernels for 16%

profile of v6, /device:TPU:0, one launch (start us, length us, event | category | flops | bytes accessed | tf_op | source)
XLA Modules:
  0.0 74.1 jit_solution(4381650738324316736)
XLA Ops:
  0.0 0.7 fusion.3
  0.7 3.0 %collective-permute-start.1 = (s32[4]{0:T(128)S(1)}, s32[4]{0:T(128)S(1)}, u32[]{:S(2)}, u32[]{:S(2)}) collective-permute-start(s32[4]{0:T(128)S(1)} %get-tuple-element.63), channel_id=1, source_target_pairs={{0,1},{2,3},{4,5},{6,7},{1,0},{3,2},{5,4},{7,6},{8,9},{10,11},{12,... | collective-permute-start | bytes 56 | tf_op jit(solution)/shard_map/ppermute | solution.py:23
  3.7 0.0 collective-permute-start.3
  3.7 3.5 %collective-permute-start.2 = (s32[4]{0:T(128)S(1)}, s32[4]{0:T(128)S(1)}, u32[]{:S(2)}, u32[]{:S(2)}) collective-permute-start(s32[4]{0:T(128)S(1)} %get-tuple-element.65), channel_id=1, source_target_pairs={{1,2},{3,4},{5,6},{7,0},{2,1},{4,3},{6,5},{0,7},{9,10},{11,12},{13... | collective-permute-start | bytes 56 | tf_op jit(solution)/shard_map/ppermute | solution.py:23
  7.2 1.2 %shard_map.73 = (f32[16,64,128]{2,1,0:T(8,128)S(1)}, bf16[16,64,128]{2,1,0:T(8,128)(2,1)S(1)}) custom-call(f32[64,2048]{1,0:T(8,128)} %bitcast.22), custom_call_target="tpu_custom_call" | custom-call | flops 5000000000 | bytes 1048576 | tf_op jit(solution)/shard_map/pallas_call | solution.py:38
  8.4 0.0 copy-start
  8.4 1.6 %collective-permute-start = (bf16[16,64,128]{2,1,0:T(8,128)(2,1)S(1)}, bf16[16,64,128]{2,1,0:T(8,128)(2,1)S(1)}, u32[]{:S(2)}, u32[]{:S(2)}) collective-permute-start(bf16[16,64,128]{2,1,0:T(8,128)(2,1)S(1)} %get-tuple-element.35), channel_id=1, source_target_pairs={{0,16},{8,24},{16,0},{24,8},{1,17},{9,25},{17,1},{25,9},{2,18},{10... | collective-permute-start | bytes 786440 | tf_op jit(solution)/shard_map/ppermute | solution.py:17
  10.0 0.1 copy.10
  10.1 0.1 reshape.28
  10.2 0.1 copy.9
  10.3 0.1 reshape.25
  10.3 0.1 pad_add_fusion.1
  10.4 2.3 %shard_map.74.refs_2_.refs_0_.refs_4_.transfer = bf16[16,8,128,128]{3,2,1,0:T(8,128)(2,1)S(1)} custom-call(f32[64,2048]{1,0:T(8,128)} %bitcast.23, bf16[16,8,128,128]{3,2,1,0:T(8,128)(2,1)} %bitcast.21), custom_call_target="tpu_custom_call" | custom-call | flops 570425344 | bytes 8912896 | tf_op jit(solution)/shard_map/pallas_call | solution.py:38
  12.7 0.0 collective-permute-done.1
  12.7 0.0 collective-permute-done.3
  12.7 0.0 collective-permute-done.2
  12.8 0.1 pad_add_fusion.2
  12.8 4.1 %collective-permute-done.refs_1_ = bf16[16,64,128]{2,1,0:T(8,128)(2,1)S(1)} collective-permute-done((bf16[16,64,128]{2,1,0:T(8,128)(2,1)S(1)}, bf16[16,64,128]{2,1,0:T(8,128)(2,1)S(1)}, u32[]{:S(2)}, u32[]{:S(2)}) %collective-permute-start) | collective-permute-done | bytes 262176 | tf_op jit(solution)/shard_map/ppermute | solution.py:17
  16.9 0.1 broadcast_in_dim.33.table
  17.0 0.0 copy-done
  17.0 0.6 shard_map.75
  17.6 0.1 broadcast_in_dim.37.table
  17.7 0.1 shard_map.76
  17.7 0.1 collective-permute-start.4
  17.8 1.9 %collective-permute-start.5 = (bf16[4,64,128]{2,1,0:T(8,128)(2,1)S(1)}, bf16[4,64,128]{2,1,0:T(8,128)(2,1)S(1)}, u32[]{:S(2)}, u32[]{:S(2)}) collective-permute-start(bf16[4,64,128]{2,1,0:T(8,128)(2,1)S(1)} %get-tuple-element.39), channel_id=1, source_target_pairs={{1,2},{3,4},{5,6},{7,0},{2,1},{4,3},{6,5},{0,7},{9,10},{11,12},{13... | collective-permute-start | bytes 196616 | tf_op jit(solution)/shard_map/ppermute | solution.py:23
  19.7 0.0 collective-permute-start.6
  19.7 2.9 %shard_map.77.blocks.refs_6_.refs_3_ = bf16[16,12,128,128]{3,2,1,0:T(8,128)(2,1)S(1)} custom-call(f32[64,2048]{1,0:T(8,128)} %bitcast.24, bf16[16,12,128,128]{3,2,1,0:T(8,128)(2,1)} %bitcast.20), custom_call_target="tpu_custom_call" | custom-call | flops 838860800 | bytes 13107200 | tf_op jit(solution)/shard_map/pallas_call | solution.py:38
  22.6 2.2 %collective-permute-done.5.right = bf16[4,64,128]{2,1,0:T(8,128)(2,1)S(1)} collective-permute-done((bf16[4,64,128]{2,1,0:T(8,128)(2,1)S(1)}, bf16[4,64,128]{2,1,0:T(8,128)(2,1)S(1)}, u32[]{:S(2)}, u32[]{:S(2)}) %collective-permute-start.5) | collective-permute-done | bytes 65568 | tf_op jit(solution)/shard_map/ppermute | solution.py:23
  24.8 0.1 broadcast_in_dim.36.table.refs_0_
  24.9 0.1 shard_map.78
  25.1 6.0 %collective-permute-start.8 = (bf16[10,64,128]{2,1,0:T(8,128)(2,1)S(1)}, bf16[10,64,128]{2,1,0:T(8,128)(2,1)S(1)}, u32[]{:S(2)}, u32[]{:S(2)}) collective-permute-start(bf16[10,64,128]{2,1,0:T(8,128)(2,1)S(1)} %shard_map.79), channel_id=1, source_target_pairs={{0,16},{8,24},{16,0},{24,8},{1,17},{9,25},{17,1},{25,9},{2,18},{10... | collective-permute-start | bytes 491528 | tf_op jit(solution)/shard_map/ppermute | solution.py:17
  31.0 0.1 collective-permute-start.7
  31.1 2.6 %shard_map.80.correction = f32[16,64,128]{2,1,0:T(8,128)S(1)} custom-call(s32[193,128]{1,0:T(8,128)S(1)} %broadcast_in_dim.36.table.refs_0_, f32[16,64,128]{2,1,0:T(8,128)S(1)} %get-tuple-element.36.current, bf16[16,64,128]{2,1,0:T(8,128)(2,1)S(1)} %get-tuple-element.37.source.first, bf16[28,64,128]{2,1,0:T(8,128)(2,1)S(1)} %get-tuple-element.42.extension, ...), custom_call_target="tpu_custom_call" | custom-call | flops 555778048 | bytes 8684032 | tf_op jit(solution)/shard_map/pallas_call | solution.py:38
  33.7 2.1 %collective-permute-done.7.early = bf16[6,64,128]{2,1,0:T(8,128)(2,1)S(1)} collective-permute-done((bf16[6,64,128]{2,1,0:T(8,128)(2,1)S(1)}, bf16[6,64,128]{2,1,0:T(8,128)(2,1)S(1)}, u32[]{:S(2)}, u32[]{:S(2)}) %collective-permute-start.7) | collective-permute-done | bytes 98336 | tf_op jit(solution)/shard_map/ppermute | solution.py:17
  35.8 0.0 collective-permute-done.8.late
  35.8 1.7 %shard_map.81 = (f32[16,64,128]{2,1,0:T(8,128)S(1)}, bf16[16,64,128]{2,1,0:T(8,128)(2,1)S(1)}) custom-call(s32[129,128]{1,0:T(8,128)S(1)} %broadcast_in_dim.33.table, bf16[6,64,128]{2,1,0:T(8,128)(2,1)S(1)} %collective-permute-done.7.early, bf16[10,64,128]{2,1,0:T(8,128)(2,1)S(1)} %collective-permute-done.8.late, f32[16,64,128]{2,1,0:T(8,128)S(1)} %shard_map.80.correction, ...), custom_call_target="tpu_custom_call" | custom-call | flops 373325824 | bytes 5833216 | tf_op jit(solution)/shard_map/pallas_call | solution.py:38
  37.6 0.1 shard_map.82
  37.6 0.7 collective-permute-start.9
  38.3 2.3 %collective-permute-start.10 = (bf16[4,64,128]{2,1,0:T(8,128)(2,1)S(1)}, bf16[4,64,128]{2,1,0:T(8,128)(2,1)S(1)}, u32[]{:S(2)}, u32[]{:S(2)}) collective-permute-start(bf16[4,64,128]{2,1,0:T(8,128)(2,1)S(1)} %get-tuple-element.45), channel_id=1, source_target_pairs={{1,2},{3,4},{5,6},{7,0},{2,1},{4,3},{6,5},{0,7},{9,10},{11,12},{13... | collective-permute-start | bytes 196616 | tf_op jit(solution)/shard_map/ppermute | solution.py:23
  40.6 0.0 collective-permute-start.11
  40.6 2.0 %collective-permute-done.9.refs_3_ = bf16[4,64,128]{2,1,0:T(8,128)(2,1)S(1)} collective-permute-done((bf16[4,64,128]{2,1,0:T(8,128)(2,1)S(1)}, bf16[4,64,128]{2,1,0:T(8,128)(2,1)S(1)}, u32[]{:S(2)}, u32[]{:S(2)}) %collective-permute-start.9) | collective-permute-done | bytes 65568 | tf_op jit(solution)/shard_map/ppermute | solution.py:23
  42.6 2.6 %collective-permute-done.10.refs_4_ = bf16[4,64,128]{2,1,0:T(8,128)(2,1)S(1)} collective-permute-done((bf16[4,64,128]{2,1,0:T(8,128)(2,1)S(1)}, bf16[4,64,128]{2,1,0:T(8,128)(2,1)S(1)}, u32[]{:S(2)}, u32[]{:S(2)}) %collective-permute-start.10) | collective-permute-done | bytes 65568 | tf_op jit(solution)/shard_map/ppermute | solution.py:23
  45.3 0.0 collective-permute-done.11.refs_5_
  45.3 1.0 %shard_map.83 = (f32[6,64,128]{2,1,0:T(8,128)S(1)}, bf16[6,64,128]{2,1,0:T(8,128)(2,1)S(1)}, bf16[28,64,128]{2,1,0:T(8,128)(2,1)S(1)}) custom-call(s32[193,128]{1,0:T(8,128)S(1)} %broadcast_in_dim.36.table.refs_0_, f32[16,64,128]{2,1,0:T(8,128)S(1)} %get-tuple-element.34.loads.refs_0_.refs_1_, bf16[16,64,128]{2,1,0:T(8,128)(2,1)S(1)} %get-tuple-element.43.source.refs_2_, ...), custom_call_target="tpu_custom_call" | custom-call | flops 520126464 | bytes 8126976 | tf_op jit(solution)/shard_map/pallas_call | solution.py:38
  46.3 1.5 %shard_map.84 = (f32[10,64,128]{2,1,0:T(8,128)S(1)}, bf16[10,64,128]{2,1,0:T(8,128)(2,1)S(1)}) custom-call(s32[193,128]{1,0:T(8,128)S(1)} %broadcast_in_dim.36.table.refs_0_, f32[16,64,128]{2,1,0:T(8,128)S(1)} %get-tuple-element.34.loads.refs_0_.refs_1_, bf16[28,64,128]{2,1,0:T(8,128)(2,1)S(1)} %get-tuple-element.48.refs_2_, ...), custom_call_target="tpu_custom_call" | custom-call | flops 503349248 | bytes 7864832 | tf_op jit(solution)/shard_map/pallas_call | solution.py:38
  47.8 0.1 collective-permute-start.13
  47.9 2.0 %collective-permute-start.12 = (bf16[6,64,128]{2,1,0:T(8,128)(2,1)S(1)}, bf16[6,64,128]{2,1,0:T(8,128)(2,1)S(1)}, u32[]{:S(2)}, u32[]{:S(2)}) collective-permute-start(bf16[6,64,128]{2,1,0:T(8,128)(2,1)S(1)} %get-tuple-element.50), channel_id=1, source_target_pairs={{0,16},{8,24},{16,0},{24,8},{1,17},{9,25},{17,1},{25,9},{2,18},{10... | collective-permute-start | bytes 294920 | tf_op jit(solution)/shard_map/ppermute | solution.py:17
  49.9 4.3 %collective-permute-done.12.refs_2_ = bf16[6,64,128]{2,1,0:T(8,128)(2,1)S(1)} collective-permute-done((bf16[6,64,128]{2,1,0:T(8,128)(2,1)S(1)}, bf16[6,64,128]{2,1,0:T(8,128)(2,1)S(1)}, u32[]{:S(2)}, u32[]{:S(2)}) %collective-permute-start.12) | collective-permute-done | bytes 98336 | tf_op jit(solution)/shard_map/ppermute | solution.py:17
  54.2 0.0 collective-permute-done.13.refs_3_
  54.3 0.6 shard_map.85
  54.8 0.1 shard_map.86
  54.9 0.1 collective-permute-start.14
  55.0 2.5 %collective-permute-start.15 = (bf16[4,64,128]{2,1,0:T(8,128)(2,1)S(1)}, bf16[4,64,128]{2,1,0:T(8,128)(2,1)S(1)}, u32[]{:S(2)}, u32[]{:S(2)}) collective-permute-start(bf16[4,64,128]{2,1,0:T(8,128)(2,1)S(1)} %get-tuple-element.55), channel_id=1, source_target_pairs={{1,2},{3,4},{5,6},{7,0},{2,1},{4,3},{6,5},{0,7},{9,10},{11,12},{13... | collective-permute-start | bytes 196616 | tf_op jit(solution)/shard_map/ppermute | solution.py:23
  57.4 0.0 collective-permute-start.16
  57.4 1.8 %collective-permute-done.14.left = bf16[4,64,128]{2,1,0:T(8,128)(2,1)S(1)} collective-permute-done((bf16[4,64,128]{2,1,0:T(8,128)(2,1)S(1)}, bf16[4,64,128]{2,1,0:T(8,128)(2,1)S(1)}, u32[]{:S(2)}, u32[]{:S(2)}) %collective-permute-start.14) | collective-permute-done | bytes 65568 | tf_op jit(solution)/shard_map/ppermute | solution.py:23
  59.2 2.8 %collective-permute-done.15.right = bf16[4,64,128]{2,1,0:T(8,128)(2,1)S(1)} collective-permute-done((bf16[4,64,128]{2,1,0:T(8,128)(2,1)S(1)}, bf16[4,64,128]{2,1,0:T(8,128)(2,1)S(1)}, u32[]{:S(2)}, u32[]{:S(2)}) %collective-permute-start.15) | collective-permute-done | bytes 65568 | tf_op jit(solution)/shard_map/ppermute | solution.py:23
  62.0 0.0 collective-permute-done.16.sibling
  62.0 0.1 shard_map.87
  62.1 4.7 %collective-permute-start.18 = (bf16[10,64,128]{2,1,0:T(8,128)(2,1)S(1)}, bf16[10,64,128]{2,1,0:T(8,128)(2,1)S(1)}, u32[]{:S(2)}, u32[]{:S(2)}) collective-permute-start(bf16[10,64,128]{2,1,0:T(8,128)(2,1)S(1)} %get-tuple-element.59), channel_id=1, source_target_pairs={{0,16},{8,24},{16,0},{24,8},{1,17},{9,25},{17,1},{25,9},{2,18},{10... | collective-permute-start | bytes 491528 | tf_op jit(solution)/shard_map/ppermute | solution.py:17
  66.9 0.1 collective-permute-start.17
  66.9 2.8 %shard_map.89.correction = f32[16,64,128]{2,1,0:T(8,128)S(1)} custom-call(s32[193,128]{1,0:T(8,128)S(1)} %broadcast_in_dim.36.table.refs_0_, f32[16,64,128]{2,1,0:T(8,128)S(1)} %get-tuple-element.52.current, bf16[16,64,128]{2,1,0:T(8,128)(2,1)S(1)} %get-tuple-element.53.source.first, bf16[28,64,128]{2,1,0:T(8,128)(2,1)S(1)} %get-tuple-element.58.extension, ...), custom_call_target="tpu_custom_call" | custom-call | flops 555778048 | bytes 8684032 | tf_op jit(solution)/shard_map/pallas_call | solution.py:38
  69.7 1.8 %collective-permute-done.17.early = bf16[6,64,128]{2,1,0:T(8,128)(2,1)S(1)} collective-permute-done((bf16[6,64,128]{2,1,0:T(8,128)(2,1)S(1)}, bf16[6,64,128]{2,1,0:T(8,128)(2,1)S(1)}, u32[]{:S(2)}, u32[]{:S(2)}) %collective-permute-start.17) | collective-permute-done | bytes 98336 | tf_op jit(solution)/shard_map/ppermute | solution.py:17
  71.5 0.0 collective-permute-done.18.late
  71.5 2.5 %shard_map.90 = f32[64,2048]{1,0:T(8,128)} custom-call(s32[129,128]{1,0:T(8,128)S(1)} %broadcast_in_dim.33.table, bf16[6,64,128]{2,1,0:T(8,128)(2,1)S(1)} %collective-permute-done.17.early, bf16[10,64,128]{2,1,0:T(8,128)(2,1)S(1)} %collective-permute-done.18.late, f32[16,64,128]{2,1,0:T(8,128)S(1)} %shard_map.89.correction, ...), custom_call_target="tpu_custom_call" | custom-call | flops 423657472 | bytes 6619648 | tf_op jit(solution)/shard_map/pallas_call | solution.py:38
  (10 shorter events, 0.1 us)
Async XLA Ops:
  0.7 12.0 %collective-permute-start.1 = (s32[4]{0:T(128)S(1)}, s32[4]{0:T(128)S(1)}, u32[]{:S(2)}, u32[]{:S(2)}) collective-permute-start(s32[4]{0:T(128)S(1)} %get-tuple-element.63), channel_id=1, source_target_pairs={{0,1},{2,3},{4,5},{6,7},{1,0},{3,2},{5,4},{7,6},{8,9},{10,11},{12,... | collective-permute-start | bytes 56 | tf_op jit(solution)/shard_map/ppermute | solution.py:23
  3.7 9.0 %collective-permute-start.3 = (s32[4]{0:T(128)S(1)}, s32[4]{0:T(128)S(1)}, u32[]{:S(2)}, u32[]{:S(2)}) collective-permute-start(s32[4]{0:T(128)S(1)} %get-tuple-element.64), channel_id=1, source_target_pairs={{0,8},{8,0},{16,24},{24,16},{1,9},{9,1},{17,25},{25,17},{2,10},{10... | collective-permute-start | bytes 56 | tf_op jit(solution)/shard_map/ppermute | solution.py:17
  3.7 9.1 %collective-permute-start.2 = (s32[4]{0:T(128)S(1)}, s32[4]{0:T(128)S(1)}, u32[]{:S(2)}, u32[]{:S(2)}) collective-permute-start(s32[4]{0:T(128)S(1)} %get-tuple-element.65), channel_id=1, source_target_pairs={{1,2},{3,4},{5,6},{7,0},{2,1},{4,3},{6,5},{0,7},{9,10},{11,12},{13... | collective-permute-start | bytes 56 | tf_op jit(solution)/shard_map/ppermute | solution.py:23
  7.2 2.8 %copy-start.1 = (s32[1,16,12]{1,0,2:T(1,128)S(1)}, s32[1,16,12]{1,0,2:T(1,128)}, u32[]{:S(2)}) copy-start(s32[1,16,12]{1,0,2:T(1,128)} %param.9) | copy-start | bytes 2308
  7.2 2.9 %copy-start.2 = (s32[1,16,8]{1,2,0:T(8,128)S(1)}, s32[1,16,8]{1,2,0:T(8,128)}, u32[]{:S(2)}) copy-start(s32[1,16,8]{1,2,0:T(8,128)} %param.12) | copy-start | bytes 1540
  8.4 8.6 %copy-start = (bf16[1,16,128,128]{3,2,1,0:T(8,128)(2,1)S(1)}, bf16[1,16,128,128]{3,2,1,0:T(8,128)(2,1)}, u32[]{:S(2)}) copy-start(bf16[1,16,128,128]{3,2,1,0:T(8,128)(2,1)} %param.10) | copy-start | bytes 1572868
  8.4 8.5 %collective-permute-start = (bf16[16,64,128]{2,1,0:T(8,128)(2,1)S(1)}, bf16[16,64,128]{2,1,0:T(8,128)(2,1)S(1)}, u32[]{:S(2)}, u32[]{:S(2)}) collective-permute-start(bf16[16,64,128]{2,1,0:T(8,128)(2,1)S(1)} %get-tuple-element.35), channel_id=1, source_target_pairs={{0,16},{8,24},{16,0},{24,8},{1,17},{9,25},{17,1},{25,9},{2,18},{10... | collective-permute-start | bytes 786440 | tf_op jit(solution)/shard_map/ppermute | solution.py:17
  17.7 4.9 %collective-permute-start.4 = (bf16[4,64,128]{2,1,0:T(8,128)(2,1)S(1)}, bf16[4,64,128]{2,1,0:T(8,128)(2,1)S(1)}, u32[]{:S(2)}, u32[]{:S(2)}) collective-permute-start(bf16[4,64,128]{2,1,0:T(8,128)(2,1)S(1)} %get-tuple-element.38), channel_id=1, source_target_pairs={{0,1},{2,3},{4,5},{6,7},{1,0},{3,2},{5,4},{7,6},{8,9},{10,11},{12,... | collective-permute-start | bytes 196616 | tf_op jit(solution)/shard_map/ppermute | solution.py:23
  17.8 7.0 %collective-permute-start.5 = (bf16[4,64,128]{2,1,0:T(8,128)(2,1)S(1)}, bf16[4,64,128]{2,1,0:T(8,128)(2,1)S(1)}, u32[]{:S(2)}, u32[]{:S(2)}) collective-permute-start(bf16[4,64,128]{2,1,0:T(8,128)(2,1)S(1)} %get-tuple-element.39), channel_id=1, source_target_pairs={{1,2},{3,4},{5,6},{7,0},{2,1},{4,3},{6,5},{0,7},{9,10},{11,12},{13... | collective-permute-start | bytes 196616 | tf_op jit(solution)/shard_map/ppermute | solution.py:23
  19.7 5.1 %collective-permute-start.6 = (bf16[4,64,128]{2,1,0:T(8,128)(2,1)S(1)}, bf16[4,64,128]{2,1,0:T(8,128)(2,1)S(1)}, u32[]{:S(2)}, u32[]{:S(2)}) collective-permute-start(bf16[4,64,128]{2,1,0:T(8,128)(2,1)S(1)} %get-tuple-element.40), channel_id=1, source_target_pairs={{0,8},{8,0},{16,24},{24,16},{1,9},{9,1},{17,25},{25,17},{2,10},{10... | collective-permute-start | bytes 196616 | tf_op jit(solution)/shard_map/ppermute | solution.py:17
  25.1 10.8 %collective-permute-start.8 = (bf16[10,64,128]{2,1,0:T(8,128)(2,1)S(1)}, bf16[10,64,128]{2,1,0:T(8,128)(2,1)S(1)}, u32[]{:S(2)}, u32[]{:S(2)}) collective-permute-start(bf16[10,64,128]{2,1,0:T(8,128)(2,1)S(1)} %shard_map.79), channel_id=1, source_target_pairs={{0,16},{8,24},{16,0},{24,8},{1,17},{9,25},{17,1},{25,9},{2,18},{10... | collective-permute-start | bytes 491528 | tf_op jit(solution)/shard_map/ppermute | solution.py:17
  31.0 4.8 %collective-permute-start.7 = (bf16[6,64,128]{2,1,0:T(8,128)(2,1)S(1)}, bf16[6,64,128]{2,1,0:T(8,128)(2,1)S(1)}, u32[]{:S(2)}, u32[]{:S(2)}) collective-permute-start(bf16[6,64,128]{2,1,0:T(8,128)(2,1)S(1)} %get-tuple-element.41), channel_id=1, source_target_pairs={{0,16},{8,24},{16,0},{24,8},{1,17},{9,25},{17,1},{25,9},{2,18},{10... | collective-permute-start | bytes 294920 | tf_op jit(solution)/shard_map/ppermute | solution.py:17
  37.6 5.0 %collective-permute-start.9 = (bf16[4,64,128]{2,1,0:T(8,128)(2,1)S(1)}, bf16[4,64,128]{2,1,0:T(8,128)(2,1)S(1)}, u32[]{:S(2)}, u32[]{:S(2)}) collective-permute-start(bf16[4,64,128]{2,1,0:T(8,128)(2,1)S(1)} %get-tuple-element.44), channel_id=1, source_target_pairs={{0,1},{2,3},{4,5},{6,7},{1,0},{3,2},{5,4},{7,6},{8,9},{10,11},{12,... | collective-permute-start | bytes 196616 | tf_op jit(solution)/shard_map/ppermute | solution.py:23
  38.3 7.0 %collective-permute-start.10 = (bf16[4,64,128]{2,1,0:T(8,128)(2,1)S(1)}, bf16[4,64,128]{2,1,0:T(8,128)(2,1)S(1)}, u32[]{:S(2)}, u32[]{:S(2)}) collective-permute-start(bf16[4,64,128]{2,1,0:T(8,128)(2,1)S(1)} %get-tuple-element.45), channel_id=1, source_target_pairs={{1,2},{3,4},{5,6},{7,0},{2,1},{4,3},{6,5},{0,7},{9,10},{11,12},{13... | collective-permute-start | bytes 196616 | tf_op jit(solution)/shard_map/ppermute | solution.py:23
  40.6 4.6 %collective-permute-start.11 = (bf16[4,64,128]{2,1,0:T(8,128)(2,1)S(1)}, bf16[4,64,128]{2,1,0:T(8,128)(2,1)S(1)}, u32[]{:S(2)}, u32[]{:S(2)}) collective-permute-start(bf16[4,64,128]{2,1,0:T(8,128)(2,1)S(1)} %get-tuple-element.46), channel_id=1, source_target_pairs={{0,8},{8,0},{16,24},{24,16},{1,9},{9,1},{17,25},{25,17},{2,10},{10... | collective-permute-start | bytes 196616 | tf_op jit(solution)/shard_map/ppermute | solution.py:17
  47.8 6.4 %collective-permute-start.13 = (bf16[10,64,128]{2,1,0:T(8,128)(2,1)S(1)}, bf16[10,64,128]{2,1,0:T(8,128)(2,1)S(1)}, u32[]{:S(2)}, u32[]{:S(2)}) collective-permute-start(bf16[10,64,128]{2,1,0:T(8,128)(2,1)S(1)} %get-tuple-element.51), channel_id=1, source_target_pairs={{0,16},{8,24},{16,0},{24,8},{1,17},{9,25},{17,1},{25,9},{2,18},{10... | collective-permute-start | bytes 491528 | tf_op jit(solution)/shard_map/ppermute | solution.py:17
  47.9 6.4 %collective-permute-start.12 = (bf16[6,64,128]{2,1,0:T(8,128)(2,1)S(1)}, bf16[6,64,128]{2,1,0:T(8,128)(2,1)S(1)}, u32[]{:S(2)}, u32[]{:S(2)}) collective-permute-start(bf16[6,64,128]{2,1,0:T(8,128)(2,1)S(1)} %get-tuple-element.50), channel_id=1, source_target_pairs={{0,16},{8,24},{16,0},{24,8},{1,17},{9,25},{17,1},{25,9},{2,18},{10... | collective-permute-start | bytes 294920 | tf_op jit(solution)/shard_map/ppermute | solution.py:17
  54.9 4.3 %collective-permute-start.14 = (bf16[4,64,128]{2,1,0:T(8,128)(2,1)S(1)}, bf16[4,64,128]{2,1,0:T(8,128)(2,1)S(1)}, u32[]{:S(2)}, u32[]{:S(2)}) collective-permute-start(bf16[4,64,128]{2,1,0:T(8,128)(2,1)S(1)} %get-tuple-element.54), channel_id=1, source_target_pairs={{0,1},{2,3},{4,5},{6,7},{1,0},{3,2},{5,4},{7,6},{8,9},{10,11},{12,... | collective-permute-start | bytes 196616 | tf_op jit(solution)/shard_map/ppermute | solution.py:23
  55.0 7.0 %collective-permute-start.15 = (bf16[4,64,128]{2,1,0:T(8,128)(2,1)S(1)}, bf16[4,64,128]{2,1,0:T(8,128)(2,1)S(1)}, u32[]{:S(2)}, u32[]{:S(2)}) collective-permute-start(bf16[4,64,128]{2,1,0:T(8,128)(2,1)S(1)} %get-tuple-element.55), channel_id=1, source_target_pairs={{1,2},{3,4},{5,6},{7,0},{2,1},{4,3},{6,5},{0,7},{9,10},{11,12},{13... | collective-permute-start | bytes 196616 | tf_op jit(solution)/shard_map/ppermute | solution.py:23
  57.4 4.6 %collective-permute-start.16 = (bf16[4,64,128]{2,1,0:T(8,128)(2,1)S(1)}, bf16[4,64,128]{2,1,0:T(8,128)(2,1)S(1)}, u32[]{:S(2)}, u32[]{:S(2)}) collective-permute-start(bf16[4,64,128]{2,1,0:T(8,128)(2,1)S(1)} %get-tuple-element.56), channel_id=1, source_target_pairs={{0,8},{8,0},{16,24},{24,16},{1,9},{9,1},{17,25},{25,17},{2,10},{10... | collective-permute-start | bytes 196616 | tf_op jit(solution)/shard_map/ppermute | solution.py:17
  62.1 9.4 %collective-permute-start.18 = (bf16[10,64,128]{2,1,0:T(8,128)(2,1)S(1)}, bf16[10,64,128]{2,1,0:T(8,128)(2,1)S(1)}, u32[]{:S(2)}, u32[]{:S(2)}) collective-permute-start(bf16[10,64,128]{2,1,0:T(8,128)(2,1)S(1)} %get-tuple-element.59), channel_id=1, source_target_pairs={{0,16},{8,24},{16,0},{24,8},{1,17},{9,25},{17,1},{25,9},{2,18},{10... | collective-permute-start | bytes 491528 | tf_op jit(solution)/shard_map/ppermute | solution.py:17
  66.9 4.6 %collective-permute-start.17 = (bf16[6,64,128]{2,1,0:T(8,128)(2,1)S(1)}, bf16[6,64,128]{2,1,0:T(8,128)(2,1)S(1)}, u32[]{:S(2)}, u32[]{:S(2)}) collective-permute-start(bf16[6,64,128]{2,1,0:T(8,128)(2,1)S(1)} %get-tuple-element.57), channel_id=1, source_target_pairs={{0,16},{8,24},{16,0},{24,8},{1,17},{9,25},{17,1},{25,9},{2,18},{10... | collective-permute-start | bytes 294920 | tf_op jit(solution)/shard_map/ppermute | solution.py:17

commit v7 on v6

--- a/solution.py
+++ b/solution.py
@@ -47,7 +47,7 @@
 
 
 def entry(table, at):
-    return table[at : at + 1, 0:1][0, 0]
+    return table[pl.ds(at, 1), 0:1][0, 0]
 
 
 def is_fine(table):
@@ -88,12 +88,6 @@
         sent[i] = panels[i].astype(jnp.bfloat16)
 
 
-def pack_body(table, source, *outs):
-    for side, out in enumerate(outs):
-        for j in range(out.shape[0]):
-            out[j] = source[entry(table, side * out.shape[0] + j)]
-
-
 def fetch_body(_, source, target, arrivals):
     copies = [
         pltpu.make_async_copy(source.at[i], target.at[i], arrivals.at[i])
@@ -105,20 +99,51 @@
         copy.wait()
 
 
-def first_body(table, loads, *refs):
-    *pieces, transfer, smoother, current, first, scratch = refs
-    residual, arrived = pieces[: len(pieces) // 2], pieces[len(pieces) // 2 :]
+def chosen(wanted, outs):
+    return [(entry(rows, j), out, j) for rows, out in zip(wanted, outs) for j in range(out.shape[0])]
+
+
+def first_listed_body(lists, pieces, table, loads, *refs):
+    wanted, refs = refs[:lists], refs[lists:]
+    residual, arrived, refs = refs[:pieces], refs[pieces : 2 * pieces], refs[2 * pieces :]
+    transfer, smoother, *refs, scratch = refs
+    outs = refs[:lists]
+    places = chosen(wanted, outs)
+    if pieces > 1:
+        joined_residual, joined_arrived = refs[lists:]
+    else:
+        (joined_residual,), (joined_arrived,) = residual, arrived
+
+    @pl.when(is_fine(table))
+    def _():
+        if pieces > 1:
+            joined(residual, joined_residual)
+        for at, (row, _, _) in enumerate(places):
+            scratch[at] = joined_residual[row].astype(jnp.bfloat16)
+
+    @pl.when(jnp.logical_not(is_fine(table)))
+    def _():
+        if pieces > 1:
+            joined(arrived, joined_arrived)
+        for at, (row, _, _) in enumerate(places):
+            value = loads[row] + gathered(joined_arrived, table, row, transfer)
+            scratch[at] = value.astype(jnp.bfloat16)
+
+    for at, (row, out, j) in enumerate(places):
+        out[j] = times(scratch[at], smoother[row]).astype(jnp.bfloat16)
+
+
+def first_body(table, loads, residual, arrived, transfer, smoother, current, first):
     rows = first.shape[0]
 
     @pl.when(is_fine(table))
     def _():
-        joined(residual, current)
+        joined([residual], current)
 
     @pl.when(jnp.logical_not(is_fine(table)))
     def _():
-        joined(arrived, scratch)
         for i in range(rows):
-            current[i] = loads[i] + gathered(scratch, table, i, transfer)
+            current[i] = loads[i] + gathered(arrived, table, i, transfer)
 
     for i in range(rows):
         value = times(current[i].astype(jnp.bfloat16), smoother[i])
@@ -165,17 +190,36 @@
         at -= part.shape[0]
 
 
-def update_body(table, early, late, correction, *refs):
-    *terms, transfer, iterate, rounded, scratch = refs
-
-    @pl.when(is_fine(table))
-    def _():
-        joined((early, late), scratch)
+def updated(row, arrived, table, transfer, correction, terms):
+    value = correction[row]
+    for term in terms:
+        value = term[row] + value
+    return value + gathered(arrived, table, row, transfer)
+
+
+def update_listed_body(lists, pieces, table, *refs):
+    wanted, arrived, refs = refs[:lists], refs[lists : lists + pieces], refs[lists + pieces :]
+    more = lists + (pieces > 1)
+    correction, *terms, transfer = refs[:-more]
+    outs = refs[-more:][:lists]
+
+    @pl.when(is_fine(table))
+    def _():
+        if pieces > 1:
+            joined(arrived, refs[-1])
+        source = refs[-1] if pieces > 1 else arrived[0]
+        for row, out, j in chosen(wanted, outs):
+            value = updated(row, source, table, transfer, correction, terms)
+            out[j] = value.astype(jnp.bfloat16)
+
+
+def update_body(table, arrived, correction, *refs):
+    *terms, transfer, iterate, rounded = refs
+
+    @pl.when(is_fine(table))
+    def _():
         for i in range(iterate.shape[0]):
-            value = correction[i]
-            for term in terms:
-                value = term[i] + value
-            value = value + gathered(scratch, table, i, transfer)
+            value = updated(i, arrived, table, transfer, correction, terms)
             iterate[i] = value
             rounded[i] = value.astype(jnp.bfloat16)
 
@@ -248,10 +292,21 @@
     )
     arrived = [partner(sent, "level", 1)]
 
+    def spread(values):
+        return jnp.broadcast_to(values[:, None], (values.shape[0], LANES))
+
+    def swap_all(odd, others):
+        behind = swapped(odd, "dom", 1)
+        ahead, beside = others()
+        ahead = swapped(ahead, "dom", 0)
+        beside = partner(beside, "level", 0)
+        return ahead, behind, beside
+
     even = lax.axis_index("dom") % 2 == 0
-    ahead = swapped(jnp.where(even, right_list, left_list), "dom", 0)
-    behind = swapped(jnp.where(even, left_list, right_list), "dom", 1)
-    wanted = jnp.concatenate([ahead, behind, partner(sibling_list, "level", 0)])
+    wanted_even, wanted_odd, wanted_beside = swap_all(
+        spread(jnp.where(even, left_list, right_list)),
+        lambda: (spread(jnp.where(even, right_list, left_list)), spread(sibling_list)),
+    )
     columns = level_cols.reshape(-1)
     from_left = (columns >= block_rows) & (columns < block_rows + list_width)
     from_right = (columns >= block_rows + list_width) & (columns < block_rows + 2 * list_width)
@@ -259,22 +314,25 @@
     columns = columns + jnp.where(even, moved, 0)
     fine = (lax.axis_index("level") < 2).astype(jnp.int32).reshape(1)
 
-    def spread(values):
-        return jnp.broadcast_to(values[:, None], (values.shape[0], LANES))
-
     level_table = spread(jnp.concatenate([columns, fine]))
     transfer_table = spread(jnp.concatenate([transfer_cols.reshape(-1), fine]))
-    wanted_table = spread(wanted)
 
     def fetched(source):
         return call(fetch_body, like(source), inside(loads), inside(source), in_specs=[HBM, HBM], scratch=[rowwise])
 
-    def exchanged(source):
-        ahead, behind, beside = call(pack_body, (listed,) * 3, wanted_table, source)
-        ahead = swapped(ahead, "dom", 0)
-        behind = swapped(behind, "dom", 1)
-        beside = partner(beside, "level", 0)
-        return ahead, behind, beside
+    def exchanged(body, fixed, pieces, rest, joins, scratch):
+        def listed_rows(wanted, pieces, joins):
+            lists, each = len(wanted), len(pieces[0])
+            held_rows = [held(lists * list_width)] * scratch
+            return call(
+                lambda *refs: body(lists, each, *refs), (listed,) * lists + joins,
+                *fixed, *wanted, *sum(pieces, []), *rest, scratch=held_rows,
+            )
+
+        odd, *whole = listed_rows([wanted_odd], pieces, joins)
+        whole = whole or sum(pieces, [])
+        sides = swap_all(odd, lambda: listed_rows([wanted_even, wanted_beside], [[x] for x in whole], ()))
+        return whole, sides
 
     def part(rows):
         return panels(rows, jnp.float32), panels(rows, jnp.bfloat16)
@@ -298,13 +356,12 @@
             )
             arrived.append(partner(sent, "level", 1))
             residual = [early, late]
-        current, first = call(
-            first_body, (wide, narrow), transfer_table, load_panels, *residual, *arrived,
-            transfer, smooth, scratch=[held(block_rows)],
+        args, rest = (transfer_table, load_panels), (transfer, smooth)
+        whole, sides = exchanged(
+            first_listed_body, args, [residual, arrived], rest,
+            (wide, narrow) if len(arrived) > 1 else (), True,
         )
-        sides = exchanged(first)
-        if cycle_index == 0:
-            blocks = fetched(blocks)
+        current, first = call(first_body, (wide, narrow), *args, *whole, *rest)
         args = (level_table, current, first)
         ends = cycle_index + 1 == ITERS
         rounded, extension, *start = call(
@@ -321,12 +378,9 @@
         returned.append(sent_on(rounded))
         correction = call(second_fine_body, wide, *args, extension, blocks, smooth, scratch=[held(block_rows)])
         if not ends:
-            terms = [] if iterate is None else [iterate]
-            iterate, rounded = call(
-                update_body, (wide, narrow), transfer_table, *returned, correction,
-                *terms, transfer, scratch=[held(block_rows)],
-            )
-            sides = exchanged(rounded)
+            rest = [correction] + ([] if iterate is None else [iterate]) + [transfer]
+            whole, sides = exchanged(update_listed_body, (transfer_table,), [returned], rest, (narrow,), False)
+            iterate, rounded = call(update_body, (wide, narrow), transfer_table, *whole, *rest)
     final = call(
         last_body, jax.ShapeDtypeStruct((load_cols, block_rows * width), jnp.float32),
         transfer_table, *returned, correction, *start, *end, iterate, transfer, out_specs=HBM,

time: 74.3 us -> 73 us (0.983)
  starting transfers between devices: 28.6 us -> 26.6 us
  waiting for transfers between devices: 23.7 us -> 24.6 us
    ppermute x11, waiting for transfers between devices: 12.4 us -> 13.9 us  [partner(): lax.ppermute(x, axis, [(i, i ^ 1 << apart) for i in range(lax.axis_size(a...]
    ppermute x11, starting transfers between devices: 14.5 us -> 13 us  [partner(): lax.ppermute(x, axis, [(i, i ^ 1 << apart) for i in range(lax.axis_size(a...]
    pallas_call x18 -> x20, Pallas kernels: 19.9 us -> 19.6 us  [call(): pl.pallas_call(body, out_shape=outs, in_specs=in_specs or [VMEM] * len(ar...]
  transfers between devices with their start and end apart: 19 -> 19, of which waited for: 9 -> 10; matrix products, arithmetic and copies ran while one was open for 1% -> 1% of each run, Pallas kernels for 16% -> 19%
where the time goes in v7:
time: 73 us; the launch traced here: 72.8 us
  starting transfers between devices  26.6 us (36%)
  waiting for transfers between devices  24.6 us (34%)
  Pallas kernels  19.6 us (27%)
  other arithmetic  0.78 us (1%)
  local copies, waits for them, and re-layouts  0.74 us (1%)
    pallas_call x20, Pallas kernels, call(): pl.pallas_call(body, out_shape=outs, in_specs=in_specs or [VMEM] * len(ar...  19.6 us
    ppermute x11, waiting for transfers between devices, partner(): lax.ppermute(x, axis, [(i, i ^ 1 << apart) for i in range(lax.axis_size(a...  13.9 us
    ppermute x8, starting transfers between devices, swapped(): return lax.ppermute(x, axis, pairs + [(b, a) for a, b in pairs])  13.6 us
    ppermute x11, starting transfers between devices, partner(): lax.ppermute(x, axis, [(i, i ^ 1 << apart) for i in range(lax.axis_size(a...  13 us
    ppermute x8, waiting for transfers between devices, swapped(): return lax.ppermute(x, axis, pairs + [(b, a) for a, b in pairs])  10.7 us
  transfers between devices with their start and end apart: 19, of which 10 were waited for; matrix products, arithmetic and copies ran while one was open for 1% of the time, Pallas kernels for 19%

profile of v7, /device:TPU:0, one launch (start us, length us, event | category | flops | bytes accessed | tf_op | source)
XLA Modules:
  0.0 72.8 jit_solution(16778501637681051)
XLA Ops:
  0.0 0.7 slice_bitcast_fusion
  0.7 0.1 broadcast_in_dim.50
  0.8 6.0 %collective-permute-start = (s32[4,128]{1,0:T(4,128)S(1)}, s32[4,128]{1,0:T(4,128)S(1)}, u32[]{:S(2)}, u32[]{:S(2)}) collective-permute-start(s32[4,128]{1,0:T(4,128)S(1)} %broadcast_in_dim.50), channel_id=1, source_target_pairs={{1,2},{3,4},{5,6},{7,0},{2,1},{4,3},{6,5},{0,7},{9,10},{11,12},{13... | collective-permute-start | bytes 6152 | tf_op jit(solution)/shard_map/ppermute | solution.py:23
  6.8 0.1 broadcast_in_dim.51
  6.9 0.0 collective-permute-start.2
  6.9 0.1 broadcast_in_dim.53
  6.9 0.0 collective-permute-start.3
  6.9 1.2 %shard_map.73 = (f32[16,64,128]{2,1,0:T(8,128)S(1)}, bf16[16,64,128]{2,1,0:T(8,128)(2,1)S(1)}) custom-call(f32[64,2048]{1,0:T(8,128)} %bitcast.35), custom_call_target="tpu_custom_call" | custom-call | flops 5000000000 | bytes 1048576 | tf_op jit(solution)/shard_map/pallas_call | solution.py:38
  8.1 1.6 %collective-permute-start.1 = (bf16[16,64,128]{2,1,0:T(8,128)(2,1)S(1)}, bf16[16,64,128]{2,1,0:T(8,128)(2,1)S(1)}, u32[]{:S(2)}, u32[]{:S(2)}) collective-permute-start(bf16[16,64,128]{2,1,0:T(8,128)(2,1)S(1)} %get-tuple-element.37), channel_id=1, source_target_pairs={{0,16},{8,24},{16,0},{24,8},{1,17},{9,25},{17,1},{25,9},{2,18},{10... | collective-permute-start | bytes 786440 | tf_op jit(solution)/shard_map/ppermute | solution.py:17
  9.7 0.1 copy.10
  9.8 0.1 reshape.46
  9.9 0.1 copy.9
  9.9 0.1 reshape.43
  10.1 0.0 copy-start
  10.1 2.3 %shard_map.74.transfer.refs_6_.refs_5_.refs_0_.refs_7_ = bf16[16,8,128,128]{3,2,1,0:T(8,128)(2,1)S(1)} custom-call(f32[64,2048]{1,0:T(8,128)} %bitcast.36, bf16[16,8,128,128]{3,2,1,0:T(8,128)(2,1)} %bitcast.34), custom_call_target="tpu_custom_call" | custom-call | flops 570425344 | bytes 8912896 | tf_op jit(solution)/shard_map/pallas_call | solution.py:38
  12.4 4.5 %collective-permute-done.1.arrived.refs_5_.refs_4_ = bf16[16,64,128]{2,1,0:T(8,128)(2,1)S(1)} collective-permute-done((bf16[16,64,128]{2,1,0:T(8,128)(2,1)S(1)}, bf16[16,64,128]{2,1,0:T(8,128)(2,1)S(1)}, u32[]{:S(2)}, u32[]{:S(2)}) %collective-permute-start.1) | collective-permute-done | bytes 262176 | tf_op jit(solution)/shard_map/ppermute | solution.py:17
  16.9 0.1 broadcast_in_dim.46.table.refs_0_
  17.0 0.0 copy-done
  17.0 0.0 slice-start
  17.0 0.3 shard_map.77
  17.3 0.0 slice-start.1
  17.3 2.0 %collective-permute-start.5 = (bf16[4,64,128]{2,1,0:T(8,128)(2,1)S(1)}, bf16[4,64,128]{2,1,0:T(8,128)(2,1)S(1)}, u32[]{:S(2)}, u32[]{:S(2)}) collective-permute-start(bf16[4,64,128]{2,1,0:T(8,128)(2,1)S(1)} %shard_map.77), channel_id=1, source_target_pairs={{1,2},{3,4},{5,6},{7,0},{2,1},{4,3},{6,5},{0,7},{9,10},{11,12},{13... | collective-permute-start | bytes 196616 | tf_op jit(solution)/shard_map/ppermute | solution.py:23
  19.3 0.0 collective-permute-done.2.refs_2_.refs_1_
  19.3 0.4 shard_map.76
  19.6 0.2 collective-permute-start.4
  19.9 0.0 collective-permute-start.6
  19.9 0.1 pad_add_fusion.1
  19.9 0.6 shard_map.75
  20.5 3.9 %collective-permute-done.5.right = bf16[4,64,128]{2,1,0:T(8,128)(2,1)S(1)} collective-permute-done((bf16[4,64,128]{2,1,0:T(8,128)(2,1)S(1)}, bf16[4,64,128]{2,1,0:T(8,128)(2,1)S(1)}, u32[]{:S(2)}, u32[]{:S(2)}) %collective-permute-start.5) | collective-permute-done | bytes 65568 | tf_op jit(solution)/shard_map/ppermute | solution.py:23
  24.4 0.2 collective-permute-done.4.left
  24.7 0.1 broadcast_in_dim.49.table.refs_0_
  24.8 0.1 shard_map.78
  24.9 5.2 %collective-permute-start.8 = (bf16[10,64,128]{2,1,0:T(8,128)(2,1)S(1)}, bf16[10,64,128]{2,1,0:T(8,128)(2,1)S(1)}, u32[]{:S(2)}, u32[]{:S(2)}) collective-permute-start(bf16[10,64,128]{2,1,0:T(8,128)(2,1)S(1)} %shard_map.79), channel_id=1, source_target_pairs={{0,16},{8,24},{16,0},{24,8},{1,17},{9,25},{17,1},{25,9},{2,18},{10... | collective-permute-start | bytes 491528 | tf_op jit(solution)/shard_map/ppermute | solution.py:17
  30.2 0.1 collective-permute-start.7
  30.2 2.6 %shard_map.80.refs_4_.correction = f32[16,64,128]{2,1,0:T(8,128)S(1)} custom-call(s32[193,128]{1,0:T(8,128)S(1)} %broadcast_in_dim.49.table.refs_0_, f32[16,64,128]{2,1,0:T(8,128)S(1)} %get-tuple-element.38.current, bf16[16,64,128]{2,1,0:T(8,128)(2,1)S(1)} %get-tuple-element.39.first, bf16[28,64,128]{2,1,0:T(8,128)(2,1)S(1)} %get-tuple-element.43.extension, ...), custom_call_target="tpu_custom_call" | custom-call | flops 555778048 | bytes 8684032 | tf_op jit(solution)/shard_map/pallas_call | solution.py:38
  32.8 2.5 %collective-permute-done.7.refs_2_ = bf16[6,64,128]{2,1,0:T(8,128)(2,1)S(1)} collective-permute-done((bf16[6,64,128]{2,1,0:T(8,128)(2,1)S(1)}, bf16[6,64,128]{2,1,0:T(8,128)(2,1)S(1)}, u32[]{:S(2)}, u32[]{:S(2)}) %collective-permute-start.7) | collective-permute-done | bytes 98336 | tf_op jit(solution)/shard_map/ppermute | solution.py:17
  35.3 0.6 shard_map.81
  35.9 2.8 %collective-permute-start.10 = (bf16[4,64,128]{2,1,0:T(8,128)(2,1)S(1)}, bf16[4,64,128]{2,1,0:T(8,128)(2,1)S(1)}, u32[]{:S(2)}, u32[]{:S(2)}) collective-permute-start(bf16[4,64,128]{2,1,0:T(8,128)(2,1)S(1)} %get-tuple-element.47), channel_id=1, source_target_pairs={{1,2},{3,4},{5,6},{7,0},{2,1},{4,3},{6,5},{0,7},{9,10},{11,12},{13... | collective-permute-start | bytes 196616 | tf_op jit(solution)/shard_map/ppermute | solution.py:23
  38.7 0.9 %shard_map.83 = (bf16[4,64,128]{2,1,0:T(8,128)(2,1)S(1)}, bf16[4,64,128]{2,1,0:T(8,128)(2,1)S(1)}) custom-call(s32[129,128]{1,0:T(8,128)S(1)} %broadcast_in_dim.46.table.refs_0_, s32[4,128]{1,0:T(4,128)S(1)} %collective-permute-done.2.refs_2_.refs_1_, s32[4,128]{1,0:T(4,128)S(1)} %collective-permute-done.3.refs_3_.refs_2_, ...), custom_call_target="tpu_custom_call" | custom-call | flops 331644928 | bytes 5181952 | tf_op jit(solution)/shard_map/pallas_call | solution.py:38
  39.7 0.1 collective-permute-start.9
  39.8 0.1 collective-permute-start.11
  39.9 1.7 %shard_map.82 = (f32[16,64,128]{2,1,0:T(8,128)S(1)}, bf16[16,64,128]{2,1,0:T(8,128)(2,1)S(1)}) custom-call(s32[129,128]{1,0:T(8,128)S(1)} %broadcast_in_dim.46.table.refs_0_, bf16[16,64,128]{2,1,0:T(8,128)(2,1)S(1)} %get-tuple-element.44.arrived.refs_3_, f32[16,64,128]{2,1,0:T(8,128)S(1)} %shard_map.80.refs_4_.correction, ...), custom_call_target="tpu_custom_call" | custom-call | flops 373325824 | bytes 5833216 | tf_op jit(solution)/shard_map/pallas_call | solution.py:38
  41.5 1.4 %collective-permute-done.10.refs_4_ = bf16[4,64,128]{2,1,0:T(8,128)(2,1)S(1)} collective-permute-done((bf16[4,64,128]{2,1,0:T(8,128)(2,1)S(1)}, bf16[4,64,128]{2,1,0:T(8,128)(2,1)S(1)}, u32[]{:S(2)}, u32[]{:S(2)}) %collective-permute-start.10) | collective-permute-done | bytes 65568 | tf_op jit(solution)/shard_map/ppermute | solution.py:23
  42.9 1.1 %collective-permute-done.9.refs_3_ = bf16[4,64,128]{2,1,0:T(8,128)(2,1)S(1)} collective-permute-done((bf16[4,64,128]{2,1,0:T(8,128)(2,1)S(1)}, bf16[4,64,128]{2,1,0:T(8,128)(2,1)S(1)}, u32[]{:S(2)}, u32[]{:S(2)}) %collective-permute-start.9) | collective-permute-done | bytes 65568 | tf_op jit(solution)/shard_map/ppermute | solution.py:23
  44.0 1.0 %shard_map.84 = (f32[6,64,128]{2,1,0:T(8,128)S(1)}, bf16[6,64,128]{2,1,0:T(8,128)(2,1)S(1)}, bf16[28,64,128]{2,1,0:T(8,128)(2,1)S(1)}) custom-call(s32[193,128]{1,0:T(8,128)S(1)} %broadcast_in_dim.49.table.refs_0_, f32[16,64,128]{2,1,0:T(8,128)S(1)} %get-tuple-element.36.loads.residual.refs_1_.refs_4_.refs_3_, ...), custom_call_target="tpu_custom_call" | custom-call | flops 520126464 | bytes 8126976 | tf_op jit(solution)/shard_map/pallas_call | solution.py:38
  45.0 1.5 %shard_map.85 = (f32[10,64,128]{2,1,0:T(8,128)S(1)}, bf16[10,64,128]{2,1,0:T(8,128)(2,1)S(1)}) custom-call(s32[193,128]{1,0:T(8,128)S(1)} %broadcast_in_dim.49.table.refs_0_, f32[16,64,128]{2,1,0:T(8,128)S(1)} %get-tuple-element.36.loads.residual.refs_1_.refs_4_.refs_3_, bf16[28,64,128]{2,1,0:T(8,128)(2,1)S(1)} %get-tuple-element.50.refs_2_, ...), custom_call_target="tpu_custom_call" | custom-call | flops 503349248 | bytes 7864832 | tf_op jit(solution)/shard_map/pallas_call | solution.py:38
  46.6 0.1 collective-permute-start.13
  46.6 2.0 %collective-permute-start.12 = (bf16[6,64,128]{2,1,0:T(8,128)(2,1)S(1)}, bf16[6,64,128]{2,1,0:T(8,128)(2,1)S(1)}, u32[]{:S(2)}, u32[]{:S(2)}) collective-permute-start(bf16[6,64,128]{2,1,0:T(8,128)(2,1)S(1)} %get-tuple-element.52), channel_id=1, source_target_pairs={{0,16},{8,24},{16,0},{24,8},{1,17},{9,25},{17,1},{25,9},{2,18},{10... | collective-permute-start | bytes 294920 | tf_op jit(solution)/shard_map/ppermute | solution.py:17
  48.7 4.3 %collective-permute-done.12.refs_5_ = bf16[6,64,128]{2,1,0:T(8,128)(2,1)S(1)} collective-permute-done((bf16[6,64,128]{2,1,0:T(8,128)(2,1)S(1)}, bf16[6,64,128]{2,1,0:T(8,128)(2,1)S(1)}, u32[]{:S(2)}, u32[]{:S(2)}) %collective-permute-start.12) | collective-permute-done | bytes 98336 | tf_op jit(solution)/shard_map/ppermute | solution.py:17
  53.0 0.0 collective-permute-done.13.refs_6_
  53.0 0.3 shard_map.86
  53.3 2.5 %collective-permute-start.15 = (bf16[4,64,128]{2,1,0:T(8,128)(2,1)S(1)}, bf16[4,64,128]{2,1,0:T(8,128)(2,1)S(1)}, u32[]{:S(2)}, u32[]{:S(2)}) collective-permute-start(bf16[4,64,128]{2,1,0:T(8,128)(2,1)S(1)} %get-tuple-element.59), channel_id=1, source_target_pairs={{1,2},{3,4},{5,6},{7,0},{2,1},{4,3},{6,5},{0,7},{9,10},{11,12},{13... | collective-permute-start | bytes 196616 | tf_op jit(solution)/shard_map/ppermute | solution.py:23
  55.7 0.4 shard_map.88
  56.1 0.1 collective-permute-start.14
  56.2 0.1 collective-permute-start.16
  56.3 0.7 %shard_map.87 = (f32[16,64,128]{2,1,0:T(8,128)S(1)}, bf16[16,64,128]{2,1,0:T(8,128)(2,1)S(1)}) custom-call(s32[129,128]{1,0:T(8,128)S(1)} %broadcast_in_dim.46.table.refs_0_, f32[16,64,128]{2,1,0:T(8,128)S(1)} %get-tuple-element.36.loads.residual.refs_1_.refs_4_.refs_3_, f32[16,64,128]{2,1,0:T(8,128)S(1)} %get-tuple-element.54.residual.refs_4_, ...), custom_call_target="tpu_custom_call" | custom-call | flops 440434688 | bytes 6881792 | tf_op jit(solution)/shard_map/pallas_call | solution.py:38
  57.0 3.4 %collective-permute-done.15.right = bf16[4,64,128]{2,1,0:T(8,128)(2,1)S(1)} collective-permute-done((bf16[4,64,128]{2,1,0:T(8,128)(2,1)S(1)}, bf16[4,64,128]{2,1,0:T(8,128)(2,1)S(1)}, u32[]{:S(2)}, u32[]{:S(2)}) %collective-permute-start.15) | collective-permute-done | bytes 65568 | tf_op jit(solution)/shard_map/ppermute | solution.py:23
  60.4 0.6 collective-permute-done.14.left
  61.0 0.1 shard_map.89
  61.2 3.8 %collective-permute-start.18 = (bf16[10,64,128]{2,1,0:T(8,128)(2,1)S(1)}, bf16[10,64,128]{2,1,0:T(8,128)(2,1)S(1)}, u32[]{:S(2)}, u32[]{:S(2)}) collective-permute-start(bf16[10,64,128]{2,1,0:T(8,128)(2,1)S(1)} %get-tuple-element.63), channel_id=1, source_target_pairs={{0,16},{8,24},{16,0},{24,8},{1,17},{9,25},{17,1},{25,9},{2,18},{10... | collective-permute-start | bytes 491528 | tf_op jit(solution)/shard_map/ppermute | solution.py:17
  65.0 0.1 collective-permute-start.17
  65.0 2.5 %shard_map.91.correction = f32[16,64,128]{2,1,0:T(8,128)S(1)} custom-call(s32[193,128]{1,0:T(8,128)S(1)} %broadcast_in_dim.49.table.refs_0_, f32[16,64,128]{2,1,0:T(8,128)S(1)} %get-tuple-element.56.current, bf16[16,64,128]{2,1,0:T(8,128)(2,1)S(1)} %get-tuple-element.57.first, bf16[28,64,128]{2,1,0:T(8,128)(2,1)S(1)} %get-tuple-element.62.extension, ...), custom_call_target="tpu_custom_call" | custom-call | flops 555778048 | bytes 8684032 | tf_op jit(solution)/shard_map/pallas_call | solution.py:38
  67.6 2.6 %collective-permute-done.17.early = bf16[6,64,128]{2,1,0:T(8,128)(2,1)S(1)} collective-permute-done((bf16[6,64,128]{2,1,0:T(8,128)(2,1)S(1)}, bf16[6,64,128]{2,1,0:T(8,128)(2,1)S(1)}, u32[]{:S(2)}, u32[]{:S(2)}) %collective-permute-start.17) | collective-permute-done | bytes 98336 | tf_op jit(solution)/shard_map/ppermute | solution.py:17
  70.2 2.5 %shard_map.92 = f32[64,2048]{1,0:T(8,128)} custom-call(s32[129,128]{1,0:T(8,128)S(1)} %broadcast_in_dim.46.table.refs_0_, bf16[6,64,128]{2,1,0:T(8,128)(2,1)S(1)} %collective-permute-done.17.early, bf16[10,64,128]{2,1,0:T(8,128)(2,1)S(1)} %collective-permute-done.18.late, f32[16,64,128]{2,1,0:T(8,128)S(1)} %shard_map.91.correction, ...), custom_call_target="tpu_custom_call" | custom-call | flops 423657472 | bytes 6619648 | tf_op jit(solution)/shard_map/pallas_call | solution.py:38
  (18 shorter events, 0.1 us)
Async XLA Ops:
  0.8 11.6 %collective-permute-start = (s32[4,128]{1,0:T(4,128)S(1)}, s32[4,128]{1,0:T(4,128)S(1)}, u32[]{:S(2)}, u32[]{:S(2)}) collective-permute-start(s32[4,128]{1,0:T(4,128)S(1)} %broadcast_in_dim.50), channel_id=1, source_target_pairs={{1,2},{3,4},{5,6},{7,0},{2,1},{4,3},{6,5},{0,7},{9,10},{11,12},{13... | collective-permute-start | bytes 6152 | tf_op jit(solution)/shard_map/ppermute | solution.py:23
  6.9 12.4 %collective-permute-start.2 = (s32[4,128]{1,0:T(4,128)S(1)}, s32[4,128]{1,0:T(4,128)S(1)}, u32[]{:S(2)}, u32[]{:S(2)}) collective-permute-start(s32[4,128]{1,0:T(4,128)S(1)} %broadcast_in_dim.51), channel_id=1, source_target_pairs={{0,1},{2,3},{4,5},{6,7},{1,0},{3,2},{5,4},{7,6},{8,9},{10,11},{12,... | collective-permute-start | bytes 6152 | tf_op jit(solution)/shard_map/ppermute | solution.py:23
  6.9 12.3 %collective-permute-start.3 = (s32[4,128]{1,0:T(4,128)S(1)}, s32[4,128]{1,0:T(4,128)S(1)}, u32[]{:S(2)}, u32[]{:S(2)}) collective-permute-start(s32[4,128]{1,0:T(4,128)S(1)} %broadcast_in_dim.53), channel_id=1, source_target_pairs={{0,8},{8,0},{16,24},{24,16},{1,9},{9,1},{17,25},{25,17},{2,10},{10... | collective-permute-start | bytes 6152 | tf_op jit(solution)/shard_map/ppermute | solution.py:17
  6.9 2.7 %copy-start.1 = (s32[1,16,12]{1,0,2:T(1,128)S(1)}, s32[1,16,12]{1,0,2:T(1,128)}, u32[]{:S(2)}) copy-start(s32[1,16,12]{1,0,2:T(1,128)} %param.9) | copy-start | bytes 2308
  6.9 2.9 %copy-start.2 = (s32[1,16,8]{1,2,0:T(8,128)S(1)}, s32[1,16,8]{1,2,0:T(8,128)}, u32[]{:S(2)}) copy-start(s32[1,16,8]{1,2,0:T(8,128)} %param.12) | copy-start | bytes 1540
  8.1 8.8 %collective-permute-start.1 = (bf16[16,64,128]{2,1,0:T(8,128)(2,1)S(1)}, bf16[16,64,128]{2,1,0:T(8,128)(2,1)S(1)}, u32[]{:S(2)}, u32[]{:S(2)}) collective-permute-start(bf16[16,64,128]{2,1,0:T(8,128)(2,1)S(1)} %get-tuple-element.37), channel_id=1, source_target_pairs={{0,16},{8,24},{16,0},{24,8},{1,17},{9,25},{17,1},{25,9},{2,18},{10... | collective-permute-start | bytes 786440 | tf_op jit(solution)/shard_map/ppermute | solution.py:17
  10.1 6.9 %copy-start = (bf16[1,16,128,128]{3,2,1,0:T(8,128)(2,1)S(1)}, bf16[1,16,128,128]{3,2,1,0:T(8,128)(2,1)}, u32[]{:S(2)}) copy-start(bf16[1,16,128,128]{3,2,1,0:T(8,128)(2,1)} %param.10) | copy-start | bytes 1572868
  17.0 7.8 %slice-start = ((s8[6291456]{0:T(1024)(128)(4,1)}), s8[4194304]{0:T(1024)(128)(4,1)S(1)}, s32[]{:S(2)}) async-start(s8[6291456]{0:T(1024)(128)(4,1)} %bitcast.12), calls=%async_computation | async-start | bytes 8388608
  17.3 7.5 %slice-start.1 = ((s8[6291456]{0:T(1024)(128)(4,1)}), s8[2097152]{0:T(1024)(128)(4,1)S(1)}, s32[]{:S(2)}) async-start(s8[6291456]{0:T(1024)(128)(4,1)} %bitcast.12), calls=%async_computation.1 | async-start | bytes 4194304
  17.3 7.1 %collective-permute-start.5 = (bf16[4,64,128]{2,1,0:T(8,128)(2,1)S(1)}, bf16[4,64,128]{2,1,0:T(8,128)(2,1)S(1)}, u32[]{:S(2)}, u32[]{:S(2)}) collective-permute-start(bf16[4,64,128]{2,1,0:T(8,128)(2,1)S(1)} %shard_map.77), channel_id=1, source_target_pairs={{1,2},{3,4},{5,6},{7,0},{2,1},{4,3},{6,5},{0,7},{9,10},{11,12},{13... | collective-permute-start | bytes 196616 | tf_op jit(solution)/shard_map/ppermute | solution.py:23
  19.6 5.0 %collective-permute-start.4 = (bf16[4,64,128]{2,1,0:T(8,128)(2,1)S(1)}, bf16[4,64,128]{2,1,0:T(8,128)(2,1)S(1)}, u32[]{:S(2)}, u32[]{:S(2)}) collective-permute-start(bf16[4,64,128]{2,1,0:T(8,128)(2,1)S(1)} %get-tuple-element.40), channel_id=1, source_target_pairs={{0,1},{2,3},{4,5},{6,7},{1,0},{3,2},{5,4},{7,6},{8,9},{10,11},{12,... | collective-permute-start | bytes 196616 | tf_op jit(solution)/shard_map/ppermute | solution.py:23
  19.9 4.8 %collective-permute-start.6 = (bf16[4,64,128]{2,1,0:T(8,128)(2,1)S(1)}, bf16[4,64,128]{2,1,0:T(8,128)(2,1)S(1)}, u32[]{:S(2)}, u32[]{:S(2)}) collective-permute-start(bf16[4,64,128]{2,1,0:T(8,128)(2,1)S(1)} %get-tuple-element.41), channel_id=1, source_target_pairs={{0,8},{8,0},{16,24},{24,16},{1,9},{9,1},{17,25},{25,17},{2,10},{10... | collective-permute-start | bytes 196616 | tf_op jit(solution)/shard_map/ppermute | solution.py:17
  24.9 10.4 %collective-permute-start.8 = (bf16[10,64,128]{2,1,0:T(8,128)(2,1)S(1)}, bf16[10,64,128]{2,1,0:T(8,128)(2,1)S(1)}, u32[]{:S(2)}, u32[]{:S(2)}) collective-permute-start(bf16[10,64,128]{2,1,0:T(8,128)(2,1)S(1)} %shard_map.79), channel_id=1, source_target_pairs={{0,16},{8,24},{16,0},{24,8},{1,17},{9,25},{17,1},{25,9},{2,18},{10... | collective-permute-start | bytes 491528 | tf_op jit(solution)/shard_map/ppermute | solution.py:17
  30.2 5.2 %collective-permute-start.7 = (bf16[6,64,128]{2,1,0:T(8,128)(2,1)S(1)}, bf16[6,64,128]{2,1,0:T(8,128)(2,1)S(1)}, u32[]{:S(2)}, u32[]{:S(2)}) collective-permute-start(bf16[6,64,128]{2,1,0:T(8,128)(2,1)S(1)} %get-tuple-element.42), channel_id=1, source_target_pairs={{0,16},{8,24},{16,0},{24,8},{1,17},{9,25},{17,1},{25,9},{2,18},{10... | collective-permute-start | bytes 294920 | tf_op jit(solution)/shard_map/ppermute | solution.py:17
  35.9 7.0 %collective-permute-start.10 = (bf16[4,64,128]{2,1,0:T(8,128)(2,1)S(1)}, bf16[4,64,128]{2,1,0:T(8,128)(2,1)S(1)}, u32[]{:S(2)}, u32[]{:S(2)}) collective-permute-start(bf16[4,64,128]{2,1,0:T(8,128)(2,1)S(1)} %get-tuple-element.47), channel_id=1, source_target_pairs={{1,2},{3,4},{5,6},{7,0},{2,1},{4,3},{6,5},{0,7},{9,10},{11,12},{13... | collective-permute-start | bytes 196616 | tf_op jit(solution)/shard_map/ppermute | solution.py:23
  39.7 4.3 %collective-permute-start.9 = (bf16[4,64,128]{2,1,0:T(8,128)(2,1)S(1)}, bf16[4,64,128]{2,1,0:T(8,128)(2,1)S(1)}, u32[]{:S(2)}, u32[]{:S(2)}) collective-permute-start(bf16[4,64,128]{2,1,0:T(8,128)(2,1)S(1)} %get-tuple-element.46), channel_id=1, source_target_pairs={{0,1},{2,3},{4,5},{6,7},{1,0},{3,2},{5,4},{7,6},{8,9},{10,11},{12,... | collective-permute-start | bytes 196616 | tf_op jit(solution)/shard_map/ppermute | solution.py:23
  39.8 4.3 %collective-permute-start.11 = (bf16[4,64,128]{2,1,0:T(8,128)(2,1)S(1)}, bf16[4,64,128]{2,1,0:T(8,128)(2,1)S(1)}, u32[]{:S(2)}, u32[]{:S(2)}) collective-permute-start(bf16[4,64,128]{2,1,0:T(8,128)(2,1)S(1)} %get-tuple-element.48), channel_id=1, source_target_pairs={{0,8},{8,0},{16,24},{24,16},{1,9},{9,1},{17,25},{25,17},{2,10},{10... | collective-permute-start | bytes 196616 | tf_op jit(solution)/shard_map/ppermute | solution.py:17
  46.6 6.4 %collective-permute-start.13 = (bf16[10,64,128]{2,1,0:T(8,128)(2,1)S(1)}, bf16[10,64,128]{2,1,0:T(8,128)(2,1)S(1)}, u32[]{:S(2)}, u32[]{:S(2)}) collective-permute-start(bf16[10,64,128]{2,1,0:T(8,128)(2,1)S(1)} %get-tuple-element.53), channel_id=1, source_target_pairs={{0,16},{8,24},{16,0},{24,8},{1,17},{9,25},{17,1},{25,9},{2,18},{10... | collective-permute-start | bytes 491528 | tf_op jit(solution)/shard_map/ppermute | solution.py:17
  46.6 6.4 %collective-permute-start.12 = (bf16[6,64,128]{2,1,0:T(8,128)(2,1)S(1)}, bf16[6,64,128]{2,1,0:T(8,128)(2,1)S(1)}, u32[]{:S(2)}, u32[]{:S(2)}) collective-permute-start(bf16[6,64,128]{2,1,0:T(8,128)(2,1)S(1)} %get-tuple-element.52), channel_id=1, source_target_pairs={{0,16},{8,24},{16,0},{24,8},{1,17},{9,25},{17,1},{25,9},{2,18},{10... | collective-permute-start | bytes 294920 | tf_op jit(solution)/shard_map/ppermute | solution.py:17
  53.3 7.1 %collective-permute-start.15 = (bf16[4,64,128]{2,1,0:T(8,128)(2,1)S(1)}, bf16[4,64,128]{2,1,0:T(8,128)(2,1)S(1)}, u32[]{:S(2)}, u32[]{:S(2)}) collective-permute-start(bf16[4,64,128]{2,1,0:T(8,128)(2,1)S(1)} %get-tuple-element.59), channel_id=1, source_target_pairs={{1,2},{3,4},{5,6},{7,0},{2,1},{4,3},{6,5},{0,7},{9,10},{11,12},{13... | collective-permute-start | bytes 196616 | tf_op jit(solution)/shard_map/ppermute | solution.py:23
  56.1 4.9 %collective-permute-start.14 = (bf16[4,64,128]{2,1,0:T(8,128)(2,1)S(1)}, bf16[4,64,128]{2,1,0:T(8,128)(2,1)S(1)}, u32[]{:S(2)}, u32[]{:S(2)}) collective-permute-start(bf16[4,64,128]{2,1,0:T(8,128)(2,1)S(1)} %get-tuple-element.58), channel_id=1, source_target_pairs={{0,1},{2,3},{4,5},{6,7},{1,0},{3,2},{5,4},{7,6},{8,9},{10,11},{12,... | collective-permute-start | bytes 196616 | tf_op jit(solution)/shard_map/ppermute | solution.py:23
  56.2 4.8 %collective-permute-start.16 = (bf16[4,64,128]{2,1,0:T(8,128)(2,1)S(1)}, bf16[4,64,128]{2,1,0:T(8,128)(2,1)S(1)}, u32[]{:S(2)}, u32[]{:S(2)}) collective-permute-start(bf16[4,64,128]{2,1,0:T(8,128)(2,1)S(1)} %get-tuple-element.60), channel_id=1, source_target_pairs={{0,8},{8,0},{16,24},{24,16},{1,9},{9,1},{17,25},{25,17},{2,10},{10... | collective-permute-start | bytes 196616 | tf_op jit(solution)/shard_map/ppermute | solution.py:17
  61.2 9.0 %collective-permute-start.18 = (bf16[10,64,128]{2,1,0:T(8,128)(2,1)S(1)}, bf16[10,64,128]{2,1,0:T(8,128)(2,1)S(1)}, u32[]{:S(2)}, u32[]{:S(2)}) collective-permute-start(bf16[10,64,128]{2,1,0:T(8,128)(2,1)S(1)} %get-tuple-element.63), channel_id=1, source_target_pairs={{0,16},{8,24},{16,0},{24,8},{1,17},{9,25},{17,1},{25,9},{2,18},{10... | collective-permute-start | bytes 491528 | tf_op jit(solution)/shard_map/ppermute | solution.py:17
  65.0 5.2 %collective-permute-start.17 = (bf16[6,64,128]{2,1,0:T(8,128)(2,1)S(1)}, bf16[6,64,128]{2,1,0:T(8,128)(2,1)S(1)}, u32[]{:S(2)}, u32[]{:S(2)}) collective-permute-start(bf16[6,64,128]{2,1,0:T(8,128)(2,1)S(1)} %get-tuple-element.61), channel_id=1, source_target_pairs={{0,16},{8,24},{16,0},{24,8},{1,17},{9,25},{17,1},{25,9},{2,18},{10... | collective-permute-start | bytes 294920 | tf_op jit(solution)/shard_map/ppermute | solution.py:17

commit v8 on v7

--- a/solution.py
+++ b/solution.py
@@ -8,6 +8,7 @@
 ITERS = 2
 LIMIT = 16 << 20
 LANES = 128
+SHARES = (0, 3, 11, 16)
 VMEM = pl.BlockSpec(memory_space=pltpu.VMEM)
 HBM = pl.BlockSpec(memory_space=pltpu.HBM)
 NT = (((1,), (1,)), ((), ()))
@@ -133,7 +134,7 @@
         out[j] = times(scratch[at], smoother[row]).astype(jnp.bfloat16)
 
 
-def first_body(table, loads, residual, arrived, transfer, smoother, current, first):
+def first_body(table, loads, wanted, residual, arrived, transfer, smoother, current, first, beside):
     rows = first.shape[0]
 
     @pl.when(is_fine(table))
@@ -148,6 +149,8 @@
     for i in range(rows):
         value = times(current[i].astype(jnp.bfloat16), smoother[i])
         first[i] = value.astype(jnp.bfloat16)
+    for row, out, j in chosen([wanted], [beside]):
+        out[j] = first[row]
 
 
 def second_rows(low, table, current, first, extension, blocks, smoother, rounded, full=None):
@@ -162,18 +165,17 @@
             full[i] = value
 
 
-def second_start_body(table, current, first, left, right, sibling, blocks, smoother, rounded, extension, *full):
+def second_start_body(low, table, current, first, left, right, sibling, blocks, smoother, rounded, extension, *full):
     joined([first, left, right, sibling], extension)
 
     @pl.when(jnp.logical_not(is_fine(table)))
     def _():
-        second_rows(0, table, current, first, extension, blocks, smoother, rounded, *full)
-
-
-def second_end_body(table, current, first, extension, blocks, smoother, rounded, *full):
+        second_rows(low, table, current, first, extension, blocks, smoother, rounded, *full)
+
+
+def second_more_body(low, table, current, first, extension, blocks, smoother, rounded, *full):
     @pl.when(jnp.logical_not(is_fine(table)))
     def _():
-        low = first.shape[0] - rounded.shape[0]
         second_rows(low, table, current, first, extension, blocks, smoother, rounded, *full)
 
 
@@ -213,8 +215,8 @@
             out[j] = value.astype(jnp.bfloat16)
 
 
-def update_body(table, arrived, correction, *refs):
-    *terms, transfer, iterate, rounded = refs
+def update_body(table, wanted, arrived, correction, *refs):
+    *terms, transfer, iterate, rounded, beside = refs
 
     @pl.when(is_fine(table))
     def _():
@@ -222,25 +224,33 @@
             value = updated(i, arrived, table, transfer, correction, terms)
             iterate[i] = value
             rounded[i] = value.astype(jnp.bfloat16)
-
-
-def residual_body(low, table, loads, *refs):
-    *sources, blocks, residual, sent = refs[: len(refs) - (low == 0)]
-
-    @pl.when(is_fine(table))
-    def _():
-        if low == 0:
-            extension = refs[-1]
-            joined(sources, extension)
-        else:
-            (extension,) = sources
-        for i in range(residual.shape[0]):
-            value = loads[low + i] - gathered(extension, table, low + i, blocks)
-            residual[i] = value
-            sent[i] = value.astype(jnp.bfloat16)
-
-
-def last_body(table, early, late, correction, start, end, iterate, transfer, out, total, scratch, leaves):
+        for row, out, j in chosen([wanted], [beside]):
+            out[j] = rounded[row]
+
+
+def residual_rows(low, table, loads, extension, blocks, sent, residual):
+    for i in range(residual.shape[0]):
+        value = loads[low + i] - gathered(extension, table, low + i, blocks)
+        residual[i] = value
+        sent[i] = value.astype(jnp.bfloat16)
+
+
+def residual_start_body(low, table, loads, own, left, right, sibling, blocks, sent, extension, residual):
+    @pl.when(is_fine(table))
+    def _():
+        joined([own, left, right, sibling], extension)
+        residual_rows(low, table, loads, extension, blocks, sent, residual)
+
+
+def residual_more_body(low, table, loads, extension, blocks, sent, residual):
+    @pl.when(is_fine(table))
+    def _():
+        residual_rows(low, table, loads, extension, blocks, sent, residual)
+
+
+def last_body(table, *refs):
+    *pieces, correction, iterate, transfer, out, total, scratch, leaves = refs
+    arrived, finals = pieces[: len(pieces) // 2], pieces[len(pieces) // 2 :]
     rows, _, width = total.shape
     copies = [
         pltpu.make_async_copy(total.at[i], out.at[:, pl.ds(i * width, width)], leaves.at[i])
@@ -249,7 +259,7 @@
 
     @pl.when(is_fine(table))
     def _():
-        joined((early, late), scratch)
+        joined(arrived, scratch)
         for i in range(rows):
             value = iterate[i] + correction[i]
             total[i] = value + gathered(scratch, table, i, transfer)
@@ -258,7 +268,7 @@
     @pl.when(jnp.logical_not(is_fine(table)))
     def _():
         for i in range(rows):
-            total[i] = row_of((start, end), i)
+            total[i] = row_of(finals, i)
             copies[i].start()
 
     for copy in copies:
@@ -280,8 +290,8 @@
         return pltpu.VMEM((count, load_cols, width), jnp.bfloat16)
 
     wide, narrow = panels(block_rows, jnp.float32), panels(block_rows, jnp.bfloat16)
-    early_rows = block_rows * 3 // 8
-    late_rows = block_rows - early_rows
+    bounds = [block_rows * share // 16 for share in SHARES]
+    parts = list(zip(bounds[:-1], bounds[1:]))
     listed = panels(list_width, jnp.bfloat16)
     extended = panels(block_rows + 3 * list_width, jnp.bfloat16)
     rowwise = pltpu.SemaphoreType.DMA((block_rows,))
@@ -295,18 +305,19 @@
     def spread(values):
         return jnp.broadcast_to(values[:, None], (values.shape[0], LANES))
 
-    def swap_all(odd, others):
-        behind = swapped(odd, "dom", 1)
-        ahead, beside = others()
-        ahead = swapped(ahead, "dom", 0)
-        beside = partner(beside, "level", 0)
-        return ahead, behind, beside
+    def swap_both(odd, even):
+        odd = swapped(odd, "dom", 1)
+        even = swapped(even, "dom", 0)
+        return even, odd
+
+    def swap_beside(x):
+        return partner(x, "level", 0)
 
     even = lax.axis_index("dom") % 2 == 0
-    wanted_even, wanted_odd, wanted_beside = swap_all(
-        spread(jnp.where(even, left_list, right_list)),
-        lambda: (spread(jnp.where(even, right_list, left_list)), spread(sibling_list)),
+    wanted_even, wanted_odd = swap_both(
+        spread(jnp.where(even, left_list, right_list)), spread(jnp.where(even, right_list, left_list))
     )
+    wanted_beside = swap_beside(spread(sibling_list))
     columns = level_cols.reshape(-1)
     from_left = (columns >= block_rows) & (columns < block_rows + list_width)
     from_right = (columns >= block_rows + list_width) & (columns < block_rows + 2 * list_width)
@@ -320,70 +331,60 @@
     def fetched(source):
         return call(fetch_body, like(source), inside(loads), inside(source), in_specs=[HBM, HBM], scratch=[rowwise])
 
-    def exchanged(body, fixed, pieces, rest, joins, scratch):
-        def listed_rows(wanted, pieces, joins):
-            lists, each = len(wanted), len(pieces[0])
-            held_rows = [held(lists * list_width)] * scratch
-            return call(
-                lambda *refs: body(lists, each, *refs), (listed,) * lists + joins,
-                *fixed, *wanted, *sum(pieces, []), *rest, scratch=held_rows,
+    def exchanged(bodies, fixed, pieces, rest, joins, scratch):
+        listed_body, body = bodies
+        each = len(pieces[0])
+        odd, even, *whole = call(
+            lambda *refs: listed_body(2, each, *refs), (listed,) * 2 + joins,
+            *fixed, wanted_odd, wanted_even, *sum(pieces, []), *rest,
+            scratch=[held(2 * list_width)] * scratch,
+        )
+        even, odd = swap_both(odd, even)
+        whole = whole or sum(pieces, [])
+        *results, beside = call(body, (wide, narrow, listed), *fixed, wanted_beside, *whole, *rest)
+        return (*results, (even, odd, swap_beside(beside)))
+
+    def in_parts(body, more_body, args, sources, rest, wanted):
+        kept, passed = [], []
+        for at, (low, high) in enumerate(parts):
+            outs = (panels(high - low, jnp.bfloat16),) + (extended,) * (at == 0)
+            outs += (panels(high - low, jnp.float32),) * wanted
+            rounded, *more = call(
+                lambda *refs: (more_body if at else body)(low, *refs), outs,
+                *args, *sources, *rest,
             )
-
-        odd, *whole = listed_rows([wanted_odd], pieces, joins)
-        whole = whole or sum(pieces, [])
-        sides = swap_all(odd, lambda: listed_rows([wanted_even, wanted_beside], [[x] for x in whole], ()))
-        return whole, sides
-
-    def part(rows):
-        return panels(rows, jnp.float32), panels(rows, jnp.bfloat16)
-
-    def sent_on(x):
-        return partner(x, "level", 1)
+            if at == 0:
+                sources = [more.pop(0)]
+            kept += more
+            passed.append(partner(rounded, "level", 1))
+        return passed, kept, sources[0]
 
     transfer = fetched(transfer)
     residual, iterate = [load_panels], None
     for cycle_index in range(ITERS):
         if cycle_index > 0:
-            args = (level_table, load_panels)
-            early, sent, extension = call(
-                lambda *refs: residual_body(0, *refs), part(early_rows) + (extended,),
-                *args, rounded, *sides, blocks,
+            arrived, residual, _ = in_parts(
+                residual_start_body, residual_more_body, (level_table, load_panels),
+                (rounded, *sides), (blocks,), True,
             )
-            arrived = [sent_on(sent)]
-            late, sent = call(
-                lambda *refs: residual_body(early_rows, *refs), part(late_rows),
-                *args, extension, blocks,
-            )
-            arrived.append(partner(sent, "level", 1))
-            residual = [early, late]
         args, rest = (transfer_table, load_panels), (transfer, smooth)
-        whole, sides = exchanged(
-            first_listed_body, args, [residual, arrived], rest,
+        current, first, sides = exchanged(
+            (first_listed_body, first_body), args, [residual, arrived], rest,
             (wide, narrow) if len(arrived) > 1 else (), True,
         )
-        current, first = call(first_body, (wide, narrow), *args, *whole, *rest)
         args = (level_table, current, first)
         ends = cycle_index + 1 == ITERS
-        rounded, extension, *start = call(
-            second_start_body,
-            (panels(early_rows, jnp.bfloat16), extended) + (panels(early_rows, jnp.float32),) * ends,
-            *args, *sides, blocks, smooth,
-        )
-        returned = [sent_on(rounded)]
-        rounded, *end = call(
-            second_end_body,
-            (panels(late_rows, jnp.bfloat16),) + (panels(late_rows, jnp.float32),) * ends,
-            *args, extension, blocks, smooth,
-        )
-        returned.append(sent_on(rounded))
+        returned, finals, extension = in_parts(second_start_body, second_more_body, args, sides, (blocks, smooth), ends)
         correction = call(second_fine_body, wide, *args, extension, blocks, smooth, scratch=[held(block_rows)])
         if not ends:
             rest = [correction] + ([] if iterate is None else [iterate]) + [transfer]
-            whole, sides = exchanged(update_listed_body, (transfer_table,), [returned], rest, (narrow,), False)
-            iterate, rounded = call(update_body, (wide, narrow), transfer_table, *whole, *rest)
+            iterate, rounded, sides = exchanged(
+                (update_listed_body, update_body), (transfer_table,), [returned], rest,
+                (narrow,), False,
+            )
     final = call(
         last_body, jax.ShapeDtypeStruct((load_cols, block_rows * width), jnp.float32),
-        transfer_table, *returned, correction, *start, *end, iterate, transfer, out_specs=HBM,
+        transfer_table, *returned, *finals, correction, iterate, transfer, out_specs=HBM,
         scratch=[pltpu.VMEM(wide.shape, jnp.float32), held(block_rows), rowwise],
     )
     return final[None]

time: 73 us -> 77.8 us (1.066)
  starting transfers between devices: 26.6 us -> 31.1 us
  waiting for transfers between devices: 24.6 us -> 25.6 us
    ppermute x11 -> x14, starting transfers between devices: 13 us -> 17.4 us  [partner(): lax.ppermute(x, axis, [(i, i ^ 1 << apart) for i in range(lax.axis_size(a...]
    ppermute x8, waiting for transfers between devices: 10.7 us -> 14.7 us  [swapped(): return lax.ppermute(x, axis, pairs + [(b, a) for a, b in pairs])]
    ppermute x11 -> x14, waiting for transfers between devices: 13.9 us -> 10.9 us  [partner(): lax.ppermute(x, axis, [(i, i ^ 1 << apart) for i in range(lax.axis_size(a...]
  transfers between devices with their start and end apart: 19 -> 22, of which waited for: 10 -> 10; matrix products, arithmetic and copies ran while one was open for 1% -> 1% of each run, Pallas kernels for 19% -> 14%
where the time goes in v8:
time: 77.8 us; the launch traced here: 77.6 us
  starting transfers between devices  31.1 us (40%)
  waiting for transfers between devices  25.6 us (33%)
  Pallas kernels  18.9 us (24%)
  other arithmetic  0.79 us (1%)
    pallas_call x20, Pallas kernels, call(): pl.pallas_call(body, out_shape=outs, in_specs=in_specs or [VMEM] * len(ar...  18.9 us
    ppermute x14, starting transfers between devices, partner(): lax.ppermute(x, axis, [(i, i ^ 1 << apart) for i in range(lax.axis_size(a...  17.4 us
    ppermute x8, waiting for transfers between devices, swapped(): return lax.ppermute(x, axis, pairs + [(b, a) for a, b in pairs])  14.7 us
    ppermute x8, starting transfers between devices, swapped(): return lax.ppermute(x, axis, pairs + [(b, a) for a, b in pairs])  13.7 us
    ppermute x14, waiting for transfers between devices, partner(): lax.ppermute(x, axis, [(i, i ^ 1 << apart) for i in range(lax.axis_size(a...  10.9 us
  transfers between devices with their start and end apart: 22, of which 10 were waited for; matrix products, arithmetic and copies ran while one was open for 1% of the time, Pallas kernels for 14%

profile of v8, /device:TPU:0, one launch (start us, length us, event | category | flops | bytes accessed | tf_op | source)
XLA Modules:
  0.0 77.6 jit_solution(14215922355512281669)
XLA Ops:
  0.0 0.7 fusion.4
  0.7 0.1 broadcast_in_dim.52
  0.8 6.0 %collective-permute-start.1 = (s32[4,128]{1,0:T(4,128)S(1)}, s32[4,128]{1,0:T(4,128)S(1)}, u32[]{:S(2)}, u32[]{:S(2)}) collective-permute-start(s32[4,128]{1,0:T(4,128)S(1)} %broadcast_in_dim.52), channel_id=1, source_target_pairs={{1,2},{3,4},{5,6},{7,0},{2,1},{4,3},{6,5},{0,7},{9,10},{11,12},{13... | collective-permute-start | bytes 6152 | tf_op jit(solution)/shard_map/ppermute | solution.py:24
  6.8 0.1 broadcast_in_dim.51
  6.9 0.0 collective-permute-start
  6.9 0.1 broadcast_in_dim.53
  6.9 1.2 %shard_map.73 = (f32[16,64,128]{2,1,0:T(8,128)S(1)}, bf16[16,64,128]{2,1,0:T(8,128)(2,1)S(1)}) custom-call(f32[64,2048]{1,0:T(8,128)} %bitcast.38), custom_call_target="tpu_custom_call" | custom-call | flops 5000000000 | bytes 1048576 | tf_op jit(solution)/shard_map/pallas_call | solution.py:39
  8.1 1.6 %collective-permute-start.3 = (bf16[16,64,128]{2,1,0:T(8,128)(2,1)S(1)}, bf16[16,64,128]{2,1,0:T(8,128)(2,1)S(1)}, u32[]{:S(2)}, u32[]{:S(2)}) collective-permute-start(bf16[16,64,128]{2,1,0:T(8,128)(2,1)S(1)} %get-tuple-element.42), channel_id=1, source_target_pairs={{0,16},{8,24},{16,0},{24,8},{1,17},{9,25},{17,1},{25,9},{2,18},{10... | collective-permute-start | bytes 786440 | tf_op jit(solution)/shard_map/ppermute | solution.py:18
  9.7 0.1 copy.10
  9.8 0.1 reshape.46
  9.9 0.1 copy.9
  9.9 0.1 reshape.43
  10.1 0.0 copy-start
  10.1 0.0 slice-start
  10.1 2.4 %shard_map.74.transfer.refs_6_.refs_7_.refs_0_.refs_10_.refs_8_ = bf16[16,8,128,128]{3,2,1,0:T(8,128)(2,1)S(1)} custom-call(f32[64,2048]{1,0:T(8,128)} %bitcast.39, bf16[16,8,128,128]{3,2,1,0:T(8,128)(2,1)} %bitcast.37), custom_call_target="tpu_custom_call" | custom-call | flops 570425344 | bytes 8912896 | tf_op jit(solution)/shard_map/pallas_call | solution.py:39
  12.5 0.0 collective-permute-done.2.refs_3_.refs_2_
  12.5 4.4 %collective-permute-done.3.arrived.refs_5_ = bf16[16,64,128]{2,1,0:T(8,128)(2,1)S(1)} collective-permute-done((bf16[16,64,128]{2,1,0:T(8,128)(2,1)S(1)}, bf16[16,64,128]{2,1,0:T(8,128)(2,1)S(1)}, u32[]{:S(2)}, u32[]{:S(2)}) %collective-permute-start.3) | collective-permute-done | bytes 262176 | tf_op jit(solution)/shard_map/ppermute | solution.py:18
  16.9 0.1 broadcast_in_dim.46.table.refs_0_
  17.0 0.0 copy-done
  17.0 0.0 slice-start.1
  17.0 0.4 shard_map.76
  17.4 1.8 %collective-permute-start.4 = (bf16[4,64,128]{2,1,0:T(8,128)(2,1)S(1)}, bf16[4,64,128]{2,1,0:T(8,128)(2,1)S(1)}, u32[]{:S(2)}, u32[]{:S(2)}) collective-permute-start(bf16[4,64,128]{2,1,0:T(8,128)(2,1)S(1)} %get-tuple-element.45), channel_id=1, source_target_pairs={{0,1},{2,3},{4,5},{6,7},{1,0},{3,2},{5,4},{7,6},{8,9},{10,11},{12,... | collective-permute-start | bytes 196616 | tf_op jit(solution)/shard_map/ppermute | solution.py:24
  19.2 0.2 collective-permute-start.5
  19.4 0.6 shard_map.75
  19.9 0.1 collective-permute-start.6
  20.0 0.1 pad_add_fusion.1
  20.1 1.6 %collective-permute-done.4.refs_3_ = bf16[4,64,128]{2,1,0:T(8,128)(2,1)S(1)} collective-permute-done((bf16[4,64,128]{2,1,0:T(8,128)(2,1)S(1)}, bf16[4,64,128]{2,1,0:T(8,128)(2,1)S(1)}, u32[]{:S(2)}, u32[]{:S(2)}) %collective-permute-start.4) | collective-permute-done | bytes 65568 | tf_op jit(solution)/shard_map/ppermute | solution.py:24
  21.7 4.4 %collective-permute-done.5.refs_4_ = bf16[4,64,128]{2,1,0:T(8,128)(2,1)S(1)} collective-permute-done((bf16[4,64,128]{2,1,0:T(8,128)(2,1)S(1)}, bf16[4,64,128]{2,1,0:T(8,128)(2,1)S(1)}, u32[]{:S(2)}, u32[]{:S(2)}) %collective-permute-start.5) | collective-permute-done | bytes 65568 | tf_op jit(solution)/shard_map/ppermute | solution.py:24
  26.1 0.1 broadcast_in_dim.49.refs_0_.table
  26.3 0.1 shard_map.77
  26.4 4.5 %collective-permute-start.8 = (bf16[8,64,128]{2,1,0:T(8,128)(2,1)S(1)}, bf16[8,64,128]{2,1,0:T(8,128)(2,1)S(1)}, u32[]{:S(2)}, u32[]{:S(2)}) collective-permute-start(bf16[8,64,128]{2,1,0:T(8,128)(2,1)S(1)} %shard_map.78), channel_id=1, source_target_pairs={{0,16},{8,24},{16,0},{24,8},{1,17},{9,25},{17,1},{25,9},{2,18},{10... | collective-permute-start | bytes 393224 | tf_op jit(solution)/shard_map/ppermute | solution.py:18
  30.9 1.1 %collective-permute-start.9 = (bf16[5,64,128]{2,1,0:T(8,128)(2,1)S(1)}, bf16[5,64,128]{2,1,0:T(8,128)(2,1)S(1)}, u32[]{:S(2)}, u32[]{:S(2)}) collective-permute-start(bf16[5,64,128]{2,1,0:T(8,128)(2,1)S(1)} %shard_map.79), channel_id=1, source_target_pairs={{0,16},{8,24},{16,0},{24,8},{1,17},{9,25},{17,1},{25,9},{2,18},{10... | collective-permute-start | bytes 245768 | tf_op jit(solution)/shard_map/ppermute | solution.py:18
  32.0 1.0 %collective-permute-start.7 = (bf16[3,64,128]{2,1,0:T(8,128)(2,1)S(1)}, bf16[3,64,128]{2,1,0:T(8,128)(2,1)S(1)}, u32[]{:S(2)}, u32[]{:S(2)}) collective-permute-start(bf16[3,64,128]{2,1,0:T(8,128)(2,1)S(1)} %get-tuple-element.48), channel_id=1, source_target_pairs={{0,16},{8,24},{16,0},{24,8},{1,17},{9,25},{17,1},{25,9},{2,18},{10... | collective-permute-start | bytes 147464 | tf_op jit(solution)/shard_map/ppermute | solution.py:18
  33.0 2.6 %shard_map.80.refs_6_.correction = f32[16,64,128]{2,1,0:T(8,128)S(1)} custom-call(s32[193,128]{1,0:T(8,128)S(1)} %broadcast_in_dim.49.refs_0_.table, f32[16,64,128]{2,1,0:T(8,128)S(1)} %get-tuple-element.43.refs_1_.current, bf16[16,64,128]{2,1,0:T(8,128)(2,1)S(1)} %get-tuple-element.44.refs_2_.first, ...), custom_call_target="tpu_custom_call" | custom-call | flops 555778048 | bytes 8684032 | tf_op jit(solution)/shard_map/pallas_call | solution.py:39
  35.6 0.5 collective-permute-done.7.refs_3_
  36.1 0.9 %shard_map.81 = (bf16[4,64,128]{2,1,0:T(8,128)(2,1)S(1)}, bf16[4,64,128]{2,1,0:T(8,128)(2,1)S(1)}, bf16[16,64,128]{2,1,0:T(8,128)(2,1)S(1)}) custom-call(s32[129,128]{1,0:T(8,128)S(1)} %broadcast_in_dim.46.table.refs_0_, s32[4,128]{1,0:T(4,128)S(1)} %collective-permute-done.1.refs_2_.refs_1_, s32[4,128]{1,0:T(4,128)S(1)} %collective-permute-done.2.refs_3_.refs_2_, ...), custom_call_target="tpu_custom_call" | custom-call | flops 348422144 | bytes 5444096 | tf_op jit(solution)/shard_map/pallas_call | solution.py:39
  37.0 1.7 %shard_map.82 = (f32[16,64,128]{2,1,0:T(8,128)S(1)}, bf16[16,64,128]{2,1,0:T(8,128)(2,1)S(1)}, bf16[4,64,128]{2,1,0:T(8,128)(2,1)S(1)}) custom-call(s32[129,128]{1,0:T(8,128)S(1)} %broadcast_in_dim.46.table.refs_0_, s32[4,128]{1,0:T(4,128)S(1)} %collective-permute-done.wanted, bf16[16,64,128]{2,1,0:T(8,128)(2,1)S(1)} %get-tuple-element.50.arrived, ...), custom_call_target="tpu_custom_call" | custom-call | flops 377651200 | bytes 5900800 | tf_op jit(solution)/shard_map/pallas_call | solution.py:39
  38.7 0.1 collective-permute-start.12
  38.8 0.1 collective-permute-start.10
  38.9 2.8 %collective-permute-start.11 = (bf16[4,64,128]{2,1,0:T(8,128)(2,1)S(1)}, bf16[4,64,128]{2,1,0:T(8,128)(2,1)S(1)}, u32[]{:S(2)}, u32[]{:S(2)}) collective-permute-start(bf16[4,64,128]{2,1,0:T(8,128)(2,1)S(1)} %get-tuple-element.53), channel_id=1, source_target_pairs={{1,2},{3,4},{5,6},{7,0},{2,1},{4,3},{6,5},{0,7},{9,10},{11,12},{13... | collective-permute-start | bytes 196616 | tf_op jit(solution)/shard_map/ppermute | solution.py:24
  41.6 1.6 %collective-permute-done.10.refs_3_ = bf16[4,64,128]{2,1,0:T(8,128)(2,1)S(1)} collective-permute-done((bf16[4,64,128]{2,1,0:T(8,128)(2,1)S(1)}, bf16[4,64,128]{2,1,0:T(8,128)(2,1)S(1)}, u32[]{:S(2)}, u32[]{:S(2)}) %collective-permute-start.10) | collective-permute-done | bytes 65568 | tf_op jit(solution)/shard_map/ppermute | solution.py:24
  43.3 2.7 %collective-permute-done.11.refs_4_ = bf16[4,64,128]{2,1,0:T(8,128)(2,1)S(1)} collective-permute-done((bf16[4,64,128]{2,1,0:T(8,128)(2,1)S(1)}, bf16[4,64,128]{2,1,0:T(8,128)(2,1)S(1)}, u32[]{:S(2)}, u32[]{:S(2)}) %collective-permute-start.11) | collective-permute-done | bytes 65568 | tf_op jit(solution)/shard_map/ppermute | solution.py:24
  46.0 0.6 shard_map.83
  46.6 1.2 %shard_map.84 = (bf16[8,64,128]{2,1,0:T(8,128)(2,1)S(1)}, f32[8,64,128]{2,1,0:T(8,128)S(1)}) custom-call(s32[193,128]{1,0:T(8,128)S(1)} %broadcast_in_dim.49.refs_0_.table, f32[16,64,128]{2,1,0:T(8,128)S(1)} %get-tuple-element.41.loads.residual.refs_1_.refs_4_, bf16[28,64,128]{2,1,0:T(8,128)(2,1)S(1)} %get-tuple-element.56.refs_2_, ...), custom_call_target="tpu_custom_call" | custom-call | flops 497057792 | bytes 7766528 | tf_op jit(solution)/shard_map/pallas_call | solution.py:39
  47.8 0.1 collective-permute-start.14
  47.9 0.8 %shard_map.85 = (bf16[5,64,128]{2,1,0:T(8,128)(2,1)S(1)}, f32[5,64,128]{2,1,0:T(8,128)S(1)}) custom-call(s32[193,128]{1,0:T(8,128)S(1)} %broadcast_in_dim.49.refs_0_.table, f32[16,64,128]{2,1,0:T(8,128)S(1)} %get-tuple-element.41.loads.residual.refs_1_.refs_4_, bf16[28,64,128]{2,1,0:T(8,128)(2,1)S(1)} %get-tuple-element.56.refs_2_, ...), custom_call_target="tpu_custom_call" | custom-call | flops 487620608 | bytes 7619072 | tf_op jit(solution)/shard_map/pallas_call | solution.py:39
  48.7 1.3 %collective-permute-start.15 = (bf16[5,64,128]{2,1,0:T(8,128)(2,1)S(1)}, bf16[5,64,128]{2,1,0:T(8,128)(2,1)S(1)}, u32[]{:S(2)}, u32[]{:S(2)}) collective-permute-start(bf16[5,64,128]{2,1,0:T(8,128)(2,1)S(1)} %get-tuple-element.61), channel_id=1, source_target_pairs={{0,16},{8,24},{16,0},{24,8},{1,17},{9,25},{17,1},{25,9},{2,18},{10... | collective-permute-start | bytes 245768 | tf_op jit(solution)/shard_map/ppermute | solution.py:18
  50.0 0.8 %collective-permute-start.13 = (bf16[3,64,128]{2,1,0:T(8,128)(2,1)S(1)}, bf16[3,64,128]{2,1,0:T(8,128)(2,1)S(1)}, u32[]{:S(2)}, u32[]{:S(2)}) collective-permute-start(bf16[3,64,128]{2,1,0:T(8,128)(2,1)S(1)} %get-tuple-element.59), channel_id=1, source_target_pairs={{0,16},{8,24},{16,0},{24,8},{1,17},{9,25},{17,1},{25,9},{2,18},{10... | collective-permute-start | bytes 147464 | tf_op jit(solution)/shard_map/ppermute | solution.py:18
  50.8 4.8 %collective-permute-done.13.refs_7_ = bf16[3,64,128]{2,1,0:T(8,128)(2,1)S(1)} collective-permute-done((bf16[3,64,128]{2,1,0:T(8,128)(2,1)S(1)}, bf16[3,64,128]{2,1,0:T(8,128)(2,1)S(1)}, u32[]{:S(2)}, u32[]{:S(2)}) %collective-permute-start.13) | collective-permute-done | bytes 49184 | tf_op jit(solution)/shard_map/ppermute | solution.py:18
  55.6 0.4 shard_map.86
  56.0 0.6 shard_map.87
  56.6 0.1 collective-permute-start.18
  56.6 0.1 collective-permute-start.16
  56.7 2.8 %collective-permute-start.17 = (bf16[4,64,128]{2,1,0:T(8,128)(2,1)S(1)}, bf16[4,64,128]{2,1,0:T(8,128)(2,1)S(1)}, u32[]{:S(2)}, u32[]{:S(2)}) collective-permute-start(bf16[4,64,128]{2,1,0:T(8,128)(2,1)S(1)} %get-tuple-element.67), channel_id=1, source_target_pairs={{1,2},{3,4},{5,6},{7,0},{2,1},{4,3},{6,5},{0,7},{9,10},{11,12},{13... | collective-permute-start | bytes 196616 | tf_op jit(solution)/shard_map/ppermute | solution.py:24
  59.5 1.6 %collective-permute-done.16.refs_3_ = bf16[4,64,128]{2,1,0:T(8,128)(2,1)S(1)} collective-permute-done((bf16[4,64,128]{2,1,0:T(8,128)(2,1)S(1)}, bf16[4,64,128]{2,1,0:T(8,128)(2,1)S(1)}, u32[]{:S(2)}, u32[]{:S(2)}) %collective-permute-start.16) | collective-permute-done | bytes 65568 | tf_op jit(solution)/shard_map/ppermute | solution.py:24
  61.1 2.7 %collective-permute-done.17.refs_4_ = bf16[4,64,128]{2,1,0:T(8,128)(2,1)S(1)} collective-permute-done((bf16[4,64,128]{2,1,0:T(8,128)(2,1)S(1)}, bf16[4,64,128]{2,1,0:T(8,128)(2,1)S(1)}, u32[]{:S(2)}, u32[]{:S(2)}) %collective-permute-start.17) | collective-permute-done | bytes 65568 | tf_op jit(solution)/shard_map/ppermute | solution.py:24
  63.8 0.1 shard_map.88
  63.9 0.2 shard_map.89
  64.1 4.8 %collective-permute-start.20 = (bf16[8,64,128]{2,1,0:T(8,128)(2,1)S(1)}, bf16[8,64,128]{2,1,0:T(8,128)(2,1)S(1)}, u32[]{:S(2)}, u32[]{:S(2)}) collective-permute-start(bf16[8,64,128]{2,1,0:T(8,128)(2,1)S(1)} %get-tuple-element.71), channel_id=1, source_target_pairs={{0,16},{8,24},{16,0},{24,8},{1,17},{9,25},{17,1},{25,9},{2,18},{10... | collective-permute-start | bytes 393224 | tf_op jit(solution)/shard_map/ppermute | solution.py:18
  69.0 1.1 %collective-permute-start.21 = (bf16[5,64,128]{2,1,0:T(8,128)(2,1)S(1)}, bf16[5,64,128]{2,1,0:T(8,128)(2,1)S(1)}, u32[]{:S(2)}, u32[]{:S(2)}) collective-permute-start(bf16[5,64,128]{2,1,0:T(8,128)(2,1)S(1)} %get-tuple-element.72), channel_id=1, source_target_pairs={{0,16},{8,24},{16,0},{24,8},{1,17},{9,25},{17,1},{25,9},{2,18},{10... | collective-permute-start | bytes 245768 | tf_op jit(solution)/shard_map/ppermute | solution.py:18
  70.1 1.0 %collective-permute-start.19 = (bf16[3,64,128]{2,1,0:T(8,128)(2,1)S(1)}, bf16[3,64,128]{2,1,0:T(8,128)(2,1)S(1)}, u32[]{:S(2)}, u32[]{:S(2)}) collective-permute-start(bf16[3,64,128]{2,1,0:T(8,128)(2,1)S(1)} %get-tuple-element.69), channel_id=1, source_target_pairs={{0,16},{8,24},{16,0},{24,8},{1,17},{9,25},{17,1},{25,9},{2,18},{10... | collective-permute-start | bytes 147464 | tf_op jit(solution)/shard_map/ppermute | solution.py:18
  71.1 2.6 %shard_map.91.refs_6_ = f32[16,64,128]{2,1,0:T(8,128)S(1)} custom-call(s32[193,128]{1,0:T(8,128)S(1)} %broadcast_in_dim.49.refs_0_.table, f32[16,64,128]{2,1,0:T(8,128)S(1)} %get-tuple-element.64.refs_1_.current, bf16[16,64,128]{2,1,0:T(8,128)(2,1)S(1)} %get-tuple-element.65.refs_2_.first, bf16[28,64,128]{2,1,0:T(8,128)(2,1)S(1)} %get-tuple-element.70.refs_3_.extension, ...), custom_call_target="tpu_custom_call" | custom-call | flops 555778048 | bytes 8684032 | tf_op jit(solution)/shard_map/pallas_call | solution.py:39
  73.7 1.2 %collective-permute-done.19.refs_0_ = bf16[3,64,128]{2,1,0:T(8,128)(2,1)S(1)} collective-permute-done((bf16[3,64,128]{2,1,0:T(8,128)(2,1)S(1)}, bf16[3,64,128]{2,1,0:T(8,128)(2,1)S(1)}, u32[]{:S(2)}, u32[]{:S(2)}) %collective-permute-start.19) | collective-permute-done | bytes 49184 | tf_op jit(solution)/shard_map/ppermute | solution.py:18
  74.9 2.5 %shard_map.92 = f32[64,2048]{1,0:T(8,128)} custom-call(s32[129,128]{1,0:T(8,128)S(1)} %broadcast_in_dim.46.table.refs_0_, bf16[3,64,128]{2,1,0:T(8,128)(2,1)S(1)} %collective-permute-done.19.refs_0_, bf16[8,64,128]{2,1,0:T(8,128)(2,1)S(1)} %collective-permute-done.20.refs_1_, bf16[5,64,128]{2,1,0:T(8,128)(2,1)S(1)} %collective-permute-done.21.refs_2_, ...), custom_call_target="tpu_custom_call" | custom-call | flops 423657472 | bytes 6619648 | tf_op jit(solution)/shard_map/pallas_call | solution.py:39
  (24 shorter events, 0.2 us)
Async XLA Ops:
  0.8 11.8 %collective-permute-start.1 = (s32[4,128]{1,0:T(4,128)S(1)}, s32[4,128]{1,0:T(4,128)S(1)}, u32[]{:S(2)}, u32[]{:S(2)}) collective-permute-start(s32[4,128]{1,0:T(4,128)S(1)} %broadcast_in_dim.52), channel_id=1, source_target_pairs={{1,2},{3,4},{5,6},{7,0},{2,1},{4,3},{6,5},{0,7},{9,10},{11,12},{13... | collective-permute-start | bytes 6152 | tf_op jit(solution)/shard_map/ppermute | solution.py:24
  6.9 12.5 %collective-permute-start = (s32[4,128]{1,0:T(4,128)S(1)}, s32[4,128]{1,0:T(4,128)S(1)}, u32[]{:S(2)}, u32[]{:S(2)}) collective-permute-start(s32[4,128]{1,0:T(4,128)S(1)} %broadcast_in_dim.51), channel_id=1, source_target_pairs={{0,8},{8,0},{16,24},{24,16},{1,9},{9,1},{17,25},{25,17},{2,10},{10... | collective-permute-start | bytes 6152 | tf_op jit(solution)/shard_map/ppermute | solution.py:18
  6.9 5.6 %collective-permute-start.2 = (s32[4,128]{1,0:T(4,128)S(1)}, s32[4,128]{1,0:T(4,128)S(1)}, u32[]{:S(2)}, u32[]{:S(2)}) collective-permute-start(s32[4,128]{1,0:T(4,128)S(1)} %broadcast_in_dim.53), channel_id=1, source_target_pairs={{0,1},{2,3},{4,5},{6,7},{1,0},{3,2},{5,4},{7,6},{8,9},{10,11},{12,... | collective-permute-start | bytes 6152 | tf_op jit(solution)/shard_map/ppermute | solution.py:24
  6.9 2.7 %copy-start.1 = (s32[1,16,12]{1,0,2:T(1,128)S(1)}, s32[1,16,12]{1,0,2:T(1,128)}, u32[]{:S(2)}) copy-start(s32[1,16,12]{1,0,2:T(1,128)} %param.9) | copy-start | bytes 2308
  6.9 2.9 %copy-start.2 = (s32[1,16,8]{1,2,0:T(8,128)S(1)}, s32[1,16,8]{1,2,0:T(8,128)}, u32[]{:S(2)}) copy-start(s32[1,16,8]{1,2,0:T(8,128)} %param.12) | copy-start | bytes 1540
  8.1 8.8 %collective-permute-start.3 = (bf16[16,64,128]{2,1,0:T(8,128)(2,1)S(1)}, bf16[16,64,128]{2,1,0:T(8,128)(2,1)S(1)}, u32[]{:S(2)}, u32[]{:S(2)}) collective-permute-start(bf16[16,64,128]{2,1,0:T(8,128)(2,1)S(1)} %get-tuple-element.42), channel_id=1, source_target_pairs={{0,16},{8,24},{16,0},{24,8},{1,17},{9,25},{17,1},{25,9},{2,18},{10... | collective-permute-start | bytes 786440 | tf_op jit(solution)/shard_map/ppermute | solution.py:18
  10.1 6.9 %copy-start = (bf16[1,16,128,128]{3,2,1,0:T(8,128)(2,1)S(1)}, bf16[1,16,128,128]{3,2,1,0:T(8,128)(2,1)}, u32[]{:S(2)}) copy-start(bf16[1,16,128,128]{3,2,1,0:T(8,128)(2,1)} %param.10) | copy-start | bytes 1572868
  10.1 16.2 %slice-start = ((s8[6291456]{0:T(1024)(128)(4,1)}), s8[4194304]{0:T(1024)(128)(4,1)S(1)}, s32[]{:S(2)}) async-start(s8[6291456]{0:T(1024)(128)(4,1)} %bitcast.12), calls=%async_computation | async-start | bytes 8388608
  17.0 9.3 %slice-start.1 = ((s8[6291456]{0:T(1024)(128)(4,1)}), s8[2097152]{0:T(1024)(128)(4,1)S(1)}, s32[]{:S(2)}) async-start(s8[6291456]{0:T(1024)(128)(4,1)} %bitcast.12), calls=%async_computation.1 | async-start | bytes 4194304
  17.4 4.3 %collective-permute-start.4 = (bf16[4,64,128]{2,1,0:T(8,128)(2,1)S(1)}, bf16[4,64,128]{2,1,0:T(8,128)(2,1)S(1)}, u32[]{:S(2)}, u32[]{:S(2)}) collective-permute-start(bf16[4,64,128]{2,1,0:T(8,128)(2,1)S(1)} %get-tuple-element.45), channel_id=1, source_target_pairs={{0,1},{2,3},{4,5},{6,7},{1,0},{3,2},{5,4},{7,6},{8,9},{10,11},{12,... | collective-permute-start | bytes 196616 | tf_op jit(solution)/shard_map/ppermute | solution.py:24
  19.2 7.0 %collective-permute-start.5 = (bf16[4,64,128]{2,1,0:T(8,128)(2,1)S(1)}, bf16[4,64,128]{2,1,0:T(8,128)(2,1)S(1)}, u32[]{:S(2)}, u32[]{:S(2)}) collective-permute-start(bf16[4,64,128]{2,1,0:T(8,128)(2,1)S(1)} %get-tuple-element.46), channel_id=1, source_target_pairs={{1,2},{3,4},{5,6},{7,0},{2,1},{4,3},{6,5},{0,7},{9,10},{11,12},{13... | collective-permute-start | bytes 196616 | tf_op jit(solution)/shard_map/ppermute | solution.py:24
  19.9 6.2 %collective-permute-start.6 = (bf16[4,64,128]{2,1,0:T(8,128)(2,1)S(1)}, bf16[4,64,128]{2,1,0:T(8,128)(2,1)S(1)}, u32[]{:S(2)}, u32[]{:S(2)}) collective-permute-start(bf16[4,64,128]{2,1,0:T(8,128)(2,1)S(1)} %get-tuple-element.47), channel_id=1, source_target_pairs={{0,8},{8,0},{16,24},{24,16},{1,9},{9,1},{17,25},{25,17},{2,10},{10... | collective-permute-start | bytes 196616 | tf_op jit(solution)/shard_map/ppermute | solution.py:18
  26.4 9.7 %collective-permute-start.8 = (bf16[8,64,128]{2,1,0:T(8,128)(2,1)S(1)}, bf16[8,64,128]{2,1,0:T(8,128)(2,1)S(1)}, u32[]{:S(2)}, u32[]{:S(2)}) collective-permute-start(bf16[8,64,128]{2,1,0:T(8,128)(2,1)S(1)} %shard_map.78), channel_id=1, source_target_pairs={{0,16},{8,24},{16,0},{24,8},{1,17},{9,25},{17,1},{25,9},{2,18},{10... | collective-permute-start | bytes 393224 | tf_op jit(solution)/shard_map/ppermute | solution.py:18
  30.9 5.2 %collective-permute-start.9 = (bf16[5,64,128]{2,1,0:T(8,128)(2,1)S(1)}, bf16[5,64,128]{2,1,0:T(8,128)(2,1)S(1)}, u32[]{:S(2)}, u32[]{:S(2)}) collective-permute-start(bf16[5,64,128]{2,1,0:T(8,128)(2,1)S(1)} %shard_map.79), channel_id=1, source_target_pairs={{0,16},{8,24},{16,0},{24,8},{1,17},{9,25},{17,1},{25,9},{2,18},{10... | collective-permute-start | bytes 245768 | tf_op jit(solution)/shard_map/ppermute | solution.py:18
  32.0 4.1 %collective-permute-start.7 = (bf16[3,64,128]{2,1,0:T(8,128)(2,1)S(1)}, bf16[3,64,128]{2,1,0:T(8,128)(2,1)S(1)}, u32[]{:S(2)}, u32[]{:S(2)}) collective-permute-start(bf16[3,64,128]{2,1,0:T(8,128)(2,1)S(1)} %get-tuple-element.48), channel_id=1, source_target_pairs={{0,16},{8,24},{16,0},{24,8},{1,17},{9,25},{17,1},{25,9},{2,18},{10... | collective-permute-start | bytes 147464 | tf_op jit(solution)/shard_map/ppermute | solution.py:18
  38.7 2.9 %collective-permute-start.12 = (bf16[4,64,128]{2,1,0:T(8,128)(2,1)S(1)}, bf16[4,64,128]{2,1,0:T(8,128)(2,1)S(1)}, u32[]{:S(2)}, u32[]{:S(2)}) collective-permute-start(bf16[4,64,128]{2,1,0:T(8,128)(2,1)S(1)} %get-tuple-element.54), channel_id=1, source_target_pairs={{0,8},{8,0},{16,24},{24,16},{1,9},{9,1},{17,25},{25,17},{2,10},{10... | collective-permute-start | bytes 196616 | tf_op jit(solution)/shard_map/ppermute | solution.py:18
  38.8 4.5 %collective-permute-start.10 = (bf16[4,64,128]{2,1,0:T(8,128)(2,1)S(1)}, bf16[4,64,128]{2,1,0:T(8,128)(2,1)S(1)}, u32[]{:S(2)}, u32[]{:S(2)}) collective-permute-start(bf16[4,64,128]{2,1,0:T(8,128)(2,1)S(1)} %get-tuple-element.52), channel_id=1, source_target_pairs={{0,1},{2,3},{4,5},{6,7},{1,0},{3,2},{5,4},{7,6},{8,9},{10,11},{12,... | collective-permute-start | bytes 196616 | tf_op jit(solution)/shard_map/ppermute | solution.py:24
  38.9 7.1 %collective-permute-start.11 = (bf16[4,64,128]{2,1,0:T(8,128)(2,1)S(1)}, bf16[4,64,128]{2,1,0:T(8,128)(2,1)S(1)}, u32[]{:S(2)}, u32[]{:S(2)}) collective-permute-start(bf16[4,64,128]{2,1,0:T(8,128)(2,1)S(1)} %get-tuple-element.53), channel_id=1, source_target_pairs={{1,2},{3,4},{5,6},{7,0},{2,1},{4,3},{6,5},{0,7},{9,10},{11,12},{13... | collective-permute-start | bytes 196616 | tf_op jit(solution)/shard_map/ppermute | solution.py:24
  47.8 7.8 %collective-permute-start.14 = (bf16[8,64,128]{2,1,0:T(8,128)(2,1)S(1)}, bf16[8,64,128]{2,1,0:T(8,128)(2,1)S(1)}, u32[]{:S(2)}, u32[]{:S(2)}) collective-permute-start(bf16[8,64,128]{2,1,0:T(8,128)(2,1)S(1)} %get-tuple-element.60), channel_id=1, source_target_pairs={{0,16},{8,24},{16,0},{24,8},{1,17},{9,25},{17,1},{25,9},{2,18},{10... | collective-permute-start | bytes 393224 | tf_op jit(solution)/shard_map/ppermute | solution.py:18
  48.7 6.9 %collective-permute-start.15 = (bf16[5,64,128]{2,1,0:T(8,128)(2,1)S(1)}, bf16[5,64,128]{2,1,0:T(8,128)(2,1)S(1)}, u32[]{:S(2)}, u32[]{:S(2)}) collective-permute-start(bf16[5,64,128]{2,1,0:T(8,128)(2,1)S(1)} %get-tuple-element.61), channel_id=1, source_target_pairs={{0,16},{8,24},{16,0},{24,8},{1,17},{9,25},{17,1},{25,9},{2,18},{10... | collective-permute-start | bytes 245768 | tf_op jit(solution)/shard_map/ppermute | solution.py:18
  50.0 5.6 %collective-permute-start.13 = (bf16[3,64,128]{2,1,0:T(8,128)(2,1)S(1)}, bf16[3,64,128]{2,1,0:T(8,128)(2,1)S(1)}, u32[]{:S(2)}, u32[]{:S(2)}) collective-permute-start(bf16[3,64,128]{2,1,0:T(8,128)(2,1)S(1)} %get-tuple-element.59), channel_id=1, source_target_pairs={{0,16},{8,24},{16,0},{24,8},{1,17},{9,25},{17,1},{25,9},{2,18},{10... | collective-permute-start | bytes 147464 | tf_op jit(solution)/shard_map/ppermute | solution.py:18
  56.6 2.9 %collective-permute-start.18 = (bf16[4,64,128]{2,1,0:T(8,128)(2,1)S(1)}, bf16[4,64,128]{2,1,0:T(8,128)(2,1)S(1)}, u32[]{:S(2)}, u32[]{:S(2)}) collective-permute-start(bf16[4,64,128]{2,1,0:T(8,128)(2,1)S(1)} %get-tuple-element.68), channel_id=1, source_target_pairs={{0,8},{8,0},{16,24},{24,16},{1,9},{9,1},{17,25},{25,17},{2,10},{10... | collective-permute-start | bytes 196616 | tf_op jit(solution)/shard_map/ppermute | solution.py:18
  56.6 4.5 %collective-permute-start.16 = (bf16[4,64,128]{2,1,0:T(8,128)(2,1)S(1)}, bf16[4,64,128]{2,1,0:T(8,128)(2,1)S(1)}, u32[]{:S(2)}, u32[]{:S(2)}) collective-permute-start(bf16[4,64,128]{2,1,0:T(8,128)(2,1)S(1)} %get-tuple-element.66), channel_id=1, source_target_pairs={{0,1},{2,3},{4,5},{6,7},{1,0},{3,2},{5,4},{7,6},{8,9},{10,11},{12,... | collective-permute-start | bytes 196616 | tf_op jit(solution)/shard_map/ppermute | solution.py:24
  56.7 7.1 %collective-permute-start.17 = (bf16[4,64,128]{2,1,0:T(8,128)(2,1)S(1)}, bf16[4,64,128]{2,1,0:T(8,128)(2,1)S(1)}, u32[]{:S(2)}, u32[]{:S(2)}) collective-permute-start(bf16[4,64,128]{2,1,0:T(8,128)(2,1)S(1)} %get-tuple-element.67), channel_id=1, source_target_pairs={{1,2},{3,4},{5,6},{7,0},{2,1},{4,3},{6,5},{0,7},{9,10},{11,12},{13... | collective-permute-start | bytes 196616 | tf_op jit(solution)/shard_map/ppermute | solution.py:24
  64.1 10.8 %collective-permute-start.20 = (bf16[8,64,128]{2,1,0:T(8,128)(2,1)S(1)}, bf16[8,64,128]{2,1,0:T(8,128)(2,1)S(1)}, u32[]{:S(2)}, u32[]{:S(2)}) collective-permute-start(bf16[8,64,128]{2,1,0:T(8,128)(2,1)S(1)} %get-tuple-element.71), channel_id=1, source_target_pairs={{0,16},{8,24},{16,0},{24,8},{1,17},{9,25},{17,1},{25,9},{2,18},{10... | collective-permute-start | bytes 393224 | tf_op jit(solution)/shard_map/ppermute | solution.py:18
  69.0 5.9 %collective-permute-start.21 = (bf16[5,64,128]{2,1,0:T(8,128)(2,1)S(1)}, bf16[5,64,128]{2,1,0:T(8,128)(2,1)S(1)}, u32[]{:S(2)}, u32[]{:S(2)}) collective-permute-start(bf16[5,64,128]{2,1,0:T(8,128)(2,1)S(1)} %get-tuple-element.72), channel_id=1, source_target_pairs={{0,16},{8,24},{16,0},{24,8},{1,17},{9,25},{17,1},{25,9},{2,18},{10... | collective-permute-start | bytes 245768 | tf_op jit(solution)/shard_map/ppermute | solution.py:18
  70.1 4.8 %collective-permute-start.19 = (bf16[3,64,128]{2,1,0:T(8,128)(2,1)S(1)}, bf16[3,64,128]{2,1,0:T(8,128)(2,1)S(1)}, u32[]{:S(2)}, u32[]{:S(2)}) collective-permute-start(bf16[3,64,128]{2,1,0:T(8,128)(2,1)S(1)} %get-tuple-element.69), channel_id=1, source_target_pairs={{0,16},{8,24},{16,0},{24,8},{1,17},{9,25},{17,1},{25,9},{2,18},{10... | collective-permute-start | bytes 147464 | tf_op jit(solution)/shard_map/ppermute | solution.py:18

commit v9 on v8

--- a/solution.py
+++ b/solution.py
@@ -8,7 +8,7 @@
 ITERS = 2
 LIMIT = 16 << 20
 LANES = 128
-SHARES = (0, 3, 11, 16)
+SHARES = (0, 6, 16)
 VMEM = pl.BlockSpec(memory_space=pltpu.VMEM)
 HBM = pl.BlockSpec(memory_space=pltpu.HBM)
 NT = (((1,), (1,)), ((), ()))
@@ -74,8 +74,9 @@
         at += part.shape[0]
 
 
-def open_body(loads, panels, sent, arrivals):
+def open_body(loads, panels, early, late, arrivals):
     rows, _, width = panels.shape
+    half = early.shape[0]
     copies = [
         pltpu.make_async_copy(
             loads.at[:, pl.ds(i * width, width)], panels.at[i], arrivals.at[i]
@@ -86,7 +87,8 @@
         copy.start()
     for i, copy in enumerate(copies):
         copy.wait()
-        sent[i] = panels[i].astype(jnp.bfloat16)
+        sent, at = (early, i) if i < half else (late, i - half)
+        sent[at] = panels[i].astype(jnp.bfloat16)
 
 
 def fetch_body(_, source, target, arrivals):
@@ -106,25 +108,24 @@
 
 def first_listed_body(lists, pieces, table, loads, *refs):
     wanted, refs = refs[:lists], refs[lists:]
-    residual, arrived, refs = refs[:pieces], refs[pieces : 2 * pieces], refs[2 * pieces :]
+    many, arrivals = pieces
+    residual, arrived, refs = refs[:many], refs[many : many + arrivals], refs[many + arrivals :]
     transfer, smoother, *refs, scratch = refs
-    outs = refs[:lists]
+    outs, refs = refs[:lists], refs[lists:]
     places = chosen(wanted, outs)
-    if pieces > 1:
-        joined_residual, joined_arrived = refs[lists:]
-    else:
-        (joined_residual,), (joined_arrived,) = residual, arrived
-
-    @pl.when(is_fine(table))
-    def _():
-        if pieces > 1:
+    joined_residual = refs.pop(0) if many > 1 else residual[0]
+    joined_arrived = refs.pop(0) if arrivals > 1 else arrived[0]
+
+    @pl.when(is_fine(table))
+    def _():
+        if many > 1:
             joined(residual, joined_residual)
         for at, (row, _, _) in enumerate(places):
             scratch[at] = joined_residual[row].astype(jnp.bfloat16)
 
     @pl.when(jnp.logical_not(is_fine(table)))
     def _():
-        if pieces > 1:
+        if arrivals > 1:
             joined(arrived, joined_arrived)
         for at, (row, _, _) in enumerate(places):
             value = loads[row] + gathered(joined_arrived, table, row, transfer)
@@ -199,7 +200,8 @@
     return value + gathered(arrived, table, row, transfer)
 
 
-def update_listed_body(lists, pieces, table, *refs):
+def update_listed_body(lists, counts, table, *refs):
+    (pieces,) = counts
     wanted, arrived, refs = refs[:lists], refs[lists : lists + pieces], refs[lists + pieces :]
     more = lists + (pieces > 1)
     correction, *terms, transfer = refs[:-more]
@@ -296,17 +298,21 @@
     extended = panels(block_rows + 3 * list_width, jnp.bfloat16)
     rowwise = pltpu.SemaphoreType.DMA((block_rows,))
 
-    load_panels, sent = call(
-        open_body, (wide, narrow), inside(loads), in_specs=[HBM], scratch=[rowwise],
+    half = panels(block_rows // 2, jnp.bfloat16)
+    load_panels, *sent = call(
+        open_body, (wide, half, half), inside(loads), in_specs=[HBM], scratch=[rowwise],
         cost=pl.CostEstimate(flops=5_000_000_000, bytes_accessed=2 * loads.size * 4, transcendentals=0),
     )
-    arrived = [partner(sent, "level", 1)]
+    arrived = []
+    for piece in sent:
+        arrived.append(partner(piece, "level", 1))
 
     def spread(values):
         return jnp.broadcast_to(values[:, None], (values.shape[0], LANES))
 
     def swap_both(odd, even):
         odd = swapped(odd, "dom", 1)
+        even = even()
         even = swapped(even, "dom", 0)
         return even, odd
 
@@ -315,7 +321,7 @@
 
     even = lax.axis_index("dom") % 2 == 0
     wanted_even, wanted_odd = swap_both(
-        spread(jnp.where(even, left_list, right_list)), spread(jnp.where(even, right_list, left_list))
+        spread(jnp.where(even, left_list, right_list)), lambda: spread(jnp.where(even, right_list, left_list))
     )
     wanted_beside = swap_beside(spread(sibling_list))
     columns = level_cols.reshape(-1)
@@ -331,16 +337,20 @@
     def fetched(source):
         return call(fetch_body, like(source), inside(loads), inside(source), in_specs=[HBM, HBM], scratch=[rowwise])
 
-    def exchanged(bodies, fixed, pieces, rest, joins, scratch):
+    def exchanged(bodies, fixed, pieces, rest, kinds, scratch):
         listed_body, body = bodies
-        each = len(pieces[0])
-        odd, even, *whole = call(
-            lambda *refs: listed_body(2, each, *refs), (listed,) * 2 + joins,
-            *fixed, wanted_odd, wanted_even, *sum(pieces, []), *rest,
-            scratch=[held(2 * list_width)] * scratch,
-        )
-        even, odd = swap_both(odd, even)
-        whole = whole or sum(pieces, [])
+
+        def listed_rows(wanted, pieces):
+            counts = [len(x) for x in pieces]
+            joins = tuple(kind for kind, count in zip(kinds, counts) if count > 1)
+            out, *more = call(
+                lambda *refs: listed_body(1, counts, *refs), (listed,) + joins,
+                *fixed, wanted, *sum(pieces, []), *rest, scratch=[held(list_width)] * scratch,
+            )
+            return out, [more.pop(0) if count > 1 else x[0] for x, count in zip(pieces, counts)]
+
+        odd, whole = listed_rows(wanted_odd, pieces)
+        even, odd = swap_both(odd, lambda: listed_rows(wanted_even, [[x] for x in whole])[0])
         *results, beside = call(body, (wide, narrow, listed), *fixed, wanted_beside, *whole, *rest)
         return (*results, (even, odd, swap_beside(beside)))
 
@@ -370,7 +380,7 @@
         args, rest = (transfer_table, load_panels), (transfer, smooth)
         current, first, sides = exchanged(
             (first_listed_body, first_body), args, [residual, arrived], rest,
-            (wide, narrow) if len(arrived) > 1 else (), True,
+            (wide, narrow), True,
         )
         args = (level_table, current, first)
         ends = cycle_index + 1 == ITERS

time: 77.8 us -> 80.7 us (1.037)
  waiting for transfers between devices: 25.6 us -> 29.1 us
    ppermute x14 -> x12, waiting for transfers between devices: 10.9 us -> 15.2 us  [partner(): lax.ppermute(x, axis, [(i, i ^ 1 << apart) for i in range(lax.axis_size(a...]
    ppermute x14 -> x12, starting transfers between devices: 17.4 us -> 15.5 us  [partner(): lax.ppermute(x, axis, [(i, i ^ 1 << apart) for i in range(lax.axis_size(a...]
    ppermute x8, starting transfers between devices: 13.7 us -> 14.8 us  [swapped(): return lax.ppermute(x, axis, pairs + [(b, a) for a, b in pairs])]
  transfers between devices with their start and end apart: 22 -> 20, of which waited for: 10 -> 11; matrix products, arithmetic and copies ran while one was open for 1% -> 1% of each run, Pallas kernels for 14% -> 13%
where the time goes in v9:
time: 80.7 us; the launch traced here: 80.5 us
  starting transfers between devices  30.3 us (38%)
  waiting for transfers between devices  29.1 us (36%)
  Pallas kernels  19.1 us (24%)
    pallas_call x20, Pallas kernels, call(): pl.pallas_call(body, out_shape=outs, in_specs=in_specs or [VMEM] * len(ar...  19.1 us
    ppermute x12, starting transfers between devices, partner(): lax.ppermute(x, axis, [(i, i ^ 1 << apart) for i in range(lax.axis_size(a...  15.5 us
    ppermute x12, waiting for transfers between devices, partner(): lax.ppermute(x, axis, [(i, i ^ 1 << apart) for i in range(lax.axis_size(a...  15.2 us
    ppermute x8, starting transfers between devices, swapped(): return lax.ppermute(x, axis, pairs + [(b, a) for a, b in pairs])  14.8 us
    ppermute x8, waiting for transfers between devices, swapped(): return lax.ppermute(x, axis, pairs + [(b, a) for a, b in pairs])  13.9 us
  transfers between devices with their start and end apart: 20, of which 11 were waited for; matrix products, arithmetic and copies ran while one was open for 1% of the time, Pallas kernels for 13%

profile of v9, /device:TPU:0, one launch (start us, length us, event | category | flops | bytes accessed | tf_op | source)
XLA Modules:
  0.0 80.5 jit_solution(1153013932741126093)
XLA Ops:
  0.0 0.7 fusion.4
  0.7 0.1 broadcast_in_dim.52
  0.8 6.0 %collective-permute-start.1 = (s32[4,128]{1,0:T(4,128)S(1)}, s32[4,128]{1,0:T(4,128)S(1)}, u32[]{:S(2)}, u32[]{:S(2)}) collective-permute-start(s32[4,128]{1,0:T(4,128)S(1)} %broadcast_in_dim.52), channel_id=1, source_target_pairs={{1,2},{3,4},{5,6},{7,0},{2,1},{4,3},{6,5},{0,7},{9,10},{11,12},{13... | collective-permute-start | bytes 6152 | tf_op jit(solution)/shard_map/ppermute | solution.py:24
  6.8 0.1 broadcast_in_dim.51
  6.9 0.0 collective-permute-start
  6.9 0.1 broadcast_in_dim.53
  6.9 1.2 %shard_map.73 = (f32[16,64,128]{2,1,0:T(8,128)S(1)}, bf16[8,64,128]{2,1,0:T(8,128)(2,1)S(1)}, bf16[8,64,128]{2,1,0:T(8,128)(2,1)S(1)}) custom-call(f32[64,2048]{1,0:T(8,128)} %bitcast.35), custom_call_target="tpu_custom_call" | custom-call | flops 5000000000 | bytes 1048576 | tf_op jit(solution)/shard_map/pallas_call | solution.py:39
  8.1 1.6 %collective-permute-start.2 = (bf16[8,64,128]{2,1,0:T(8,128)(2,1)S(1)}, bf16[8,64,128]{2,1,0:T(8,128)(2,1)S(1)}, u32[]{:S(2)}, u32[]{:S(2)}) collective-permute-start(bf16[8,64,128]{2,1,0:T(8,128)(2,1)S(1)} %get-tuple-element.37), channel_id=1, source_target_pairs={{0,16},{8,24},{16,0},{24,8},{1,17},{9,25},{17,1},{25,9},{2,18},{10... | collective-permute-start | bytes 393224 | tf_op jit(solution)/shard_map/ppermute | solution.py:18
  9.7 0.5 collective-permute-start.3
  10.2 0.1 copy.10
  10.3 0.1 reshape.46
  10.4 0.1 copy.9
  10.5 0.1 reshape.43
  10.6 0.0 copy-start
  10.6 2.3 %shard_map.74.refs_6_.transfer.refs_5_.refs_0_.refs_4_.refs_7_ = bf16[16,8,128,128]{3,2,1,0:T(8,128)(2,1)S(1)} custom-call(f32[64,2048]{1,0:T(8,128)} %bitcast.36, bf16[16,8,128,128]{3,2,1,0:T(8,128)(2,1)} %bitcast.34), custom_call_target="tpu_custom_call" | custom-call | flops 570425344 | bytes 8912896 | tf_op jit(solution)/shard_map/pallas_call | solution.py:39
  13.0 1.6 %collective-permute-done.2.refs_4_ = bf16[8,64,128]{2,1,0:T(8,128)(2,1)S(1)} collective-permute-done((bf16[8,64,128]{2,1,0:T(8,128)(2,1)S(1)}, bf16[8,64,128]{2,1,0:T(8,128)(2,1)S(1)}, u32[]{:S(2)}, u32[]{:S(2)}) %collective-permute-start.2) | collective-permute-done | bytes 131104 | tf_op jit(solution)/shard_map/ppermute | solution.py:18
  14.6 2.3 %collective-permute-done.3.refs_5_ = bf16[8,64,128]{2,1,0:T(8,128)(2,1)S(1)} collective-permute-done((bf16[8,64,128]{2,1,0:T(8,128)(2,1)S(1)}, bf16[8,64,128]{2,1,0:T(8,128)(2,1)S(1)}, u32[]{:S(2)}, u32[]{:S(2)}) %collective-permute-start.3) | collective-permute-done | bytes 131104 | tf_op jit(solution)/shard_map/ppermute | solution.py:18
  16.9 0.1 broadcast_in_dim.46.refs_0_.table
  17.0 0.0 copy-done
  17.0 0.0 slice-start
  17.0 0.3 shard_map.75
  17.3 0.0 collective-permute-done.4.refs_2_.refs_1_
  17.3 0.0 slice-start.1
  17.3 0.3 shard_map.77
  17.6 1.8 %collective-permute-start.5 = (bf16[4,64,128]{2,1,0:T(8,128)(2,1)S(1)}, bf16[4,64,128]{2,1,0:T(8,128)(2,1)S(1)}, u32[]{:S(2)}, u32[]{:S(2)}) collective-permute-start(bf16[4,64,128]{2,1,0:T(8,128)(2,1)S(1)} %shard_map.77), channel_id=1, source_target_pairs={{0,1},{2,3},{4,5},{6,7},{1,0},{3,2},{5,4},{7,6},{8,9},{10,11},{12,... | collective-permute-start | bytes 196616 | tf_op jit(solution)/shard_map/ppermute | solution.py:24
  19.4 0.2 collective-permute-start.6
  19.6 0.6 shard_map.76
  20.1 0.1 collective-permute-start.7
  20.2 0.1 pad_add_fusion.1
  20.3 1.6 %collective-permute-done.5.refs_3_ = bf16[4,64,128]{2,1,0:T(8,128)(2,1)S(1)} collective-permute-done((bf16[4,64,128]{2,1,0:T(8,128)(2,1)S(1)}, bf16[4,64,128]{2,1,0:T(8,128)(2,1)S(1)}, u32[]{:S(2)}, u32[]{:S(2)}) %collective-permute-start.5) | collective-permute-done | bytes 65568 | tf_op jit(solution)/shard_map/ppermute | solution.py:24
  21.9 4.4 %collective-permute-done.6.refs_4_ = bf16[4,64,128]{2,1,0:T(8,128)(2,1)S(1)} collective-permute-done((bf16[4,64,128]{2,1,0:T(8,128)(2,1)S(1)}, bf16[4,64,128]{2,1,0:T(8,128)(2,1)S(1)}, u32[]{:S(2)}, u32[]{:S(2)}) %collective-permute-start.6) | collective-permute-done | bytes 65568 | tf_op jit(solution)/shard_map/ppermute | solution.py:24
  26.4 0.1 broadcast_in_dim.49.refs_0_.table
  26.5 0.1 shard_map.78
  26.6 5.3 %collective-permute-start.9 = (bf16[10,64,128]{2,1,0:T(8,128)(2,1)S(1)}, bf16[10,64,128]{2,1,0:T(8,128)(2,1)S(1)}, u32[]{:S(2)}, u32[]{:S(2)}) collective-permute-start(bf16[10,64,128]{2,1,0:T(8,128)(2,1)S(1)} %shard_map.79), channel_id=1, source_target_pairs={{0,16},{8,24},{16,0},{24,8},{1,17},{9,25},{17,1},{25,9},{2,18},{10... | collective-permute-start | bytes 491528 | tf_op jit(solution)/shard_map/ppermute | solution.py:18
  31.9 0.1 collective-permute-start.8
  32.0 2.6 %shard_map.80.refs_4_.correction.refs_3_ = f32[16,64,128]{2,1,0:T(8,128)S(1)} custom-call(s32[193,128]{1,0:T(8,128)S(1)} %broadcast_in_dim.49.refs_0_.table, f32[16,64,128]{2,1,0:T(8,128)S(1)} %get-tuple-element.40.refs_1_.current, bf16[16,64,128]{2,1,0:T(8,128)(2,1)S(1)} %get-tuple-element.41.refs_2_.first, ...), custom_call_target="tpu_custom_call" | custom-call | flops 555778048 | bytes 8684032 | tf_op jit(solution)/shard_map/pallas_call | solution.py:39
  34.5 2.0 %collective-permute-done.8.refs_2_ = bf16[6,64,128]{2,1,0:T(8,128)(2,1)S(1)} collective-permute-done((bf16[6,64,128]{2,1,0:T(8,128)(2,1)S(1)}, bf16[6,64,128]{2,1,0:T(8,128)(2,1)S(1)}, u32[]{:S(2)}, u32[]{:S(2)}) %collective-permute-start.8) | collective-permute-done | bytes 98336 | tf_op jit(solution)/shard_map/ppermute | solution.py:18
  36.5 0.6 shard_map.81
  37.1 1.7 %shard_map.82 = (f32[16,64,128]{2,1,0:T(8,128)S(1)}, bf16[16,64,128]{2,1,0:T(8,128)(2,1)S(1)}, bf16[4,64,128]{2,1,0:T(8,128)(2,1)S(1)}) custom-call(s32[129,128]{1,0:T(8,128)S(1)} %broadcast_in_dim.46.refs_0_.table, s32[4,128]{1,0:T(4,128)S(1)} %collective-permute-done.wanted, bf16[16,64,128]{2,1,0:T(8,128)(2,1)S(1)} %get-tuple-element.46.arrived.refs_2_, ...), custom_call_target="tpu_custom_call" | custom-call | flops 377651200 | bytes 5900800 | tf_op jit(solution)/shard_map/pallas_call | solution.py:39
  38.8 0.1 collective-permute-start.12
  38.8 0.6 shard_map.83
  39.4 0.1 collective-permute-start.10
  39.5 3.3 %collective-permute-start.11 = (bf16[4,64,128]{2,1,0:T(8,128)(2,1)S(1)}, bf16[4,64,128]{2,1,0:T(8,128)(2,1)S(1)}, u32[]{:S(2)}, u32[]{:S(2)}) collective-permute-start(bf16[4,64,128]{2,1,0:T(8,128)(2,1)S(1)} %get-tuple-element.48), channel_id=1, source_target_pairs={{1,2},{3,4},{5,6},{7,0},{2,1},{4,3},{6,5},{0,7},{9,10},{11,12},{13... | collective-permute-start | bytes 196616 | tf_op jit(solution)/shard_map/ppermute | solution.py:24
  42.8 1.1 %collective-permute-done.10.refs_3_ = bf16[4,64,128]{2,1,0:T(8,128)(2,1)S(1)} collective-permute-done((bf16[4,64,128]{2,1,0:T(8,128)(2,1)S(1)}, bf16[4,64,128]{2,1,0:T(8,128)(2,1)S(1)}, u32[]{:S(2)}, u32[]{:S(2)}) %collective-permute-start.10) | collective-permute-done | bytes 65568 | tf_op jit(solution)/shard_map/ppermute | solution.py:24
  44.0 2.8 %collective-permute-done.11.refs_4_ = bf16[4,64,128]{2,1,0:T(8,128)(2,1)S(1)} collective-permute-done((bf16[4,64,128]{2,1,0:T(8,128)(2,1)S(1)}, bf16[4,64,128]{2,1,0:T(8,128)(2,1)S(1)}, u32[]{:S(2)}, u32[]{:S(2)}) %collective-permute-start.11) | collective-permute-done | bytes 65568 | tf_op jit(solution)/shard_map/ppermute | solution.py:24
  46.7 1.0 %shard_map.84 = (bf16[6,64,128]{2,1,0:T(8,128)(2,1)S(1)}, bf16[28,64,128]{2,1,0:T(8,128)(2,1)S(1)}, f32[6,64,128]{2,1,0:T(8,128)S(1)}) custom-call(s32[193,128]{1,0:T(8,128)S(1)} %broadcast_in_dim.49.refs_0_.table, f32[16,64,128]{2,1,0:T(8,128)S(1)} %get-tuple-element.36.refs_1_.refs_3_.loads.residual, bf16[16,64,128]{2,1,0:T(8,128)(2,1)S(1)} %get-tuple-element.47.refs_2_, ...), custom_call_target="tpu_custom_call" | custom-call | flops 520126464 | bytes 8126976 | tf_op jit(solution)/shard_map/pallas_call | solution.py:39
  47.7 1.5 %shard_map.85 = (bf16[10,64,128]{2,1,0:T(8,128)(2,1)S(1)}, f32[10,64,128]{2,1,0:T(8,128)S(1)}) custom-call(s32[193,128]{1,0:T(8,128)S(1)} %broadcast_in_dim.49.refs_0_.table, f32[16,64,128]{2,1,0:T(8,128)S(1)} %get-tuple-element.36.refs_1_.refs_3_.loads.residual, bf16[28,64,128]{2,1,0:T(8,128)(2,1)S(1)} %get-tuple-element.51.refs_2_, ...), custom_call_target="tpu_custom_call" | custom-call | flops 503349248 | bytes 7864832 | tf_op jit(solution)/shard_map/pallas_call | solution.py:39
  49.3 0.1 collective-permute-start.14
  49.3 2.0 %collective-permute-start.13 = (bf16[6,64,128]{2,1,0:T(8,128)(2,1)S(1)}, bf16[6,64,128]{2,1,0:T(8,128)(2,1)S(1)}, u32[]{:S(2)}, u32[]{:S(2)}) collective-permute-start(bf16[6,64,128]{2,1,0:T(8,128)(2,1)S(1)} %get-tuple-element.53), channel_id=1, source_target_pairs={{0,16},{8,24},{16,0},{24,8},{1,17},{9,25},{17,1},{25,9},{2,18},{10... | collective-permute-start | bytes 294920 | tf_op jit(solution)/shard_map/ppermute | solution.py:18
  51.4 5.8 %collective-permute-done.13.refs_5_ = bf16[6,64,128]{2,1,0:T(8,128)(2,1)S(1)} collective-permute-done((bf16[6,64,128]{2,1,0:T(8,128)(2,1)S(1)}, bf16[6,64,128]{2,1,0:T(8,128)(2,1)S(1)}, u32[]{:S(2)}, u32[]{:S(2)}) %collective-permute-start.13) | collective-permute-done | bytes 98336 | tf_op jit(solution)/shard_map/ppermute | solution.py:18
  57.2 0.3 shard_map.86
  57.5 0.6 shard_map.87
  58.1 0.1 collective-permute-start.17
  58.2 0.3 shard_map.88
  58.4 0.1 collective-permute-start.15
  58.5 3.3 %collective-permute-start.16 = (bf16[4,64,128]{2,1,0:T(8,128)(2,1)S(1)}, bf16[4,64,128]{2,1,0:T(8,128)(2,1)S(1)}, u32[]{:S(2)}, u32[]{:S(2)}) collective-permute-start(bf16[4,64,128]{2,1,0:T(8,128)(2,1)S(1)} %get-tuple-element.59), channel_id=1, source_target_pairs={{1,2},{3,4},{5,6},{7,0},{2,1},{4,3},{6,5},{0,7},{9,10},{11,12},{13... | collective-permute-start | bytes 196616 | tf_op jit(solution)/shard_map/ppermute | solution.py:24
  61.8 1.2 %collective-permute-done.15.refs_3_ = bf16[4,64,128]{2,1,0:T(8,128)(2,1)S(1)} collective-permute-done((bf16[4,64,128]{2,1,0:T(8,128)(2,1)S(1)}, bf16[4,64,128]{2,1,0:T(8,128)(2,1)S(1)}, u32[]{:S(2)}, u32[]{:S(2)}) %collective-permute-start.15) | collective-permute-done | bytes 65568 | tf_op jit(solution)/shard_map/ppermute | solution.py:24
  63.0 2.8 %collective-permute-done.16.refs_4_ = bf16[4,64,128]{2,1,0:T(8,128)(2,1)S(1)} collective-permute-done((bf16[4,64,128]{2,1,0:T(8,128)(2,1)S(1)}, bf16[4,64,128]{2,1,0:T(8,128)(2,1)S(1)}, u32[]{:S(2)}, u32[]{:S(2)}) %collective-permute-start.16) | collective-permute-done | bytes 65568 | tf_op jit(solution)/shard_map/ppermute | solution.py:24
  65.8 0.2 shard_map.89
  66.1 5.7 %collective-permute-start.19 = (bf16[10,64,128]{2,1,0:T(8,128)(2,1)S(1)}, bf16[10,64,128]{2,1,0:T(8,128)(2,1)S(1)}, u32[]{:S(2)}, u32[]{:S(2)}) collective-permute-start(bf16[10,64,128]{2,1,0:T(8,128)(2,1)S(1)} %get-tuple-element.63), channel_id=1, source_target_pairs={{0,16},{8,24},{16,0},{24,8},{1,17},{9,25},{17,1},{25,9},{2,18},{10... | collective-permute-start | bytes 491528 | tf_op jit(solution)/shard_map/ppermute | solution.py:18
  71.8 0.1 collective-permute-start.18
  71.9 2.6 %shard_map.91.refs_4_ = f32[16,64,128]{2,1,0:T(8,128)S(1)} custom-call(s32[193,128]{1,0:T(8,128)S(1)} %broadcast_in_dim.49.refs_0_.table, f32[16,64,128]{2,1,0:T(8,128)S(1)} %get-tuple-element.57.refs_1_.current, bf16[16,64,128]{2,1,0:T(8,128)(2,1)S(1)} %get-tuple-element.58.refs_2_.first, bf16[28,64,128]{2,1,0:T(8,128)(2,1)S(1)} %get-tuple-element.62.refs_3_.extension, ...), custom_call_target="tpu_custom_call" | custom-call | flops 555778048 | bytes 8684032 | tf_op jit(solution)/shard_map/pallas_call | solution.py:39
  74.4 3.4 %collective-permute-done.18.refs_0_ = bf16[6,64,128]{2,1,0:T(8,128)(2,1)S(1)} collective-permute-done((bf16[6,64,128]{2,1,0:T(8,128)(2,1)S(1)}, bf16[6,64,128]{2,1,0:T(8,128)(2,1)S(1)}, u32[]{:S(2)}, u32[]{:S(2)}) %collective-permute-start.18) | collective-permute-done | bytes 98336 | tf_op jit(solution)/shard_map/ppermute | solution.py:18
  77.9 2.5 %shard_map.92 = f32[64,2048]{1,0:T(8,128)} custom-call(s32[129,128]{1,0:T(8,128)S(1)} %broadcast_in_dim.46.refs_0_.table, bf16[6,64,128]{2,1,0:T(8,128)(2,1)S(1)} %collective-permute-done.18.refs_0_, bf16[10,64,128]{2,1,0:T(8,128)(2,1)S(1)} %collective-permute-done.19.refs_1_, f32[6,64,128]{2,1,0:T(8,128)S(1)} %get-tuple-element.64.refs_2_, ...), custom_call_target="tpu_custom_call" | custom-call | flops 423657472 | bytes 6619648 | tf_op jit(solution)/shard_map/pallas_call | solution.py:39
  (20 shorter events, 0.1 us)
Async XLA Ops:
  0.8 12.2 %collective-permute-start.1 = (s32[4,128]{1,0:T(4,128)S(1)}, s32[4,128]{1,0:T(4,128)S(1)}, u32[]{:S(2)}, u32[]{:S(2)}) collective-permute-start(s32[4,128]{1,0:T(4,128)S(1)} %broadcast_in_dim.52), channel_id=1, source_target_pairs={{1,2},{3,4},{5,6},{7,0},{2,1},{4,3},{6,5},{0,7},{9,10},{11,12},{13... | collective-permute-start | bytes 6152 | tf_op jit(solution)/shard_map/ppermute | solution.py:24
  6.9 12.7 %collective-permute-start = (s32[4,128]{1,0:T(4,128)S(1)}, s32[4,128]{1,0:T(4,128)S(1)}, u32[]{:S(2)}, u32[]{:S(2)}) collective-permute-start(s32[4,128]{1,0:T(4,128)S(1)} %broadcast_in_dim.51), channel_id=1, source_target_pairs={{0,8},{8,0},{16,24},{24,16},{1,9},{9,1},{17,25},{25,17},{2,10},{10... | collective-permute-start | bytes 6152 | tf_op jit(solution)/shard_map/ppermute | solution.py:18
  6.9 10.4 %collective-permute-start.4 = (s32[4,128]{1,0:T(4,128)S(1)}, s32[4,128]{1,0:T(4,128)S(1)}, u32[]{:S(2)}, u32[]{:S(2)}) collective-permute-start(s32[4,128]{1,0:T(4,128)S(1)} %broadcast_in_dim.53), channel_id=1, source_target_pairs={{0,1},{2,3},{4,5},{6,7},{1,0},{3,2},{5,4},{7,6},{8,9},{10,11},{12,... | collective-permute-start | bytes 6152 | tf_op jit(solution)/shard_map/ppermute | solution.py:24
  6.9 3.3 %copy-start.1 = (s32[1,16,12]{1,0,2:T(1,128)S(1)}, s32[1,16,12]{1,0,2:T(1,128)}, u32[]{:S(2)}) copy-start(s32[1,16,12]{1,0,2:T(1,128)} %param.9) | copy-start | bytes 2308
  6.9 3.5 %copy-start.2 = (s32[1,16,8]{1,2,0:T(8,128)S(1)}, s32[1,16,8]{1,2,0:T(8,128)}, u32[]{:S(2)}) copy-start(s32[1,16,8]{1,2,0:T(8,128)} %param.12) | copy-start | bytes 1540
  8.1 6.4 %collective-permute-start.2 = (bf16[8,64,128]{2,1,0:T(8,128)(2,1)S(1)}, bf16[8,64,128]{2,1,0:T(8,128)(2,1)S(1)}, u32[]{:S(2)}, u32[]{:S(2)}) collective-permute-start(bf16[8,64,128]{2,1,0:T(8,128)(2,1)S(1)} %get-tuple-element.37), channel_id=1, source_target_pairs={{0,16},{8,24},{16,0},{24,8},{1,17},{9,25},{17,1},{25,9},{2,18},{10... | collective-permute-start | bytes 393224 | tf_op jit(solution)/shard_map/ppermute | solution.py:18
  9.7 7.2 %collective-permute-start.3 = (bf16[8,64,128]{2,1,0:T(8,128)(2,1)S(1)}, bf16[8,64,128]{2,1,0:T(8,128)(2,1)S(1)}, u32[]{:S(2)}, u32[]{:S(2)}) collective-permute-start(bf16[8,64,128]{2,1,0:T(8,128)(2,1)S(1)} %get-tuple-element.38), channel_id=1, source_target_pairs={{0,16},{8,24},{16,0},{24,8},{1,17},{9,25},{17,1},{25,9},{2,18},{10... | collective-permute-start | bytes 393224 | tf_op jit(solution)/shard_map/ppermute | solution.py:18
  10.6 6.4 %copy-start = (bf16[1,16,128,128]{3,2,1,0:T(8,128)(2,1)S(1)}, bf16[1,16,128,128]{3,2,1,0:T(8,128)(2,1)}, u32[]{:S(2)}) copy-start(bf16[1,16,128,128]{3,2,1,0:T(8,128)(2,1)} %param.10) | copy-start | bytes 1572868
  17.0 9.5 %slice-start = ((s8[6291456]{0:T(1024)(128)(4,1)}), s8[4194304]{0:T(1024)(128)(4,1)S(1)}, s32[]{:S(2)}) async-start(s8[6291456]{0:T(1024)(128)(4,1)} %bitcast.12), calls=%async_computation | async-start | bytes 8388608
  17.3 9.2 %slice-start.1 = ((s8[6291456]{0:T(1024)(128)(4,1)}), s8[2097152]{0:T(1024)(128)(4,1)S(1)}, s32[]{:S(2)}) async-start(s8[6291456]{0:T(1024)(128)(4,1)} %bitcast.12), calls=%async_computation.1 | async-start | bytes 4194304
  17.6 4.3 %collective-permute-start.5 = (bf16[4,64,128]{2,1,0:T(8,128)(2,1)S(1)}, bf16[4,64,128]{2,1,0:T(8,128)(2,1)S(1)}, u32[]{:S(2)}, u32[]{:S(2)}) collective-permute-start(bf16[4,64,128]{2,1,0:T(8,128)(2,1)S(1)} %shard_map.77), channel_id=1, source_target_pairs={{0,1},{2,3},{4,5},{6,7},{1,0},{3,2},{5,4},{7,6},{8,9},{10,11},{12,... | collective-permute-start | bytes 196616 | tf_op jit(solution)/shard_map/ppermute | solution.py:24
  19.4 7.0 %collective-permute-start.6 = (bf16[4,64,128]{2,1,0:T(8,128)(2,1)S(1)}, bf16[4,64,128]{2,1,0:T(8,128)(2,1)S(1)}, u32[]{:S(2)}, u32[]{:S(2)}) collective-permute-start(bf16[4,64,128]{2,1,0:T(8,128)(2,1)S(1)} %get-tuple-element.42), channel_id=1, source_target_pairs={{1,2},{3,4},{5,6},{7,0},{2,1},{4,3},{6,5},{0,7},{9,10},{11,12},{13... | collective-permute-start | bytes 196616 | tf_op jit(solution)/shard_map/ppermute | solution.py:24
  20.1 6.2 %collective-permute-start.7 = (bf16[4,64,128]{2,1,0:T(8,128)(2,1)S(1)}, bf16[4,64,128]{2,1,0:T(8,128)(2,1)S(1)}, u32[]{:S(2)}, u32[]{:S(2)}) collective-permute-start(bf16[4,64,128]{2,1,0:T(8,128)(2,1)S(1)} %get-tuple-element.43), channel_id=1, source_target_pairs={{0,8},{8,0},{16,24},{24,16},{1,9},{9,1},{17,25},{25,17},{2,10},{10... | collective-permute-start | bytes 196616 | tf_op jit(solution)/shard_map/ppermute | solution.py:18
  26.6 9.9 %collective-permute-start.9 = (bf16[10,64,128]{2,1,0:T(8,128)(2,1)S(1)}, bf16[10,64,128]{2,1,0:T(8,128)(2,1)S(1)}, u32[]{:S(2)}, u32[]{:S(2)}) collective-permute-start(bf16[10,64,128]{2,1,0:T(8,128)(2,1)S(1)} %shard_map.79), channel_id=1, source_target_pairs={{0,16},{8,24},{16,0},{24,8},{1,17},{9,25},{17,1},{25,9},{2,18},{10... | collective-permute-start | bytes 491528 | tf_op jit(solution)/shard_map/ppermute | solution.py:18
  31.9 4.6 %collective-permute-start.8 = (bf16[6,64,128]{2,1,0:T(8,128)(2,1)S(1)}, bf16[6,64,128]{2,1,0:T(8,128)(2,1)S(1)}, u32[]{:S(2)}, u32[]{:S(2)}) collective-permute-start(bf16[6,64,128]{2,1,0:T(8,128)(2,1)S(1)} %get-tuple-element.44), channel_id=1, source_target_pairs={{0,16},{8,24},{16,0},{24,8},{1,17},{9,25},{17,1},{25,9},{2,18},{10... | collective-permute-start | bytes 294920 | tf_op jit(solution)/shard_map/ppermute | solution.py:18
  38.8 4.1 %collective-permute-start.12 = (bf16[4,64,128]{2,1,0:T(8,128)(2,1)S(1)}, bf16[4,64,128]{2,1,0:T(8,128)(2,1)S(1)}, u32[]{:S(2)}, u32[]{:S(2)}) collective-permute-start(bf16[4,64,128]{2,1,0:T(8,128)(2,1)S(1)} %get-tuple-element.49), channel_id=1, source_target_pairs={{0,8},{8,0},{16,24},{24,16},{1,9},{9,1},{17,25},{25,17},{2,10},{10... | collective-permute-start | bytes 196616 | tf_op jit(solution)/shard_map/ppermute | solution.py:18
  39.4 4.6 %collective-permute-start.10 = (bf16[4,64,128]{2,1,0:T(8,128)(2,1)S(1)}, bf16[4,64,128]{2,1,0:T(8,128)(2,1)S(1)}, u32[]{:S(2)}, u32[]{:S(2)}) collective-permute-start(bf16[4,64,128]{2,1,0:T(8,128)(2,1)S(1)} %shard_map.83), channel_id=1, source_target_pairs={{0,1},{2,3},{4,5},{6,7},{1,0},{3,2},{5,4},{7,6},{8,9},{10,11},{12,... | collective-permute-start | bytes 196616 | tf_op jit(solution)/shard_map/ppermute | solution.py:24
  39.5 7.3 %collective-permute-start.11 = (bf16[4,64,128]{2,1,0:T(8,128)(2,1)S(1)}, bf16[4,64,128]{2,1,0:T(8,128)(2,1)S(1)}, u32[]{:S(2)}, u32[]{:S(2)}) collective-permute-start(bf16[4,64,128]{2,1,0:T(8,128)(2,1)S(1)} %get-tuple-element.48), channel_id=1, source_target_pairs={{1,2},{3,4},{5,6},{7,0},{2,1},{4,3},{6,5},{0,7},{9,10},{11,12},{13... | collective-permute-start | bytes 196616 | tf_op jit(solution)/shard_map/ppermute | solution.py:24
  49.3 7.9 %collective-permute-start.14 = (bf16[10,64,128]{2,1,0:T(8,128)(2,1)S(1)}, bf16[10,64,128]{2,1,0:T(8,128)(2,1)S(1)}, u32[]{:S(2)}, u32[]{:S(2)}) collective-permute-start(bf16[10,64,128]{2,1,0:T(8,128)(2,1)S(1)} %get-tuple-element.54), channel_id=1, source_target_pairs={{0,16},{8,24},{16,0},{24,8},{1,17},{9,25},{17,1},{25,9},{2,18},{10... | collective-permute-start | bytes 491528 | tf_op jit(solution)/shard_map/ppermute | solution.py:18
  49.3 7.8 %collective-permute-start.13 = (bf16[6,64,128]{2,1,0:T(8,128)(2,1)S(1)}, bf16[6,64,128]{2,1,0:T(8,128)(2,1)S(1)}, u32[]{:S(2)}, u32[]{:S(2)}) collective-permute-start(bf16[6,64,128]{2,1,0:T(8,128)(2,1)S(1)} %get-tuple-element.53), channel_id=1, source_target_pairs={{0,16},{8,24},{16,0},{24,8},{1,17},{9,25},{17,1},{25,9},{2,18},{10... | collective-permute-start | bytes 294920 | tf_op jit(solution)/shard_map/ppermute | solution.py:18
  58.1 3.8 %collective-permute-start.17 = (bf16[4,64,128]{2,1,0:T(8,128)(2,1)S(1)}, bf16[4,64,128]{2,1,0:T(8,128)(2,1)S(1)}, u32[]{:S(2)}, u32[]{:S(2)}) collective-permute-start(bf16[4,64,128]{2,1,0:T(8,128)(2,1)S(1)} %get-tuple-element.60), channel_id=1, source_target_pairs={{0,8},{8,0},{16,24},{24,16},{1,9},{9,1},{17,25},{25,17},{2,10},{10... | collective-permute-start | bytes 196616 | tf_op jit(solution)/shard_map/ppermute | solution.py:18
  58.4 4.6 %collective-permute-start.15 = (bf16[4,64,128]{2,1,0:T(8,128)(2,1)S(1)}, bf16[4,64,128]{2,1,0:T(8,128)(2,1)S(1)}, u32[]{:S(2)}, u32[]{:S(2)}) collective-permute-start(bf16[4,64,128]{2,1,0:T(8,128)(2,1)S(1)} %shard_map.88), channel_id=1, source_target_pairs={{0,1},{2,3},{4,5},{6,7},{1,0},{3,2},{5,4},{7,6},{8,9},{10,11},{12,... | collective-permute-start | bytes 196616 | tf_op jit(solution)/shard_map/ppermute | solution.py:24
  58.5 7.3 %collective-permute-start.16 = (bf16[4,64,128]{2,1,0:T(8,128)(2,1)S(1)}, bf16[4,64,128]{2,1,0:T(8,128)(2,1)S(1)}, u32[]{:S(2)}, u32[]{:S(2)}) collective-permute-start(bf16[4,64,128]{2,1,0:T(8,128)(2,1)S(1)} %get-tuple-element.59), channel_id=1, source_target_pairs={{1,2},{3,4},{5,6},{7,0},{2,1},{4,3},{6,5},{0,7},{9,10},{11,12},{13... | collective-permute-start | bytes 196616 | tf_op jit(solution)/shard_map/ppermute | solution.py:24
  66.1 11.8 %collective-permute-start.19 = (bf16[10,64,128]{2,1,0:T(8,128)(2,1)S(1)}, bf16[10,64,128]{2,1,0:T(8,128)(2,1)S(1)}, u32[]{:S(2)}, u32[]{:S(2)}) collective-permute-start(bf16[10,64,128]{2,1,0:T(8,128)(2,1)S(1)} %get-tuple-element.63), channel_id=1, source_target_pairs={{0,16},{8,24},{16,0},{24,8},{1,17},{9,25},{17,1},{25,9},{2,18},{10... | collective-permute-start | bytes 491528 | tf_op jit(solution)/shard_map/ppermute | solution.py:18
  71.8 6.1 %collective-permute-start.18 = (bf16[6,64,128]{2,1,0:T(8,128)(2,1)S(1)}, bf16[6,64,128]{2,1,0:T(8,128)(2,1)S(1)}, u32[]{:S(2)}, u32[]{:S(2)}) collective-permute-start(bf16[6,64,128]{2,1,0:T(8,128)(2,1)S(1)} %get-tuple-element.61), channel_id=1, source_target_pairs={{0,16},{8,24},{16,0},{24,8},{1,17},{9,25},{17,1},{25,9},{2,18},{10... | collective-permute-start | bytes 294920 | tf_op jit(solution)/shard_map/ppermute | solution.py:18

commit v10 on v7

--- a/solution.py
+++ b/solution.py
@@ -133,7 +133,7 @@
         out[j] = times(scratch[at], smoother[row]).astype(jnp.bfloat16)
 
 
-def first_body(table, loads, residual, arrived, transfer, smoother, current, first):
+def first_body(table, loads, wanted, residual, arrived, transfer, smoother, current, first, beside):
     rows = first.shape[0]
 
     @pl.when(is_fine(table))
@@ -148,6 +148,8 @@
     for i in range(rows):
         value = times(current[i].astype(jnp.bfloat16), smoother[i])
         first[i] = value.astype(jnp.bfloat16)
+    for row, out, j in chosen([wanted], [beside]):
+        out[j] = first[row]
 
 
 def second_rows(low, table, current, first, extension, blocks, smoother, rounded, full=None):
@@ -213,8 +215,8 @@
             out[j] = value.astype(jnp.bfloat16)
 
 
-def update_body(table, arrived, correction, *refs):
-    *terms, transfer, iterate, rounded = refs
+def update_body(table, wanted, arrived, correction, *refs):
+    *terms, transfer, iterate, rounded, beside = refs
 
     @pl.when(is_fine(table))
     def _():
@@ -222,6 +224,8 @@
             value = updated(i, arrived, table, transfer, correction, terms)
             iterate[i] = value
             rounded[i] = value.astype(jnp.bfloat16)
+        for row, out, j in chosen([wanted], [beside]):
+            out[j] = rounded[row]
 
 
 def residual_body(low, table, loads, *refs):
@@ -280,7 +284,7 @@
         return pltpu.VMEM((count, load_cols, width), jnp.bfloat16)
 
     wide, narrow = panels(block_rows, jnp.float32), panels(block_rows, jnp.bfloat16)
-    early_rows = block_rows * 3 // 8
+    early_rows = block_rows // 2
     late_rows = block_rows - early_rows
     listed = panels(list_width, jnp.bfloat16)
     extended = panels(block_rows + 3 * list_width, jnp.bfloat16)
@@ -295,18 +299,19 @@
     def spread(values):
         return jnp.broadcast_to(values[:, None], (values.shape[0], LANES))
 
-    def swap_all(odd, others):
-        behind = swapped(odd, "dom", 1)
-        ahead, beside = others()
-        ahead = swapped(ahead, "dom", 0)
-        beside = partner(beside, "level", 0)
-        return ahead, behind, beside
+    def swap_both(odd, even):
+        odd = swapped(odd, "dom", 1)
+        even = swapped(even, "dom", 0)
+        return even, odd
+
+    def swap_beside(x):
+        return partner(x, "level", 0)
 
     even = lax.axis_index("dom") % 2 == 0
-    wanted_even, wanted_odd, wanted_beside = swap_all(
-        spread(jnp.where(even, left_list, right_list)),
-        lambda: (spread(jnp.where(even, right_list, left_list)), spread(sibling_list)),
+    wanted_even, wanted_odd = swap_both(
+        spread(jnp.where(even, left_list, right_list)), spread(jnp.where(even, right_list, left_list))
     )
+    wanted_beside = swap_beside(spread(sibling_list))
     columns = level_cols.reshape(-1)
     from_left = (columns >= block_rows) & (columns < block_rows + list_width)
     from_right = (columns >= block_rows + list_width) & (columns < block_rows + 2 * list_width)
@@ -320,19 +325,18 @@
     def fetched(source):
         return call(fetch_body, like(source), inside(loads), inside(source), in_specs=[HBM, HBM], scratch=[rowwise])
 
-    def exchanged(body, fixed, pieces, rest, joins, scratch):
-        def listed_rows(wanted, pieces, joins):
-            lists, each = len(wanted), len(pieces[0])
-            held_rows = [held(lists * list_width)] * scratch
-            return call(
-                lambda *refs: body(lists, each, *refs), (listed,) * lists + joins,
-                *fixed, *wanted, *sum(pieces, []), *rest, scratch=held_rows,
-            )
-
-        odd, *whole = listed_rows([wanted_odd], pieces, joins)
+    def exchanged(bodies, fixed, pieces, rest, joins, scratch):
+        listed_body, body = bodies
+        each = len(pieces[0])
+        odd, even, *whole = call(
+            lambda *refs: listed_body(2, each, *refs), (listed,) * 2 + joins,
+            *fixed, wanted_odd, wanted_even, *sum(pieces, []), *rest,
+            scratch=[held(2 * list_width)] * scratch,
+        )
+        even, odd = swap_both(odd, even)
         whole = whole or sum(pieces, [])
-        sides = swap_all(odd, lambda: listed_rows([wanted_even, wanted_beside], [[x] for x in whole], ()))
-        return whole, sides
+        *results, beside = call(body, (wide, narrow, listed), *fixed, wanted_beside, *whole, *rest)
+        return (*results, (even, odd, swap_beside(beside)))
 
     def part(rows):
         return panels(rows, jnp.float32), panels(rows, jnp.bfloat16)
@@ -357,11 +361,10 @@
             arrived.append(partner(sent, "level", 1))
             residual = [early, late]
         args, rest = (transfer_table, load_panels), (transfer, smooth)
-        whole, sides = exchanged(
-            first_listed_body, args, [residual, arrived], rest,
+        current, first, sides = exchanged(
+            (first_listed_body, first_body), args, [residual, arrived], rest,
             (wide, narrow) if len(arrived) > 1 else (), True,
         )
-        current, first = call(first_body, (wide, narrow), *args, *whole, *rest)
         args = (level_table, current, first)
         ends = cycle_index + 1 == ITERS
         rounded, extension, *start = call(
@@ -379,8 +382,10 @@
         correction = call(second_fine_body, wide, *args, extension, blocks, smooth, scratch=[held(block_rows)])
         if not ends:
             rest = [correction] + ([] if iterate is None else [iterate]) + [transfer]
-            whole, sides = exchanged(update_listed_body, (transfer_table,), [returned], rest, (narrow,), False)
-            iterate, rounded = call(update_body, (wide, narrow), transfer_table, *whole, *rest)
+            iterate, rounded, sides = exchanged(
+                (update_listed_body, update_body), (transfer_table,), [returned], rest,
+                (narrow,), False,
+            )
     final = call(
         last_body, jax.ShapeDtypeStruct((load_cols, block_rows * width), jnp.float32),
         transfer_table, *returned, correction, *start, *end, iterate, transfer, out_specs=HBM,

time: 73 us -> 76.7 us (1.051)
  waiting for transfers between devices: 24.6 us -> 28.2 us
  starting transfers between devices: 26.6 us -> 27.7 us
  Pallas kernels: 19.6 us -> 18.7 us
    ppermute x8, waiting for transfers between devices: 10.7 us -> 14.2 us  [swapped(): return lax.ppermute(x, axis, pairs + [(b, a) for a, b in pairs])]
    pallas_call x20 -> x17, Pallas kernels: 19.6 us -> 18.7 us  [call(): pl.pallas_call(body, out_shape=outs, in_specs=in_specs or [VMEM] * len(ar...]
  transfers between devices with their start and end apart: 19 -> 19, of which waited for: 10 -> 12; matrix products, arithmetic and copies ran while one was open for 1% -> 1% of each run, Pallas kernels for 19% -> 15%
where the time goes in v10:
time: 76.7 us; the launch traced here: 76.5 us
  waiting for transfers between devices  28.2 us (37%)
  starting transfers between devices  27.7 us (36%)
  Pallas kernels  18.7 us (24%)
  other arithmetic  0.79 us (1%)
    pallas_call x17, Pallas kernels, call(): pl.pallas_call(body, out_shape=outs, in_specs=in_specs or [VMEM] * len(ar...  18.7 us
    ppermute x8, starting transfers between devices, swapped(): return lax.ppermute(x, axis, pairs + [(b, a) for a, b in pairs])  14.2 us
    ppermute x8, waiting for transfers between devices, swapped(): return lax.ppermute(x, axis, pairs + [(b, a) for a, b in pairs])  14.2 us
    ppermute x11, waiting for transfers between devices, partner(): lax.ppermute(x, axis, [(i, i ^ 1 << apart) for i in range(lax.axis_size(a...  14 us
    ppermute x11, starting transfers between devices, partner(): lax.ppermute(x, axis, [(i, i ^ 1 << apart) for i in range(lax.axis_size(a...  13.4 us
  transfers between devices with their start and end apart: 19, of which 12 were waited for; matrix products, arithmetic and copies ran while one was open for 1% of the time, Pallas kernels for 15%

profile of v10, /device:TPU:0, one launch (start us, length us, event | category | flops | bytes accessed | tf_op | source)
XLA Modules:
  0.0 76.5 jit_solution(13799401429845068462)
XLA Ops:
  0.0 0.7 fusion.4
  0.7 0.1 broadcast_in_dim.52
  0.8 6.0 %collective-permute-start.1 = (s32[4,128]{1,0:T(4,128)S(1)}, s32[4,128]{1,0:T(4,128)S(1)}, u32[]{:S(2)}, u32[]{:S(2)}) collective-permute-start(s32[4,128]{1,0:T(4,128)S(1)} %broadcast_in_dim.52), channel_id=1, source_target_pairs={{1,2},{3,4},{5,6},{7,0},{2,1},{4,3},{6,5},{0,7},{9,10},{11,12},{13... | collective-permute-start | bytes 6152 | tf_op jit(solution)/shard_map/ppermute | solution.py:23
  6.8 0.1 broadcast_in_dim.51
  6.9 0.0 collective-permute-start
  6.9 0.1 broadcast_in_dim.53
  6.9 1.2 %shard_map.73 = (f32[16,64,128]{2,1,0:T(8,128)S(1)}, bf16[16,64,128]{2,1,0:T(8,128)(2,1)S(1)}) custom-call(f32[64,2048]{1,0:T(8,128)} %bitcast.33), custom_call_target="tpu_custom_call" | custom-call | flops 5000000000 | bytes 1048576 | tf_op jit(solution)/shard_map/pallas_call | solution.py:38
  8.1 1.6 %collective-permute-start.3 = (bf16[16,64,128]{2,1,0:T(8,128)(2,1)S(1)}, bf16[16,64,128]{2,1,0:T(8,128)(2,1)S(1)}, u32[]{:S(2)}, u32[]{:S(2)}) collective-permute-start(bf16[16,64,128]{2,1,0:T(8,128)(2,1)S(1)} %get-tuple-element.38), channel_id=1, source_target_pairs={{0,16},{8,24},{16,0},{24,8},{1,17},{9,25},{17,1},{25,9},{2,18},{10... | collective-permute-start | bytes 786440 | tf_op jit(solution)/shard_map/ppermute | solution.py:17
  9.7 0.1 copy.10
  9.8 0.1 reshape.46
  9.9 0.1 copy.9
  9.9 0.1 reshape.43
  10.1 0.0 copy-start
  10.1 0.0 slice-start
  10.1 2.4 %shard_map.74.transfer.refs_6_.refs_0_.refs_8_ = bf16[16,8,128,128]{3,2,1,0:T(8,128)(2,1)S(1)} custom-call(f32[64,2048]{1,0:T(8,128)} %bitcast.34, bf16[16,8,128,128]{3,2,1,0:T(8,128)(2,1)} %bitcast.32), custom_call_target="tpu_custom_call" | custom-call | flops 570425344 | bytes 8912896 | tf_op jit(solution)/shard_map/pallas_call | solution.py:38
  12.5 0.0 collective-permute-done.2.refs_3_.refs_2_
  12.5 4.4 %collective-permute-done.3.arrived.refs_5_ = bf16[16,64,128]{2,1,0:T(8,128)(2,1)S(1)} collective-permute-done((bf16[16,64,128]{2,1,0:T(8,128)(2,1)S(1)}, bf16[16,64,128]{2,1,0:T(8,128)(2,1)S(1)}, u32[]{:S(2)}, u32[]{:S(2)}) %collective-permute-start.3) | collective-permute-done | bytes 262176 | tf_op jit(solution)/shard_map/ppermute | solution.py:17
  16.9 0.1 broadcast_in_dim.46.table.refs_0_
  17.0 0.0 copy-done
  17.0 0.0 slice-start.1
  17.0 0.4 shard_map.76
  17.4 1.8 %collective-permute-start.4 = (bf16[4,64,128]{2,1,0:T(8,128)(2,1)S(1)}, bf16[4,64,128]{2,1,0:T(8,128)(2,1)S(1)}, u32[]{:S(2)}, u32[]{:S(2)}) collective-permute-start(bf16[4,64,128]{2,1,0:T(8,128)(2,1)S(1)} %get-tuple-element.41), channel_id=1, source_target_pairs={{0,1},{2,3},{4,5},{6,7},{1,0},{3,2},{5,4},{7,6},{8,9},{10,11},{12,... | collective-permute-start | bytes 196616 | tf_op jit(solution)/shard_map/ppermute | solution.py:23
  19.2 0.2 collective-permute-start.5
  19.3 0.0 collective-permute-done.wanted
  19.4 0.6 shard_map.75
  19.9 0.1 collective-permute-start.6
  20.0 0.1 pad_add_fusion.1
  20.1 1.6 %collective-permute-done.4.left = bf16[4,64,128]{2,1,0:T(8,128)(2,1)S(1)} collective-permute-done((bf16[4,64,128]{2,1,0:T(8,128)(2,1)S(1)}, bf16[4,64,128]{2,1,0:T(8,128)(2,1)S(1)}, u32[]{:S(2)}, u32[]{:S(2)}) %collective-permute-start.4) | collective-permute-done | bytes 65568 | tf_op jit(solution)/shard_map/ppermute | solution.py:23
  21.7 4.4 %collective-permute-done.5.right = bf16[4,64,128]{2,1,0:T(8,128)(2,1)S(1)} collective-permute-done((bf16[4,64,128]{2,1,0:T(8,128)(2,1)S(1)}, bf16[4,64,128]{2,1,0:T(8,128)(2,1)S(1)}, u32[]{:S(2)}, u32[]{:S(2)}) %collective-permute-start.5) | collective-permute-done | bytes 65568 | tf_op jit(solution)/shard_map/ppermute | solution.py:23
  26.1 0.0 collective-permute-done.6.sibling
  26.1 0.1 broadcast_in_dim.49.table.refs_0_
  26.3 0.1 shard_map.77
  26.4 5.1 %collective-permute-start.8 = (bf16[8,64,128]{2,1,0:T(8,128)(2,1)S(1)}, bf16[8,64,128]{2,1,0:T(8,128)(2,1)S(1)}, u32[]{:S(2)}, u32[]{:S(2)}) collective-permute-start(bf16[8,64,128]{2,1,0:T(8,128)(2,1)S(1)} %shard_map.78), channel_id=1, source_target_pairs={{0,16},{8,24},{16,0},{24,8},{1,17},{9,25},{17,1},{25,9},{2,18},{10... | collective-permute-start | bytes 393224 | tf_op jit(solution)/shard_map/ppermute | solution.py:17
  31.5 0.1 collective-permute-start.7
  31.6 2.6 %shard_map.79.refs_5_.correction = f32[16,64,128]{2,1,0:T(8,128)S(1)} custom-call(s32[193,128]{1,0:T(8,128)S(1)} %broadcast_in_dim.49.table.refs_0_, f32[16,64,128]{2,1,0:T(8,128)S(1)} %get-tuple-element.39.current, bf16[16,64,128]{2,1,0:T(8,128)(2,1)S(1)} %get-tuple-element.40.first, bf16[28,64,128]{2,1,0:T(8,128)(2,1)S(1)} %get-tuple-element.45.extension, ...), custom_call_target="tpu_custom_call" | custom-call | flops 555778048 | bytes 8684032 | tf_op jit(solution)/shard_map/pallas_call | solution.py:38
  34.1 0.4 collective-permute-done.8.refs_4_
  34.5 1.9 %collective-permute-done.7.refs_3_ = bf16[8,64,128]{2,1,0:T(8,128)(2,1)S(1)} collective-permute-done((bf16[8,64,128]{2,1,0:T(8,128)(2,1)S(1)}, bf16[8,64,128]{2,1,0:T(8,128)(2,1)S(1)}, u32[]{:S(2)}, u32[]{:S(2)}) %collective-permute-start.7) | collective-permute-done | bytes 131104 | tf_op jit(solution)/shard_map/ppermute | solution.py:17
  36.5 1.0 %shard_map.80 = (bf16[4,64,128]{2,1,0:T(8,128)(2,1)S(1)}, bf16[4,64,128]{2,1,0:T(8,128)(2,1)S(1)}, bf16[16,64,128]{2,1,0:T(8,128)(2,1)S(1)}) custom-call(s32[129,128]{1,0:T(8,128)S(1)} %broadcast_in_dim.46.table.refs_0_, s32[4,128]{1,0:T(4,128)S(1)} %collective-permute-done.1.refs_2_.refs_1_, s32[4,128]{1,0:T(4,128)S(1)} %collective-permute-done.2.refs_3_.refs_2_, ...), custom_call_target="tpu_custom_call" | custom-call | flops 348422144 | bytes 5444096 | tf_op jit(solution)/shard_map/pallas_call | solution.py:38
  37.4 1.7 %shard_map.81 = (f32[16,64,128]{2,1,0:T(8,128)S(1)}, bf16[16,64,128]{2,1,0:T(8,128)(2,1)S(1)}, bf16[4,64,128]{2,1,0:T(8,128)(2,1)S(1)}) custom-call(s32[129,128]{1,0:T(8,128)S(1)} %broadcast_in_dim.46.table.refs_0_, s32[4,128]{1,0:T(4,128)S(1)} %collective-permute-done.wanted, bf16[16,64,128]{2,1,0:T(8,128)(2,1)S(1)} %get-tuple-element.46.arrived, ...), custom_call_target="tpu_custom_call" | custom-call | flops 377651200 | bytes 5900800 | tf_op jit(solution)/shard_map/pallas_call | solution.py:38
  39.1 0.1 collective-permute-start.11
  39.2 0.1 collective-permute-start.9
  39.3 3.0 %collective-permute-start.10 = (bf16[4,64,128]{2,1,0:T(8,128)(2,1)S(1)}, bf16[4,64,128]{2,1,0:T(8,128)(2,1)S(1)}, u32[]{:S(2)}, u32[]{:S(2)}) collective-permute-start(bf16[4,64,128]{2,1,0:T(8,128)(2,1)S(1)} %get-tuple-element.49), channel_id=1, source_target_pairs={{1,2},{3,4},{5,6},{7,0},{2,1},{4,3},{6,5},{0,7},{9,10},{11,12},{13... | collective-permute-start | bytes 196616 | tf_op jit(solution)/shard_map/ppermute | solution.py:23
  42.3 1.4 %collective-permute-done.9.refs_3_ = bf16[4,64,128]{2,1,0:T(8,128)(2,1)S(1)} collective-permute-done((bf16[4,64,128]{2,1,0:T(8,128)(2,1)S(1)}, bf16[4,64,128]{2,1,0:T(8,128)(2,1)S(1)}, u32[]{:S(2)}, u32[]{:S(2)}) %collective-permute-start.9) | collective-permute-done | bytes 65568 | tf_op jit(solution)/shard_map/ppermute | solution.py:23
  43.7 2.7 %collective-permute-done.10.refs_4_ = bf16[4,64,128]{2,1,0:T(8,128)(2,1)S(1)} collective-permute-done((bf16[4,64,128]{2,1,0:T(8,128)(2,1)S(1)}, bf16[4,64,128]{2,1,0:T(8,128)(2,1)S(1)}, u32[]{:S(2)}, u32[]{:S(2)}) %collective-permute-start.10) | collective-permute-done | bytes 65568 | tf_op jit(solution)/shard_map/ppermute | solution.py:23
  46.4 1.3 %shard_map.82 = (f32[8,64,128]{2,1,0:T(8,128)S(1)}, bf16[8,64,128]{2,1,0:T(8,128)(2,1)S(1)}, bf16[28,64,128]{2,1,0:T(8,128)(2,1)S(1)}) custom-call(s32[193,128]{1,0:T(8,128)S(1)} %broadcast_in_dim.49.table.refs_0_, f32[16,64,128]{2,1,0:T(8,128)S(1)} %get-tuple-element.37.loads.residual.refs_1_.refs_4_, bf16[16,64,128]{2,1,0:T(8,128)(2,1)S(1)} %get-tuple-element.47.refs_2_, ...), custom_call_target="tpu_custom_call" | custom-call | flops 526417920 | bytes 8225280 | tf_op jit(solution)/shard_map/pallas_call | solution.py:38
  47.7 0.1 collective-permute-start.12
  47.7 1.2 %shard_map.83 = (f32[8,64,128]{2,1,0:T(8,128)S(1)}, bf16[8,64,128]{2,1,0:T(8,128)(2,1)S(1)}) custom-call(s32[193,128]{1,0:T(8,128)S(1)} %broadcast_in_dim.49.table.refs_0_, f32[16,64,128]{2,1,0:T(8,128)S(1)} %get-tuple-element.37.loads.residual.refs_1_.refs_4_, bf16[28,64,128]{2,1,0:T(8,128)(2,1)S(1)} %get-tuple-element.52.refs_2_, ...), custom_call_target="tpu_custom_call" | custom-call | flops 497057792 | bytes 7766528 | tf_op jit(solution)/shard_map/pallas_call | solution.py:38
  49.0 0.9 %collective-permute-start.13 = (bf16[8,64,128]{2,1,0:T(8,128)(2,1)S(1)}, bf16[8,64,128]{2,1,0:T(8,128)(2,1)S(1)}, u32[]{:S(2)}, u32[]{:S(2)}) collective-permute-start(bf16[8,64,128]{2,1,0:T(8,128)(2,1)S(1)} %get-tuple-element.55), channel_id=1, source_target_pairs={{0,16},{8,24},{16,0},{24,8},{1,17},{9,25},{17,1},{25,9},{2,18},{10... | collective-permute-start | bytes 393224 | tf_op jit(solution)/shard_map/ppermute | solution.py:17
  49.9 4.2 %collective-permute-done.12.refs_6_ = bf16[8,64,128]{2,1,0:T(8,128)(2,1)S(1)} collective-permute-done((bf16[8,64,128]{2,1,0:T(8,128)(2,1)S(1)}, bf16[8,64,128]{2,1,0:T(8,128)(2,1)S(1)}, u32[]{:S(2)}, u32[]{:S(2)}) %collective-permute-start.12) | collective-permute-done | bytes 131104 | tf_op jit(solution)/shard_map/ppermute | solution.py:17
  54.0 1.4 %collective-permute-done.13.refs_7_ = bf16[8,64,128]{2,1,0:T(8,128)(2,1)S(1)} collective-permute-done((bf16[8,64,128]{2,1,0:T(8,128)(2,1)S(1)}, bf16[8,64,128]{2,1,0:T(8,128)(2,1)S(1)}, u32[]{:S(2)}, u32[]{:S(2)}) %collective-permute-start.13) | collective-permute-done | bytes 131104 | tf_op jit(solution)/shard_map/ppermute | solution.py:17
  55.4 0.4 shard_map.84
  55.8 0.6 shard_map.85
  56.4 0.1 collective-permute-start.16
  56.5 0.1 collective-permute-start.14
  56.6 3.0 %collective-permute-start.15 = (bf16[4,64,128]{2,1,0:T(8,128)(2,1)S(1)}, bf16[4,64,128]{2,1,0:T(8,128)(2,1)S(1)}, u32[]{:S(2)}, u32[]{:S(2)}) collective-permute-start(bf16[4,64,128]{2,1,0:T(8,128)(2,1)S(1)} %get-tuple-element.61), channel_id=1, source_target_pairs={{1,2},{3,4},{5,6},{7,0},{2,1},{4,3},{6,5},{0,7},{9,10},{11,12},{13... | collective-permute-start | bytes 196616 | tf_op jit(solution)/shard_map/ppermute | solution.py:23
  59.6 1.4 %collective-permute-done.14.left = bf16[4,64,128]{2,1,0:T(8,128)(2,1)S(1)} collective-permute-done((bf16[4,64,128]{2,1,0:T(8,128)(2,1)S(1)}, bf16[4,64,128]{2,1,0:T(8,128)(2,1)S(1)}, u32[]{:S(2)}, u32[]{:S(2)}) %collective-permute-start.14) | collective-permute-done | bytes 65568 | tf_op jit(solution)/shard_map/ppermute | solution.py:23
  61.0 2.7 %collective-permute-done.15.right = bf16[4,64,128]{2,1,0:T(8,128)(2,1)S(1)} collective-permute-done((bf16[4,64,128]{2,1,0:T(8,128)(2,1)S(1)}, bf16[4,64,128]{2,1,0:T(8,128)(2,1)S(1)}, u32[]{:S(2)}, u32[]{:S(2)}) %collective-permute-start.15) | collective-permute-done | bytes 65568 | tf_op jit(solution)/shard_map/ppermute | solution.py:23
  63.7 0.1 shard_map.86
  63.8 4.1 %collective-permute-start.17 = (bf16[8,64,128]{2,1,0:T(8,128)(2,1)S(1)}, bf16[8,64,128]{2,1,0:T(8,128)(2,1)S(1)}, u32[]{:S(2)}, u32[]{:S(2)}) collective-permute-start(bf16[8,64,128]{2,1,0:T(8,128)(2,1)S(1)} %get-tuple-element.63), channel_id=1, source_target_pairs={{0,16},{8,24},{16,0},{24,8},{1,17},{9,25},{17,1},{25,9},{2,18},{10... | collective-permute-start | bytes 393224 | tf_op jit(solution)/shard_map/ppermute | solution.py:17
  67.9 0.2 shard_map.87
  68.1 1.4 %collective-permute-start.18 = (bf16[8,64,128]{2,1,0:T(8,128)(2,1)S(1)}, bf16[8,64,128]{2,1,0:T(8,128)(2,1)S(1)}, u32[]{:S(2)}, u32[]{:S(2)}) collective-permute-start(bf16[8,64,128]{2,1,0:T(8,128)(2,1)S(1)} %get-tuple-element.65), channel_id=1, source_target_pairs={{0,16},{8,24},{16,0},{24,8},{1,17},{9,25},{17,1},{25,9},{2,18},{10... | collective-permute-start | bytes 393224 | tf_op jit(solution)/shard_map/ppermute | solution.py:17
  69.5 2.6 %shard_map.88.correction = f32[16,64,128]{2,1,0:T(8,128)S(1)} custom-call(s32[193,128]{1,0:T(8,128)S(1)} %broadcast_in_dim.49.table.refs_0_, f32[16,64,128]{2,1,0:T(8,128)S(1)} %get-tuple-element.58.current, bf16[16,64,128]{2,1,0:T(8,128)(2,1)S(1)} %get-tuple-element.59.first, bf16[28,64,128]{2,1,0:T(8,128)(2,1)S(1)} %get-tuple-element.64.extension, ...), custom_call_target="tpu_custom_call" | custom-call | flops 555778048 | bytes 8684032 | tf_op jit(solution)/shard_map/pallas_call | solution.py:38
  72.1 1.7 %collective-permute-done.18.late = bf16[8,64,128]{2,1,0:T(8,128)(2,1)S(1)} collective-permute-done((bf16[8,64,128]{2,1,0:T(8,128)(2,1)S(1)}, bf16[8,64,128]{2,1,0:T(8,128)(2,1)S(1)}, u32[]{:S(2)}, u32[]{:S(2)}) %collective-permute-start.18) | collective-permute-done | bytes 131104 | tf_op jit(solution)/shard_map/ppermute | solution.py:17
  73.9 2.5 %shard_map.89 = f32[64,2048]{1,0:T(8,128)} custom-call(s32[129,128]{1,0:T(8,128)S(1)} %broadcast_in_dim.46.table.refs_0_, bf16[8,64,128]{2,1,0:T(8,128)(2,1)S(1)} %collective-permute-done.17.early, bf16[8,64,128]{2,1,0:T(8,128)(2,1)S(1)} %collective-permute-done.18.late, f32[16,64,128]{2,1,0:T(8,128)S(1)} %shard_map.88.correction, ...), custom_call_target="tpu_custom_call" | custom-call | flops 423657472 | bytes 6619648 | tf_op jit(solution)/shard_map/pallas_call | solution.py:38
  (15 shorter events, 0.1 us)
Async XLA Ops:
  0.8 11.8 %collective-permute-start.1 = (s32[4,128]{1,0:T(4,128)S(1)}, s32[4,128]{1,0:T(4,128)S(1)}, u32[]{:S(2)}, u32[]{:S(2)}) collective-permute-start(s32[4,128]{1,0:T(4,128)S(1)} %broadcast_in_dim.52), channel_id=1, source_target_pairs={{1,2},{3,4},{5,6},{7,0},{2,1},{4,3},{6,5},{0,7},{9,10},{11,12},{13... | collective-permute-start | bytes 6152 | tf_op jit(solution)/shard_map/ppermute | solution.py:23
  6.9 12.5 %collective-permute-start = (s32[4,128]{1,0:T(4,128)S(1)}, s32[4,128]{1,0:T(4,128)S(1)}, u32[]{:S(2)}, u32[]{:S(2)}) collective-permute-start(s32[4,128]{1,0:T(4,128)S(1)} %broadcast_in_dim.51), channel_id=1, source_target_pairs={{0,8},{8,0},{16,24},{24,16},{1,9},{9,1},{17,25},{25,17},{2,10},{10... | collective-permute-start | bytes 6152 | tf_op jit(solution)/shard_map/ppermute | solution.py:17
  6.9 5.6 %collective-permute-start.2 = (s32[4,128]{1,0:T(4,128)S(1)}, s32[4,128]{1,0:T(4,128)S(1)}, u32[]{:S(2)}, u32[]{:S(2)}) collective-permute-start(s32[4,128]{1,0:T(4,128)S(1)} %broadcast_in_dim.53), channel_id=1, source_target_pairs={{0,1},{2,3},{4,5},{6,7},{1,0},{3,2},{5,4},{7,6},{8,9},{10,11},{12,... | collective-permute-start | bytes 6152 | tf_op jit(solution)/shard_map/ppermute | solution.py:23
  6.9 2.7 %copy-start.1 = (s32[1,16,12]{1,0,2:T(1,128)S(1)}, s32[1,16,12]{1,0,2:T(1,128)}, u32[]{:S(2)}) copy-start(s32[1,16,12]{1,0,2:T(1,128)} %param.9) | copy-start | bytes 2308
  6.9 2.9 %copy-start.2 = (s32[1,16,8]{1,2,0:T(8,128)S(1)}, s32[1,16,8]{1,2,0:T(8,128)}, u32[]{:S(2)}) copy-start(s32[1,16,8]{1,2,0:T(8,128)} %param.12) | copy-start | bytes 1540
  8.1 8.8 %collective-permute-start.3 = (bf16[16,64,128]{2,1,0:T(8,128)(2,1)S(1)}, bf16[16,64,128]{2,1,0:T(8,128)(2,1)S(1)}, u32[]{:S(2)}, u32[]{:S(2)}) collective-permute-start(bf16[16,64,128]{2,1,0:T(8,128)(2,1)S(1)} %get-tuple-element.38), channel_id=1, source_target_pairs={{0,16},{8,24},{16,0},{24,8},{1,17},{9,25},{17,1},{25,9},{2,18},{10... | collective-permute-start | bytes 786440 | tf_op jit(solution)/shard_map/ppermute | solution.py:17
  10.1 6.9 %copy-start = (bf16[1,16,128,128]{3,2,1,0:T(8,128)(2,1)S(1)}, bf16[1,16,128,128]{3,2,1,0:T(8,128)(2,1)}, u32[]{:S(2)}) copy-start(bf16[1,16,128,128]{3,2,1,0:T(8,128)(2,1)} %param.10) | copy-start | bytes 1572868
  10.1 16.2 %slice-start = ((s8[6291456]{0:T(1024)(128)(4,1)}), s8[4194304]{0:T(1024)(128)(4,1)S(1)}, s32[]{:S(2)}) async-start(s8[6291456]{0:T(1024)(128)(4,1)} %bitcast.12), calls=%async_computation | async-start | bytes 8388608
  17.0 9.3 %slice-start.1 = ((s8[6291456]{0:T(1024)(128)(4,1)}), s8[2097152]{0:T(1024)(128)(4,1)S(1)}, s32[]{:S(2)}) async-start(s8[6291456]{0:T(1024)(128)(4,1)} %bitcast.12), calls=%async_computation.1 | async-start | bytes 4194304
  17.4 4.3 %collective-permute-start.4 = (bf16[4,64,128]{2,1,0:T(8,128)(2,1)S(1)}, bf16[4,64,128]{2,1,0:T(8,128)(2,1)S(1)}, u32[]{:S(2)}, u32[]{:S(2)}) collective-permute-start(bf16[4,64,128]{2,1,0:T(8,128)(2,1)S(1)} %get-tuple-element.41), channel_id=1, source_target_pairs={{0,1},{2,3},{4,5},{6,7},{1,0},{3,2},{5,4},{7,6},{8,9},{10,11},{12,... | collective-permute-start | bytes 196616 | tf_op jit(solution)/shard_map/ppermute | solution.py:23
  19.2 7.0 %collective-permute-start.5 = (bf16[4,64,128]{2,1,0:T(8,128)(2,1)S(1)}, bf16[4,64,128]{2,1,0:T(8,128)(2,1)S(1)}, u32[]{:S(2)}, u32[]{:S(2)}) collective-permute-start(bf16[4,64,128]{2,1,0:T(8,128)(2,1)S(1)} %get-tuple-element.42), channel_id=1, source_target_pairs={{1,2},{3,4},{5,6},{7,0},{2,1},{4,3},{6,5},{0,7},{9,10},{11,12},{13... | collective-permute-start | bytes 196616 | tf_op jit(solution)/shard_map/ppermute | solution.py:23
  19.9 6.2 %collective-permute-start.6 = (bf16[4,64,128]{2,1,0:T(8,128)(2,1)S(1)}, bf16[4,64,128]{2,1,0:T(8,128)(2,1)S(1)}, u32[]{:S(2)}, u32[]{:S(2)}) collective-permute-start(bf16[4,64,128]{2,1,0:T(8,128)(2,1)S(1)} %get-tuple-element.43), channel_id=1, source_target_pairs={{0,8},{8,0},{16,24},{24,16},{1,9},{9,1},{17,25},{25,17},{2,10},{10... | collective-permute-start | bytes 196616 | tf_op jit(solution)/shard_map/ppermute | solution.py:17
  26.4 8.2 %collective-permute-start.8 = (bf16[8,64,128]{2,1,0:T(8,128)(2,1)S(1)}, bf16[8,64,128]{2,1,0:T(8,128)(2,1)S(1)}, u32[]{:S(2)}, u32[]{:S(2)}) collective-permute-start(bf16[8,64,128]{2,1,0:T(8,128)(2,1)S(1)} %shard_map.78), channel_id=1, source_target_pairs={{0,16},{8,24},{16,0},{24,8},{1,17},{9,25},{17,1},{25,9},{2,18},{10... | collective-permute-start | bytes 393224 | tf_op jit(solution)/shard_map/ppermute | solution.py:17
  31.5 5.0 %collective-permute-start.7 = (bf16[8,64,128]{2,1,0:T(8,128)(2,1)S(1)}, bf16[8,64,128]{2,1,0:T(8,128)(2,1)S(1)}, u32[]{:S(2)}, u32[]{:S(2)}) collective-permute-start(bf16[8,64,128]{2,1,0:T(8,128)(2,1)S(1)} %get-tuple-element.44), channel_id=1, source_target_pairs={{0,16},{8,24},{16,0},{24,8},{1,17},{9,25},{17,1},{25,9},{2,18},{10... | collective-permute-start | bytes 393224 | tf_op jit(solution)/shard_map/ppermute | solution.py:17
  39.1 3.2 %collective-permute-start.11 = (bf16[4,64,128]{2,1,0:T(8,128)(2,1)S(1)}, bf16[4,64,128]{2,1,0:T(8,128)(2,1)S(1)}, u32[]{:S(2)}, u32[]{:S(2)}) collective-permute-start(bf16[4,64,128]{2,1,0:T(8,128)(2,1)S(1)} %get-tuple-element.50), channel_id=1, source_target_pairs={{0,8},{8,0},{16,24},{24,16},{1,9},{9,1},{17,25},{25,17},{2,10},{10... | collective-permute-start | bytes 196616 | tf_op jit(solution)/shard_map/ppermute | solution.py:17
  39.2 4.5 %collective-permute-start.9 = (bf16[4,64,128]{2,1,0:T(8,128)(2,1)S(1)}, bf16[4,64,128]{2,1,0:T(8,128)(2,1)S(1)}, u32[]{:S(2)}, u32[]{:S(2)}) collective-permute-start(bf16[4,64,128]{2,1,0:T(8,128)(2,1)S(1)} %get-tuple-element.48), channel_id=1, source_target_pairs={{0,1},{2,3},{4,5},{6,7},{1,0},{3,2},{5,4},{7,6},{8,9},{10,11},{12,... | collective-permute-start | bytes 196616 | tf_op jit(solution)/shard_map/ppermute | solution.py:23
  39.3 7.1 %collective-permute-start.10 = (bf16[4,64,128]{2,1,0:T(8,128)(2,1)S(1)}, bf16[4,64,128]{2,1,0:T(8,128)(2,1)S(1)}, u32[]{:S(2)}, u32[]{:S(2)}) collective-permute-start(bf16[4,64,128]{2,1,0:T(8,128)(2,1)S(1)} %get-tuple-element.49), channel_id=1, source_target_pairs={{1,2},{3,4},{5,6},{7,0},{2,1},{4,3},{6,5},{0,7},{9,10},{11,12},{13... | collective-permute-start | bytes 196616 | tf_op jit(solution)/shard_map/ppermute | solution.py:23
  47.7 6.4 %collective-permute-start.12 = (bf16[8,64,128]{2,1,0:T(8,128)(2,1)S(1)}, bf16[8,64,128]{2,1,0:T(8,128)(2,1)S(1)}, u32[]{:S(2)}, u32[]{:S(2)}) collective-permute-start(bf16[8,64,128]{2,1,0:T(8,128)(2,1)S(1)} %get-tuple-element.54), channel_id=1, source_target_pairs={{0,16},{8,24},{16,0},{24,8},{1,17},{9,25},{17,1},{25,9},{2,18},{10... | collective-permute-start | bytes 393224 | tf_op jit(solution)/shard_map/ppermute | solution.py:17
  49.0 6.5 %collective-permute-start.13 = (bf16[8,64,128]{2,1,0:T(8,128)(2,1)S(1)}, bf16[8,64,128]{2,1,0:T(8,128)(2,1)S(1)}, u32[]{:S(2)}, u32[]{:S(2)}) collective-permute-start(bf16[8,64,128]{2,1,0:T(8,128)(2,1)S(1)} %get-tuple-element.55), channel_id=1, source_target_pairs={{0,16},{8,24},{16,0},{24,8},{1,17},{9,25},{17,1},{25,9},{2,18},{10... | collective-permute-start | bytes 393224 | tf_op jit(solution)/shard_map/ppermute | solution.py:17
  56.4 3.2 %collective-permute-start.16 = (bf16[4,64,128]{2,1,0:T(8,128)(2,1)S(1)}, bf16[4,64,128]{2,1,0:T(8,128)(2,1)S(1)}, u32[]{:S(2)}, u32[]{:S(2)}) collective-permute-start(bf16[4,64,128]{2,1,0:T(8,128)(2,1)S(1)} %get-tuple-element.62), channel_id=1, source_target_pairs={{0,8},{8,0},{16,24},{24,16},{1,9},{9,1},{17,25},{25,17},{2,10},{10... | collective-permute-start | bytes 196616 | tf_op jit(solution)/shard_map/ppermute | solution.py:17
  56.5 4.5 %collective-permute-start.14 = (bf16[4,64,128]{2,1,0:T(8,128)(2,1)S(1)}, bf16[4,64,128]{2,1,0:T(8,128)(2,1)S(1)}, u32[]{:S(2)}, u32[]{:S(2)}) collective-permute-start(bf16[4,64,128]{2,1,0:T(8,128)(2,1)S(1)} %get-tuple-element.60), channel_id=1, source_target_pairs={{0,1},{2,3},{4,5},{6,7},{1,0},{3,2},{5,4},{7,6},{8,9},{10,11},{12,... | collective-permute-start | bytes 196616 | tf_op jit(solution)/shard_map/ppermute | solution.py:23
  56.6 7.1 %collective-permute-start.15 = (bf16[4,64,128]{2,1,0:T(8,128)(2,1)S(1)}, bf16[4,64,128]{2,1,0:T(8,128)(2,1)S(1)}, u32[]{:S(2)}, u32[]{:S(2)}) collective-permute-start(bf16[4,64,128]{2,1,0:T(8,128)(2,1)S(1)} %get-tuple-element.61), channel_id=1, source_target_pairs={{1,2},{3,4},{5,6},{7,0},{2,1},{4,3},{6,5},{0,7},{9,10},{11,12},{13... | collective-permute-start | bytes 196616 | tf_op jit(solution)/shard_map/ppermute | solution.py:23
  63.8 8.3 %collective-permute-start.17 = (bf16[8,64,128]{2,1,0:T(8,128)(2,1)S(1)}, bf16[8,64,128]{2,1,0:T(8,128)(2,1)S(1)}, u32[]{:S(2)}, u32[]{:S(2)}) collective-permute-start(bf16[8,64,128]{2,1,0:T(8,128)(2,1)S(1)} %get-tuple-element.63), channel_id=1, source_target_pairs={{0,16},{8,24},{16,0},{24,8},{1,17},{9,25},{17,1},{25,9},{2,18},{10... | collective-permute-start | bytes 393224 | tf_op jit(solution)/shard_map/ppermute | solution.py:17
  68.1 5.7 %collective-permute-start.18 = (bf16[8,64,128]{2,1,0:T(8,128)(2,1)S(1)}, bf16[8,64,128]{2,1,0:T(8,128)(2,1)S(1)}, u32[]{:S(2)}, u32[]{:S(2)}) collective-permute-start(bf16[8,64,128]{2,1,0:T(8,128)(2,1)S(1)} %get-tuple-element.65), channel_id=1, source_target_pairs={{0,16},{8,24},{16,0},{24,8},{1,17},{9,25},{17,1},{25,9},{2,18},{10... | collective-permute-start | bytes 393224 | tf_op jit(solution)/shard_map/ppermute | solution.py:17

commit v11 on v8

--- a/solution.py
+++ b/solution.py
@@ -8,7 +8,7 @@
 ITERS = 2
 LIMIT = 16 << 20
 LANES = 128
-SHARES = (0, 3, 11, 16)
+SHARES = (0, 8, 16)
 VMEM = pl.BlockSpec(memory_space=pltpu.VMEM)
 HBM = pl.BlockSpec(memory_space=pltpu.HBM)
 NT = (((1,), (1,)), ((), ()))
@@ -307,6 +307,7 @@
 
     def swap_both(odd, even):
         odd = swapped(odd, "dom", 1)
+        even = even()
         even = swapped(even, "dom", 0)
         return even, odd
 
@@ -315,7 +316,7 @@
 
     even = lax.axis_index("dom") % 2 == 0
     wanted_even, wanted_odd = swap_both(
-        spread(jnp.where(even, left_list, right_list)), spread(jnp.where(even, right_list, left_list))
+        spread(jnp.where(even, left_list, right_list)), lambda: spread(jnp.where(even, right_list, left_list))
     )
     wanted_beside = swap_beside(spread(sibling_list))
     columns = level_cols.reshape(-1)
@@ -333,14 +334,17 @@
 
     def exchanged(bodies, fixed, pieces, rest, joins, scratch):
         listed_body, body = bodies
-        each = len(pieces[0])
-        odd, even, *whole = call(
-            lambda *refs: listed_body(2, each, *refs), (listed,) * 2 + joins,
-            *fixed, wanted_odd, wanted_even, *sum(pieces, []), *rest,
-            scratch=[held(2 * list_width)] * scratch,
-        )
-        even, odd = swap_both(odd, even)
+
+        def listed_rows(wanted, pieces, joins):
+            each = len(pieces[0])
+            return call(
+                lambda *refs: listed_body(1, each, *refs), (listed,) + joins,
+                *fixed, wanted, *sum(pieces, []), *rest, scratch=[held(list_width)] * scratch,
+            )
+
+        odd, *whole = listed_rows(wanted_odd, pieces, joins)
         whole = whole or sum(pieces, [])
+        even, odd = swap_both(odd, lambda: listed_rows(wanted_even, [[x] for x in whole], ())[0])
         *results, beside = call(body, (wide, narrow, listed), *fixed, wanted_beside, *whole, *rest)
         return (*results, (even, odd, swap_beside(beside)))
 

time: 77.8 us -> 78.3 us (level)
  waiting for transfers between devices: 25.6 us -> 29.1 us
  starting transfers between devices: 31.1 us -> 28 us
    ppermute x14 -> x11, waiting for transfers between devices: 10.9 us -> 14.6 us  [partner(): lax.ppermute(x, axis, [(i, i ^ 1 << apart) for i in range(lax.axis_size(a...]
    ppermute x14 -> x11, starting transfers between devices: 17.4 us -> 13.7 us  [partner(): lax.ppermute(x, axis, [(i, i ^ 1 << apart) for i in range(lax.axis_size(a...]
  transfers between devices with their start and end apart: 22 -> 19, of which waited for: 10 -> 13; matrix products, arithmetic and copies ran while one was open for 1% -> 1% of each run, Pallas kernels for 14% -> 15%
where the time goes in v11:
time: 78.3 us; the launch traced here: 78.1 us
  waiting for transfers between devices  29.1 us (37%)
  starting transfers between devices  28 us (36%)
  Pallas kernels  19 us (24%)
  other arithmetic  0.79 us (1%)
    pallas_call x20, Pallas kernels, call(): pl.pallas_call(body, out_shape=outs, in_specs=in_specs or [VMEM] * len(ar...  19 us
    ppermute x11, waiting for transfers between devices, partner(): lax.ppermute(x, axis, [(i, i ^ 1 << apart) for i in range(lax.axis_size(a...  14.6 us
    ppermute x8, waiting for transfers between devices, swapped(): return lax.ppermute(x, axis, pairs + [(b, a) for a, b in pairs])  14.5 us
    ppermute x8, starting transfers between devices, swapped(): return lax.ppermute(x, axis, pairs + [(b, a) for a, b in pairs])  14.3 us
    ppermute x11, starting transfers between devices, partner(): lax.ppermute(x, axis, [(i, i ^ 1 << apart) for i in range(lax.axis_size(a...  13.7 us
  transfers between devices with their start and end apart: 19, of which 13 were waited for; matrix products, arithmetic and copies ran while one was open for 1% of the time, Pallas kernels for 15%

profile of v11, /device:TPU:0, one launch (start us, length us, event | category | flops | bytes accessed | tf_op | source)
XLA Modules:
  0.0 78.1 jit_solution(13430967521919209753)
XLA Ops:
  0.0 0.7 fusion.4
  0.7 0.1 broadcast_in_dim.52
  0.8 6.0 %collective-permute-start.1 = (s32[4,128]{1,0:T(4,128)S(1)}, s32[4,128]{1,0:T(4,128)S(1)}, u32[]{:S(2)}, u32[]{:S(2)}) collective-permute-start(s32[4,128]{1,0:T(4,128)S(1)} %broadcast_in_dim.52), channel_id=1, source_target_pairs={{1,2},{3,4},{5,6},{7,0},{2,1},{4,3},{6,5},{0,7},{9,10},{11,12},{13... | collective-permute-start | bytes 6152 | tf_op jit(solution)/shard_map/ppermute | solution.py:24
  6.8 0.1 broadcast_in_dim.51
  6.9 0.0 collective-permute-start
  6.9 0.1 broadcast_in_dim.53
  6.9 1.2 %shard_map.73 = (f32[16,64,128]{2,1,0:T(8,128)S(1)}, bf16[16,64,128]{2,1,0:T(8,128)(2,1)S(1)}) custom-call(f32[64,2048]{1,0:T(8,128)} %bitcast.35), custom_call_target="tpu_custom_call" | custom-call | flops 5000000000 | bytes 1048576 | tf_op jit(solution)/shard_map/pallas_call | solution.py:39
  8.1 1.6 %collective-permute-start.2 = (bf16[16,64,128]{2,1,0:T(8,128)(2,1)S(1)}, bf16[16,64,128]{2,1,0:T(8,128)(2,1)S(1)}, u32[]{:S(2)}, u32[]{:S(2)}) collective-permute-start(bf16[16,64,128]{2,1,0:T(8,128)(2,1)S(1)} %get-tuple-element.34), channel_id=1, source_target_pairs={{0,16},{8,24},{16,0},{24,8},{1,17},{9,25},{17,1},{25,9},{2,18},{10... | collective-permute-start | bytes 786440 | tf_op jit(solution)/shard_map/ppermute | solution.py:18
  9.7 0.1 copy.10
  9.8 0.1 reshape.46
  9.9 0.1 copy.9
  9.9 0.1 reshape.43
  10.1 0.0 copy-start
  10.1 2.3 %shard_map.74.transfer.refs_5_.refs_0_.refs_4_.refs_7_.refs_6_ = bf16[16,8,128,128]{3,2,1,0:T(8,128)(2,1)S(1)} custom-call(f32[64,2048]{1,0:T(8,128)} %bitcast.36, bf16[16,8,128,128]{3,2,1,0:T(8,128)(2,1)} %bitcast.34), custom_call_target="tpu_custom_call" | custom-call | flops 570425344 | bytes 8912896 | tf_op jit(solution)/shard_map/pallas_call | solution.py:39
  12.4 4.5 %collective-permute-done.2.arrived.refs_4_ = bf16[16,64,128]{2,1,0:T(8,128)(2,1)S(1)} collective-permute-done((bf16[16,64,128]{2,1,0:T(8,128)(2,1)S(1)}, bf16[16,64,128]{2,1,0:T(8,128)(2,1)S(1)}, u32[]{:S(2)}, u32[]{:S(2)}) %collective-permute-start.2) | collective-permute-done | bytes 262176 | tf_op jit(solution)/shard_map/ppermute | solution.py:18
  16.9 0.1 broadcast_in_dim.46.table.refs_0_
  17.0 0.0 copy-done
  17.0 0.0 slice-start
  17.0 0.3 shard_map.76
  17.3 0.0 slice-start.1
  17.3 1.8 %collective-permute-start.4 = (bf16[4,64,128]{2,1,0:T(8,128)(2,1)S(1)}, bf16[4,64,128]{2,1,0:T(8,128)(2,1)S(1)}, u32[]{:S(2)}, u32[]{:S(2)}) collective-permute-start(bf16[4,64,128]{2,1,0:T(8,128)(2,1)S(1)} %shard_map.76), channel_id=1, source_target_pairs={{0,1},{2,3},{4,5},{6,7},{1,0},{3,2},{5,4},{7,6},{8,9},{10,11},{12,... | collective-permute-start | bytes 196616 | tf_op jit(solution)/shard_map/ppermute | solution.py:24
  19.1 0.3 shard_map.77
  19.4 0.2 collective-permute-start.5
  19.6 0.6 shard_map.75
  20.2 0.1 collective-permute-start.6
  20.3 0.1 pad_add_fusion.1
  20.4 1.3 %collective-permute-done.4.refs_3_ = bf16[4,64,128]{2,1,0:T(8,128)(2,1)S(1)} collective-permute-done((bf16[4,64,128]{2,1,0:T(8,128)(2,1)S(1)}, bf16[4,64,128]{2,1,0:T(8,128)(2,1)S(1)}, u32[]{:S(2)}, u32[]{:S(2)}) %collective-permute-start.4) | collective-permute-done | bytes 65568 | tf_op jit(solution)/shard_map/ppermute | solution.py:24
  21.6 4.8 %collective-permute-done.5.refs_4_ = bf16[4,64,128]{2,1,0:T(8,128)(2,1)S(1)} collective-permute-done((bf16[4,64,128]{2,1,0:T(8,128)(2,1)S(1)}, bf16[4,64,128]{2,1,0:T(8,128)(2,1)S(1)}, u32[]{:S(2)}, u32[]{:S(2)}) %collective-permute-start.5) | collective-permute-done | bytes 65568 | tf_op jit(solution)/shard_map/ppermute | solution.py:24
  26.4 0.1 broadcast_in_dim.49.refs_0_.table
  26.5 0.1 shard_map.78
  26.7 5.2 %collective-permute-start.8 = (bf16[8,64,128]{2,1,0:T(8,128)(2,1)S(1)}, bf16[8,64,128]{2,1,0:T(8,128)(2,1)S(1)}, u32[]{:S(2)}, u32[]{:S(2)}) collective-permute-start(bf16[8,64,128]{2,1,0:T(8,128)(2,1)S(1)} %shard_map.79), channel_id=1, source_target_pairs={{0,16},{8,24},{16,0},{24,8},{1,17},{9,25},{17,1},{25,9},{2,18},{10... | collective-permute-start | bytes 393224 | tf_op jit(solution)/shard_map/ppermute | solution.py:18
  31.9 0.1 collective-permute-start.7
  31.9 2.6 %shard_map.80.refs_4_.correction.refs_3_ = f32[16,64,128]{2,1,0:T(8,128)S(1)} custom-call(s32[193,128]{1,0:T(8,128)S(1)} %broadcast_in_dim.49.refs_0_.table, f32[16,64,128]{2,1,0:T(8,128)S(1)} %get-tuple-element.35.refs_1_.current, bf16[16,64,128]{2,1,0:T(8,128)(2,1)S(1)} %get-tuple-element.36.refs_2_.first, ...), custom_call_target="tpu_custom_call" | custom-call | flops 555778048 | bytes 8684032 | tf_op jit(solution)/shard_map/pallas_call | solution.py:39
  34.5 0.4 collective-permute-done.8.refs_3_
  34.9 1.9 %collective-permute-done.7.refs_2_ = bf16[8,64,128]{2,1,0:T(8,128)(2,1)S(1)} collective-permute-done((bf16[8,64,128]{2,1,0:T(8,128)(2,1)S(1)}, bf16[8,64,128]{2,1,0:T(8,128)(2,1)S(1)}, u32[]{:S(2)}, u32[]{:S(2)}) %collective-permute-start.7) | collective-permute-done | bytes 131104 | tf_op jit(solution)/shard_map/ppermute | solution.py:18
  36.8 0.6 shard_map.81
  37.4 1.7 %shard_map.82 = (f32[16,64,128]{2,1,0:T(8,128)S(1)}, bf16[16,64,128]{2,1,0:T(8,128)(2,1)S(1)}, bf16[4,64,128]{2,1,0:T(8,128)(2,1)S(1)}) custom-call(s32[129,128]{1,0:T(8,128)S(1)} %broadcast_in_dim.46.table.refs_0_, s32[4,128]{1,0:T(4,128)S(1)} %collective-permute-done.wanted, bf16[16,64,128]{2,1,0:T(8,128)(2,1)S(1)} %get-tuple-element.40.arrived.refs_2_, ...), custom_call_target="tpu_custom_call" | custom-call | flops 377651200 | bytes 5900800 | tf_op jit(solution)/shard_map/pallas_call | solution.py:39
  39.1 0.1 collective-permute-start.11
  39.2 0.6 shard_map.83
  39.7 0.1 collective-permute-start.9
  39.8 3.0 %collective-permute-start.10 = (bf16[4,64,128]{2,1,0:T(8,128)(2,1)S(1)}, bf16[4,64,128]{2,1,0:T(8,128)(2,1)S(1)}, u32[]{:S(2)}, u32[]{:S(2)}) collective-permute-start(bf16[4,64,128]{2,1,0:T(8,128)(2,1)S(1)} %get-tuple-element.42), channel_id=1, source_target_pairs={{1,2},{3,4},{5,6},{7,0},{2,1},{4,3},{6,5},{0,7},{9,10},{11,12},{13... | collective-permute-start | bytes 196616 | tf_op jit(solution)/shard_map/ppermute | solution.py:24
  42.9 1.4 %collective-permute-done.9.refs_3_ = bf16[4,64,128]{2,1,0:T(8,128)(2,1)S(1)} collective-permute-done((bf16[4,64,128]{2,1,0:T(8,128)(2,1)S(1)}, bf16[4,64,128]{2,1,0:T(8,128)(2,1)S(1)}, u32[]{:S(2)}, u32[]{:S(2)}) %collective-permute-start.9) | collective-permute-done | bytes 65568 | tf_op jit(solution)/shard_map/ppermute | solution.py:24
  44.3 2.8 %collective-permute-done.10.refs_4_ = bf16[4,64,128]{2,1,0:T(8,128)(2,1)S(1)} collective-permute-done((bf16[4,64,128]{2,1,0:T(8,128)(2,1)S(1)}, bf16[4,64,128]{2,1,0:T(8,128)(2,1)S(1)}, u32[]{:S(2)}, u32[]{:S(2)}) %collective-permute-start.10) | collective-permute-done | bytes 65568 | tf_op jit(solution)/shard_map/ppermute | solution.py:24
  47.1 1.3 %shard_map.84 = (bf16[8,64,128]{2,1,0:T(8,128)(2,1)S(1)}, bf16[28,64,128]{2,1,0:T(8,128)(2,1)S(1)}, f32[8,64,128]{2,1,0:T(8,128)S(1)}) custom-call(s32[193,128]{1,0:T(8,128)S(1)} %broadcast_in_dim.49.refs_0_.table, f32[16,64,128]{2,1,0:T(8,128)S(1)} %get-tuple-element.33.loads.residual.refs_1_.refs_3_, bf16[16,64,128]{2,1,0:T(8,128)(2,1)S(1)} %get-tuple-element.41.refs_2_, ...), custom_call_target="tpu_custom_call" | custom-call | flops 526417920 | bytes 8225280 | tf_op jit(solution)/shard_map/pallas_call | solution.py:39
  48.3 0.1 collective-permute-start.12
  48.4 1.2 %shard_map.85 = (bf16[8,64,128]{2,1,0:T(8,128)(2,1)S(1)}, f32[8,64,128]{2,1,0:T(8,128)S(1)}) custom-call(s32[193,128]{1,0:T(8,128)S(1)} %broadcast_in_dim.49.refs_0_.table, f32[16,64,128]{2,1,0:T(8,128)S(1)} %get-tuple-element.33.loads.residual.refs_1_.refs_3_, bf16[28,64,128]{2,1,0:T(8,128)(2,1)S(1)} %get-tuple-element.45.refs_2_, ...), custom_call_target="tpu_custom_call" | custom-call | flops 497057792 | bytes 7766528 | tf_op jit(solution)/shard_map/pallas_call | solution.py:39
  49.6 0.9 %collective-permute-start.13 = (bf16[8,64,128]{2,1,0:T(8,128)(2,1)S(1)}, bf16[8,64,128]{2,1,0:T(8,128)(2,1)S(1)}, u32[]{:S(2)}, u32[]{:S(2)}) collective-permute-start(bf16[8,64,128]{2,1,0:T(8,128)(2,1)S(1)} %get-tuple-element.48), channel_id=1, source_target_pairs={{0,16},{8,24},{16,0},{24,8},{1,17},{9,25},{17,1},{25,9},{2,18},{10... | collective-permute-start | bytes 393224 | tf_op jit(solution)/shard_map/ppermute | solution.py:18
  50.5 4.2 %collective-permute-done.12.refs_5_ = bf16[8,64,128]{2,1,0:T(8,128)(2,1)S(1)} collective-permute-done((bf16[8,64,128]{2,1,0:T(8,128)(2,1)S(1)}, bf16[8,64,128]{2,1,0:T(8,128)(2,1)S(1)}, u32[]{:S(2)}, u32[]{:S(2)}) %collective-permute-start.12) | collective-permute-done | bytes 131104 | tf_op jit(solution)/shard_map/ppermute | solution.py:18
  54.8 1.5 %collective-permute-done.13.refs_6_ = bf16[8,64,128]{2,1,0:T(8,128)(2,1)S(1)} collective-permute-done((bf16[8,64,128]{2,1,0:T(8,128)(2,1)S(1)}, bf16[8,64,128]{2,1,0:T(8,128)(2,1)S(1)}, u32[]{:S(2)}, u32[]{:S(2)}) %collective-permute-start.13) | collective-permute-done | bytes 131104 | tf_op jit(solution)/shard_map/ppermute | solution.py:18
  56.2 0.3 shard_map.86
  56.5 0.6 shard_map.87
  57.1 0.1 collective-permute-start.16
  57.2 0.3 shard_map.88
  57.5 0.1 collective-permute-start.14
  57.6 3.0 %collective-permute-start.15 = (bf16[4,64,128]{2,1,0:T(8,128)(2,1)S(1)}, bf16[4,64,128]{2,1,0:T(8,128)(2,1)S(1)}, u32[]{:S(2)}, u32[]{:S(2)}) collective-permute-start(bf16[4,64,128]{2,1,0:T(8,128)(2,1)S(1)} %get-tuple-element.53), channel_id=1, source_target_pairs={{1,2},{3,4},{5,6},{7,0},{2,1},{4,3},{6,5},{0,7},{9,10},{11,12},{13... | collective-permute-start | bytes 196616 | tf_op jit(solution)/shard_map/ppermute | solution.py:24
  60.6 1.4 %collective-permute-done.14.refs_3_ = bf16[4,64,128]{2,1,0:T(8,128)(2,1)S(1)} collective-permute-done((bf16[4,64,128]{2,1,0:T(8,128)(2,1)S(1)}, bf16[4,64,128]{2,1,0:T(8,128)(2,1)S(1)}, u32[]{:S(2)}, u32[]{:S(2)}) %collective-permute-start.14) | collective-permute-done | bytes 65568 | tf_op jit(solution)/shard_map/ppermute | solution.py:24
  62.0 2.8 %collective-permute-done.15.refs_4_ = bf16[4,64,128]{2,1,0:T(8,128)(2,1)S(1)} collective-permute-done((bf16[4,64,128]{2,1,0:T(8,128)(2,1)S(1)}, bf16[4,64,128]{2,1,0:T(8,128)(2,1)S(1)}, u32[]{:S(2)}, u32[]{:S(2)}) %collective-permute-start.15) | collective-permute-done | bytes 65568 | tf_op jit(solution)/shard_map/ppermute | solution.py:24
  64.8 0.2 shard_map.89
  65.1 4.3 %collective-permute-start.17 = (bf16[8,64,128]{2,1,0:T(8,128)(2,1)S(1)}, bf16[8,64,128]{2,1,0:T(8,128)(2,1)S(1)}, u32[]{:S(2)}, u32[]{:S(2)}) collective-permute-start(bf16[8,64,128]{2,1,0:T(8,128)(2,1)S(1)} %get-tuple-element.55), channel_id=1, source_target_pairs={{0,16},{8,24},{16,0},{24,8},{1,17},{9,25},{17,1},{25,9},{2,18},{10... | collective-permute-start | bytes 393224 | tf_op jit(solution)/shard_map/ppermute | solution.py:18
  69.4 1.4 %collective-permute-start.18 = (bf16[8,64,128]{2,1,0:T(8,128)(2,1)S(1)}, bf16[8,64,128]{2,1,0:T(8,128)(2,1)S(1)}, u32[]{:S(2)}, u32[]{:S(2)}) collective-permute-start(bf16[8,64,128]{2,1,0:T(8,128)(2,1)S(1)} %get-tuple-element.57), channel_id=1, source_target_pairs={{0,16},{8,24},{16,0},{24,8},{1,17},{9,25},{17,1},{25,9},{2,18},{10... | collective-permute-start | bytes 393224 | tf_op jit(solution)/shard_map/ppermute | solution.py:18
  70.8 2.6 %shard_map.91.refs_4_ = f32[16,64,128]{2,1,0:T(8,128)S(1)} custom-call(s32[193,128]{1,0:T(8,128)S(1)} %broadcast_in_dim.49.refs_0_.table, f32[16,64,128]{2,1,0:T(8,128)S(1)} %get-tuple-element.51.refs_1_.current, bf16[16,64,128]{2,1,0:T(8,128)(2,1)S(1)} %get-tuple-element.52.refs_2_.first, bf16[28,64,128]{2,1,0:T(8,128)(2,1)S(1)} %get-tuple-element.56.refs_3_.extension, ...), custom_call_target="tpu_custom_call" | custom-call | flops 555778048 | bytes 8684032 | tf_op jit(solution)/shard_map/pallas_call | solution.py:39
  73.4 0.3 collective-permute-done.17.refs_0_
  73.7 1.8 %collective-permute-done.18.refs_1_ = bf16[8,64,128]{2,1,0:T(8,128)(2,1)S(1)} collective-permute-done((bf16[8,64,128]{2,1,0:T(8,128)(2,1)S(1)}, bf16[8,64,128]{2,1,0:T(8,128)(2,1)S(1)}, u32[]{:S(2)}, u32[]{:S(2)}) %collective-permute-start.18) | collective-permute-done | bytes 131104 | tf_op jit(solution)/shard_map/ppermute | solution.py:18
  75.5 2.5 %shard_map.92 = f32[64,2048]{1,0:T(8,128)} custom-call(s32[129,128]{1,0:T(8,128)S(1)} %broadcast_in_dim.46.table.refs_0_, bf16[8,64,128]{2,1,0:T(8,128)(2,1)S(1)} %collective-permute-done.17.refs_0_, bf16[8,64,128]{2,1,0:T(8,128)(2,1)S(1)} %collective-permute-done.18.refs_1_, f32[8,64,128]{2,1,0:T(8,128)S(1)} %get-tuple-element.58.refs_2_, ...), custom_call_target="tpu_custom_call" | custom-call | flops 423657472 | bytes 6619648 | tf_op jit(solution)/shard_map/pallas_call | solution.py:39
  (18 shorter events, 0.1 us)
Async XLA Ops:
  0.8 18.3 %collective-permute-start.1 = (s32[4,128]{1,0:T(4,128)S(1)}, s32[4,128]{1,0:T(4,128)S(1)}, u32[]{:S(2)}, u32[]{:S(2)}) collective-permute-start(s32[4,128]{1,0:T(4,128)S(1)} %broadcast_in_dim.52), channel_id=1, source_target_pairs={{1,2},{3,4},{5,6},{7,0},{2,1},{4,3},{6,5},{0,7},{9,10},{11,12},{13... | collective-permute-start | bytes 6152 | tf_op jit(solution)/shard_map/ppermute | solution.py:24
  6.9 12.7 %collective-permute-start = (s32[4,128]{1,0:T(4,128)S(1)}, s32[4,128]{1,0:T(4,128)S(1)}, u32[]{:S(2)}, u32[]{:S(2)}) collective-permute-start(s32[4,128]{1,0:T(4,128)S(1)} %broadcast_in_dim.51), channel_id=1, source_target_pairs={{0,8},{8,0},{16,24},{24,16},{1,9},{9,1},{17,25},{25,17},{2,10},{10... | collective-permute-start | bytes 6152 | tf_op jit(solution)/shard_map/ppermute | solution.py:18
  6.9 5.5 %collective-permute-start.3 = (s32[4,128]{1,0:T(4,128)S(1)}, s32[4,128]{1,0:T(4,128)S(1)}, u32[]{:S(2)}, u32[]{:S(2)}) collective-permute-start(s32[4,128]{1,0:T(4,128)S(1)} %broadcast_in_dim.53), channel_id=1, source_target_pairs={{0,1},{2,3},{4,5},{6,7},{1,0},{3,2},{5,4},{7,6},{8,9},{10,11},{12,... | collective-permute-start | bytes 6152 | tf_op jit(solution)/shard_map/ppermute | solution.py:24
  6.9 2.7 %copy-start.1 = (s32[1,16,12]{1,0,2:T(1,128)S(1)}, s32[1,16,12]{1,0,2:T(1,128)}, u32[]{:S(2)}) copy-start(s32[1,16,12]{1,0,2:T(1,128)} %param.9) | copy-start | bytes 2308
  6.9 2.9 %copy-start.2 = (s32[1,16,8]{1,2,0:T(8,128)S(1)}, s32[1,16,8]{1,2,0:T(8,128)}, u32[]{:S(2)}) copy-start(s32[1,16,8]{1,2,0:T(8,128)} %param.12) | copy-start | bytes 1540
  8.1 8.8 %collective-permute-start.2 = (bf16[16,64,128]{2,1,0:T(8,128)(2,1)S(1)}, bf16[16,64,128]{2,1,0:T(8,128)(2,1)S(1)}, u32[]{:S(2)}, u32[]{:S(2)}) collective-permute-start(bf16[16,64,128]{2,1,0:T(8,128)(2,1)S(1)} %get-tuple-element.34), channel_id=1, source_target_pairs={{0,16},{8,24},{16,0},{24,8},{1,17},{9,25},{17,1},{25,9},{2,18},{10... | collective-permute-start | bytes 786440 | tf_op jit(solution)/shard_map/ppermute | solution.py:18
  10.1 6.9 %copy-start = (bf16[1,16,128,128]{3,2,1,0:T(8,128)(2,1)S(1)}, bf16[1,16,128,128]{3,2,1,0:T(8,128)(2,1)}, u32[]{:S(2)}) copy-start(bf16[1,16,128,128]{3,2,1,0:T(8,128)(2,1)} %param.10) | copy-start | bytes 1572868
  17.0 9.5 %slice-start = ((s8[6291456]{0:T(1024)(128)(4,1)}), s8[4194304]{0:T(1024)(128)(4,1)S(1)}, s32[]{:S(2)}) async-start(s8[6291456]{0:T(1024)(128)(4,1)} %bitcast.12), calls=%async_computation | async-start | bytes 8388608
  17.3 9.2 %slice-start.1 = ((s8[6291456]{0:T(1024)(128)(4,1)}), s8[2097152]{0:T(1024)(128)(4,1)S(1)}, s32[]{:S(2)}) async-start(s8[6291456]{0:T(1024)(128)(4,1)} %bitcast.12), calls=%async_computation.1 | async-start | bytes 4194304
  17.3 4.3 %collective-permute-start.4 = (bf16[4,64,128]{2,1,0:T(8,128)(2,1)S(1)}, bf16[4,64,128]{2,1,0:T(8,128)(2,1)S(1)}, u32[]{:S(2)}, u32[]{:S(2)}) collective-permute-start(bf16[4,64,128]{2,1,0:T(8,128)(2,1)S(1)} %shard_map.76), channel_id=1, source_target_pairs={{0,1},{2,3},{4,5},{6,7},{1,0},{3,2},{5,4},{7,6},{8,9},{10,11},{12,... | collective-permute-start | bytes 196616 | tf_op jit(solution)/shard_map/ppermute | solution.py:24
  19.4 7.0 %collective-permute-start.5 = (bf16[4,64,128]{2,1,0:T(8,128)(2,1)S(1)}, bf16[4,64,128]{2,1,0:T(8,128)(2,1)S(1)}, u32[]{:S(2)}, u32[]{:S(2)}) collective-permute-start(bf16[4,64,128]{2,1,0:T(8,128)(2,1)S(1)} %shard_map.77), channel_id=1, source_target_pairs={{1,2},{3,4},{5,6},{7,0},{2,1},{4,3},{6,5},{0,7},{9,10},{11,12},{13... | collective-permute-start | bytes 196616 | tf_op jit(solution)/shard_map/ppermute | solution.py:24
  20.2 6.2 %collective-permute-start.6 = (bf16[4,64,128]{2,1,0:T(8,128)(2,1)S(1)}, bf16[4,64,128]{2,1,0:T(8,128)(2,1)S(1)}, u32[]{:S(2)}, u32[]{:S(2)}) collective-permute-start(bf16[4,64,128]{2,1,0:T(8,128)(2,1)S(1)} %get-tuple-element.37), channel_id=1, source_target_pairs={{0,8},{8,0},{16,24},{24,16},{1,9},{9,1},{17,25},{25,17},{2,10},{10... | collective-permute-start | bytes 196616 | tf_op jit(solution)/shard_map/ppermute | solution.py:18
  26.7 8.3 %collective-permute-start.8 = (bf16[8,64,128]{2,1,0:T(8,128)(2,1)S(1)}, bf16[8,64,128]{2,1,0:T(8,128)(2,1)S(1)}, u32[]{:S(2)}, u32[]{:S(2)}) collective-permute-start(bf16[8,64,128]{2,1,0:T(8,128)(2,1)S(1)} %shard_map.79), channel_id=1, source_target_pairs={{0,16},{8,24},{16,0},{24,8},{1,17},{9,25},{17,1},{25,9},{2,18},{10... | collective-permute-start | bytes 393224 | tf_op jit(solution)/shard_map/ppermute | solution.py:18
  31.9 5.0 %collective-permute-start.7 = (bf16[8,64,128]{2,1,0:T(8,128)(2,1)S(1)}, bf16[8,64,128]{2,1,0:T(8,128)(2,1)S(1)}, u32[]{:S(2)}, u32[]{:S(2)}) collective-permute-start(bf16[8,64,128]{2,1,0:T(8,128)(2,1)S(1)} %get-tuple-element.38), channel_id=1, source_target_pairs={{0,16},{8,24},{16,0},{24,8},{1,17},{9,25},{17,1},{25,9},{2,18},{10... | collective-permute-start | bytes 393224 | tf_op jit(solution)/shard_map/ppermute | solution.py:18
  39.1 3.8 %collective-permute-start.11 = (bf16[4,64,128]{2,1,0:T(8,128)(2,1)S(1)}, bf16[4,64,128]{2,1,0:T(8,128)(2,1)S(1)}, u32[]{:S(2)}, u32[]{:S(2)}) collective-permute-start(bf16[4,64,128]{2,1,0:T(8,128)(2,1)S(1)} %get-tuple-element.43), channel_id=1, source_target_pairs={{0,8},{8,0},{16,24},{24,16},{1,9},{9,1},{17,25},{25,17},{2,10},{10... | collective-permute-start | bytes 196616 | tf_op jit(solution)/shard_map/ppermute | solution.py:18
  39.7 4.6 %collective-permute-start.9 = (bf16[4,64,128]{2,1,0:T(8,128)(2,1)S(1)}, bf16[4,64,128]{2,1,0:T(8,128)(2,1)S(1)}, u32[]{:S(2)}, u32[]{:S(2)}) collective-permute-start(bf16[4,64,128]{2,1,0:T(8,128)(2,1)S(1)} %shard_map.83), channel_id=1, source_target_pairs={{0,1},{2,3},{4,5},{6,7},{1,0},{3,2},{5,4},{7,6},{8,9},{10,11},{12,... | collective-permute-start | bytes 196616 | tf_op jit(solution)/shard_map/ppermute | solution.py:24
  39.8 7.3 %collective-permute-start.10 = (bf16[4,64,128]{2,1,0:T(8,128)(2,1)S(1)}, bf16[4,64,128]{2,1,0:T(8,128)(2,1)S(1)}, u32[]{:S(2)}, u32[]{:S(2)}) collective-permute-start(bf16[4,64,128]{2,1,0:T(8,128)(2,1)S(1)} %get-tuple-element.42), channel_id=1, source_target_pairs={{1,2},{3,4},{5,6},{7,0},{2,1},{4,3},{6,5},{0,7},{9,10},{11,12},{13... | collective-permute-start | bytes 196616 | tf_op jit(solution)/shard_map/ppermute | solution.py:24
  48.3 6.4 %collective-permute-start.12 = (bf16[8,64,128]{2,1,0:T(8,128)(2,1)S(1)}, bf16[8,64,128]{2,1,0:T(8,128)(2,1)S(1)}, u32[]{:S(2)}, u32[]{:S(2)}) collective-permute-start(bf16[8,64,128]{2,1,0:T(8,128)(2,1)S(1)} %get-tuple-element.47), channel_id=1, source_target_pairs={{0,16},{8,24},{16,0},{24,8},{1,17},{9,25},{17,1},{25,9},{2,18},{10... | collective-permute-start | bytes 393224 | tf_op jit(solution)/shard_map/ppermute | solution.py:18
  49.6 6.6 %collective-permute-start.13 = (bf16[8,64,128]{2,1,0:T(8,128)(2,1)S(1)}, bf16[8,64,128]{2,1,0:T(8,128)(2,1)S(1)}, u32[]{:S(2)}, u32[]{:S(2)}) collective-permute-start(bf16[8,64,128]{2,1,0:T(8,128)(2,1)S(1)} %get-tuple-element.48), channel_id=1, source_target_pairs={{0,16},{8,24},{16,0},{24,8},{1,17},{9,25},{17,1},{25,9},{2,18},{10... | collective-permute-start | bytes 393224 | tf_op jit(solution)/shard_map/ppermute | solution.py:18
  57.1 3.5 %collective-permute-start.16 = (bf16[4,64,128]{2,1,0:T(8,128)(2,1)S(1)}, bf16[4,64,128]{2,1,0:T(8,128)(2,1)S(1)}, u32[]{:S(2)}, u32[]{:S(2)}) collective-permute-start(bf16[4,64,128]{2,1,0:T(8,128)(2,1)S(1)} %get-tuple-element.54), channel_id=1, source_target_pairs={{0,8},{8,0},{16,24},{24,16},{1,9},{9,1},{17,25},{25,17},{2,10},{10... | collective-permute-start | bytes 196616 | tf_op jit(solution)/shard_map/ppermute | solution.py:18
  57.5 4.6 %collective-permute-start.14 = (bf16[4,64,128]{2,1,0:T(8,128)(2,1)S(1)}, bf16[4,64,128]{2,1,0:T(8,128)(2,1)S(1)}, u32[]{:S(2)}, u32[]{:S(2)}) collective-permute-start(bf16[4,64,128]{2,1,0:T(8,128)(2,1)S(1)} %shard_map.88), channel_id=1, source_target_pairs={{0,1},{2,3},{4,5},{6,7},{1,0},{3,2},{5,4},{7,6},{8,9},{10,11},{12,... | collective-permute-start | bytes 196616 | tf_op jit(solution)/shard_map/ppermute | solution.py:24
  57.6 7.3 %collective-permute-start.15 = (bf16[4,64,128]{2,1,0:T(8,128)(2,1)S(1)}, bf16[4,64,128]{2,1,0:T(8,128)(2,1)S(1)}, u32[]{:S(2)}, u32[]{:S(2)}) collective-permute-start(bf16[4,64,128]{2,1,0:T(8,128)(2,1)S(1)} %get-tuple-element.53), channel_id=1, source_target_pairs={{1,2},{3,4},{5,6},{7,0},{2,1},{4,3},{6,5},{0,7},{9,10},{11,12},{13... | collective-permute-start | bytes 196616 | tf_op jit(solution)/shard_map/ppermute | solution.py:24
  65.1 8.6 %collective-permute-start.17 = (bf16[8,64,128]{2,1,0:T(8,128)(2,1)S(1)}, bf16[8,64,128]{2,1,0:T(8,128)(2,1)S(1)}, u32[]{:S(2)}, u32[]{:S(2)}) collective-permute-start(bf16[8,64,128]{2,1,0:T(8,128)(2,1)S(1)} %get-tuple-element.55), channel_id=1, source_target_pairs={{0,16},{8,24},{16,0},{24,8},{1,17},{9,25},{17,1},{25,9},{2,18},{10... | collective-permute-start | bytes 393224 | tf_op jit(solution)/shard_map/ppermute | solution.py:18
  69.4 6.1 %collective-permute-start.18 = (bf16[8,64,128]{2,1,0:T(8,128)(2,1)S(1)}, bf16[8,64,128]{2,1,0:T(8,128)(2,1)S(1)}, u32[]{:S(2)}, u32[]{:S(2)}) collective-permute-start(bf16[8,64,128]{2,1,0:T(8,128)(2,1)S(1)} %get-tuple-element.57), channel_id=1, source_target_pairs={{0,16},{8,24},{16,0},{24,8},{1,17},{9,25},{17,1},{25,9},{2,18},{10... | collective-permute-start | bytes 393224 | tf_op jit(solution)/shard_map/ppermute | solution.py:18

commit v12 on v10

--- a/solution.py
+++ b/solution.py
@@ -73,23 +73,28 @@
         at += part.shape[0]
 
 
-def open_body(loads, panels, sent, arrivals):
+def panel_copies(loads, panels, arrivals):
     rows, _, width = panels.shape
-    copies = [
-        pltpu.make_async_copy(
-            loads.at[:, pl.ds(i * width, width)], panels.at[i], arrivals.at[i]
-        )
+    return [
+        pltpu.make_async_copy(loads.at[:, pl.ds(i * width, width)], panels.at[i], arrivals.at[i])
         for i in range(rows)
     ]
-    for copy in copies:
-        copy.start()
-    for i, copy in enumerate(copies):
-        copy.wait()
-        sent[i] = panels[i].astype(jnp.bfloat16)
-
-
-def fetch_body(_, source, target, arrivals):
-    copies = [
+
+
+def open_body(table, loads, sent, panels, arrivals):
+    @pl.when(is_fine(table))
+    def _():
+        copies = panel_copies(loads, panels, arrivals)
+        for copy in copies:
+            copy.start()
+        for i, copy in enumerate(copies):
+            copy.wait()
+            sent[i] = panels[i].astype(jnp.bfloat16)
+
+
+def fetch_body(loads, source, panels, target, load_arrivals, arrivals):
+    copies = panel_copies(loads, panels, load_arrivals)
+    copies += [
         pltpu.make_async_copy(source.at[i], target.at[i], arrivals.at[i])
         for i in range(source.shape[0])
     ]
@@ -284,14 +289,16 @@
         return pltpu.VMEM((count, load_cols, width), jnp.bfloat16)
 
     wide, narrow = panels(block_rows, jnp.float32), panels(block_rows, jnp.bfloat16)
-    early_rows = block_rows // 2
+    early_rows = block_rows * 5 // 8
     late_rows = block_rows - early_rows
     listed = panels(list_width, jnp.bfloat16)
     extended = panels(block_rows + 3 * list_width, jnp.bfloat16)
     rowwise = pltpu.SemaphoreType.DMA((block_rows,))
 
-    load_panels, sent = call(
-        open_body, (wide, narrow), inside(loads), in_specs=[HBM], scratch=[rowwise],
+    fine = (lax.axis_index("level") < 2).astype(jnp.int32).reshape(1)
+    sent = call(
+        open_body, narrow, jnp.broadcast_to(fine[:, None], (1, LANES)), inside(loads),
+        in_specs=[VMEM, HBM], scratch=[pltpu.VMEM(wide.shape, jnp.float32), rowwise],
         cost=pl.CostEstimate(flops=5_000_000_000, bytes_accessed=2 * loads.size * 4, transcendentals=0),
     )
     arrived = [partner(sent, "level", 1)]
@@ -317,13 +324,9 @@
     from_right = (columns >= block_rows + list_width) & (columns < block_rows + 2 * list_width)
     moved = jnp.where(from_left, list_width, 0) - jnp.where(from_right, list_width, 0)
     columns = columns + jnp.where(even, moved, 0)
-    fine = (lax.axis_index("level") < 2).astype(jnp.int32).reshape(1)
 
     level_table = spread(jnp.concatenate([columns, fine]))
     transfer_table = spread(jnp.concatenate([transfer_cols.reshape(-1), fine]))
-
-    def fetched(source):
-        return call(fetch_body, like(source), inside(loads), inside(source), in_specs=[HBM, HBM], scratch=[rowwise])
 
     def exchanged(bodies, fixed, pieces, rest, joins, scratch):
         listed_body, body = bodies
@@ -344,7 +347,10 @@
     def sent_on(x):
         return partner(x, "level", 1)
 
-    transfer = fetched(transfer)
+    load_panels, transfer = call(
+        fetch_body, (wide, like(transfer)), inside(loads), inside(transfer),
+        in_specs=[HBM, HBM], scratch=[rowwise, rowwise],
+    )
     residual, iterate = [load_panels], None
     for cycle_index in range(ITERS):
         if cycle_index > 0:

time: 76.7 us -> 75.2 us (0.980)
  starting transfers between devices: 27.7 us -> 26.5 us
    ppermute x11, starting transfers between devices: 13.4 us -> 11.8 us  [partner(): lax.ppermute(x, axis, [(i, i ^ 1 << apart) for i in range(lax.axis_size(a...]
  transfers between devices with their start and end apart: 19 -> 19, of which waited for: 12 -> 10; matrix products, arithmetic and copies ran while one was open for 1% -> 1% of each run, Pallas kernels for 15% -> 15%
where the time goes in v12:
time: 75.2 us; the launch traced here: 75 us
  waiting for transfers between devices  27.5 us (37%)
  starting transfers between devices  26.5 us (35%)
  Pallas kernels  19 us (25%)
  other arithmetic  0.78 us (1%)
    pallas_call x17, Pallas kernels, call(): pl.pallas_call(body, out_shape=outs, in_specs=in_specs or [VMEM] * len(ar...  19 us
    ppermute x8, starting transfers between devices, swapped(): return lax.ppermute(x, axis, pairs + [(b, a) for a, b in pairs])  14.7 us
    ppermute x11, waiting for transfers between devices, partner(): lax.ppermute(x, axis, [(i, i ^ 1 << apart) for i in range(lax.axis_size(a...  13.8 us
    ppermute x8, waiting for transfers between devices, swapped(): return lax.ppermute(x, axis, pairs + [(b, a) for a, b in pairs])  13.7 us
    ppermute x11, starting transfers between devices, partner(): lax.ppermute(x, axis, [(i, i ^ 1 << apart) for i in range(lax.axis_size(a...  11.8 us
  transfers between devices with their start and end apart: 19, of which 10 were waited for; matrix products, arithmetic and copies ran while one was open for 1% of the time, Pallas kernels for 15%

profile of v12, /device:TPU:0, one launch (start us, length us, event | category | flops | bytes accessed | tf_op | source)
XLA Modules:
  0.0 75.0 jit_solution(13580214472833634972)
XLA Ops:
  0.0 0.7 fusion.4
  0.7 0.1 broadcast_in_dim.57
  0.8 6.0 %collective-permute-start.1 = (s32[4,128]{1,0:T(4,128)S(1)}, s32[4,128]{1,0:T(4,128)S(1)}, u32[]{:S(2)}, u32[]{:S(2)}) collective-permute-start(s32[4,128]{1,0:T(4,128)S(1)} %broadcast_in_dim.57), channel_id=1, source_target_pairs={{1,2},{3,4},{5,6},{7,0},{2,1},{4,3},{6,5},{0,7},{9,10},{11,12},{13... | collective-permute-start | bytes 6152 | tf_op jit(solution)/shard_map/ppermute | solution.py:23
  6.8 0.1 broadcast_in_dim.56
  6.9 0.0 collective-permute-start
  6.9 0.1 broadcast_in_dim.58
  7.0 1.2 %shard_map.74 = bf16[16,64,128]{2,1,0:T(8,128)(2,1)S(1)} custom-call(s32[1,128]{1,0:T(1,128)S(1)} %broadcast_in_dim.59.table, f32[64,2048]{1,0:T(8,128)} %bitcast.33), custom_call_target="tpu_custom_call" | custom-call | flops 5000000000 | bytes 1048576 | tf_op jit(solution)/shard_map/pallas_call | solution.py:38
  8.1 0.0 copy-start
  8.2 0.6 collective-permute-start.3
  8.7 0.1 copy.10
  8.8 0.1 reshape.45
  8.9 0.1 copy.9
  9.0 0.1 reshape.43
  9.1 0.0 slice-start
  9.1 2.8 %shard_map.73 = (f32[16,64,128]{2,1,0:T(8,128)S(1)}, bf16[16,8,128,128]{3,2,1,0:T(8,128)(2,1)S(1)}) custom-call(f32[64,2048]{1,0:T(8,128)} %bitcast.34, bf16[16,8,128,128]{3,2,1,0:T(8,128)(2,1)} %bitcast.32), custom_call_target="tpu_custom_call" | custom-call | flops 603979776 | bytes 9437184 | tf_op jit(solution)/shard_map/pallas_call | solution.py:38
  11.9 0.0 collective-permute-done.1.refs_2_.refs_1_
  11.9 0.0 collective-permute-done.2.refs_3_.refs_2_
  11.9 5.1 %collective-permute-done.3.arrived.refs_5_ = bf16[16,64,128]{2,1,0:T(8,128)(2,1)S(1)} collective-permute-done((bf16[16,64,128]{2,1,0:T(8,128)(2,1)S(1)}, bf16[16,64,128]{2,1,0:T(8,128)(2,1)S(1)}, u32[]{:S(2)}, u32[]{:S(2)}) %collective-permute-start.3) | collective-permute-done | bytes 262176 | tf_op jit(solution)/shard_map/ppermute | solution.py:17
  16.9 0.1 broadcast_in_dim.28.table.refs_0_
  17.0 0.0 copy-done
  17.0 0.0 slice-start.1
  17.0 0.4 shard_map.76
  17.4 1.8 %collective-permute-start.4 = (bf16[4,64,128]{2,1,0:T(8,128)(2,1)S(1)}, bf16[4,64,128]{2,1,0:T(8,128)(2,1)S(1)}, u32[]{:S(2)}, u32[]{:S(2)}) collective-permute-start(bf16[4,64,128]{2,1,0:T(8,128)(2,1)S(1)} %get-tuple-element.41), channel_id=1, source_target_pairs={{0,1},{2,3},{4,5},{6,7},{1,0},{3,2},{5,4},{7,6},{8,9},{10,11},{12,... | collective-permute-start | bytes 196616 | tf_op jit(solution)/shard_map/ppermute | solution.py:23
  19.2 0.2 collective-permute-start.5
  19.4 0.6 shard_map.75
  20.0 0.1 collective-permute-start.6
  20.0 0.1 pad_add_fusion.1
  20.1 1.6 %collective-permute-done.4.left = bf16[4,64,128]{2,1,0:T(8,128)(2,1)S(1)} collective-permute-done((bf16[4,64,128]{2,1,0:T(8,128)(2,1)S(1)}, bf16[4,64,128]{2,1,0:T(8,128)(2,1)S(1)}, u32[]{:S(2)}, u32[]{:S(2)}) %collective-permute-start.4) | collective-permute-done | bytes 65568 | tf_op jit(solution)/shard_map/ppermute | solution.py:23
  21.7 4.4 %collective-permute-done.5.right = bf16[4,64,128]{2,1,0:T(8,128)(2,1)S(1)} collective-permute-done((bf16[4,64,128]{2,1,0:T(8,128)(2,1)S(1)}, bf16[4,64,128]{2,1,0:T(8,128)(2,1)S(1)}, u32[]{:S(2)}, u32[]{:S(2)}) %collective-permute-start.5) | collective-permute-done | bytes 65568 | tf_op jit(solution)/shard_map/ppermute | solution.py:23
  26.2 0.0 collective-permute-done.6.sibling
  26.2 0.1 broadcast_in_dim.54.table.refs_0_
  26.3 0.1 shard_map.77
  26.4 3.1 %collective-permute-start.7 = (bf16[10,64,128]{2,1,0:T(8,128)(2,1)S(1)}, bf16[10,64,128]{2,1,0:T(8,128)(2,1)S(1)}, u32[]{:S(2)}, u32[]{:S(2)}) collective-permute-start(bf16[10,64,128]{2,1,0:T(8,128)(2,1)S(1)} %get-tuple-element.44), channel_id=1, source_target_pairs={{0,16},{8,24},{16,0},{24,8},{1,17},{9,25},{17,1},{25,9},{2,18},{10... | collective-permute-start | bytes 491528 | tf_op jit(solution)/shard_map/ppermute | solution.py:17
  29.5 1.1 %collective-permute-start.8 = (bf16[6,64,128]{2,1,0:T(8,128)(2,1)S(1)}, bf16[6,64,128]{2,1,0:T(8,128)(2,1)S(1)}, u32[]{:S(2)}, u32[]{:S(2)}) collective-permute-start(bf16[6,64,128]{2,1,0:T(8,128)(2,1)S(1)} %shard_map.78), channel_id=1, source_target_pairs={{0,16},{8,24},{16,0},{24,8},{1,17},{9,25},{17,1},{25,9},{2,18},{10... | collective-permute-start | bytes 294920 | tf_op jit(solution)/shard_map/ppermute | solution.py:17
  30.6 2.6 %shard_map.79.refs_5_.correction = f32[16,64,128]{2,1,0:T(8,128)S(1)} custom-call(s32[193,128]{1,0:T(8,128)S(1)} %broadcast_in_dim.54.table.refs_0_, f32[16,64,128]{2,1,0:T(8,128)S(1)} %get-tuple-element.39.current, bf16[16,64,128]{2,1,0:T(8,128)(2,1)S(1)} %get-tuple-element.40.first, bf16[28,64,128]{2,1,0:T(8,128)(2,1)S(1)} %get-tuple-element.45.extension, ...), custom_call_target="tpu_custom_call" | custom-call | flops 555778048 | bytes 8684032 | tf_op jit(solution)/shard_map/pallas_call | solution.py:38
  33.2 1.0 %collective-permute-done.8.refs_4_ = bf16[6,64,128]{2,1,0:T(8,128)(2,1)S(1)} collective-permute-done((bf16[6,64,128]{2,1,0:T(8,128)(2,1)S(1)}, bf16[6,64,128]{2,1,0:T(8,128)(2,1)S(1)}, u32[]{:S(2)}, u32[]{:S(2)}) %collective-permute-start.8) | collective-permute-done | bytes 98336 | tf_op jit(solution)/shard_map/ppermute | solution.py:17
  34.2 1.0 %shard_map.80 = (bf16[4,64,128]{2,1,0:T(8,128)(2,1)S(1)}, bf16[4,64,128]{2,1,0:T(8,128)(2,1)S(1)}, bf16[16,64,128]{2,1,0:T(8,128)(2,1)S(1)}) custom-call(s32[129,128]{1,0:T(8,128)S(1)} %broadcast_in_dim.28.table.refs_0_, s32[4,128]{1,0:T(4,128)S(1)} %collective-permute-done.1.refs_2_.refs_1_, s32[4,128]{1,0:T(4,128)S(1)} %collective-permute-done.2.refs_3_.refs_2_, ...), custom_call_target="tpu_custom_call" | custom-call | flops 348422144 | bytes 5444096 | tf_op jit(solution)/shard_map/pallas_call | solution.py:38
  35.1 1.7 %shard_map.81 = (f32[16,64,128]{2,1,0:T(8,128)S(1)}, bf16[16,64,128]{2,1,0:T(8,128)(2,1)S(1)}, bf16[4,64,128]{2,1,0:T(8,128)(2,1)S(1)}) custom-call(s32[129,128]{1,0:T(8,128)S(1)} %broadcast_in_dim.28.table.refs_0_, s32[4,128]{1,0:T(4,128)S(1)} %collective-permute-done.wanted, bf16[16,64,128]{2,1,0:T(8,128)(2,1)S(1)} %get-tuple-element.46.arrived, ...), custom_call_target="tpu_custom_call" | custom-call | flops 377651200 | bytes 5900800 | tf_op jit(solution)/shard_map/pallas_call | solution.py:38
  36.8 0.1 collective-permute-start.11
  36.9 0.1 collective-permute-start.9
  37.0 3.3 %collective-permute-start.10 = (bf16[4,64,128]{2,1,0:T(8,128)(2,1)S(1)}, bf16[4,64,128]{2,1,0:T(8,128)(2,1)S(1)}, u32[]{:S(2)}, u32[]{:S(2)}) collective-permute-start(bf16[4,64,128]{2,1,0:T(8,128)(2,1)S(1)} %get-tuple-element.49), channel_id=1, source_target_pairs={{1,2},{3,4},{5,6},{7,0},{2,1},{4,3},{6,5},{0,7},{9,10},{11,12},{13... | collective-permute-start | bytes 196616 | tf_op jit(solution)/shard_map/ppermute | solution.py:23
  40.3 0.0 collective-permute-done.11.refs_5_
  40.3 1.1 %collective-permute-done.9.refs_3_ = bf16[4,64,128]{2,1,0:T(8,128)(2,1)S(1)} collective-permute-done((bf16[4,64,128]{2,1,0:T(8,128)(2,1)S(1)}, bf16[4,64,128]{2,1,0:T(8,128)(2,1)S(1)}, u32[]{:S(2)}, u32[]{:S(2)}) %collective-permute-start.9) | collective-permute-done | bytes 65568 | tf_op jit(solution)/shard_map/ppermute | solution.py:23
  41.4 2.7 %collective-permute-done.10.refs_4_ = bf16[4,64,128]{2,1,0:T(8,128)(2,1)S(1)} collective-permute-done((bf16[4,64,128]{2,1,0:T(8,128)(2,1)S(1)}, bf16[4,64,128]{2,1,0:T(8,128)(2,1)S(1)}, u32[]{:S(2)}, u32[]{:S(2)}) %collective-permute-start.10) | collective-permute-done | bytes 65568 | tf_op jit(solution)/shard_map/ppermute | solution.py:23
  44.1 1.5 %shard_map.82 = (f32[10,64,128]{2,1,0:T(8,128)S(1)}, bf16[10,64,128]{2,1,0:T(8,128)(2,1)S(1)}, bf16[28,64,128]{2,1,0:T(8,128)(2,1)S(1)}) custom-call(s32[193,128]{1,0:T(8,128)S(1)} %broadcast_in_dim.54.table.refs_0_, f32[16,64,128]{2,1,0:T(8,128)S(1)} %get-tuple-element.37.loads.residual.refs_1_.refs_4_, bf16[16,64,128]{2,1,0:T(8,128)(2,1)S(1)} %get-tuple-element.47.refs_2_, ...), custom_call_target="tpu_custom_call" | custom-call | flops 532709376 | bytes 8323584 | tf_op jit(solution)/shard_map/pallas_call | solution.py:38
  45.6 0.1 collective-permute-start.12
  45.7 1.0 %shard_map.83 = (f32[6,64,128]{2,1,0:T(8,128)S(1)}, bf16[6,64,128]{2,1,0:T(8,128)(2,1)S(1)}) custom-call(s32[193,128]{1,0:T(8,128)S(1)} %broadcast_in_dim.54.table.refs_0_, f32[16,64,128]{2,1,0:T(8,128)S(1)} %get-tuple-element.37.loads.residual.refs_1_.refs_4_, bf16[28,64,128]{2,1,0:T(8,128)(2,1)S(1)} %get-tuple-element.52.refs_2_, ...), custom_call_target="tpu_custom_call" | custom-call | flops 490766336 | bytes 7668224 | tf_op jit(solution)/shard_map/pallas_call | solution.py:38
  46.7 1.1 %collective-permute-start.13 = (bf16[6,64,128]{2,1,0:T(8,128)(2,1)S(1)}, bf16[6,64,128]{2,1,0:T(8,128)(2,1)S(1)}, u32[]{:S(2)}, u32[]{:S(2)}) collective-permute-start(bf16[6,64,128]{2,1,0:T(8,128)(2,1)S(1)} %get-tuple-element.55), channel_id=1, source_target_pairs={{0,16},{8,24},{16,0},{24,8},{1,17},{9,25},{17,1},{25,9},{2,18},{10... | collective-permute-start | bytes 294920 | tf_op jit(solution)/shard_map/ppermute | solution.py:17
  47.8 5.6 %collective-permute-done.13.refs_7_ = bf16[6,64,128]{2,1,0:T(8,128)(2,1)S(1)} collective-permute-done((bf16[6,64,128]{2,1,0:T(8,128)(2,1)S(1)}, bf16[6,64,128]{2,1,0:T(8,128)(2,1)S(1)}, u32[]{:S(2)}, u32[]{:S(2)}) %collective-permute-start.13) | collective-permute-done | bytes 98336 | tf_op jit(solution)/shard_map/ppermute | solution.py:17
  53.4 0.0 collective-permute-done.12.refs_6_
  53.4 0.4 shard_map.84
  53.8 0.6 shard_map.85
  54.4 0.1 collective-permute-start.16
  54.5 0.1 collective-permute-start.14
  54.6 3.3 %collective-permute-start.15 = (bf16[4,64,128]{2,1,0:T(8,128)(2,1)S(1)}, bf16[4,64,128]{2,1,0:T(8,128)(2,1)S(1)}, u32[]{:S(2)}, u32[]{:S(2)}) collective-permute-start(bf16[4,64,128]{2,1,0:T(8,128)(2,1)S(1)} %get-tuple-element.61), channel_id=1, source_target_pairs={{1,2},{3,4},{5,6},{7,0},{2,1},{4,3},{6,5},{0,7},{9,10},{11,12},{13... | collective-permute-start | bytes 196616 | tf_op jit(solution)/shard_map/ppermute | solution.py:23
  57.9 1.1 %collective-permute-done.14.left = bf16[4,64,128]{2,1,0:T(8,128)(2,1)S(1)} collective-permute-done((bf16[4,64,128]{2,1,0:T(8,128)(2,1)S(1)}, bf16[4,64,128]{2,1,0:T(8,128)(2,1)S(1)}, u32[]{:S(2)}, u32[]{:S(2)}) %collective-permute-start.14) | collective-permute-done | bytes 65568 | tf_op jit(solution)/shard_map/ppermute | solution.py:23
  59.0 2.7 %collective-permute-done.15.right = bf16[4,64,128]{2,1,0:T(8,128)(2,1)S(1)} collective-permute-done((bf16[4,64,128]{2,1,0:T(8,128)(2,1)S(1)}, bf16[4,64,128]{2,1,0:T(8,128)(2,1)S(1)}, u32[]{:S(2)}, u32[]{:S(2)}) %collective-permute-start.15) | collective-permute-done | bytes 65568 | tf_op jit(solution)/shard_map/ppermute | solution.py:23
  61.7 0.3 shard_map.86
  62.0 4.4 %collective-permute-start.17 = (bf16[10,64,128]{2,1,0:T(8,128)(2,1)S(1)}, bf16[10,64,128]{2,1,0:T(8,128)(2,1)S(1)}, u32[]{:S(2)}, u32[]{:S(2)}) collective-permute-start(bf16[10,64,128]{2,1,0:T(8,128)(2,1)S(1)} %get-tuple-element.63), channel_id=1, source_target_pairs={{0,16},{8,24},{16,0},{24,8},{1,17},{9,25},{17,1},{25,9},{2,18},{10... | collective-permute-start | bytes 491528 | tf_op jit(solution)/shard_map/ppermute | solution.py:17
  66.4 1.2 %collective-permute-start.18 = (bf16[6,64,128]{2,1,0:T(8,128)(2,1)S(1)}, bf16[6,64,128]{2,1,0:T(8,128)(2,1)S(1)}, u32[]{:S(2)}, u32[]{:S(2)}) collective-permute-start(bf16[6,64,128]{2,1,0:T(8,128)(2,1)S(1)} %get-tuple-element.65), channel_id=1, source_target_pairs={{0,16},{8,24},{16,0},{24,8},{1,17},{9,25},{17,1},{25,9},{2,18},{10... | collective-permute-start | bytes 294920 | tf_op jit(solution)/shard_map/ppermute | solution.py:17
  67.6 2.6 %shard_map.88.correction = f32[16,64,128]{2,1,0:T(8,128)S(1)} custom-call(s32[193,128]{1,0:T(8,128)S(1)} %broadcast_in_dim.54.table.refs_0_, f32[16,64,128]{2,1,0:T(8,128)S(1)} %get-tuple-element.58.current, bf16[16,64,128]{2,1,0:T(8,128)(2,1)S(1)} %get-tuple-element.59.first, bf16[28,64,128]{2,1,0:T(8,128)(2,1)S(1)} %get-tuple-element.64.extension, ...), custom_call_target="tpu_custom_call" | custom-call | flops 555778048 | bytes 8684032 | tf_op jit(solution)/shard_map/pallas_call | solution.py:38
  70.2 2.2 %collective-permute-done.18.late = bf16[6,64,128]{2,1,0:T(8,128)(2,1)S(1)} collective-permute-done((bf16[6,64,128]{2,1,0:T(8,128)(2,1)S(1)}, bf16[6,64,128]{2,1,0:T(8,128)(2,1)S(1)}, u32[]{:S(2)}, u32[]{:S(2)}) %collective-permute-start.18) | collective-permute-done | bytes 98336 | tf_op jit(solution)/shard_map/ppermute | solution.py:17
  72.3 0.0 collective-permute-done.17.early
  72.3 2.5 %shard_map.89 = f32[64,2048]{1,0:T(8,128)} custom-call(s32[129,128]{1,0:T(8,128)S(1)} %broadcast_in_dim.28.table.refs_0_, bf16[10,64,128]{2,1,0:T(8,128)(2,1)S(1)} %collective-permute-done.17.early, bf16[6,64,128]{2,1,0:T(8,128)(2,1)S(1)} %collective-permute-done.18.late, f32[16,64,128]{2,1,0:T(8,128)S(1)} %shard_map.88.correction, ...), custom_call_target="tpu_custom_call" | custom-call | flops 423657472 | bytes 6619648 | tf_op jit(solution)/shard_map/pallas_call | solution.py:38
  (16 shorter events, 0.1 us)
Async XLA Ops:
  0.8 11.1 %collective-permute-start.1 = (s32[4,128]{1,0:T(4,128)S(1)}, s32[4,128]{1,0:T(4,128)S(1)}, u32[]{:S(2)}, u32[]{:S(2)}) collective-permute-start(s32[4,128]{1,0:T(4,128)S(1)} %broadcast_in_dim.57), channel_id=1, source_target_pairs={{1,2},{3,4},{5,6},{7,0},{2,1},{4,3},{6,5},{0,7},{9,10},{11,12},{13... | collective-permute-start | bytes 6152 | tf_op jit(solution)/shard_map/ppermute | solution.py:23
  6.9 12.5 %collective-permute-start = (s32[4,128]{1,0:T(4,128)S(1)}, s32[4,128]{1,0:T(4,128)S(1)}, u32[]{:S(2)}, u32[]{:S(2)}) collective-permute-start(s32[4,128]{1,0:T(4,128)S(1)} %broadcast_in_dim.56), channel_id=1, source_target_pairs={{0,8},{8,0},{16,24},{24,16},{1,9},{9,1},{17,25},{25,17},{2,10},{10... | collective-permute-start | bytes 6152 | tf_op jit(solution)/shard_map/ppermute | solution.py:17
  6.9 4.9 %collective-permute-start.2 = (s32[4,128]{1,0:T(4,128)S(1)}, s32[4,128]{1,0:T(4,128)S(1)}, u32[]{:S(2)}, u32[]{:S(2)}) collective-permute-start(s32[4,128]{1,0:T(4,128)S(1)} %broadcast_in_dim.58), channel_id=1, source_target_pairs={{0,1},{2,3},{4,5},{6,7},{1,0},{3,2},{5,4},{7,6},{8,9},{10,11},{12,... | collective-permute-start | bytes 6152 | tf_op jit(solution)/shard_map/ppermute | solution.py:23
  6.9 1.8 %copy-start.1 = (s32[1,16,12]{1,0,2:T(1,128)S(1)}, s32[1,16,12]{1,0,2:T(1,128)}, u32[]{:S(2)}) copy-start(s32[1,16,12]{1,0,2:T(1,128)} %param.9) | copy-start | bytes 2308
  6.9 1.9 %copy-start.2 = (s32[1,16,8]{1,2,0:T(8,128)S(1)}, s32[1,16,8]{1,2,0:T(8,128)}, u32[]{:S(2)}) copy-start(s32[1,16,8]{1,2,0:T(8,128)} %param.12) | copy-start | bytes 1540
  8.1 8.9 %copy-start = (bf16[1,16,128,128]{3,2,1,0:T(8,128)(2,1)S(1)}, bf16[1,16,128,128]{3,2,1,0:T(8,128)(2,1)}, u32[]{:S(2)}) copy-start(bf16[1,16,128,128]{3,2,1,0:T(8,128)(2,1)} %param.10) | copy-start | bytes 1572868
  8.2 8.8 %collective-permute-start.3 = (bf16[16,64,128]{2,1,0:T(8,128)(2,1)S(1)}, bf16[16,64,128]{2,1,0:T(8,128)(2,1)S(1)}, u32[]{:S(2)}, u32[]{:S(2)}) collective-permute-start(bf16[16,64,128]{2,1,0:T(8,128)(2,1)S(1)} %shard_map.74), channel_id=1, source_target_pairs={{0,16},{8,24},{16,0},{24,8},{1,17},{9,25},{17,1},{25,9},{2,18},{10... | collective-permute-start | bytes 786440 | tf_op jit(solution)/shard_map/ppermute | solution.py:17
  9.1 17.2 %slice-start = ((s8[6291456]{0:T(1024)(128)(4,1)}), s8[4194304]{0:T(1024)(128)(4,1)S(1)}, s32[]{:S(2)}) async-start(s8[6291456]{0:T(1024)(128)(4,1)} %bitcast.12), calls=%async_computation | async-start | bytes 8388608
  17.0 9.2 %slice-start.1 = ((s8[6291456]{0:T(1024)(128)(4,1)}), s8[2097152]{0:T(1024)(128)(4,1)S(1)}, s32[]{:S(2)}) async-start(s8[6291456]{0:T(1024)(128)(4,1)} %bitcast.12), calls=%async_computation.1 | async-start | bytes 4194304
  17.4 4.3 %collective-permute-start.4 = (bf16[4,64,128]{2,1,0:T(8,128)(2,1)S(1)}, bf16[4,64,128]{2,1,0:T(8,128)(2,1)S(1)}, u32[]{:S(2)}, u32[]{:S(2)}) collective-permute-start(bf16[4,64,128]{2,1,0:T(8,128)(2,1)S(1)} %get-tuple-element.41), channel_id=1, source_target_pairs={{0,1},{2,3},{4,5},{6,7},{1,0},{3,2},{5,4},{7,6},{8,9},{10,11},{12,... | collective-permute-start | bytes 196616 | tf_op jit(solution)/shard_map/ppermute | solution.py:23
  19.2 7.0 %collective-permute-start.5 = (bf16[4,64,128]{2,1,0:T(8,128)(2,1)S(1)}, bf16[4,64,128]{2,1,0:T(8,128)(2,1)S(1)}, u32[]{:S(2)}, u32[]{:S(2)}) collective-permute-start(bf16[4,64,128]{2,1,0:T(8,128)(2,1)S(1)} %get-tuple-element.42), channel_id=1, source_target_pairs={{1,2},{3,4},{5,6},{7,0},{2,1},{4,3},{6,5},{0,7},{9,10},{11,12},{13... | collective-permute-start | bytes 196616 | tf_op jit(solution)/shard_map/ppermute | solution.py:23
  20.0 6.2 %collective-permute-start.6 = (bf16[4,64,128]{2,1,0:T(8,128)(2,1)S(1)}, bf16[4,64,128]{2,1,0:T(8,128)(2,1)S(1)}, u32[]{:S(2)}, u32[]{:S(2)}) collective-permute-start(bf16[4,64,128]{2,1,0:T(8,128)(2,1)S(1)} %get-tuple-element.43), channel_id=1, source_target_pairs={{0,8},{8,0},{16,24},{24,16},{1,9},{9,1},{17,25},{25,17},{2,10},{10... | collective-permute-start | bytes 196616 | tf_op jit(solution)/shard_map/ppermute | solution.py:17
  26.4 7.8 %collective-permute-start.7 = (bf16[10,64,128]{2,1,0:T(8,128)(2,1)S(1)}, bf16[10,64,128]{2,1,0:T(8,128)(2,1)S(1)}, u32[]{:S(2)}, u32[]{:S(2)}) collective-permute-start(bf16[10,64,128]{2,1,0:T(8,128)(2,1)S(1)} %get-tuple-element.44), channel_id=1, source_target_pairs={{0,16},{8,24},{16,0},{24,8},{1,17},{9,25},{17,1},{25,9},{2,18},{10... | collective-permute-start | bytes 491528 | tf_op jit(solution)/shard_map/ppermute | solution.py:17
  29.5 4.7 %collective-permute-start.8 = (bf16[6,64,128]{2,1,0:T(8,128)(2,1)S(1)}, bf16[6,64,128]{2,1,0:T(8,128)(2,1)S(1)}, u32[]{:S(2)}, u32[]{:S(2)}) collective-permute-start(bf16[6,64,128]{2,1,0:T(8,128)(2,1)S(1)} %shard_map.78), channel_id=1, source_target_pairs={{0,16},{8,24},{16,0},{24,8},{1,17},{9,25},{17,1},{25,9},{2,18},{10... | collective-permute-start | bytes 294920 | tf_op jit(solution)/shard_map/ppermute | solution.py:17
  36.8 3.4 %collective-permute-start.11 = (bf16[4,64,128]{2,1,0:T(8,128)(2,1)S(1)}, bf16[4,64,128]{2,1,0:T(8,128)(2,1)S(1)}, u32[]{:S(2)}, u32[]{:S(2)}) collective-permute-start(bf16[4,64,128]{2,1,0:T(8,128)(2,1)S(1)} %get-tuple-element.50), channel_id=1, source_target_pairs={{0,8},{8,0},{16,24},{24,16},{1,9},{9,1},{17,25},{25,17},{2,10},{10... | collective-permute-start | bytes 196616 | tf_op jit(solution)/shard_map/ppermute | solution.py:17
  36.9 4.5 %collective-permute-start.9 = (bf16[4,64,128]{2,1,0:T(8,128)(2,1)S(1)}, bf16[4,64,128]{2,1,0:T(8,128)(2,1)S(1)}, u32[]{:S(2)}, u32[]{:S(2)}) collective-permute-start(bf16[4,64,128]{2,1,0:T(8,128)(2,1)S(1)} %get-tuple-element.48), channel_id=1, source_target_pairs={{0,1},{2,3},{4,5},{6,7},{1,0},{3,2},{5,4},{7,6},{8,9},{10,11},{12,... | collective-permute-start | bytes 196616 | tf_op jit(solution)/shard_map/ppermute | solution.py:23
  37.0 7.1 %collective-permute-start.10 = (bf16[4,64,128]{2,1,0:T(8,128)(2,1)S(1)}, bf16[4,64,128]{2,1,0:T(8,128)(2,1)S(1)}, u32[]{:S(2)}, u32[]{:S(2)}) collective-permute-start(bf16[4,64,128]{2,1,0:T(8,128)(2,1)S(1)} %get-tuple-element.49), channel_id=1, source_target_pairs={{1,2},{3,4},{5,6},{7,0},{2,1},{4,3},{6,5},{0,7},{9,10},{11,12},{13... | collective-permute-start | bytes 196616 | tf_op jit(solution)/shard_map/ppermute | solution.py:23
  45.6 7.8 %collective-permute-start.12 = (bf16[10,64,128]{2,1,0:T(8,128)(2,1)S(1)}, bf16[10,64,128]{2,1,0:T(8,128)(2,1)S(1)}, u32[]{:S(2)}, u32[]{:S(2)}) collective-permute-start(bf16[10,64,128]{2,1,0:T(8,128)(2,1)S(1)} %get-tuple-element.54), channel_id=1, source_target_pairs={{0,16},{8,24},{16,0},{24,8},{1,17},{9,25},{17,1},{25,9},{2,18},{10... | collective-permute-start | bytes 491528 | tf_op jit(solution)/shard_map/ppermute | solution.py:17
  46.7 6.7 %collective-permute-start.13 = (bf16[6,64,128]{2,1,0:T(8,128)(2,1)S(1)}, bf16[6,64,128]{2,1,0:T(8,128)(2,1)S(1)}, u32[]{:S(2)}, u32[]{:S(2)}) collective-permute-start(bf16[6,64,128]{2,1,0:T(8,128)(2,1)S(1)} %get-tuple-element.55), channel_id=1, source_target_pairs={{0,16},{8,24},{16,0},{24,8},{1,17},{9,25},{17,1},{25,9},{2,18},{10... | collective-permute-start | bytes 294920 | tf_op jit(solution)/shard_map/ppermute | solution.py:17
  54.4 3.4 %collective-permute-start.16 = (bf16[4,64,128]{2,1,0:T(8,128)(2,1)S(1)}, bf16[4,64,128]{2,1,0:T(8,128)(2,1)S(1)}, u32[]{:S(2)}, u32[]{:S(2)}) collective-permute-start(bf16[4,64,128]{2,1,0:T(8,128)(2,1)S(1)} %get-tuple-element.62), channel_id=1, source_target_pairs={{0,8},{8,0},{16,24},{24,16},{1,9},{9,1},{17,25},{25,17},{2,10},{10... | collective-permute-start | bytes 196616 | tf_op jit(solution)/shard_map/ppermute | solution.py:17
  54.5 4.5 %collective-permute-start.14 = (bf16[4,64,128]{2,1,0:T(8,128)(2,1)S(1)}, bf16[4,64,128]{2,1,0:T(8,128)(2,1)S(1)}, u32[]{:S(2)}, u32[]{:S(2)}) collective-permute-start(bf16[4,64,128]{2,1,0:T(8,128)(2,1)S(1)} %get-tuple-element.60), channel_id=1, source_target_pairs={{0,1},{2,3},{4,5},{6,7},{1,0},{3,2},{5,4},{7,6},{8,9},{10,11},{12,... | collective-permute-start | bytes 196616 | tf_op jit(solution)/shard_map/ppermute | solution.py:23
  54.6 7.1 %collective-permute-start.15 = (bf16[4,64,128]{2,1,0:T(8,128)(2,1)S(1)}, bf16[4,64,128]{2,1,0:T(8,128)(2,1)S(1)}, u32[]{:S(2)}, u32[]{:S(2)}) collective-permute-start(bf16[4,64,128]{2,1,0:T(8,128)(2,1)S(1)} %get-tuple-element.61), channel_id=1, source_target_pairs={{1,2},{3,4},{5,6},{7,0},{2,1},{4,3},{6,5},{0,7},{9,10},{11,12},{13... | collective-permute-start | bytes 196616 | tf_op jit(solution)/shard_map/ppermute | solution.py:23
  62.0 10.4 %collective-permute-start.17 = (bf16[10,64,128]{2,1,0:T(8,128)(2,1)S(1)}, bf16[10,64,128]{2,1,0:T(8,128)(2,1)S(1)}, u32[]{:S(2)}, u32[]{:S(2)}) collective-permute-start(bf16[10,64,128]{2,1,0:T(8,128)(2,1)S(1)} %get-tuple-element.63), channel_id=1, source_target_pairs={{0,16},{8,24},{16,0},{24,8},{1,17},{9,25},{17,1},{25,9},{2,18},{10... | collective-permute-start | bytes 491528 | tf_op jit(solution)/shard_map/ppermute | solution.py:17
  66.4 5.9 %collective-permute-start.18 = (bf16[6,64,128]{2,1,0:T(8,128)(2,1)S(1)}, bf16[6,64,128]{2,1,0:T(8,128)(2,1)S(1)}, u32[]{:S(2)}, u32[]{:S(2)}) collective-permute-start(bf16[6,64,128]{2,1,0:T(8,128)(2,1)S(1)} %get-tuple-element.65), channel_id=1, source_target_pairs={{0,16},{8,24},{16,0},{24,8},{1,17},{9,25},{17,1},{25,9},{2,18},{10... | collective-permute-start | bytes 294920 | tf_op jit(solution)/shard_map/ppermute | solution.py:17
